TPU v7x, 32 devices: a whole 2x2x4 slice. The times are simulated.
32 devices in a mesh: dp: 4 (over x, core), fsdp: 8 (over z, y).
Axes of the slice: x: 2, y: 2, z: 4, core: 2. Of those that a mesh axis runs over, the one named last changes fastest.
Arguments:
- tokens: bfloat16 [32, 256, 768], P(('dp', 'fsdp')), may hold values from -6 to 6
- lengths: int32 [32], P(('dp', 'fsdp')), may hold values from 129 to 256
- query_weight: bfloat16 [2, 768, 768], P(None, ('dp', 'fsdp')), may hold values from -0.21875 to 0.21875
- key_weight: bfloat16 [2, 768, 768], P(None, ('dp', 'fsdp')), may hold values from -0.21875 to 0.21875
- value_weight: bfloat16 [2, 768, 768], P(None, ('dp', 'fsdp')), may hold values from -0.21875 to 0.21875
- attn_out_weight: bfloat16 [2, 768, 768], P(None, ('dp', 'fsdp')), may hold values from -1.75 to 1.75
- up_weight: bfloat16 [2, 768, 3072], P(None, ('dp', 'fsdp')), may hold values from -0.21875 to 0.21875
- down_weight: bfloat16 [2, 3072, 768], P(None, None, ('dp', 'fsdp')), may hold values from -0.109375 to 0.109375
- norm_gains: bfloat16 [2, 2, 768], P(None, None, ('dp', 'fsdp')), may hold values from 0.5 to 1.5
- cotangent: bfloat16 [32, 256, 768], P(('dp', 'fsdp')), may hold values from -6 to 6
Outputs:
- activations: bfloat16 [32, 256, 768], P(('dp', 'fsdp'))
- input_grad: float32 [32, 256, 768], P(('dp', 'fsdp'))
- grad_query: float32 [2, 768, 768], P(None, ('dp', 'fsdp'))
- grad_key: float32 [2, 768, 768], P(None, ('dp', 'fsdp'))
- grad_value: float32 [2, 768, 768], P(None, ('dp', 'fsdp'))
- grad_attn_out: float32 [2, 768, 768], P(None, ('dp', 'fsdp'))
- grad_up: float32 [2, 768, 3072], P(None, ('dp', 'fsdp'))
- grad_down: float32 [2, 3072, 768], P(None, None, ('dp', 'fsdp'))
- grad_gains: float32 [2, 2, 768], P(None, None, ('dp', 'fsdp'))
All inputs are finite; a program needn't handle non-finite values.
Results may differ from a plain program's by a relative error of at most 0.025.
Values may be sent and summed in bfloat16 or wider, within the bound.
No kernel may reach another device: no remote copies, remote signals or barrier semaphores. Data moves between devices by JAX's collectives and lax.ppermute only.
A program may use at most 256 MiB of HBM per device.

v0:
```python
import jax
import jax.numpy as jnp
from jax import lax
from jax.sharding import PartitionSpec as P

D = 768
HEADS = 12
HEAD_DIM = 64
FF = 3072
LAYERS = 2


def norm(value, gain):
    centred = value - jnp.mean(value, axis=-1, keepdims=True)
    spread = jnp.mean(centred * centred, axis=-1, keepdims=True)
    return centred * lax.rsqrt(spread + 1e-05) * gain


def gelu_tanh(value):
    return jax.nn.gelu(value, approximate=True)


def product(left, right):
    return jnp.dot(left, right, preferred_element_type=jnp.float32)


def product_left_t(left, right):
    return lax.dot_general(
        left, right, (((0,), (0,)), ((), ())), preferred_element_type=jnp.float32
    )


def product_right_t(left, right):
    return lax.dot_general(
        left, right, (((1,), (1,)), ((), ())), preferred_element_type=jnp.float32
    )


def collect(shards, layer):
    pieces = tuple((member[layer] for member in shards))
    return (
        lax.all_gather(pieces[0], ("dp", "fsdp"), axis=0, tiled=True),
        lax.all_gather(pieces[1], ("dp", "fsdp"), axis=0, tiled=True),
        lax.all_gather(pieces[2], ("dp", "fsdp"), axis=0, tiled=True),
        lax.all_gather(pieces[3], ("dp", "fsdp"), axis=0, tiled=True),
        lax.all_gather(pieces[4], ("dp", "fsdp"), axis=0, tiled=True),
        lax.all_gather(pieces[5], ("dp", "fsdp"), axis=1, tiled=True),
        lax.all_gather(pieces[6], ("dp", "fsdp"), axis=1, tiled=True),
    )


def collect_again(shards, layer):
    pieces = tuple((member[layer] for member in shards))
    return (
        lax.all_gather(pieces[0], ("dp", "fsdp"), axis=0, tiled=True),
        lax.all_gather(pieces[1], ("dp", "fsdp"), axis=0, tiled=True),
        lax.all_gather(pieces[2], ("dp", "fsdp"), axis=0, tiled=True),
        lax.all_gather(pieces[3], ("dp", "fsdp"), axis=0, tiled=True),
        lax.all_gather(pieces[4], ("dp", "fsdp"), axis=0, tiled=True),
        lax.all_gather(pieces[5], ("dp", "fsdp"), axis=1, tiled=True),
        lax.all_gather(pieces[6], ("dp", "fsdp"), axis=1, tiled=True),
    )


def visible_keys(length, token_count, swap):
    half = token_count // 2
    positions = lax.broadcasted_iota(jnp.int32, (2, half), 0) * half + lax.broadcasted_iota(
        jnp.int32, (2, half), 1
    )
    if swap:
        positions = positions[::-1]
    return positions < length


def split_heads(value):
    return value.reshape(2, value.shape[0] // 2, HEADS, HEAD_DIM)


def paired_heads(query, keys, values, swap):
    query_heads = split_heads(query)
    key_heads = split_heads(keys)
    value_heads = split_heads(values)
    if swap:
        key_heads = key_heads[::-1]
        value_heads = value_heads[::-1]
    return (query_heads, key_heads, value_heads)


def masked_scores(query_heads, key_heads, visible):
    scores = (
        jnp.einsum("bqhd,bkhd->bhqk", query_heads, key_heads, preferred_element_type=jnp.float32)
        * 0.125
    )
    return jnp.where(visible[:, None, None, :], scores, -1e30)


def attend_forward(query, keys, values, visible, swap):
    token_count = query.shape[0]
    query_heads, key_heads, value_heads = paired_heads(query, keys, values, swap)
    scores = masked_scores(query_heads, key_heads, visible)
    highest = jnp.max(scores, axis=-1, keepdims=True)
    raised = jnp.exp(scores - highest)
    total = jnp.sum(raised, axis=-1, keepdims=True)
    shares = (raised / total).astype(jnp.bfloat16)
    mixed = jnp.einsum("bhqk,bkhd->bqhd", shares, value_heads, preferred_element_type=jnp.float32)
    return (mixed.reshape(token_count, -1), highest + jnp.log(total))


def attend_backward(query, keys, values, visible, swap, log_total, grad_mixed):
    token_count = query.shape[0]
    query_heads, key_heads, value_heads = paired_heads(query, keys, values, swap)
    scores = masked_scores(query_heads, key_heads, visible)
    shares = jnp.exp(scores - log_total)
    shares_low = shares.astype(jnp.bfloat16)
    grad_heads = split_heads(grad_mixed)
    grad_values = jnp.einsum(
        "bhqk,bqhd->bkhd", shares_low, grad_heads, preferred_element_type=jnp.float32
    )
    grad_shares = jnp.einsum(
        "bqhd,bkhd->bhqk", grad_heads, value_heads, preferred_element_type=jnp.float32
    )
    inner = jnp.sum(shares * grad_shares, axis=-1, keepdims=True)
    grad_scores = (shares * (grad_shares - inner)).astype(jnp.bfloat16)
    grad_query = (
        jnp.einsum("bhqk,bkhd->bqhd", grad_scores, key_heads, preferred_element_type=jnp.float32)
        * 0.125
    )
    grad_keys = (
        jnp.einsum("bhqk,bqhd->bkhd", grad_scores, query_heads, preferred_element_type=jnp.float32)
        * 0.125
    )
    if swap:
        grad_keys = grad_keys[::-1]
        grad_values = grad_values[::-1]
    return tuple(
        (
            member.reshape(token_count, -1).astype(jnp.bfloat16)
            for member in (grad_query, grad_keys, grad_values)
        )
    )


def layer_forward(hidden, length, weights, swap):
    query_w, key_w, value_w, out_w, up_w, down_w, gains = weights
    gain_first = gains[0].astype(jnp.float32)
    gain_second = gains[1].astype(jnp.float32)
    inputs_low = hidden.astype(jnp.bfloat16)
    query = product(inputs_low, query_w).astype(jnp.bfloat16)
    keys = product(inputs_low, key_w).astype(jnp.bfloat16)
    values = product(inputs_low, value_w).astype(jnp.bfloat16)
    visible = visible_keys(length, hidden.shape[0], swap)
    mixed, log_total = attend_forward(query, keys, values, visible, swap)
    mixed_low = mixed.astype(jnp.bfloat16)
    first_sum = hidden + product(mixed_low, out_w)
    normed = norm(first_sum, gain_first)
    normed_low = normed.astype(jnp.bfloat16)
    expanded = product(normed_low, up_w)
    activated = gelu_tanh(expanded).astype(jnp.bfloat16)
    second_sum = normed + product(activated, down_w)
    output = norm(second_sum, gain_second)
    kept = (
        inputs_low,
        query,
        keys,
        values,
        log_total,
        mixed_low,
        first_sum,
        normed_low,
        expanded,
        activated,
        second_sum,
    )
    return (output, kept)


def layer_backward(grad_output, kept, weights, swap, length):
    query_w, key_w, value_w, out_w, up_w, down_w, gains = weights
    (
        inputs_low,
        query,
        keys,
        values,
        log_total,
        mixed_low,
        first_sum,
        normed_low,
        expanded,
        activated,
        second_sum,
    ) = kept
    gain_first = gains[0].astype(jnp.float32)
    gain_second = gains[1].astype(jnp.float32)
    grad_second, grad_gain_second = jax.vjp(norm, second_sum, gain_second)[1](grad_output)
    down_low = grad_second.astype(jnp.bfloat16)
    grad_active = product_right_t(down_low, down_w)
    up_low = jax.vjp(gelu_tanh, expanded)[1](grad_active)[0].astype(jnp.bfloat16)
    grad_normed = grad_second + product_right_t(up_low, up_w)
    grad_first, grad_gain_first = jax.vjp(norm, first_sum, gain_first)[1](grad_normed)
    attn_low = grad_first.astype(jnp.bfloat16)
    grad_mixed = product_right_t(attn_low, out_w).astype(jnp.bfloat16)
    visible = visible_keys(length, query.shape[0], swap)
    grad_query, grad_keys, grad_values = attend_backward(
        query, keys, values, visible, swap, log_total, grad_mixed
    )
    grad_inputs = (
        grad_first
        + product_right_t(grad_query, query_w)
        + product_right_t(grad_keys, key_w)
        + product_right_t(grad_values, value_w)
    )
    gain_pair = jnp.stack([grad_gain_first, grad_gain_second], axis=1)
    context = (
        inputs_low,
        grad_query,
        grad_keys,
        grad_values,
        mixed_low,
        attn_low,
        normed_low,
        up_low,
        down_low,
        activated,
        gain_pair,
    )
    return (grad_inputs, context)


def weight_terms(contexts):
    result = []
    for context in contexts:
        (
            inputs_low,
            grad_query,
            grad_keys,
            grad_values,
            mixed_low,
            attn_low,
            normed_low,
            up_low,
            down_low,
            activated,
            gain_pair,
        ) = context
        result.append(product_left_t(inputs_low, grad_query))
        result.append(product_left_t(inputs_low, grad_keys))
        result.append(product_left_t(inputs_low, grad_values))
        result.append(product_left_t(mixed_low, attn_low))
        result.append(product_left_t(normed_low, up_low))
        result.append(product_left_t(down_low, activated))
        result.append(gain_pair)
    return jnp.concatenate(result, axis=1)


def arrange(summed):
    width = 4 * D + 2 * FF + 2
    bounds = [0, D, 2 * D, 3 * D, 4 * D, 4 * D + FF, 4 * D + 2 * FF, width]
    member = [summed[:, bounds[j] : bounds[j + 1]] for j in range(7)]
    grouped = [(member[0], member[1], member[2], member[3], member[4], member[5].T, member[6].T)]
    return grouped


def per_device(
    tokens,
    lengths,
    query_weight,
    key_weight,
    value_weight,
    attn_out_weight,
    up_weight,
    down_weight,
    norm_gains,
    cotangent,
):
    shards = (
        query_weight,
        key_weight,
        value_weight,
        attn_out_weight,
        up_weight,
        down_weight,
        norm_gains,
    )
    hidden = tokens[0].astype(jnp.float32)
    length = lengths[0]
    gathered_all = []
    kept_all = []
    for layer in range(LAYERS):
        gathered = collect(shards, layer)
        hidden, kept = layer_forward(hidden, length, gathered, layer % 2 == 1)
        gathered_all.append(gathered)
        kept_all.append(kept)
    activations = hidden.astype(jnp.bfloat16)[None]
    grad_hidden = cotangent[0].astype(jnp.float32)
    layer_grads = [None] * LAYERS
    for layer in reversed(range(LAYERS)):
        weights_now = collect_again(shards, layer)
        grad_hidden, context = layer_backward(
            grad_hidden, kept_all[layer], weights_now, layer % 2 == 1, length
        )
        summed = lax.psum_scatter(
            weight_terms([context]), ("dp", "fsdp"), scatter_dimension=0, tiled=True
        )
        layer_grads[layer] = arrange(summed)[0]
    stacked = tuple((jnp.stack([entry[member] for entry in layer_grads]) for member in range(7)))
    return (
        activations,
        grad_hidden[None],
        stacked[0],
        stacked[1],
        stacked[2],
        stacked[3],
        stacked[4],
        stacked[5],
        stacked[6],
    )


def solution(mesh):
    placed = (
        P(("dp", "fsdp"), None, None),
        P(("dp", "fsdp")),
        P(None, ("dp", "fsdp"), None),
        P(None, ("dp", "fsdp"), None),
        P(None, ("dp", "fsdp"), None),
        P(None, ("dp", "fsdp"), None),
        P(None, ("dp", "fsdp"), None),
        P(None, None, ("dp", "fsdp")),
        P(None, None, ("dp", "fsdp")),
        P(("dp", "fsdp"), None, None),
    )
    return jax.shard_map(
        per_device,
        mesh=mesh,
        in_specs=placed,
        out_specs=(
            P(("dp", "fsdp"), None, None),
            P(("dp", "fsdp"), None, None),
            P(None, ("dp", "fsdp"), None),
            P(None, ("dp", "fsdp"), None),
            P(None, ("dp", "fsdp"), None),
            P(None, ("dp", "fsdp"), None),
            P(None, ("dp", "fsdp"), None),
            P(None, None, ("dp", "fsdp")),
            P(None, None, ("dp", "fsdp")),
        ),
        check_vma=False,
    )
```

profile of v0, /device:TPU:0, one launch (start us, length us, event | category | flops | bytes accessed | tf_op | source)
XLA Modules:
  0.0 1717.6 jit_solution(4034619591472432295)
XLA Ops:
  10.2 1.5 fusion.164
  11.8 1.4 fusion.167
  13.3 1.7 fusion.162
  15.1 1.7 fusion.163
  22.0 71.9 %all-gather.4 = bf16[1,2,768]{1,0,2:T(2,128)(2,1)S(1)} all-gather(bf16[1,2,24]{1,0,2:T(2,128)(2,1)S(1)} %copy.230), channel_id=6, replica_groups=mesh['dp'=4,'fsdp'=8] {'dp','fsdp'}, dimensions={2}, use_global_device_ids=true | all-gather | bytes 3168 | tf_op jit(solution)/shard_map/all_gather | solution.py:48
  93.8 66.3 %all-gather.11 = bf16[1,2,768]{1,0,2:T(2,128)(2,1)S(1)} all-gather(bf16[1,2,24]{1,0,2:T(2,128)(2,1)S(1)} %copy.231), channel_id=13, replica_groups=mesh['dp'=4,'fsdp'=8] {'dp','fsdp'}, dimensions={2}, use_global_device_ids=true | all-gather | bytes 3168 | tf_op jit(solution)/shard_map/all_gather | solution.py:48
  160.1 5.2 fusion.108
  165.3 5.2 fusion.106
  171.0 1.7 convolution_convert_fusion.8
  173.1 1.9 convolution_convert_fusion.9
  175.2 6.2 all-gather.27.cloned.1.call-done
  181.4 1.7 convolution_convert_fusion.10
  185.4 52.5 %all-gather.33.cloned.1.call-done = bf16[1,768,768]{2,1,0:T(8,128)(2,1)} async-done(((bf16[1,24,768]{2,1,0:T(8,128)(2,1)}), bf16[1,768,768]{2,1,0:T(8,128)(2,1)}) %all-gather.33.cloned.1.call-update) | async-done | bytes 1179664 | tf_op jit(solution)/shard_map/all_gather | solution.py:45
  237.9 1.9 fusion.170
  240.1 63.7 %all-gather.35.cloned.1.call-done = bf16[1,768,3072]{2,1,0:T(8,128)(2,1)} async-done(((bf16[1,24,3072]{2,1,0:T(8,128)(2,1)}), bf16[1,768,3072]{2,1,0:T(8,128)(2,1)}) %all-gather.35.cloned.1.call-update) | async-done | bytes 4718608 | tf_op jit(solution)/shard_map/all_gather | solution.py:46
  303.8 5.8 fusion.14
  309.6 60.0 %all-gather.37.cloned.1.call-done = bf16[1,3072,768]{1,2,0:T(8,128)(2,1)} async-done(((bf16[1,3072,24]{1,2,0:T(8,128)(2,1)}), bf16[1,3072,768]{1,2,0:T(8,128)(2,1)}) %all-gather.37.cloned.1.call-update) | async-done | bytes 4718608 | tf_op jit(solution)/shard_map/all_gather | solution.py:47
  369.7 5.4 fusion.171
  376.1 50.0 %all-gather.43.cloned.1.call-done = bf16[1,768,768]{2,1,0:T(8,128)(2,1)} async-done(((bf16[1,24,768]{2,1,0:T(8,128)(2,1)}), bf16[1,768,768]{2,1,0:T(8,128)(2,1)}) %all-gather.43.cloned.1.call-update) | async-done | bytes 1179664 | tf_op jit(solution)/shard_map/all_gather | solution.py:43
  426.2 1.7 convolution_convert_fusion.4
  428.2 3.6 rev.20
  431.9 50.3 %all-gather.41.cloned.1.call-done = bf16[1,768,768]{2,1,0:T(8,128)(2,1)} async-done(((bf16[1,24,768]{2,1,0:T(8,128)(2,1)}), bf16[1,768,768]{2,1,0:T(8,128)(2,1)}) %all-gather.41.cloned.1.call-update) | async-done | bytes 1179664 | tf_op jit(solution)/shard_map/all_gather | solution.py:42
  482.2 1.7 convolution_convert_fusion.5
  484.9 53.2 %all-gather.39.cloned.1.call-done = bf16[1,768,768]{2,1,0:T(8,128)(2,1)} async-done(((bf16[1,24,768]{2,1,0:T(8,128)(2,1)}), bf16[1,768,768]{2,1,0:T(8,128)(2,1)}) %all-gather.39.cloned.1.call-update) | async-done | bytes 1179664 | tf_op jit(solution)/shard_map/all_gather | solution.py:44
  538.2 1.7 convolution_convert_fusion.6
  540.2 3.7 rev.18
  543.9 1.7 fusion.172
  547.7 46.3 %all-gather.45.cloned.1.call-done = bf16[1,768,768]{2,1,0:T(8,128)(2,1)} async-done(((bf16[1,24,768]{2,1,0:T(8,128)(2,1)}), bf16[1,768,768]{2,1,0:T(8,128)(2,1)}) %all-gather.45.cloned.1.call-update) | async-done | bytes 1179664 | tf_op jit(solution)/shard_map/all_gather | solution.py:45
  594.1 2.2 fusion.173
  598.7 61.4 %all-gather.47.cloned.1.call-done = bf16[1,768,3072]{2,1,0:T(8,128)(2,1)} async-done(((bf16[1,24,3072]{2,1,0:T(8,128)(2,1)}), bf16[1,768,3072]{2,1,0:T(8,128)(2,1)}) %all-gather.47.cloned.1.call-update) | async-done | bytes 4718608 | tf_op jit(solution)/shard_map/all_gather | solution.py:46
  660.1 5.8 fusion.6
  665.9 60.1 %all-gather.49.cloned.1.call-done = bf16[1,3072,768]{1,2,0:T(8,128)(2,1)} async-done(((bf16[1,3072,24]{1,2,0:T(8,128)(2,1)}), bf16[1,3072,768]{1,2,0:T(8,128)(2,1)}) %all-gather.49.cloned.1.call-update) | async-done | bytes 4718608 | tf_op jit(solution)/shard_map/all_gather | solution.py:47
  726.0 5.7 fusion.174
  734.1 4.1 fusion.29
  738.4 2.3 multiply_reduce_fusion.2
  743.2 1.9 copy.179
  745.1 1.8 reshape.224
  747.0 1.7 multiply_reduce_fusion.1
  753.0 1.8 rev.25
  754.8 1.5 copy.190
  756.3 1.9 convolution_add_fusion.5
  761.7 6.9 fusion.22
  768.7 2.3 multiply_reduce_fusion.4
  774.9 1.7 multiply_reduce_fusion
  778.6 1.6 fusion.57
  780.3 1.9 fusion.97
  782.2 1.9 fusion.94
  784.1 1.9 fusion.91
  786.1 1.9 fusion.100
  788.1 5.2 fusion.157
  793.2 5.3 fusion.154
  798.6 2.0 fusion.103
  800.6 5.1 fusion.156
  805.7 5.5 fusion.155
  812.8 1.9 convolution_bitcast_fusion.2
  814.7 3.1 copy.203
  817.8 1.9 convolution_bitcast_fusion.1
  819.6 3.0 copy.204
  822.7 1.9 convolution_bitcast_fusion
  824.5 3.1 copy.205
  828.0 30.8 %concatenate.7 = f32[768,9218]{1,0:T(8,128)} concatenate(f32[768,768]{1,0:T(8,128)} %fusion.97, f32[768,768]{1,0:T(8,128)} %fusion.94, f32[768,768]{1,0:T(8,128)} %fusion.91, f32[768,768]{1,0:T(8,128)} %fusion.100, f32[768,3072]{1,0:T(8,128)} %fusion.157, f32[768,3072]{1,0:T(8,128)} %fusion.154, f32[768,1]{1,0:T(8,128)S(1)} %stack.102, f32[768,1]{1,0:T(8,128)S(1)} %stack.103), dimensions={1} | concatenate | bytes 56635392 | tf_op jit(solution)/shard_map/concatenate | solution.py:252
  858.8 30.8 %concatenate.6 = f32[768,9218]{1,0:T(8,128)} concatenate(f32[768,768]{1,0:T(8,128)} %copy.203, f32[768,768]{1,0:T(8,128)} %copy.204, f32[768,768]{1,0:T(8,128)} %copy.205, f32[768,768]{1,0:T(8,128)} %fusion.103, f32[768,3072]{1,0:T(8,128)} %fusion.156, f32[768,3072]{1,0:T(8,128)} %fusion.155, f32[768,1]{1,0:T(8,128)S(1)} %stack.100, f32[768,1]{1,0:T(8,128)S(1)} %stack.101), dimensions={1} | concatenate | bytes 56635392 | tf_op jit(solution)/shard_map/concatenate | solution.py:252
  889.6 1.9 convolution_add_fusion.2
  894.2 804.9 %all-reduce.5.cloned.1.call-done = (f32[768,9218]{1,0:T(8,128)}, f32[768,9218]{1,0:T(8,128)}) async-done(((f32[768,9218]{1,0:T(8,128)}, f32[768,9218]{1,0:T(8,128)}), (f32[768,9218]{1,0:T(8,128)}, f32[768,9218]{1,0:T(8,128)})) %all-reduce.5.cloned.1.call-update) | async-done | bytes 56635408
  (338 shorter events, 52.5 us)
Async XLA Ops:
  7.2 14.6 copy-start.100
  7.2 163.8 %all-gather.31.cloned.1.call-start = ((), (), s32[]{:S(2)}) async-start(), calls=%async_computation.2 | async-start | bytes 1216512 | tf_op jit(solution)/shard_map/all_gather | solution.py:43
  8.7 164.4 %all-gather.29.cloned.1.call-start = ((), (), s32[]{:S(2)}) async-start(), calls=%async_computation.1 | async-start | bytes 1216512 | tf_op jit(solution)/shard_map/all_gather | solution.py:42
  10.2 160.8 %copy-start.2 = (bf16[1,256,768]{2,1,0:T(8,128)(2,1)S(1)}, bf16[1,256,768]{2,1,0:T(8,128)(2,1)}, u32[]{:S(2)}) copy-start(bf16[1,256,768]{2,1,0:T(8,128)(2,1)} %param.10) | copy-start | bytes 1179652
  10.2 171.2 %all-gather.27.cloned.1.call-start = ((), (), s32[]{:S(2)}) async-start(), calls=%async_computation | async-start | bytes 1216512 | tf_op jit(solution)/shard_map/all_gather | solution.py:44
  11.7 226.2 %all-gather.33.cloned.1.call-start = ((), (), s32[]{:S(2)}) async-start(), calls=%async_computation.3 | async-start | bytes 1216512 | tf_op jit(solution)/shard_map/all_gather | solution.py:45
  13.2 290.6 %all-gather.35.cloned.1.call-start = ((), (), s32[]{:S(2)}) async-start(), calls=%async_computation.4 | async-start | bytes 4866048 | tf_op jit(solution)/shard_map/all_gather | solution.py:46
  15.0 354.6 %all-gather.37.cloned.1.call-start = ((), (), s32[]{:S(2)}) async-start(), calls=%async_computation.5 | async-start | bytes 4866048 | tf_op jit(solution)/shard_map/all_gather | solution.py:47
  16.8 409.4 %all-gather.43.cloned.1.call-start = ((), (), s32[]{:S(2)}) async-start(), calls=%async_computation.8 | async-start | bytes 1216512 | tf_op jit(solution)/shard_map/all_gather | solution.py:43
  17.5 464.6 %all-gather.41.cloned.1.call-start = ((), (), s32[]{:S(2)}) async-start(), calls=%async_computation.7 | async-start | bytes 1216512 | tf_op jit(solution)/shard_map/all_gather | solution.py:42
  18.3 519.9 %all-gather.39.cloned.1.call-start = ((), (), s32[]{:S(2)}) async-start(), calls=%async_computation.6 | async-start | bytes 1216512 | tf_op jit(solution)/shard_map/all_gather | solution.py:44
  19.0 575.0 %all-gather.45.cloned.1.call-start = ((), (), s32[]{:S(2)}) async-start(), calls=%async_computation.9 | async-start | bytes 1216512 | tf_op jit(solution)/shard_map/all_gather | solution.py:45
  19.6 640.5 %all-gather.47.cloned.1.call-start = ((), (), s32[]{:S(2)}) async-start(), calls=%async_computation.10 | async-start | bytes 4866048 | tf_op jit(solution)/shard_map/all_gather | solution.py:46
  20.3 705.6 %all-gather.49.cloned.1.call-start = ((), (), s32[]{:S(2)}) async-start(), calls=%async_computation.11 | async-start | bytes 4866048 | tf_op jit(solution)/shard_map/all_gather | solution.py:47
  20.9 1678.1 %all-reduce.5.cloned.1.call-start = ((), (), s32[]{:S(2)}) async-start(), calls=%async_computation.12 | async-start | bytes 114819072
  173.0 10.4 copy-start.38
  175.2 8.8 copy-start.40
  185.3 124.3 %copy-start.20 = (bf16[2,128,12,64]{1,0,3,2:T(2,128)(2,1)}, bf16[2,128,12,64]{1,0,3,2:T(2,128)(2,1)S(1)}, u32[]{:S(2)}) copy-start(bf16[2,128,12,64]{1,0,3,2:T(2,128)(2,1)S(1)} %copy.168) | copy-start | bytes 1179652
  185.3 54.7 %copy-start.59 = (f32[2,12,128]{2,1,0:T(8,128)S(1)}, f32[2,12,128]{2,1,0:T(8,128)}, u32[]{:S(2)}) copy-start(f32[2,12,128]{2,1,0:T(8,128)} %copy-done.58) | copy-start | bytes 36868
  185.4 54.7 %copy-start.63 = (f32[2,12,128]{2,1,0:T(8,128)S(1)}, f32[2,12,128]{2,1,0:T(8,128)}, u32[]{:S(2)}) copy-start(f32[2,12,128]{2,1,0:T(8,128)} %copy-done.62) | copy-start | bytes 36868
  185.4 118.4 %copy-start.51 = (f32[768]{0:T(1024)S(1)}, f32[768]{0:T(1024)}, u32[]{:S(2)}) copy-start(f32[768]{0:T(1024)} %get-tuple-element.20) | copy-start | bytes 9220
  239.7 129.9 %copy-start.8 = (f32[256,768]{1,0:T(8,128)}, f32[256,768]{1,0:T(8,128)S(1)}, u32[]{:S(2)}) copy-start(f32[256,768]{1,0:T(8,128)S(1)} %get-tuple-element.61) | copy-start | bytes 2359300
  239.8 129.9 %copy-start.75 = (f32[256]{0:T(256)}, f32[256]{0:T(256)S(1)}, u32[]{:S(2)}) copy-start(f32[256]{0:T(256)S(1)} %broadcast_multiply_fusion.3) | copy-start | bytes 3076
  240.0 69.6 %copy-start.92 = (f32[256]{0:T(256)}, f32[256]{0:T(256)S(1)}, u32[]{:S(2)}) copy-start(f32[256]{0:T(256)S(1)} %multiply_reduce_fusion.11) | copy-start | bytes 3076
  240.0 129.6 %copy-start.87 = (f32[256]{0:T(256)}, f32[256]{0:T(256)S(1)}, u32[]{:S(2)}) copy-start(f32[256]{0:T(256)S(1)} %fusion.150) | copy-start | bytes 3076
  309.6 66.3 %copy-start.56 = (f32[768]{0:T(1024)S(1)}, f32[768]{0:T(1024)}, u32[]{:S(2)}) copy-start(f32[768]{0:T(1024)} %get-tuple-element.19) | copy-start | bytes 9220
  375.1 53.0 %copy-start.71 = (f32[256]{0:T(256)}, f32[256]{0:T(256)S(1)}, u32[]{:S(2)}) copy-start(f32[256]{0:T(256)S(1)} %broadcast_multiply_fusion.2) | copy-start | bytes 3076
  375.3 52.9 %copy-start.94 = (f32[256]{0:T(256)}, f32[256]{0:T(256)S(1)}, u32[]{:S(2)}) copy-start(f32[256]{0:T(256)S(1)} %multiply_reduce_fusion.10) | copy-start | bytes 3076
  375.3 52.9 %copy-start.73 = (f32[256]{0:T(256)}, f32[256]{0:T(256)S(1)}, u32[]{:S(2)}) copy-start(f32[256]{0:T(256)S(1)} %fusion.151) | copy-start | bytes 3076
  376.1 162.1 %copy-start.3 = (bf16[256,768]{1,0:T(8,128)(2,1)}, bf16[256,768]{1,0:T(8,128)(2,1)S(1)}, u32[]{:S(2)}) copy-start(bf16[256,768]{1,0:T(8,128)(2,1)S(1)} %multiply_convert_fusion.7) | copy-start | bytes 1179652
  594.1 4.0 copy-start.61
  594.1 4.0 copy-start.65
  726.0 6.0 copy-start.37
  726.0 6.0 copy-start.70
  726.0 8.1 copy-start.101
  732.9 5.3 slice-start.2
  734.0 4.2 copy-start.33
  734.0 4.2 copy-start.66
  734.1 4.2 copy-start.12
  734.1 4.2 copy-start.54
  734.1 4.2 copy-start.79
  734.1 4.2 copy-start.90
  734.1 4.2 slice-start.3
  752.1 4.2 copy-start.6
  752.5 3.8 copy-start.23
  754.8 3.5 copy-start.17
  761.2 7.5 slice-start
  761.5 7.1 copy-start.35
  761.5 7.1 copy-start.68
  761.7 7.0 copy-start.9
  761.7 7.0 copy-start.52
  761.7 7.0 copy-start.76
  761.7 7.0 copy-start.88
  761.7 7.0 slice-start.1
  788.0 5.2 copy-start.32
  788.0 5.2 copy-start.34
  788.0 5.2 copy-start.67
  793.2 5.3 copy-start.21
  793.2 5.3 copy-start.84
  800.6 5.1 copy-start.30
  800.6 5.1 copy-start.36
  800.6 5.1 copy-start.69
  824.5 3.1 copy-start.99
  824.5 3.3 copy-start.82
  (55 other events, 87.1 us)
Sparse Core Ops, SparseCore 0:
  11.5 56.9 all-gather.30
  72.0 53.4 all-gather.28
  128.4 52.9 all-gather.26
  184.7 53.1 all-gather.32
  241.2 62.5 all-gather.34
  307.1 62.4 all-gather.36
  373.1 52.9 all-gather.42
  429.1 53.0 all-gather.40
  485.1 53.0 all-gather.38
  540.9 53.0 all-gather.44
  597.5 62.5 all-gather.46
  663.5 62.4 all-gather.48
  889.7 809.2 all-reduce.4
where the time goes:
time: 1730 us; the launch traced here: 1720 us
  waiting for transfers between devices  1310 us (76%)
  blocking collectives  138 us (8%)
  local copies, waits for them, and re-layouts  117 us (7%)
  matrix products  110 us (6%)
  other arithmetic  22.9 us (1%)
    unnamed x14, waiting for transfers between devices  809 us
    all_gather x2, blocking collectives, collect(): lax.all_gather(pieces[6], ('dp', 'fsdp'), axis=1, tiled=True)  138 us
    all_gather x2, waiting for transfers between devices, collect(): lax.all_gather(pieces[4], ('dp', 'fsdp'), axis=0, tiled=True)  125 us
    all_gather x2, waiting for transfers between devices, collect(): lax.all_gather(pieces[5], ('dp', 'fsdp'), axis=1, tiled=True)  120 us
    all_gather x2, waiting for transfers between devices, collect(): lax.all_gather(pieces[3], ('dp', 'fsdp'), axis=0, tiled=True)  98.8 us
    concatenate x2, local copies, waits for them, and re-layouts, weight_terms(): return jnp.concatenate(result, axis=1)  61.6 us
    all_gather x2, waiting for transfers between devices, collect(): lax.all_gather(pieces[2], ('dp', 'fsdp'), axis=0, tiled=True)  59.4 us
    all_gather x2, waiting for transfers between devices, collect(): lax.all_gather(pieces[0], ('dp', 'fsdp'), axis=0, tiled=True)  50.3 us
  transfers between devices with their start and end apart: 13, of which 11 were waited for; matrix products, arithmetic and copies ran while one was open for 4% of the time, Pallas kernels for 0%

commit v1 on v0

--- a/solution.py
+++ b/solution.py
@@ -8,6 +8,7 @@
 HEAD_DIM = 64
 FF = 3072
 LAYERS = 2
+PAD = 128
 
 
 def norm(value, gain):
@@ -36,30 +37,24 @@
     )
 
 
+def pack(shards, layer):
+    query_w, key_w, value_w, out_w, up_w, down_w, gains = (member[layer] for member in shards)
+    rows = query_w.shape[0]
+    gain_columns = jnp.pad(gains.T, ((0, 0), (0, PAD - 2)))
+    return jnp.concatenate([query_w, key_w, value_w, out_w, up_w, down_w.T, gain_columns], axis=1)
+
+
 def collect(shards, layer):
-    pieces = tuple((member[layer] for member in shards))
-    return (
-        lax.all_gather(pieces[0], ("dp", "fsdp"), axis=0, tiled=True),
-        lax.all_gather(pieces[1], ("dp", "fsdp"), axis=0, tiled=True),
-        lax.all_gather(pieces[2], ("dp", "fsdp"), axis=0, tiled=True),
-        lax.all_gather(pieces[3], ("dp", "fsdp"), axis=0, tiled=True),
-        lax.all_gather(pieces[4], ("dp", "fsdp"), axis=0, tiled=True),
-        lax.all_gather(pieces[5], ("dp", "fsdp"), axis=1, tiled=True),
-        lax.all_gather(pieces[6], ("dp", "fsdp"), axis=1, tiled=True),
-    )
-
-
-def collect_again(shards, layer):
-    pieces = tuple((member[layer] for member in shards))
-    return (
-        lax.all_gather(pieces[0], ("dp", "fsdp"), axis=0, tiled=True),
-        lax.all_gather(pieces[1], ("dp", "fsdp"), axis=0, tiled=True),
-        lax.all_gather(pieces[2], ("dp", "fsdp"), axis=0, tiled=True),
-        lax.all_gather(pieces[3], ("dp", "fsdp"), axis=0, tiled=True),
-        lax.all_gather(pieces[4], ("dp", "fsdp"), axis=0, tiled=True),
-        lax.all_gather(pieces[5], ("dp", "fsdp"), axis=1, tiled=True),
-        lax.all_gather(pieces[6], ("dp", "fsdp"), axis=1, tiled=True),
-    )
+    return lax.all_gather(pack(shards, layer), ("dp", "fsdp"), axis=0, tiled=True)
+
+
+def unpack(gathered):
+    qkv_w = gathered[:, : 3 * D]
+    out_w = gathered[:, 3 * D : 4 * D]
+    up_w = gathered[:, 4 * D : 4 * D + FF]
+    down_t = gathered[:, 4 * D + FF : 4 * D + 2 * FF]
+    gains = gathered[:, 4 * D + 2 * FF : 4 * D + 2 * FF + 2].T.astype(jnp.float32)
+    return (qkv_w, out_w, up_w, down_t, gains)
 
 
 def visible_keys(length, token_count, swap):
@@ -141,23 +136,20 @@
 
 
 def layer_forward(hidden, length, weights, swap):
-    query_w, key_w, value_w, out_w, up_w, down_w, gains = weights
-    gain_first = gains[0].astype(jnp.float32)
-    gain_second = gains[1].astype(jnp.float32)
+    qkv_w, out_w, up_w, down_t, gains = weights
     inputs_low = hidden.astype(jnp.bfloat16)
-    query = product(inputs_low, query_w).astype(jnp.bfloat16)
-    keys = product(inputs_low, key_w).astype(jnp.bfloat16)
-    values = product(inputs_low, value_w).astype(jnp.bfloat16)
+    qkv = product(inputs_low, qkv_w).astype(jnp.bfloat16)
+    query, keys, values = qkv[:, :D], qkv[:, D : 2 * D], qkv[:, 2 * D :]
     visible = visible_keys(length, hidden.shape[0], swap)
     mixed, log_total = attend_forward(query, keys, values, visible, swap)
     mixed_low = mixed.astype(jnp.bfloat16)
     first_sum = hidden + product(mixed_low, out_w)
-    normed = norm(first_sum, gain_first)
+    normed = norm(first_sum, gains[0])
     normed_low = normed.astype(jnp.bfloat16)
     expanded = product(normed_low, up_w)
     activated = gelu_tanh(expanded).astype(jnp.bfloat16)
-    second_sum = normed + product(activated, down_w)
-    output = norm(second_sum, gain_second)
+    second_sum = normed + product_right_t(activated, down_t)
+    output = norm(second_sum, gains[1])
     kept = (
         inputs_low,
         query,
@@ -175,7 +167,7 @@
 
 
 def layer_backward(grad_output, kept, weights, swap, length):
-    query_w, key_w, value_w, out_w, up_w, down_w, gains = weights
+    qkv_w, out_w, up_w, down_t, gains = weights
     (
         inputs_low,
         query,
@@ -189,75 +181,41 @@
         activated,
         second_sum,
     ) = kept
-    gain_first = gains[0].astype(jnp.float32)
-    gain_second = gains[1].astype(jnp.float32)
-    grad_second, grad_gain_second = jax.vjp(norm, second_sum, gain_second)[1](grad_output)
+    grad_second, grad_gain_second = jax.vjp(norm, second_sum, gains[1])[1](grad_output)
     down_low = grad_second.astype(jnp.bfloat16)
-    grad_active = product_right_t(down_low, down_w)
+    grad_active = product(down_low, down_t)
     up_low = jax.vjp(gelu_tanh, expanded)[1](grad_active)[0].astype(jnp.bfloat16)
     grad_normed = grad_second + product_right_t(up_low, up_w)
-    grad_first, grad_gain_first = jax.vjp(norm, first_sum, gain_first)[1](grad_normed)
+    grad_first, grad_gain_first = jax.vjp(norm, first_sum, gains[0])[1](grad_normed)
     attn_low = grad_first.astype(jnp.bfloat16)
     grad_mixed = product_right_t(attn_low, out_w).astype(jnp.bfloat16)
     visible = visible_keys(length, query.shape[0], swap)
-    grad_query, grad_keys, grad_values = attend_backward(
-        query, keys, values, visible, swap, log_total, grad_mixed
-    )
-    grad_inputs = (
-        grad_first
-        + product_right_t(grad_query, query_w)
-        + product_right_t(grad_keys, key_w)
-        + product_right_t(grad_values, value_w)
-    )
-    gain_pair = jnp.stack([grad_gain_first, grad_gain_second], axis=1)
-    context = (
-        inputs_low,
-        grad_query,
-        grad_keys,
-        grad_values,
-        mixed_low,
-        attn_low,
-        normed_low,
-        up_low,
-        down_low,
-        activated,
-        gain_pair,
-    )
-    return (grad_inputs, context)
-
-
-def weight_terms(contexts):
-    result = []
-    for context in contexts:
-        (
-            inputs_low,
-            grad_query,
-            grad_keys,
-            grad_values,
-            mixed_low,
-            attn_low,
-            normed_low,
-            up_low,
-            down_low,
-            activated,
-            gain_pair,
-        ) = context
-        result.append(product_left_t(inputs_low, grad_query))
-        result.append(product_left_t(inputs_low, grad_keys))
-        result.append(product_left_t(inputs_low, grad_values))
-        result.append(product_left_t(mixed_low, attn_low))
-        result.append(product_left_t(normed_low, up_low))
-        result.append(product_left_t(down_low, activated))
-        result.append(gain_pair)
-    return jnp.concatenate(result, axis=1)
+    grad_qkv = jnp.concatenate(
+        attend_backward(query, keys, values, visible, swap, log_total, grad_mixed), axis=1
+    )
+    grad_inputs = grad_first + product_right_t(grad_qkv, qkv_w)
+    gain_columns = jnp.pad(
+        jnp.stack([grad_gain_first, grad_gain_second], axis=1), ((0, 0), (0, PAD - 2))
+    )
+    low = jnp.bfloat16
+    terms = jnp.concatenate(
+        [
+            product_left_t(inputs_low, grad_qkv).astype(low),
+            product_left_t(mixed_low, attn_low).astype(low),
+            product_left_t(normed_low, up_low).astype(low),
+            product_left_t(down_low, activated).astype(low),
+            gain_columns.astype(low),
+        ],
+        axis=1,
+    )
+    return (grad_inputs, terms)
 
 
 def arrange(summed):
-    width = 4 * D + 2 * FF + 2
-    bounds = [0, D, 2 * D, 3 * D, 4 * D, 4 * D + FF, 4 * D + 2 * FF, width]
+    summed = summed.astype(jnp.float32)
+    bounds = [0, D, 2 * D, 3 * D, 4 * D, 4 * D + FF, 4 * D + 2 * FF, 4 * D + 2 * FF + 2]
     member = [summed[:, bounds[j] : bounds[j + 1]] for j in range(7)]
-    grouped = [(member[0], member[1], member[2], member[3], member[4], member[5].T, member[6].T)]
-    return grouped
+    return (*member[:5], member[5].T, member[6].T)
 
 
 def per_device(
@@ -283,37 +241,22 @@
     )
     hidden = tokens[0].astype(jnp.float32)
     length = lengths[0]
-    gathered_all = []
+    weights_all = [unpack(collect(shards, layer)) for layer in range(LAYERS)]
     kept_all = []
     for layer in range(LAYERS):
-        gathered = collect(shards, layer)
-        hidden, kept = layer_forward(hidden, length, gathered, layer % 2 == 1)
-        gathered_all.append(gathered)
+        hidden, kept = layer_forward(hidden, length, weights_all[layer], layer % 2 == 1)
         kept_all.append(kept)
     activations = hidden.astype(jnp.bfloat16)[None]
     grad_hidden = cotangent[0].astype(jnp.float32)
     layer_grads = [None] * LAYERS
     for layer in reversed(range(LAYERS)):
-        weights_now = collect_again(shards, layer)
-        grad_hidden, context = layer_backward(
-            grad_hidden, kept_all[layer], weights_now, layer % 2 == 1, length
+        grad_hidden, terms = layer_backward(
+            grad_hidden, kept_all[layer], weights_all[layer], layer % 2 == 1, length
         )
-        summed = lax.psum_scatter(
-            weight_terms([context]), ("dp", "fsdp"), scatter_dimension=0, tiled=True
-        )
-        layer_grads[layer] = arrange(summed)[0]
+        summed = lax.psum_scatter(terms, ("dp", "fsdp"), scatter_dimension=0, tiled=True)
+        layer_grads[layer] = arrange(summed)
     stacked = tuple((jnp.stack([entry[member] for entry in layer_grads]) for member in range(7)))
-    return (
-        activations,
-        grad_hidden[None],
-        stacked[0],
-        stacked[1],
-        stacked[2],
-        stacked[3],
-        stacked[4],
-        stacked[5],
-        stacked[6],
-    )
+    return (activations, grad_hidden[None], *stacked)
 
 
 def solution(mesh):

time: 1730 us -> 651 us (0.38)
  waiting for transfers between devices: 1310 us -> 465 us
  blocking collectives: 138 us -> 0 us
  local copies, waits for them, and re-layouts: 117 us -> 54.9 us
  matrix products: 110 us -> 91.8 us
    unnamed x14 -> x6, waiting for transfers between devices: 809 us -> 275 us
    all_gather x12 -> x2, waiting for transfers between devices: 504 us -> 191 us  [collect(): lax.all_gather(pack(shards, layer), ('dp', 'fsdp'), axis=0, tiled=True)]
    all_gather x2 -> x0, blocking collectives: 138 us -> none  [collect(): lax.all_gather(pieces[6], ('dp', 'fsdp'), axis=1, tiled=True)]
    concatenate x2 -> x6, local copies, waits for them, and re-layouts: 61.6 us -> 2.4 us  [the longest x2 1.5 us: layer_backward(): jnp.concatenate([product_left_t(inputs_low, grad_qkv).astype(low), produc...]
    dot_general x12 -> x8, matrix products: 36.3 us -> 25.9 us  [product_left_t(): lax.dot_general(left, right, (((0,), (0,)), ((), ())), preferred_element_...]
    dot_general x12 -> x8, matrix products: 37.4 us -> 27.1 us  [product(): return jnp.dot(left, right, preferred_element_type=jnp.float32)]
  transfers between devices with their start and end apart: 13 -> 4, of which waited for: 11 -> 4; matrix products, arithmetic and copies ran while one was open for 4% -> 11% of each run, Pallas kernels for 0% -> 0%
where the time goes in v1:
time: 651 us; the launch traced here: 644 us
  waiting for transfers between devices  465 us (71%)
  matrix products  91.8 us (14%)
  local copies, waits for them, and re-layouts  54.9 us (8%)
  between operations  16.3 us (3%)
  other arithmetic  15 us (2%)
    unnamed x6, waiting for transfers between devices  275 us
    all_gather x2, waiting for transfers between devices, collect(): lax.all_gather(pack(shards, layer), ('dp', 'fsdp'), axis=0, tiled=True)  191 us
    dot_general x8, matrix products, product_right_t(): lax.dot_general(left, right, (((1,), (1,)), ((), ())), preferred_element_...  29.8 us
    dot_general x8, matrix products, product(): return jnp.dot(left, right, preferred_element_type=jnp.float32)  27.1 us
    dot_general x8, matrix products, product_left_t(): lax.dot_general(left, right, (((0,), (0,)), ((), ())), preferred_element_...  25.9 us
    unnamed x197, local copies, waits for them, and re-layouts  22.8 us
  transfers between devices with their start and end apart: 4, of which 4 were waited for; matrix products, arithmetic and copies ran while one was open for 11% of the time, Pallas kernels for 0%

profile of v1, /device:TPU:0, one launch (start us, length us, event | category | flops | bytes accessed | tf_op | source)
XLA Modules:
  0.0 643.6 jit_solution(14956861835481307938)
XLA Ops:
  7.2 0.8 constant_dynamic-update-slice_fusion.4
  8.8 0.8 constant_dynamic-update-slice_fusion.3
  11.2 1.0 bitcast_dynamic-update-slice_fusion.9
  12.2 1.0 bitcast_dynamic-update-slice_fusion.7
  15.8 105.1 %all-gather.3.cloned.1.call-done = bf16[768,9344]{1,0:T(8,128)(2,1)} async-done(((bf16[24,9344]{1,0:T(8,128)(2,1)}), bf16[768,9344]{1,0:T(8,128)(2,1)}) %all-gather.3.cloned.1.call-update) | async-done | bytes 14352400 | tf_op jit(solution)/shard_map/all_gather | solution.py:48
  120.9 3.2 fusion.22
  126.4 1.1 convert_bitcast_fusion.1
  128.0 1.9 fusion.133
  130.7 4.0 fusion.20
  134.7 5.6 fusion.134
  141.2 85.4 %all-gather.5.cloned.1.call-done = bf16[768,9344]{1,0:T(8,128)(2,1)} async-done(((bf16[24,9344]{1,0:T(8,128)(2,1)}), bf16[768,9344]{1,0:T(8,128)(2,1)}) %all-gather.5.cloned.1.call-update) | async-done | bytes 14352400 | tf_op jit(solution)/shard_map/all_gather | solution.py:48
  226.7 3.1 convolution_convert_fusion.6
  230.2 2.8 rev.20
  233.2 0.8 reshape.219
  234.3 3.6 rev.18
  237.9 1.6 fusion.135
  240.7 1.1 convert_bitcast_fusion
  242.3 1.9 fusion.136
  244.5 4.0 fusion.12
  248.5 5.6 fusion.137
  254.4 1.0 fusion.88
  255.3 1.1 fusion.129
  256.5 3.1 fusion.36
  259.7 2.2 multiply_reduce_fusion.2
  262.3 0.9 copy-done.11
  263.7 0.9 copy.111
  264.6 1.1 reshape.221
  265.7 1.6 multiply_reduce_fusion.1
  268.9 1.4 convolution_bitcast_fusion
  271.4 0.8 bitcast_dynamic-update-slice_fusion.5
  272.3 1.2 copy.119
  273.5 1.8 rev.25
  275.3 1.4 copy.122
  276.7 1.8 bitcast_dynamic-update-slice_fusion.4
  278.4 0.8 bitcast_dynamic-update-slice_fusion.3
  279.3 4.3 fusion
  283.6 1.4 copy.139
  285.1 2.4 constant_dynamic-update-slice_fusion.12
  287.5 5.5 fusion.3
  293.0 3.8 fusion.4
  298.1 0.8 copy-done.13
  298.9 4.5 multiply_reduce_fusion.3
  303.9 5.9 fusion.29
  309.9 5.5 multiply_reduce_fusion.4
  315.8 0.8 copy-done.14
  316.6 1.9 convolution_convert_fusion.11
  323.0 1.0 copy-done.2
  324.0 1.1 fusion.5
  325.0 4.2 copy.136
  329.3 3.1 convolution_convert_fusion.9
  332.4 2.4 copy.137
  336.2 0.8 copy.135
  337.0 2.1 constant_dynamic-update-slice_fusion.11
  339.1 1.2 constant_dynamic-update-slice_fusion.10
  340.8 3.7 fusion.1
  344.5 3.7 fusion.2
  349.0 1.3 copy-done.3
  350.6 4.0 fusion.52
  354.6 105.6 %reduce-scatter.9.cloned.1.call-done = bf16[24,9344]{1,0:T(8,128)(2,1)} async-done(((bf16[768,9344]{1,0:T(8,128)(2,1)}), bf16[24,9344]{1,0:T(8,128)(2,1)}) %reduce-scatter.9.cloned.1.call-update) | async-done | bytes 448528
  460.2 1.1 convert_element_type.260
  461.4 168.9 %reduce-scatter.7.cloned.1.call-done = bf16[24,9344]{1,0:T(8,128)(2,1)} async-done(((bf16[768,9344]{1,0:T(8,128)(2,1)}), bf16[24,9344]{1,0:T(8,128)(2,1)}) %reduce-scatter.7.cloned.1.call-update) | async-done | bytes 448528
  630.3 1.1 convert_element_type.255
  634.3 0.9 pad_maximum_fusion
  635.2 0.9 pad_maximum_fusion.1
  (283 shorter events, 27.8 us)
Async XLA Ops:
  7.2 113.8 %all-gather.3.cloned.1.call-start = ((), (), s32[]{:S(2)}) async-start(), calls=%async_computation.2 | async-start | bytes 14800896 | tf_op jit(solution)/shard_map/all_gather | solution.py:48
  14.0 212.7 %all-gather.5.cloned.1.call-start = ((), (), s32[]{:S(2)}) async-start(), calls=%async_computation.3 | async-start | bytes 14800896 | tf_op jit(solution)/shard_map/all_gather | solution.py:48
  14.9 445.3 %reduce-scatter.9.cloned.1.call-start = ((), (), s32[]{:S(2)}) async-start(), calls=%async_computation.5 | async-start | bytes 14800896
  125.4 2.6 copy-start.37
  127.9 6.7 %copy-start.43 = (f32[768]{0:T(1024)}, f32[768]{0:T(1024)S(1)}, u32[]{:S(2)}) copy-start(f32[768]{0:T(1024)S(1)} %get-tuple-element.20) | copy-start | bytes 9220
  127.9 98.7 %copy-start.45 = (f32[768]{0:T(1024)}, f32[768]{0:T(1024)S(1)}, u32[]{:S(2)}) copy-start(f32[768]{0:T(1024)S(1)} %get-tuple-element.19) | copy-start | bytes 9220
  129.8 4.9 copy-start.4
  129.9 4.8 copy-start.50
  130.1 4.6 copy-start.62
  134.7 5.7 copy-start.79
  140.4 89.4 %copy-start.7 = (f32[256,768]{1,0:T(8,128)}, f32[256,768]{1,0:T(8,128)S(1)}, u32[]{:S(2)}) copy-start(f32[256,768]{1,0:T(8,128)S(1)} %get-tuple-element.67) | copy-start | bytes 2359300
  140.4 86.3 %copy-start.52 = (f32[256]{0:T(256)}, f32[256]{0:T(256)S(1)}, u32[]{:S(2)}) copy-start(f32[256]{0:T(256)S(1)} %broadcast_multiply_fusion.2) | copy-start | bytes 3076
  141.2 85.4 %copy-start.64 = (f32[256]{0:T(256)}, f32[256]{0:T(256)S(1)}, u32[]{:S(2)}) copy-start(f32[256]{0:T(256)S(1)} %fusion.123) | copy-start | bytes 3076
  233.0 6.6 %copy-start.21 = (bf16[2,128,12,64]{1,0,3,2:T(2,128)(2,1)}, bf16[2,128,12,64]{1,0,3,2:T(2,128)(2,1)S(1)}, u32[]{:S(2)}) copy-start(bf16[2,128,12,64]{1,0,3,2:T(2,128)(2,1)S(1)} %rev.20) | copy-start | bytes 1179652
  240.7 3.4 copy-start.25
  242.2 19.6 %copy-start.48 = (f32[768]{0:T(1024)}, f32[768]{0:T(1024)S(1)}, u32[]{:S(2)}) copy-start(f32[768]{0:T(1024)S(1)} %get-tuple-element.18) | copy-start | bytes 9220
  244.2 17.7 %copy-start.10 = (f32[256,768]{1,0:T(8,128)}, f32[256,768]{1,0:T(8,128)S(1)}, u32[]{:S(2)}) copy-start(f32[256,768]{1,0:T(8,128)S(1)} %get-tuple-element.71) | copy-start | bytes 2359300
  244.2 17.7 %copy-start.55 = (f32[256]{0:T(256)}, f32[256]{0:T(256)S(1)}, u32[]{:S(2)}) copy-start(f32[256]{0:T(256)S(1)} %broadcast_multiply_fusion.1) | copy-start | bytes 3076
  244.4 17.5 %copy-start.68 = (f32[256]{0:T(256)}, f32[256]{0:T(256)S(1)}, u32[]{:S(2)}) copy-start(f32[256]{0:T(256)S(1)} %fusion.124) | copy-start | bytes 3076
  244.4 12.0 %slice-start = ((s8[14352384]{0:T(1024)(128)(4,1)}), s8[4194304]{0:T(1024)(128)(4,1)S(1)}, s32[]{:S(2)}) async-start(s8[14352384]{0:T(1024)(128)(4,1)} %bitcast.210), calls=%async_computation.6 | async-start | bytes 8388608
  244.5 12.0 %slice-start.1 = ((s8[14352384]{0:T(1024)(128)(4,1)}), s8[4194304]{0:T(1024)(128)(4,1)S(1)}, s32[]{:S(2)}) async-start(s8[14352384]{0:T(1024)(128)(4,1)} %bitcast.210), calls=%async_computation.7 | async-start | bytes 8388608
  248.4 8.0 %copy-start.82 = (f32[256,3072]{1,0:T(8,128)}, f32[256,3072]{1,0:T(8,128)S(1)}, u32[]{:S(2)}) copy-start(f32[256,3072]{1,0:T(8,128)S(1)} %fusion.12) | copy-start | bytes 9437188
  248.4 5.9 copy-start.16
  248.4 8.0 %slice-start.2 = ((s8[14352384]{0:T(1024)(128)(4,1)}), s8[4194304]{0:T(1024)(128)(4,1)S(1)}, s32[]{:S(2)}) async-start(s8[14352384]{0:T(1024)(128)(4,1)} %bitcast.210), calls=%async_computation.8 | async-start | bytes 8388608
  248.5 8.0 %slice-start.3 = ((s8[14352384]{0:T(1024)(128)(4,1)}), s8[1769472]{0:T(1024)(128)(4,1)S(1)}, s32[]{:S(2)}) async-start(s8[14352384]{0:T(1024)(128)(4,1)} %bitcast.210), calls=%async_computation.9 | async-start | bytes 3538944
  256.4 3.2 copy-start.33
  256.4 3.2 copy-start.77
  267.7 2.6 copy-start.12
  267.7 2.6 copy-start.26
  267.7 2.6 copy-start.70
  271.3 7.9 %copy-start.9 = (f32[256,768]{1,0:T(8,128)S(1)}, f32[256,768]{1,0:T(8,128)}, u32[]{:S(2)}) copy-start(f32[256,768]{1,0:T(8,128)} %copy-done.7) | copy-start | bytes 2359300
  271.4 7.9 %copy-start.47 = (f32[768]{0:T(1024)S(1)}, f32[768]{0:T(1024)}, u32[]{:S(2)}) copy-start(f32[768]{0:T(1024)} %copy-done.45) | copy-start | bytes 9220
  271.4 7.9 %copy-start.54 = (f32[256]{0:T(256)S(1)}, f32[256]{0:T(256)}, u32[]{:S(2)}) copy-start(f32[256]{0:T(256)} %copy-done.52) | copy-start | bytes 3076
  271.4 7.9 %copy-start.66 = (f32[256]{0:T(256)S(1)}, f32[256]{0:T(256)}, u32[]{:S(2)}) copy-start(f32[256]{0:T(256)} %copy-done.64) | copy-start | bytes 3076
  283.6 3.9 copy-start.49
  283.6 3.9 copy-start.56
  287.5 5.5 copy-start.34
  287.5 5.5 copy-start.78
  287.5 5.5 copy-start.83
  293.0 3.8 copy-start.61
  293.0 3.8 copy-start.74
  297.8 5.6 copy-start.60
  297.8 332.5 %reduce-scatter.7.cloned.1.call-start = ((), (), s32[]{:S(2)}) async-start(), calls=%async_computation.4 | async-start | bytes 14800896
  298.9 4.9 copy-start.80
  303.8 6.0 copy-start.31
  303.8 6.0 copy-start.75
  303.8 6.0 copy-start.5
  303.9 6.0 copy-start.44
  303.9 6.0 copy-start.51
  303.9 6.0 copy-start.63
  309.9 5.5 copy-start.84
  309.9 5.5 copy-start.58
  315.4 3.4 copy-start.40
  315.4 3.4 copy-start.42
  315.4 3.4 copy-start.28
  315.8 13.5 %copy-start.72 = (f32[256]{0:T(256)}, f32[256]{0:T(256)S(1)}, u32[]{:S(2)}) copy-start(f32[256]{0:T(256)S(1)} %negate_multiply_fusion) | copy-start | bytes 3076
  321.3 2.7 copy-start.38
  329.3 7.8 %copy-start = (bf16[768,2304]{1,0:T(8,128)(2,1)S(1)}, bf16[768,2304]{1,0:T(8,128)(2,1)}, u32[]{:S(2)}) copy-start(bf16[768,2304]{1,0:T(8,128)(2,1)} %copy.136) | copy-start | bytes 10616836
  337.0 3.2 copy-start.6
  337.0 3.7 copy-start.85
  340.8 3.7 copy-start.32
  340.8 3.7 copy-start.76
  340.8 3.7 copy-start.81
  344.5 3.7 copy-start.30
  (31 other events, 42.5 us)
Sparse Core Ops, SparseCore 0:
  14.1 106.7 all-gather.2
  124.4 102.2 all-gather.4
  298.0 162.2 reduce-scatter.8
  467.3 162.9 reduce-scatter.6

commit v2 on v1

--- a/solution.py
+++ b/solution.py
@@ -1,6 +1,11 @@
+import functools
+
 import jax
 import jax.numpy as jnp
 from jax import lax
+from jax.experimental import pallas as pl
+from jax.experimental.pallas import tpu as pltpu
+import numpy as np
 from jax.sharding import PartitionSpec as P
 
 D = 768
@@ -194,31 +199,239 @@
         attend_backward(query, keys, values, visible, swap, log_total, grad_mixed), axis=1
     )
     grad_inputs = grad_first + product_right_t(grad_qkv, qkv_w)
-    gain_columns = jnp.pad(
-        jnp.stack([grad_gain_first, grad_gain_second], axis=1), ((0, 0), (0, PAD - 2))
+    operands = (
+        inputs_low,
+        grad_qkv,
+        mixed_low,
+        attn_low,
+        normed_low,
+        up_low,
+        down_low,
+        activated,
+        jnp.stack([grad_gain_first, grad_gain_second]),
+    )
+    return (grad_inputs, operands)
+
+
+def plain_terms(operands):
+    (inputs_low, grad_qkv, mixed_low, attn_low, normed_low, up_low, down_low, activated, gains) = (
+        operands
     )
     low = jnp.bfloat16
-    terms = jnp.concatenate(
+    return jnp.concatenate(
         [
             product_left_t(inputs_low, grad_qkv).astype(low),
             product_left_t(mixed_low, attn_low).astype(low),
             product_left_t(normed_low, up_low).astype(low),
             product_left_t(down_low, activated).astype(low),
-            gain_columns.astype(low),
+            jnp.pad(gains.T, ((0, 0), (0, PAD - 2))).astype(low),
         ],
         axis=1,
     )
-    return (grad_inputs, terms)
-
-
-def arrange(summed):
-    summed = summed.astype(jnp.float32)
+
+
+def plain_reduce(operands):
+    summed = lax.psum_scatter(
+        plain_terms(operands), ("dp", "fsdp"), scatter_dimension=0, tiled=True
+    ).astype(jnp.float32)
     bounds = [0, D, 2 * D, 3 * D, 4 * D, 4 * D + FF, 4 * D + 2 * FF, 4 * D + 2 * FF + 2]
     member = [summed[:, bounds[j] : bounds[j + 1]] for j in range(7)]
     return (*member[:5], member[5].T, member[6].T)
 
 
+class Grid:
+    def __init__(self):
+        places = [
+            (x, core, z, y) for x in range(2) for core in range(2) for z in range(4) for y in range(2)
+        ]
+        number = {place: index for index, place in enumerate(places)}
+
+        def route(move, senders=range(4)):
+            return [
+                (number[place], number[move(*place)]) for place in places if place[2] in senders
+            ]
+
+        self.core = route(lambda x, core, z, y: (x, 1 - core, z, y))
+        self.along_x = route(lambda x, core, z, y: (1 - x, core, z, y))
+        self.along_y = route(lambda x, core, z, y: (x, core, z, 1 - y))
+        self.pair = route(lambda x, core, z, y: (x, core, z ^ 1, y))
+        self.middle = route(lambda x, core, z, y: (x, core, 3 - z, y), (1, 2))
+        self.outward = route(lambda x, core, z, y: (x, core, z ^ 1, y), (1, 2))
+        self.inward = route(lambda x, core, z, y: (x, core, z ^ 1, y), (0, 3))
+
+
+def swap(value, route):
+    return lax.ppermute(value, ("dp", "fsdp"), route)
+
+
+SLOTS = np.array([(dx, dy, s) for dx, dy in ((1, 1), (1, 0), (0, 1), (0, 0)) for s in range(4)])
+
+
+def row_orders(unit):
+    dp, fsdp = lax.axis_index("dp"), lax.axis_index("fsdp")
+    x, core, z, y = dp // 2, dp % 2, fsdp // 2, fsdp % 2
+    dx, dy, s = (jnp.asarray(np.repeat(SLOTS[:, j], unit), jnp.int32) for j in range(3))
+    offset = jnp.asarray(np.tile(np.arange(unit), 16), jnp.int32)
+    place = jnp.where(s < 2, z ^ s, jnp.where(z < 2, s, 3 - s))
+    natural = lax.broadcasted_iota(jnp.int32, (32 * unit, 16 * unit), 0)
+
+    def order(owner):
+        row = ((((x ^ dx) * 2 + owner) * 4 + place) * 2 + (y ^ dy)) * unit + offset
+        return (natural == row[None]).astype(jnp.bfloat16)
+
+    return order(core), order(1 - core)
+
+
+def share_left(value, orders, grid):
+    mine, other = (
+        lax.dot_general(
+            order, value, (((0,), (1,)), ((), ())), preferred_element_type=jnp.float32
+        ).astype(jnp.bfloat16)
+        for order in orders
+    )
+    return (mine, swap(other, grid.core))
+
+
+def both(value, grid):
+    return (value, swap(value, grid.core))
+
+
+ROWS = ((0, 2), (2, 4), (4, 8), (8, 12), (12, 16))
+
+
+def dot(left, right):
+    return jnp.dot(left, right, preferred_element_type=jnp.float32)
+
+
+def ffn_terms(normed_t, up_low, down_t, activated, unit):
+    tile = D
+    steps = FF // tile
+
+    def body(na, nb, ua, ub, da, db, aa, ab, *outs):
+        def put(value):
+            value = value.astype(jnp.bfloat16)
+            for (low, high), out in zip(ROWS, outs):
+                out[...] = value[low * unit : high * unit]
+
+        step = pl.program_id(0)
+
+        @pl.when(step < steps)
+        def _():
+            put(dot(na[...], ua[...]) + dot(nb[...], ub[...]))
+
+        @pl.when(step >= steps)
+        def _():
+            put(dot(da[...], aa[...]) + dot(db[...], ab[...]))
+
+    def whole(value):
+        return pl.BlockSpec(value.shape, lambda j: (0, 0))
+
+    first = pl.BlockSpec((up_low[0].shape[0], tile), lambda j: (0, jnp.minimum(j, steps - 1)))
+    second = pl.BlockSpec((up_low[0].shape[0], tile), lambda j: (0, jnp.maximum(j - steps, 0)))
+    return pl.pallas_call(
+        body,
+        grid=(2 * steps,),
+        in_specs=[whole(v) for v in normed_t]
+        + [first, first]
+        + [whole(v) for v in down_t]
+        + [second, second],
+        out_specs=[pl.BlockSpec(((b - a) * unit, tile), lambda j: (0, j)) for a, b in ROWS],
+        out_shape=[
+            jax.ShapeDtypeStruct(((b - a) * unit, 2 * FF), jnp.bfloat16) for a, b in ROWS
+        ],
+        cost_estimate=pl.CostEstimate(
+            flops=2 * 512 * 16 * unit * 2 * FF, bytes_accessed=12 << 20, transcendentals=0
+        ),
+        compiler_params=pltpu.CompilerParams(vmem_limit_bytes=32 << 20),
+    )(*normed_t, *up_low, *down_t, *activated)
+
+
+def attention_terms(inputs_t, grad_qkv, mixed_t, attn_low, unit):
+    tokens = attn_low[0].shape[0]
+
+    def body(ia, ib, qa, qb, ma, mb, oa, ob, *outs):
+        def put(value, column):
+            value = value.astype(jnp.bfloat16)
+            for (low, high), out in zip(ROWS, outs):
+                out[:, column : column + value.shape[1]] = value[low * unit : high * unit]
+
+        for j in range(3):
+            part = slice(j * D, (j + 1) * D)
+            put(dot(ia[...], qa[:, part]) + dot(ib[...], qb[:, part]), j * D)
+        put(dot(ma[:, :tokens], oa[...]) + dot(mb[:, :tokens], ob[...]), 3 * D)
+        put(ma[:, tokens:].astype(jnp.float32) + mb[:, tokens:].astype(jnp.float32), 4 * D)
+
+    return pl.pallas_call(
+        body,
+        in_specs=[pl.BlockSpec(memory_space=pltpu.VMEM)] * 8,
+        out_specs=[pl.BlockSpec(memory_space=pltpu.VMEM)] * 5,
+        out_shape=[
+            jax.ShapeDtypeStruct(((b - a) * unit, 4 * D + PAD), jnp.bfloat16) for a, b in ROWS
+        ],
+        cost_estimate=pl.CostEstimate(
+            flops=2 * 512 * 16 * unit * 4 * D, bytes_accessed=6 << 20, transcendentals=0
+        ),
+        compiler_params=pltpu.CompilerParams(vmem_limit_bytes=32 << 20),
+    )(*inputs_t, *grad_qkv, *mixed_t, *attn_low)
+
+
+def add(*values):
+    return sum(value.astype(jnp.float32) for value in values)
+
+
+def reduce_chunk(pieces, grid, unit):
+    low = jnp.bfloat16
+    two = 2 * unit
+    diagonal_a, diagonal_b, to_x, to_y, own = pieces
+    from_x = swap(diagonal_a, grid.along_x)
+    from_y = swap(diagonal_b, grid.along_y)
+    to_x = jnp.concatenate([to_x[:two], add(to_x[two:], from_y).astype(low)], axis=0)
+    to_y = jnp.concatenate([add(to_y[:two], from_x).astype(low), to_y[two:]], axis=0)
+    from_x = swap(to_x, grid.along_x)
+    from_y = swap(to_y, grid.along_y)
+    far = add(own[two:], from_x[two:], from_y[two:]).astype(low)
+    received = swap(far, grid.inward)
+    far = add(far, received).astype(low)
+    received = swap(far, grid.middle)
+    near = add(own[:two], from_x[:two], from_y[:two], received)
+    received = swap(near[unit:].astype(low), grid.pair)
+    return add(near[:unit], received)
+
+
+def grid_reduce(operands, orders, grid, unit):
+    (inputs_low, grad_qkv, mixed_low, attn_low, normed_low, up_low, down_low, activated, gains) = (
+        operands
+    )
+    ffn = ffn_terms(
+        share_left(normed_low, orders, grid),
+        both(up_low, grid),
+        share_left(down_low, orders, grid),
+        both(activated, grid),
+        unit,
+    )
+    gain_rows = jnp.pad(gains.astype(jnp.bfloat16), ((0, PAD - 2), (0, 0)))
+    attention = attention_terms(
+        share_left(inputs_low, orders, grid),
+        both(grad_qkv, grid),
+        share_left(jnp.concatenate([mixed_low, gain_rows], axis=0), orders, grid),
+        both(attn_low, grid),
+        unit,
+    )
+    ffn = reduce_chunk(ffn, grid, unit)
+    attention = reduce_chunk(attention, grid, unit)
+    return (
+        attention[:, :D],
+        attention[:, D : 2 * D],
+        attention[:, 2 * D : 3 * D],
+        attention[:, 3 * D : 4 * D],
+        ffn[:, :FF],
+        ffn[:, FF:].T,
+        attention[:, 4 * D : 4 * D + 2].T,
+    )
+
+
 def per_device(
+    sizes,
     tokens,
     lengths,
     query_weight,
@@ -249,12 +462,18 @@
     activations = hidden.astype(jnp.bfloat16)[None]
     grad_hidden = cotangent[0].astype(jnp.float32)
     layer_grads = [None] * LAYERS
+    tuned = sizes == (4, 8)
+    if tuned:
+        unit = query_weight.shape[1]
+        grid, orders = Grid(), row_orders(unit)
     for layer in reversed(range(LAYERS)):
-        grad_hidden, terms = layer_backward(
+        grad_hidden, operands = layer_backward(
             grad_hidden, kept_all[layer], weights_all[layer], layer % 2 == 1, length
         )
-        summed = lax.psum_scatter(terms, ("dp", "fsdp"), scatter_dimension=0, tiled=True)
-        layer_grads[layer] = arrange(summed)
+        if tuned:
+            layer_grads[layer] = grid_reduce(operands, orders, grid, unit)
+        else:
+            layer_grads[layer] = plain_reduce(operands)
     stacked = tuple((jnp.stack([entry[member] for entry in layer_grads]) for member in range(7)))
     return (activations, grad_hidden[None], *stacked)
 
@@ -273,7 +492,7 @@
         P(("dp", "fsdp"), None, None),
     )
     return jax.shard_map(
-        per_device,
+        functools.partial(per_device, (mesh.shape["dp"], mesh.shape["fsdp"])),
         mesh=mesh,
         in_specs=placed,
         out_specs=(

time: 651 us -> 540 us (0.83)
  waiting for transfers between devices: 465 us -> 273 us
  starting transfers between devices: 0.38 us -> 69.7 us
  Pallas kernels: 0 us -> 15.6 us
  other arithmetic: 15 us -> 29.4 us
  matrix products: 91.8 us -> 79.4 us
    unnamed x6 -> x2, waiting for transfers between devices: 275 us -> 0.03 us
    ppermute x0 -> x44, waiting for transfers between devices: none -> 82.7 us  [swap(): return lax.ppermute(value, ('dp', 'fsdp'), route)]
    ppermute x0 -> x44, starting transfers between devices: none -> 69.6 us  [swap(): return lax.ppermute(value, ('dp', 'fsdp'), route)]
    pallas_call x0 -> x4, Pallas kernels: none -> 15.6 us  [the longest x2 10 us: ffn_terms(): pl.pallas_call(body, grid=(2 * steps,), in_specs=[whole(v) for v in norme...]
    dot_general x8 -> x16, matrix products: 25.9 us -> 17.4 us  [share_left(): lax.dot_general(order, value, (((0,), (1,)), ((), ())), preferred_element...]
    convert_element_type x3 -> x0, local copies, waits for them, and re-layouts: 8.04 us -> none  [the longest x1 4.23 us: layer_backward(): product_left_t(inputs_low, grad_qkv).astype(low)]
    convert_element_type x6 -> x12, local copies, waits for them, and re-layouts: 4.19 us -> 11.1 us  [attend_backward(): member.reshape(token_count, -1).astype(jnp.bfloat16)]
    unnamed x197 -> x244, local copies, waits for them, and re-layouts: 22.8 us -> 19.4 us
  transfers between devices with their start and end apart: 4 -> 46, of which waited for: 4 -> 19; matrix products, arithmetic and copies ran while one was open for 11% -> 12% of each run, Pallas kernels for 0% -> 3%
where the time goes in v2:
time: 540 us; the launch traced here: 534 us
  waiting for transfers between devices  273 us (51%)
  matrix products  79.4 us (15%)
  starting transfers between devices  69.7 us (13%)
  local copies, waits for them, and re-layouts  49.6 us (9%)
  other arithmetic  29.4 us (5%)
  between operations  17 us (3%)
  Pallas kernels  15.6 us (3%)
    all_gather x2, waiting for transfers between devices, collect(): lax.all_gather(pack(shards, layer), ('dp', 'fsdp'), axis=0, tiled=True)  190 us
    ppermute x44, waiting for transfers between devices, swap(): return lax.ppermute(value, ('dp', 'fsdp'), route)  82.7 us
    ppermute x44, starting transfers between devices, swap(): return lax.ppermute(value, ('dp', 'fsdp'), route)  69.6 us
    dot_general x8, matrix products, product(): return jnp.dot(left, right, preferred_element_type=jnp.float32)  26.3 us
    dot_general x8, matrix products, product_right_t(): lax.dot_general(left, right, (((1,), (1,)), ((), ())), preferred_element_...  25.6 us
    unnamed x244, local copies, waits for them, and re-layouts  19.4 us
    dot_general x16, matrix products, share_left(): lax.dot_general(order, value, (((0,), (1,)), ((), ())), preferred_element...  17.4 us
    convert_element_type x12, local copies, waits for them, and re-layouts, attend_backward(): member.reshape(token_count, -1).astype(jnp.bfloat16)  11.1 us
  transfers between devices with their start and end apart: 46, of which 19 were waited for; matrix products, arithmetic and copies ran while one was open for 12% of the time, Pallas kernels for 3%

profile of v2, /device:TPU:0, one launch (start us, length us, event | category | flops | bytes accessed | tf_op | source)
XLA Modules:
  0.0 533.7 jit_solution(7144619133443516480)
XLA Ops:
  18.8 102.3 %all-gather.3.cloned.1.call-done = bf16[768,9344]{1,0:T(8,128)(2,1)} async-done(((bf16[24,9344]{1,0:T(8,128)(2,1)}), bf16[768,9344]{1,0:T(8,128)(2,1)}) %all-gather.3.cloned.1.call-update) | async-done | bytes 14352400 | tf_op jit(solution)/shard_map/all_gather | solution.py:53
  121.1 3.1 fusion.16
  126.6 1.6 convert_bitcast_fusion.1
  128.7 2.5 fusion.220
  132.2 3.6 multiply_convert_fusion.1
  135.8 1.5 fusion.221
  138.8 88.0 %all-gather.5.cloned.1.call-done = bf16[768,9344]{1,0:T(8,128)(2,1)} async-done(((bf16[24,9344]{1,0:T(8,128)(2,1)}), bf16[768,9344]{1,0:T(8,128)(2,1)}) %all-gather.5.cloned.1.call-update) | async-done | bytes 14352400 | tf_op jit(solution)/shard_map/all_gather | solution.py:53
  226.8 3.1 convolution_convert_fusion
  230.3 3.6 rev.20
  235.2 3.7 rev.18
  238.9 1.7 fusion.222
  243.3 1.9 fusion.223
  245.7 3.8 multiply_convert_fusion
  249.5 4.7 fusion.224
  256.7 3.0 fusion.30.ua
  259.7 2.1 multiply_reduce_fusion.2
  264.5 1.9 copy.168
  266.4 1.8 reshape.227
  268.3 2.5 convolution_bitcast_fusion
  277.2 2.1 copy.181
  281.4 1.9 copy.180
  283.4 4.2 multiply_reduce_fusion.3
  289.7 5.4 %fusion.23.ua = bf16[256,3072]{1,0:T(8,128)(2,1)S(1)} fusion(f32[256,3072]{1,0:T(8,128)S(1)} %copy-done.109, bf16[256,768]{1,0:T(8,128)(2,1)S(1)} %add_convert_fusion.9, bf16[768,9344]{1,0:T(8,128)(2,1)} %all-gather.3.cloned.1.call-done), kind=kOutput, calls=%fused_computation.29 | convolution fusion | flops 1223688192 | bytes 9830400 | tf_op jit(solution)/shard_map/dot_general | solution.py:30
  295.1 5.6 %multiply_reduce_fusion.4 = (bf16[768]{0:T(1024)(128)(2,1)}, f32[256]{0:T(256)S(1)}, f32[256,768]{1,0:T(8,128)S(1)}) fusion(f32[256,768]{1,0:T(8,128)S(1)} %copy-done.16, f32[256]{0:T(256)S(1)} %copy-done.76, f32[256]{0:T(256)S(1)} %copy-done.71, f32[768]{0:T(1024)S(1)} %copy-done.66, bf16[256,3072]{1,0:T(8,128)(2,1)S(1)} %fusion.23.ua, ...), kind=kOutput, calls=%fused_computation.166 | convolution fusion | flops 1209728000 | bytes 8659456 | tf_op jit(solution)/shard_map/dot_general | solution.py:40
  302.1 1.8 convolution_convert_fusion.3
  325.0 4.5 fusion.70
  336.4 1.8 convolution_convert_fusion.9
  338.8 3.0 shard_map.206
  341.8 1.5 collective-permute-start.17
  345.0 2.7 shard_map.205
  347.8 3.5 collective-permute-done.17
  351.3 1.5 collective-permute-start.15
  352.8 7.1 %collective-permute-done.15 = bf16[48,3200]{1,0:T(8,128)(2,1)S(1)} collective-permute-done((bf16[48,3200]{1,0:T(8,128)(2,1)S(1)}, bf16[48,3200]{1,0:T(8,128)(2,1)S(1)}, u32[]{:S(2)}, u32[]{:S(2)}) %collective-permute-start.15) | collective-permute-done | bytes 307232 | tf_op jit(solution)/shard_map/ppermute | solution.py:264
  361.4 6.2 %collective-permute-done.6 = bf16[48,3200]{1,0:T(8,128)(2,1)S(1)} collective-permute-done((bf16[48,3200]{1,0:T(8,128)(2,1)S(1)}, bf16[48,3200]{1,0:T(8,128)(2,1)S(1)}, u32[]{:S(2)}, u32[]{:S(2)}) %collective-permute-start.6) | collective-permute-done | bytes 307232 | tf_op jit(solution)/shard_map/ppermute | solution.py:264
  367.6 1.4 collective-permute-start.4
  369.2 5.3 collective-permute-done.4
  378.8 1.4 collective-permute-start.18
  381.0 5.0 shard_map.208
  386.2 1.5 collective-permute-start.7
  389.7 5.0 shard_map.207
  395.5 1.4 collective-permute-start.37
  397.7 11.0 %collective-permute-done.7 = bf16[96,3200]{1,0:T(8,128)(2,1)S(1)} collective-permute-done((bf16[96,3200]{1,0:T(8,128)(2,1)S(1)}, bf16[96,3200]{1,0:T(8,128)(2,1)S(1)}, u32[]{:S(2)}, u32[]{:S(2)}) %collective-permute-start.7) | collective-permute-done | bytes 614432 | tf_op jit(solution)/shard_map/ppermute | solution.py:264
  408.7 1.4 collective-permute-start.26
  410.2 2.5 collective-permute-start.19
  412.9 10.0 %collective-permute-done.39 = bf16[48,6144]{1,0:T(8,128)(2,1)S(1)} collective-permute-done((bf16[48,6144]{1,0:T(8,128)(2,1)S(1)}, bf16[48,6144]{1,0:T(8,128)(2,1)S(1)}, u32[]{:S(2)}, u32[]{:S(2)}) %collective-permute-start.39) | collective-permute-done | bytes 589856 | tf_op jit(solution)/shard_map/ppermute | solution.py:264
  422.8 2.5 collective-permute-start.8
  428.6 5.8 %collective-permute-done.28 = bf16[48,6144]{1,0:T(8,128)(2,1)S(1)} collective-permute-done((bf16[48,6144]{1,0:T(8,128)(2,1)S(1)}, bf16[48,6144]{1,0:T(8,128)(2,1)S(1)}, u32[]{:S(2)}, u32[]{:S(2)}) %collective-permute-start.28) | collective-permute-done | bytes 589856 | tf_op jit(solution)/shard_map/ppermute | solution.py:264
  436.2 1.4 collective-permute-start.29
  441.2 16.9 %collective-permute-start.21 = (bf16[24,3200]{1,0:T(8,128)(2,1)S(1)}, bf16[24,3200]{1,0:T(8,128)(2,1)S(1)}, u32[]{:S(2)}, u32[]{:S(2)}) collective-permute-start(bf16[24,3200]{1,0:T(8,128)(2,1)S(1)} %slice.576), channel_id=1, source_target_pairs={{0,2},{1,3},{2,0},{3,1},{4,6},{5,7},{6,4},{7,5},{8,10},{9,11},{10,... | collective-permute-start | bytes 460808 | tf_op jit(solution)/shard_map/ppermute | solution.py:264
  458.3 4.4 collective-permute-done.21
  462.7 2.2 collective-permute-start.10
  465.0 3.2 collective-permute-done.10
  474.3 1.5 add_convert_fusion.1
  475.7 4.0 collective-permute-start.41
  479.7 4.2 collective-permute-done.29
  483.8 3.0 collective-permute-done.27
  486.8 1.5 add_convert_fusion.5
  488.3 2.6 collective-permute-start.30
  491.7 9.9 %collective-permute-done.30 = bf16[48,6144]{1,0:T(8,128)(2,1)S(1)} collective-permute-done((bf16[48,6144]{1,0:T(8,128)(2,1)S(1)}, bf16[48,6144]{1,0:T(8,128)(2,1)S(1)}, u32[]{:S(2)}, u32[]{:S(2)}) %collective-permute-start.30) | collective-permute-done | bytes 589856 | tf_op jit(solution)/shard_map/ppermute | solution.py:264
  502.5 1.5 convert_add_fusion
  504.0 5.2 collective-permute-start.43
  509.2 1.5 convert_add_fusion.1
  510.8 9.3 %collective-permute-start.32 = (bf16[24,6144]{1,0:T(8,128)(2,1)S(1)}, bf16[24,6144]{1,0:T(8,128)(2,1)S(1)}, u32[]{:S(2)}, u32[]{:S(2)}) collective-permute-start(bf16[24,6144]{1,0:T(8,128)(2,1)S(1)} %slice.575), channel_id=1, source_target_pairs={{0,2},{1,3},{2,0},{3,1},{4,6},{5,7},{6,4},{7,5},{8,10},{9,11},{10,... | collective-permute-start | bytes 884744 | tf_op jit(solution)/shard_map/ppermute | solution.py:264
  520.2 4.6 collective-permute-done.32
  (475 shorter events, 96.6 us)
Async XLA Ops:
  7.2 8.8 %copy-start.93 = (s32[384]{0:T(512)S(1)}, s32[384]{0:T(512)}, u32[]{:S(2)}) copy-start(s32[384]{0:T(512)} %constant.111.clone) | copy-start | bytes 4612
  7.2 8.8 %copy-start.94 = (s32[384]{0:T(512)S(1)}, s32[384]{0:T(512)}, u32[]{:S(2)}) copy-start(s32[384]{0:T(512)} %constant.109.clone) | copy-start | bytes 4612
  7.2 8.8 %copy-start.101 = (pred[384]{0:T(512)(128)(4,1)S(1)}, pred[384]{0:T(512)(128)(4,1)}, u32[]{:S(2)}) copy-start(pred[384]{0:T(512)(128)(4,1)} %constant.130) | copy-start | bytes 1156
  7.2 8.8 %copy-start.95 = (s32[384]{0:T(512)S(1)}, s32[384]{0:T(512)}, u32[]{:S(2)}) copy-start(s32[384]{0:T(512)} %constant.110.clone) | copy-start | bytes 4612
  7.2 8.8 %copy-start.96 = (s32[384]{0:T(512)S(1)}, s32[384]{0:T(512)}, u32[]{:S(2)}) copy-start(s32[384]{0:T(512)} %constant.132) | copy-start | bytes 4612
  7.2 8.8 %copy-start.97 = (s32[384]{0:T(512)S(1)}, s32[384]{0:T(512)}, u32[]{:S(2)}) copy-start(s32[384]{0:T(512)} %constant.108.clone) | copy-start | bytes 4612
  7.3 9.4 %copy-start.102 = (bf16[1,256,768]{2,1,0:T(8,128)(2,1)S(1)}, bf16[1,256,768]{2,1,0:T(8,128)(2,1)}, u32[]{:S(2)}) copy-start(bf16[1,256,768]{2,1,0:T(8,128)(2,1)} %param.14) | copy-start | bytes 1179652
  7.3 113.8 %all-gather.3.cloned.1.call-start = ((), (), s32[]{:S(2)}) async-start(), calls=%async_computation | async-start | bytes 14800896 | tf_op jit(solution)/shard_map/all_gather | solution.py:53
  14.1 212.7 %all-gather.5.cloned.1.call-start = ((), (), s32[]{:S(2)}) async-start(), calls=%async_computation.1 | async-start | bytes 14800896 | tf_op jit(solution)/shard_map/all_gather | solution.py:53
  125.3 6.9 %copy-start.88 = (bf16[768,9344]{1,0:T(8,128)(2,1)S(1)}, bf16[768,9344]{1,0:T(8,128)(2,1)}, u32[]{:S(2)}) copy-start(bf16[768,9344]{1,0:T(8,128)(2,1)} %all-gather.3.cloned.1.call-done) | copy-start | bytes 43057156
  128.7 7.1 %copy-start.65 = (f32[768]{0:T(1024)}, f32[768]{0:T(1024)S(1)}, u32[]{:S(2)}) copy-start(f32[768]{0:T(1024)S(1)} %get-tuple-element.60) | copy-start | bytes 9220
  128.7 9.4 %copy-start.67 = (f32[768]{0:T(1024)}, f32[768]{0:T(1024)S(1)}, u32[]{:S(2)}) copy-start(f32[768]{0:T(1024)S(1)} %get-tuple-element.59) | copy-start | bytes 9220
  138.8 88.0 %copy-start.51 = (bf16[256,768]{1,0:T(8,128)(2,1)}, bf16[256,768]{1,0:T(8,128)(2,1)S(1)}, u32[]{:S(2)}) copy-start(bf16[256,768]{1,0:T(8,128)(2,1)S(1)} %multiply_convert_fusion.7) | copy-start | bytes 1179652
  245.7 11.0 %slice-start = ((s8[14352384]{0:T(1024)(128)(4,1)}), s8[4194304]{0:T(1024)(128)(4,1)S(1)}, s32[]{:S(2)}) async-start(s8[14352384]{0:T(1024)(128)(4,1)} %bitcast.237), calls=%async_computation.2 | async-start | bytes 8388608
  245.7 11.0 %slice-start.1 = ((s8[14352384]{0:T(1024)(128)(4,1)}), s8[4194304]{0:T(1024)(128)(4,1)S(1)}, s32[]{:S(2)}) async-start(s8[14352384]{0:T(1024)(128)(4,1)} %bitcast.237), calls=%async_computation.3 | async-start | bytes 8388608
  249.5 7.2 %slice-start.2 = ((s8[14352384]{0:T(1024)(128)(4,1)}), s8[4194304]{0:T(1024)(128)(4,1)S(1)}, s32[]{:S(2)}) async-start(s8[14352384]{0:T(1024)(128)(4,1)} %bitcast.237), calls=%async_computation.4 | async-start | bytes 8388608
  249.5 7.2 %slice-start.3 = ((s8[14352384]{0:T(1024)(128)(4,1)}), s8[1769472]{0:T(1024)(128)(4,1)S(1)}, s32[]{:S(2)}) async-start(s8[14352384]{0:T(1024)(128)(4,1)} %bitcast.237), calls=%async_computation.5 | async-start | bytes 3538944
  311.0 27.5 %collective-permute-start.14 = (bf16[256,768]{1,0:T(8,128)(2,1)S(1)}, bf16[256,768]{1,0:T(8,128)(2,1)S(1)}, u32[]{:S(2)}, u32[]{:S(2)}) collective-permute-start(bf16[256,768]{1,0:T(8,128)(2,1)S(1)} %add_convert_fusion.10.oa), channel_id=1, source_target_pairs={{0,8},{1,9},{2,10},{3,11},{4,12},{5,13},{6,14},{7,15},{8,0},{9,1},... | collective-permute-start | bytes 1179656 | tf_op jit(solution)/shard_map/ppermute | solution.py:264
  321.9 14.2 %collective-permute-start.11 = (bf16[384,256]{1,0:T(8,128)(2,1)}, bf16[384,256]{1,0:T(8,128)(2,1)}, u32[]{:S(2)}, u32[]{:S(2)}) collective-permute-start(bf16[384,256]{1,0:T(8,128)(2,1)} %fusion.122), channel_id=1, source_target_pairs={{0,8},{1,9},{2,10},{3,11},{4,12},{5,13},{6,14},{7,15},{8,0},{9,1},... | collective-permute-start | bytes 589832 | tf_op jit(solution)/shard_map/ppermute | solution.py:264
  322.1 16.7 %collective-permute-start.12 = (bf16[256,2304]{1,0:T(8,128)(2,1)S(1)}, bf16[256,2304]{1,0:T(8,128)(2,1)}, u32[]{:S(2)}, u32[]{:S(2)}) collective-permute-start(bf16[256,2304]{1,0:T(8,128)(2,1)S(1)} %pad_maximum_fusion.qa), channel_id=1, source_target_pairs={{0,8},{1,9},{2,10},{3,11},{4,12},{5,13},{6,14},{7,15},{8,0},{9,1},... | collective-permute-start | bytes 3538952 | tf_op jit(solution)/shard_map/ppermute | solution.py:264
  324.7 19.9 %collective-permute-start.1 = (bf16[256,2304]{1,0:T(8,128)(2,1)S(1)}, bf16[256,2304]{1,0:T(8,128)(2,1)}, u32[]{:S(2)}, u32[]{:S(2)}) collective-permute-start(bf16[256,2304]{1,0:T(8,128)(2,1)S(1)} %pad_maximum_fusion.1.qa), channel_id=1, source_target_pairs={{0,8},{1,9},{2,10},{3,11},{4,12},{5,13},{6,14},{7,15},{8,0},{9,1},... | collective-permute-start | bytes 3538952 | tf_op jit(solution)/shard_map/ppermute | solution.py:264
  334.9 3.3 collective-permute-start.13
  336.0 8.4 %collective-permute-start.3 = (bf16[256,768]{1,0:T(8,128)(2,1)S(1)}, bf16[256,768]{1,0:T(8,128)(2,1)S(1)}, u32[]{:S(2)}, u32[]{:S(2)}) collective-permute-start(bf16[256,768]{1,0:T(8,128)(2,1)S(1)} %add_convert_fusion.8.oa), channel_id=1, source_target_pairs={{0,8},{1,9},{2,10},{3,11},{4,12},{5,13},{6,14},{7,15},{8,0},{9,1},... | collective-permute-start | bytes 1179656 | tf_op jit(solution)/shard_map/ppermute | solution.py:264
  338.2 5.7 %collective-permute-start = (bf16[384,256]{1,0:T(8,128)(2,1)S(1)}, bf16[384,256]{1,0:T(8,128)(2,1)S(1)}, u32[]{:S(2)}, u32[]{:S(2)}) collective-permute-start(bf16[384,256]{1,0:T(8,128)(2,1)S(1)} %copy-done.104), channel_id=1, source_target_pairs={{0,8},{1,9},{2,10},{3,11},{4,12},{5,13},{6,14},{7,15},{8,0},{9,1},... | collective-permute-start | bytes 589832 | tf_op jit(solution)/shard_map/ppermute | solution.py:264
  338.5 5.4 %collective-permute-start.2 = (bf16[384,384]{1,0:T(8,128)(2,1)S(1)}, bf16[384,384]{1,0:T(8,128)(2,1)S(1)}, u32[]{:S(2)}, u32[]{:S(2)}) collective-permute-start(bf16[384,384]{1,0:T(8,128)(2,1)S(1)} %convolution_convert_fusion.9), channel_id=1, source_target_pairs={{0,8},{1,9},{2,10},{3,11},{4,12},{5,13},{6,14},{7,15},{8,0},{9,1},... | collective-permute-start | bytes 884744 | tf_op jit(solution)/shard_map/ppermute | solution.py:264
  341.8 9.5 %collective-permute-start.17 = (bf16[48,3200]{1,0:T(8,128)(2,1)S(1)}, bf16[48,3200]{1,0:T(8,128)(2,1)S(1)}, u32[]{:S(2)}, u32[]{:S(2)}) collective-permute-start(bf16[48,3200]{1,0:T(8,128)(2,1)S(1)} %get-tuple-element.38), channel_id=1, source_target_pairs={{0,16},{1,17},{2,18},{3,19},{4,20},{5,21},{6,22},{7,23},{8,24},{9,... | collective-permute-start | bytes 921608 | tf_op jit(solution)/shard_map/ppermute | solution.py:264
  343.9 36.4 %collective-permute-start.34 = (bf16[256,3072]{1,0:T(8,128)(2,1)S(1)}, bf16[256,3072]{1,0:T(8,128)(2,1)S(1)}, u32[]{:S(2)}, u32[]{:S(2)}) collective-permute-start(bf16[256,3072]{1,0:T(8,128)(2,1)S(1)} %copy-done.5), channel_id=1, source_target_pairs={{0,8},{1,9},{2,10},{3,11},{4,12},{5,13},{6,14},{7,15},{8,0},{9,1},... | collective-permute-start | bytes 4718600 | tf_op jit(solution)/shard_map/ppermute | solution.py:264
  344.0 36.9 %collective-permute-start.36 = (bf16[256,3072]{1,0:T(8,128)(2,1)S(1)}, bf16[256,3072]{1,0:T(8,128)(2,1)S(1)}, u32[]{:S(2)}, u32[]{:S(2)}) collective-permute-start(bf16[256,3072]{1,0:T(8,128)(2,1)S(1)} %copy-done.3), channel_id=1, source_target_pairs={{0,8},{1,9},{2,10},{3,11},{4,12},{5,13},{6,14},{7,15},{8,0},{9,1},... | collective-permute-start | bytes 4718600 | tf_op jit(solution)/shard_map/ppermute | solution.py:264
  344.5 43.2 %collective-permute-start.23 = (bf16[256,3072]{1,0:T(8,128)(2,1)S(1)}, bf16[256,3072]{1,0:T(8,128)(2,1)S(1)}, u32[]{:S(2)}, u32[]{:S(2)}) collective-permute-start(bf16[256,3072]{1,0:T(8,128)(2,1)S(1)} %copy-done.7), channel_id=1, source_target_pairs={{0,8},{1,9},{2,10},{3,11},{4,12},{5,13},{6,14},{7,15},{8,0},{9,1},... | collective-permute-start | bytes 4718600 | tf_op jit(solution)/shard_map/ppermute | solution.py:264
  344.6 43.7 %collective-permute-start.25 = (bf16[256,3072]{1,0:T(8,128)(2,1)S(1)}, bf16[256,3072]{1,0:T(8,128)(2,1)S(1)}, u32[]{:S(2)}, u32[]{:S(2)}) collective-permute-start(bf16[256,3072]{1,0:T(8,128)(2,1)S(1)} %copy-done.1), channel_id=1, source_target_pairs={{0,8},{1,9},{2,10},{3,11},{4,12},{5,13},{6,14},{7,15},{8,0},{9,1},... | collective-permute-start | bytes 4718600 | tf_op jit(solution)/shard_map/ppermute | solution.py:264
  347.7 26.8 %copy-start.108 = (bf16[384,256]{1,0:T(8,128)(2,1)S(1)}, bf16[384,256]{1,0:T(8,128)(2,1)}, u32[]{:S(2)}) copy-start(bf16[384,256]{1,0:T(8,128)(2,1)} %fusion.131) | copy-start | bytes 589828
  351.3 8.6 %collective-permute-start.15 = (bf16[48,3200]{1,0:T(8,128)(2,1)S(1)}, bf16[48,3200]{1,0:T(8,128)(2,1)S(1)}, u32[]{:S(2)}, u32[]{:S(2)}) collective-permute-start(bf16[48,3200]{1,0:T(8,128)(2,1)S(1)} %get-tuple-element.36), channel_id=1, source_target_pairs={{0,1},{1,0},{2,3},{3,2},{4,5},{5,4},{6,7},{7,6},{8,9},{9,8},{10,11... | collective-permute-start | bytes 921608 | tf_op jit(solution)/shard_map/ppermute | solution.py:264
  359.9 7.7 %collective-permute-start.6 = (bf16[48,3200]{1,0:T(8,128)(2,1)S(1)}, bf16[48,3200]{1,0:T(8,128)(2,1)S(1)}, u32[]{:S(2)}, u32[]{:S(2)}) collective-permute-start(bf16[48,3200]{1,0:T(8,128)(2,1)S(1)} %get-tuple-element.33), channel_id=1, source_target_pairs={{0,16},{1,17},{2,18},{3,19},{4,20},{5,21},{6,22},{7,23},{8,24},{9,... | collective-permute-start | bytes 921608 | tf_op jit(solution)/shard_map/ppermute | solution.py:264
  361.4 14.5 %copy-start.106 = (bf16[384,256]{1,0:T(8,128)(2,1)S(1)}, bf16[384,256]{1,0:T(8,128)(2,1)}, u32[]{:S(2)}) copy-start(bf16[384,256]{1,0:T(8,128)(2,1)} %fusion.134) | copy-start | bytes 589828
  367.6 6.9 %collective-permute-start.4 = (bf16[48,3200]{1,0:T(8,128)(2,1)S(1)}, bf16[48,3200]{1,0:T(8,128)(2,1)S(1)}, u32[]{:S(2)}, u32[]{:S(2)}) collective-permute-start(bf16[48,3200]{1,0:T(8,128)(2,1)S(1)} %get-tuple-element.31), channel_id=1, source_target_pairs={{0,1},{1,0},{2,3},{3,2},{4,5},{5,4},{6,7},{7,6},{8,9},{9,8},{10,11... | collective-permute-start | bytes 921608 | tf_op jit(solution)/shard_map/ppermute | solution.py:264
  369.2 8.2 %copy-start.105 = (bf16[384,256]{1,0:T(8,128)(2,1)S(1)}, bf16[384,256]{1,0:T(8,128)(2,1)}, u32[]{:S(2)}) copy-start(bf16[384,256]{1,0:T(8,128)(2,1)} %fusion.125) | copy-start | bytes 589828
  374.5 1.4 collective-permute-start.33
  375.9 1.4 collective-permute-start.35
  377.4 1.4 collective-permute-start.22
  378.8 16.7 %collective-permute-start.18 = (bf16[96,3200]{1,0:T(8,128)(2,1)S(1)}, bf16[96,3200]{1,0:T(8,128)(2,1)S(1)}, u32[]{:S(2)}, u32[]{:S(2)}) collective-permute-start(bf16[96,3200]{1,0:T(8,128)(2,1)S(1)} %pad_maximum_fusion.9), channel_id=1, source_target_pairs={{0,1},{1,0},{2,3},{3,2},{4,5},{5,4},{6,7},{7,6},{8,9},{9,8},{10,11... | collective-permute-start | bytes 1843208 | tf_op jit(solution)/shard_map/ppermute | solution.py:264
  380.3 16.7 %collective-permute-start.16 = (bf16[96,3200]{1,0:T(8,128)(2,1)S(1)}, bf16[96,3200]{1,0:T(8,128)(2,1)S(1)}, u32[]{:S(2)}, u32[]{:S(2)}) collective-permute-start(bf16[96,3200]{1,0:T(8,128)(2,1)S(1)} %pad_maximum_fusion.8), channel_id=1, source_target_pairs={{0,16},{1,17},{2,18},{3,19},{4,20},{5,21},{6,22},{7,23},{8,24},{9,... | collective-permute-start | bytes 1843208 | tf_op jit(solution)/shard_map/ppermute | solution.py:264
  380.9 5.2 collective-permute-start.24
  386.2 22.5 %collective-permute-start.7 = (bf16[96,3200]{1,0:T(8,128)(2,1)S(1)}, bf16[96,3200]{1,0:T(8,128)(2,1)S(1)}, u32[]{:S(2)}, u32[]{:S(2)}) collective-permute-start(bf16[96,3200]{1,0:T(8,128)(2,1)S(1)} %pad_maximum_fusion.7), channel_id=1, source_target_pairs={{0,1},{1,0},{2,3},{3,2},{4,5},{5,4},{6,7},{7,6},{8,9},{9,8},{10,11... | collective-permute-start | bytes 1843208 | tf_op jit(solution)/shard_map/ppermute | solution.py:264
  387.7 22.5 %collective-permute-start.5 = (bf16[96,3200]{1,0:T(8,128)(2,1)S(1)}, bf16[96,3200]{1,0:T(8,128)(2,1)S(1)}, u32[]{:S(2)}, u32[]{:S(2)}) collective-permute-start(bf16[96,3200]{1,0:T(8,128)(2,1)S(1)} %pad_maximum_fusion.6), channel_id=1, source_target_pairs={{0,16},{1,17},{2,18},{3,19},{4,20},{5,21},{6,22},{7,23},{8,24},{9,... | collective-permute-start | bytes 1843208 | tf_op jit(solution)/shard_map/ppermute | solution.py:264
  388.3 34.5 %collective-permute-start.39 = (bf16[48,6144]{1,0:T(8,128)(2,1)S(1)}, bf16[48,6144]{1,0:T(8,128)(2,1)S(1)}, u32[]{:S(2)}, u32[]{:S(2)}) collective-permute-start(bf16[48,6144]{1,0:T(8,128)(2,1)S(1)} %get-tuple-element.48), channel_id=1, source_target_pairs={{0,16},{1,17},{2,18},{3,19},{4,20},{5,21},{6,22},{7,23},{8,24},{9,... | collective-permute-start | bytes 1769480 | tf_op jit(solution)/shard_map/ppermute | solution.py:264
  395.5 31.1 %collective-permute-start.37 = (bf16[48,6144]{1,0:T(8,128)(2,1)S(1)}, bf16[48,6144]{1,0:T(8,128)(2,1)S(1)}, u32[]{:S(2)}, u32[]{:S(2)}) collective-permute-start(bf16[48,6144]{1,0:T(8,128)(2,1)S(1)} %get-tuple-element.46), channel_id=1, source_target_pairs={{0,1},{1,0},{2,3},{3,2},{4,5},{5,4},{6,7},{7,6},{8,9},{9,8},{10,11... | collective-permute-start | bytes 1769480 | tf_op jit(solution)/shard_map/ppermute | solution.py:264
  397.0 37.3 %collective-permute-start.28 = (bf16[48,6144]{1,0:T(8,128)(2,1)S(1)}, bf16[48,6144]{1,0:T(8,128)(2,1)S(1)}, u32[]{:S(2)}, u32[]{:S(2)}) collective-permute-start(bf16[48,6144]{1,0:T(8,128)(2,1)S(1)} %get-tuple-element.43), channel_id=1, source_target_pairs={{0,16},{1,17},{2,18},{3,19},{4,20},{5,21},{6,22},{7,23},{8,24},{9,... | collective-permute-start | bytes 1769480 | tf_op jit(solution)/shard_map/ppermute | solution.py:264
  408.7 27.5 %collective-permute-start.26 = (bf16[48,6144]{1,0:T(8,128)(2,1)S(1)}, bf16[48,6144]{1,0:T(8,128)(2,1)S(1)}, u32[]{:S(2)}, u32[]{:S(2)}) collective-permute-start(bf16[48,6144]{1,0:T(8,128)(2,1)S(1)} %get-tuple-element.41), channel_id=1, source_target_pairs={{0,1},{1,0},{2,3},{3,2},{4,5},{5,4},{6,7},{7,6},{8,9},{9,8},{10,11... | collective-permute-start | bytes 1769480 | tf_op jit(solution)/shard_map/ppermute | solution.py:264
  410.2 28.7 %collective-permute-start.19 = (bf16[48,3200]{1,0:T(8,128)(2,1)S(1)}, bf16[48,3200]{1,0:T(8,128)(2,1)S(1)}, u32[]{:S(2)}, u32[]{:S(2)}) collective-permute-start(bf16[48,3200]{1,0:T(8,128)(2,1)S(1)} %add_convert_fusion.13), channel_id=1, source_target_pairs={{0,2},{1,3},{6,4},{7,5},{8,10},{9,11},{14,12},{15,13},{16,18},{17,... | collective-permute-start | bytes 921608 | tf_op jit(solution)/shard_map/ppermute | solution.py:264
  422.8 16.7 %collective-permute-start.8 = (bf16[48,3200]{1,0:T(8,128)(2,1)S(1)}, bf16[48,3200]{1,0:T(8,128)(2,1)S(1)}, u32[]{:S(2)}, u32[]{:S(2)}) collective-permute-start(bf16[48,3200]{1,0:T(8,128)(2,1)S(1)} %add_convert_fusion.17), channel_id=1, source_target_pairs={{0,2},{1,3},{6,4},{7,5},{8,10},{9,11},{14,12},{15,13},{16,18},{17,... | collective-permute-start | bytes 921608 | tf_op jit(solution)/shard_map/ppermute | solution.py:264
  426.7 47.6 %collective-permute-start.40 = (bf16[96,6144]{1,0:T(8,128)(2,1)}, bf16[96,6144]{1,0:T(8,128)(2,1)}, u32[]{:S(2)}, u32[]{:S(2)}) collective-permute-start(bf16[96,6144]{1,0:T(8,128)(2,1)} %pad_maximum_fusion.5), channel_id=1, source_target_pairs={{0,1},{1,0},{2,3},{3,2},{4,5},{5,4},{6,7},{7,6},{8,9},{9,8},{10,11... | collective-permute-start | bytes 3538952 | tf_op jit(solution)/shard_map/ppermute | solution.py:264
  434.3 39.9 %collective-permute-start.38 = (bf16[96,6144]{1,0:T(8,128)(2,1)}, bf16[96,6144]{1,0:T(8,128)(2,1)}, u32[]{:S(2)}, u32[]{:S(2)}) collective-permute-start(bf16[96,6144]{1,0:T(8,128)(2,1)} %pad_maximum_fusion.4), channel_id=1, source_target_pairs={{0,16},{1,17},{2,18},{3,19},{4,20},{5,21},{6,22},{7,23},{8,24},{9,... | collective-permute-start | bytes 3538952 | tf_op jit(solution)/shard_map/ppermute | solution.py:264
  436.2 47.7 %collective-permute-start.29 = (bf16[96,6144]{1,0:T(8,128)(2,1)}, bf16[96,6144]{1,0:T(8,128)(2,1)}, u32[]{:S(2)}, u32[]{:S(2)}) collective-permute-start(bf16[96,6144]{1,0:T(8,128)(2,1)} %pad_maximum_fusion.3), channel_id=1, source_target_pairs={{0,1},{1,0},{2,3},{3,2},{4,5},{5,4},{6,7},{7,6},{8,9},{9,8},{10,11... | collective-permute-start | bytes 3538952 | tf_op jit(solution)/shard_map/ppermute | solution.py:264
  438.8 48.0 %collective-permute-start.27 = (bf16[96,6144]{1,0:T(8,128)(2,1)}, bf16[96,6144]{1,0:T(8,128)(2,1)}, u32[]{:S(2)}, u32[]{:S(2)}) collective-permute-start(bf16[96,6144]{1,0:T(8,128)(2,1)} %pad_maximum_fusion.2), channel_id=1, source_target_pairs={{0,16},{1,17},{2,18},{3,19},{4,20},{5,21},{6,22},{7,23},{8,24},{9,... | collective-permute-start | bytes 3538952 | tf_op jit(solution)/shard_map/ppermute | solution.py:264
  439.5 0.8 collective-permute-start.20
  440.3 0.9 collective-permute-start.9
  441.2 21.5 %collective-permute-start.21 = (bf16[24,3200]{1,0:T(8,128)(2,1)S(1)}, bf16[24,3200]{1,0:T(8,128)(2,1)S(1)}, u32[]{:S(2)}, u32[]{:S(2)}) collective-permute-start(bf16[24,3200]{1,0:T(8,128)(2,1)S(1)} %slice.576), channel_id=1, source_target_pairs={{0,2},{1,3},{2,0},{3,1},{4,6},{5,7},{6,4},{7,5},{8,10},{9,11},{10,... | collective-permute-start | bytes 460808 | tf_op jit(solution)/shard_map/ppermute | solution.py:264
  462.7 5.5 %collective-permute-start.10 = (bf16[24,3200]{1,0:T(8,128)(2,1)S(1)}, bf16[24,3200]{1,0:T(8,128)(2,1)}, u32[]{:S(2)}, u32[]{:S(2)}) collective-permute-start(bf16[24,3200]{1,0:T(8,128)(2,1)S(1)} %slice.577), channel_id=1, source_target_pairs={{0,2},{1,3},{2,0},{3,1},{4,6},{5,7},{6,4},{7,5},{8,10},{9,11},{10,... | collective-permute-start | bytes 460808 | tf_op jit(solution)/shard_map/ppermute | solution.py:264
  475.7 15.1 %collective-permute-start.41 = (bf16[48,6144]{1,0:T(8,128)(2,1)S(1)}, bf16[48,6144]{1,0:T(8,128)(2,1)S(1)}, u32[]{:S(2)}, u32[]{:S(2)}) collective-permute-start(bf16[48,6144]{1,0:T(8,128)(2,1)S(1)} %add_convert_fusion.1), channel_id=1, source_target_pairs={{0,2},{1,3},{6,4},{7,5},{8,10},{9,11},{14,12},{15,13},{16,18},{17,... | collective-permute-start | bytes 1769480 | tf_op jit(solution)/shard_map/ppermute | solution.py:264
  488.3 13.3 %collective-permute-start.30 = (bf16[48,6144]{1,0:T(8,128)(2,1)S(1)}, bf16[48,6144]{1,0:T(8,128)(2,1)S(1)}, u32[]{:S(2)}, u32[]{:S(2)}) collective-permute-start(bf16[48,6144]{1,0:T(8,128)(2,1)S(1)} %add_convert_fusion.5), channel_id=1, source_target_pairs={{0,2},{1,3},{6,4},{7,5},{8,10},{9,11},{14,12},{15,13},{16,18},{17,... | collective-permute-start | bytes 1769480 | tf_op jit(solution)/shard_map/ppermute | solution.py:264
  491.0 11.5 %collective-permute-start.42 = (bf16[48,6144]{1,0:T(8,128)(2,1)S(1)}, bf16[48,6144]{1,0:T(8,128)(2,1)S(1)}, u32[]{:S(2)}, u32[]{:S(2)}) collective-permute-start(bf16[48,6144]{1,0:T(8,128)(2,1)S(1)} %add_convert_fusion), channel_id=1, source_target_pairs={{2,4},{3,5},{4,2},{5,3},{10,12},{11,13},{12,10},{13,11},{18,20},{1... | collective-permute-start | bytes 1769480 | tf_op jit(solution)/shard_map/ppermute | solution.py:264
  501.8 7.5 %collective-permute-start.31 = (bf16[48,6144]{1,0:T(8,128)(2,1)S(1)}, bf16[48,6144]{1,0:T(8,128)(2,1)S(1)}, u32[]{:S(2)}, u32[]{:S(2)}) collective-permute-start(bf16[48,6144]{1,0:T(8,128)(2,1)S(1)} %add_convert_fusion.4), channel_id=1, source_target_pairs={{2,4},{3,5},{4,2},{5,3},{10,12},{11,13},{12,10},{13,11},{18,20},{1... | collective-permute-start | bytes 1769480 | tf_op jit(solution)/shard_map/ppermute | solution.py:264
  504.0 16.1 %collective-permute-start.43 = (bf16[24,6144]{1,0:T(8,128)(2,1)S(1)}, bf16[24,6144]{1,0:T(8,128)(2,1)S(1)}, u32[]{:S(2)}, u32[]{:S(2)}) collective-permute-start(bf16[24,6144]{1,0:T(8,128)(2,1)S(1)} %slice.574), channel_id=1, source_target_pairs={{0,2},{1,3},{2,0},{3,1},{4,6},{5,7},{6,4},{7,5},{8,10},{9,11},{10,... | collective-permute-start | bytes 884744 | tf_op jit(solution)/shard_map/ppermute | solution.py:264
  510.8 14.0 %collective-permute-start.32 = (bf16[24,6144]{1,0:T(8,128)(2,1)S(1)}, bf16[24,6144]{1,0:T(8,128)(2,1)S(1)}, u32[]{:S(2)}, u32[]{:S(2)}) collective-permute-start(bf16[24,6144]{1,0:T(8,128)(2,1)S(1)} %slice.575), channel_id=1, source_target_pairs={{0,2},{1,3},{2,0},{3,1},{4,6},{5,7},{6,4},{7,5},{8,10},{9,11},{10,... | collective-permute-start | bytes 884744 | tf_op jit(solution)/shard_map/ppermute | solution.py:264
  (96 other events, 272.8 us)
Sparse Core Ops, SparseCore 0:
  14.2 106.7 all-gather.2
  124.5 102.2 all-gather.4

commit v3 on v1

--- a/solution.py
+++ b/solution.py
@@ -1,6 +1,11 @@
+import functools
+
 import jax
 import jax.numpy as jnp
 from jax import lax
+from jax.experimental import pallas as pl
+from jax.experimental.pallas import tpu as pltpu
+import numpy as np
 from jax.sharding import PartitionSpec as P
 
 D = 768
@@ -37,24 +42,28 @@
     )
 
 
-def pack(shards, layer):
-    query_w, key_w, value_w, out_w, up_w, down_w, gains = (member[layer] for member in shards)
-    rows = query_w.shape[0]
+def pack_attention(shards, layer):
+    query_w, key_w, value_w, out_w, _, _, gains = (member[layer] for member in shards)
     gain_columns = jnp.pad(gains.T, ((0, 0), (0, PAD - 2)))
-    return jnp.concatenate([query_w, key_w, value_w, out_w, up_w, down_w.T, gain_columns], axis=1)
-
-
-def collect(shards, layer):
-    return lax.all_gather(pack(shards, layer), ("dp", "fsdp"), axis=0, tiled=True)
-
-
-def unpack(gathered):
-    qkv_w = gathered[:, : 3 * D]
-    out_w = gathered[:, 3 * D : 4 * D]
-    up_w = gathered[:, 4 * D : 4 * D + FF]
-    down_t = gathered[:, 4 * D + FF : 4 * D + 2 * FF]
-    gains = gathered[:, 4 * D + 2 * FF : 4 * D + 2 * FF + 2].T.astype(jnp.float32)
-    return (qkv_w, out_w, up_w, down_t, gains)
+    return jnp.concatenate([query_w, key_w, value_w, out_w, gain_columns], axis=1)
+
+
+def pack_ffn(shards, layer):
+    return jnp.concatenate([shards[4][layer], shards[5][layer].T], axis=1)
+
+
+def plain_gather(block):
+    return lax.all_gather(block, ("dp", "fsdp"), axis=0, tiled=True)
+
+
+def unpack(attention, ffn):
+    return (
+        attention[:, : 3 * D],
+        attention[:, 3 * D : 4 * D],
+        ffn[:, :FF],
+        ffn[:, FF:],
+        attention[:, 4 * D : 4 * D + 2].T.astype(jnp.float32),
+    )
 
 
 def visible_keys(length, token_count, swap):
@@ -166,59 +175,699 @@
     return (output, kept)
 
 
-def layer_backward(grad_output, kept, weights, swap, length):
-    qkv_w, out_w, up_w, down_t, gains = weights
-    (
-        inputs_low,
-        query,
-        keys,
-        values,
-        log_total,
-        mixed_low,
-        first_sum,
-        normed_low,
-        expanded,
-        activated,
-        second_sum,
-    ) = kept
-    grad_second, grad_gain_second = jax.vjp(norm, second_sum, gains[1])[1](grad_output)
-    down_low = grad_second.astype(jnp.bfloat16)
-    grad_active = product(down_low, down_t)
-    up_low = jax.vjp(gelu_tanh, expanded)[1](grad_active)[0].astype(jnp.bfloat16)
-    grad_normed = grad_second + product_right_t(up_low, up_w)
-    grad_first, grad_gain_first = jax.vjp(norm, first_sum, gains[0])[1](grad_normed)
+def down_backward(grad_output, kept, weights):
+    grad_second, grad_gain = jax.vjp(norm, kept[10], weights[4][1])[1](grad_output)
+    return (grad_second, grad_second.astype(jnp.bfloat16), grad_gain)
+
+
+def up_backward(grad_second, down_low, kept, weights):
+    grad_active = product(down_low, weights[3])
+    up_low = jax.vjp(gelu_tanh, kept[8])[1](grad_active)[0].astype(jnp.bfloat16)
+    return (grad_second + product_right_t(up_low, weights[2]), up_low)
+
+
+def mixed_backward(grad_normed, kept, weights):
+    grad_first, grad_gain = jax.vjp(norm, kept[6], weights[4][0])[1](grad_normed)
     attn_low = grad_first.astype(jnp.bfloat16)
-    grad_mixed = product_right_t(attn_low, out_w).astype(jnp.bfloat16)
-    visible = visible_keys(length, query.shape[0], swap)
-    grad_qkv = jnp.concatenate(
-        attend_backward(query, keys, values, visible, swap, log_total, grad_mixed), axis=1
-    )
-    grad_inputs = grad_first + product_right_t(grad_qkv, qkv_w)
-    gain_columns = jnp.pad(
-        jnp.stack([grad_gain_first, grad_gain_second], axis=1), ((0, 0), (0, PAD - 2))
-    )
-    low = jnp.bfloat16
-    terms = jnp.concatenate(
+    grad_mixed = product_right_t(attn_low, weights[1]).astype(jnp.bfloat16)
+    return (grad_first, attn_low, grad_mixed, grad_gain)
+
+
+def scores_backward(grad_mixed, kept, swapped, length):
+    query, keys, values, log_total = kept[1:5]
+    visible = visible_keys(length, query.shape[0], swapped)
+    return jnp.concatenate(
+        attend_backward(query, keys, values, visible, swapped, log_total, grad_mixed), axis=1
+    )
+
+
+def inputs_backward(grad_first, grad_qkv, weights):
+    return grad_first + product_right_t(grad_qkv, weights[0])
+
+
+def plain_scatter(terms):
+    return lax.psum_scatter(
+        terms.astype(jnp.bfloat16), ("dp", "fsdp"), scatter_dimension=0, tiled=True
+    ).astype(jnp.float32)
+
+
+def plain_ffn_terms(operands):
+    normed_low, up_low, down_low, activated = operands
+    return jnp.concatenate(
         [
-            product_left_t(inputs_low, grad_qkv).astype(low),
-            product_left_t(mixed_low, attn_low).astype(low),
-            product_left_t(normed_low, up_low).astype(low),
-            product_left_t(down_low, activated).astype(low),
-            gain_columns.astype(low),
+            product_left_t(normed_low, up_low).astype(jnp.bfloat16),
+            product_left_t(down_low, activated).astype(jnp.bfloat16),
         ],
         axis=1,
     )
-    return (grad_inputs, terms)
-
-
-def arrange(summed):
-    summed = summed.astype(jnp.float32)
-    bounds = [0, D, 2 * D, 3 * D, 4 * D, 4 * D + FF, 4 * D + 2 * FF, 4 * D + 2 * FF + 2]
-    member = [summed[:, bounds[j] : bounds[j + 1]] for j in range(7)]
-    return (*member[:5], member[5].T, member[6].T)
+
+
+def plain_attention_terms(operands, gains):
+    inputs_low, grad_qkv, mixed_low, attn_low = operands
+    return jnp.concatenate(
+        [
+            product_left_t(inputs_low, grad_qkv).astype(jnp.bfloat16),
+            product_left_t(mixed_low, attn_low).astype(jnp.bfloat16),
+            jnp.pad(gains.T, ((0, 0), (0, PAD - 2))).astype(jnp.bfloat16),
+        ],
+        axis=1,
+    )
+
+
+def attention_outputs(summed):
+    return (
+        *(summed[:, j * D : (j + 1) * D] for j in range(4)),
+        summed[:, 4 * D : 4 * D + 2].T,
+    )
+
+
+def ffn_outputs(summed):
+    return (summed[:, :FF], summed[:, FF:].T)
+
+
+class Grid:
+    def __init__(self):
+        places = [
+            (x, core, z, y) for x in range(2) for core in range(2) for z in range(4) for y in range(2)
+        ]
+        number = {place: index for index, place in enumerate(places)}
+
+        def route(move, senders=range(4)):
+            return [
+                (number[place], number[move(*place)]) for place in places if place[2] in senders
+            ]
+
+        self.core = route(lambda x, core, z, y: (x, 1 - core, z, y))
+        self.along_x = route(lambda x, core, z, y: (1 - x, core, z, y))
+        self.along_y = route(lambda x, core, z, y: (x, core, z, 1 - y))
+        self.pair = route(lambda x, core, z, y: (x, core, z ^ 1, y))
+        self.middle = route(lambda x, core, z, y: (x, core, 3 - z, y), (1, 2))
+        self.outward = route(lambda x, core, z, y: (x, core, z ^ 1, y), (1, 2))
+        self.inward = route(lambda x, core, z, y: (x, core, z ^ 1, y), (0, 3))
+
+
+def swap(value, route):
+    return lax.ppermute(value, ("dp", "fsdp"), route)
+
+
+SLOTS = np.array([(dx, dy, s) for dx, dy in ((1, 1), (1, 0), (0, 1), (0, 0)) for s in range(4)])
+
+
+def row_order(unit):
+    dp, fsdp = lax.axis_index("dp"), lax.axis_index("fsdp")
+    x, core, z, y = dp // 2, dp % 2, fsdp // 2, fsdp % 2
+    dx, dy, s = (jnp.asarray(np.repeat(SLOTS[:, j], unit), jnp.int32) for j in range(3))
+    offset = jnp.asarray(np.tile(np.arange(unit), 16), jnp.int32)
+    place = jnp.where(s < 2, z ^ s, jnp.where(z < 2, s, 3 - s))
+    rows = jnp.concatenate(
+        [
+            ((((x ^ dx) * 2 + owner) * 4 + place) * 2 + (y ^ dy)) * unit + offset
+            for owner in (core, 1 - core)
+        ]
+    )
+    natural = lax.broadcasted_iota(jnp.int32, (32 * unit, 32 * unit), 0)
+    return (natural == rows[None]).astype(jnp.bfloat16)
+
+
+def share_left(values, order, grid):
+    lengths = [max(value.shape[0], PAD) for value in values]
+    half = D // 2
+
+    def body(order_ref, *refs):
+        for j, value_ref in enumerate(refs[: len(values)]):
+            ordered = dot(value_ref[...].astype(jnp.bfloat16), order_ref[...])
+            short = lengths[j] - ordered.shape[0]
+            if short:
+                ordered = jnp.concatenate([ordered, jnp.zeros((short, D), jnp.float32)], axis=0)
+            turned = ordered.T.astype(jnp.bfloat16)
+            refs[len(values) + 2 * j][...] = turned[:half]
+            refs[len(values) + 2 * j + 1][...] = turned[half:]
+
+    turned = pl.pallas_call(
+        body,
+        in_specs=[VMEM_SPEC] * (1 + len(values)),
+        out_specs=[VMEM_SPEC] * (2 * len(values)),
+        out_shape=shapes(*(((half, n), jnp.bfloat16) for n in lengths for _ in range(2))),
+        cost_estimate=pl.CostEstimate(
+            flops=2 * D * D * sum(lengths), bytes_accessed=2 << 20, transcendentals=0
+        ),
+        compiler_params=params(24),
+    )(order, *values)
+    return [(turned[2 * j], swap(turned[2 * j + 1], grid.core)) for j in range(len(values))]
+
+
+def both(value, grid):
+    return (value, swap(value, grid.core))
+
+
+ROWS = ((0, 2), (2, 4), (4, 8), (8, 12), (12, 16))
+
+
+def dot(left, right):
+    return jnp.dot(left, right, preferred_element_type=jnp.float32)
+
+
+def dot_nt(left, right):
+    return lax.dot_general(
+        left, right, (((1,), (1,)), ((), ())), preferred_element_type=jnp.float32
+    )
+
+
+def dot_tn(left, right):
+    return lax.dot_general(
+        left, right, (((0,), (0,)), ((), ())), preferred_element_type=jnp.float32
+    )
+
+
+def lane_masks():
+    lane = lax.broadcasted_iota(jnp.int32, (1, 2 * HEAD_DIM), 1)
+    first = (lane < HEAD_DIM).astype(jnp.float32)
+    return first.astype(jnp.bfloat16), (1.0 - first).astype(jnp.bfloat16), lane < HEAD_DIM
+
+
+def two_heads(value, masks):
+    return jnp.concatenate([value * masks[0], value * masks[1]], axis=0)
+
+
+def pair_softmax(query_pair, keys, key_block, length):
+    half = keys.shape[0]
+    scores = dot_nt(query_pair, keys) * 0.125
+    position = lax.broadcasted_iota(jnp.int32, scores.shape, 1) + key_block * half
+    scores = jnp.where(position < length, scores, -1e30)
+    raised = jnp.exp(scores - jnp.max(scores, axis=-1, keepdims=True))
+    return raised / jnp.sum(raised, axis=-1, keepdims=True)
+
+
+def normalised(value):
+    centred = value - jnp.mean(value, axis=-1, keepdims=True)
+    rate = lax.rsqrt(jnp.mean(centred * centred, axis=-1, keepdims=True) + 1e-05)
+    return centred * rate, rate
+
+
+def norm_backward(value, gain, grad):
+    ratio, rate = normalised(value)
+    scaled = grad * gain
+    slope = jnp.mean(scaled * ratio, axis=-1, keepdims=True)
+    result = rate * (scaled - jnp.mean(scaled, axis=-1, keepdims=True) - ratio * slope)
+    return result, jnp.sum(grad * ratio, axis=0, keepdims=True)
+
+
+def head_parts(half, swapped):
+    for block in range(2):
+        key_block = 1 - block if swapped else block
+        rows = slice(block * half, (block + 1) * half)
+        key_rows = slice(key_block * half, (key_block + 1) * half)
+        for pair in range(HEADS // 2):
+            yield key_block, rows, key_rows, pair * 2 * HEAD_DIM
+
+
+VMEM_SPEC = pl.BlockSpec(memory_space=pltpu.VMEM)
+SMEM_SPEC = pl.BlockSpec(memory_space=pltpu.SMEM)
+ANY_SPEC = pl.BlockSpec(memory_space=pl.ANY)
+
+
+def params(mebibytes):
+    return pltpu.CompilerParams(vmem_limit_bytes=mebibytes << 20)
+
+
+def shapes(*pairs):
+    return [jax.ShapeDtypeStruct(shape, dtype) for shape, dtype in pairs]
+
+
+def attention_columns(weights, start, target, sems):
+    copies = []
+    for part in range(5):
+        width = D if part < 4 else PAD
+        copies.append(
+            pltpu.make_async_copy(
+                weights.at[:, pl.ds(start + part * D, width)],
+                target.at[:, pl.ds(part * D, width)],
+                sems.at[part],
+            )
+        )
+    for copy in copies:
+        copy.start()
+    return copies
+
+
+def attention_forward(hidden, lengths, weights, start, swapped):
+    tokens = hidden.shape[0]
+    half = tokens // 2
+    low = jnp.bfloat16
+
+    def body(length_ref, hidden_ref, w_any, low_out, qkv, mixed, first_sum, gains, w, sems):
+        copies = attention_columns(w_any, start, w, sems)
+        value = hidden_ref[...].astype(low)
+        low_out[...] = value
+        masks = lane_masks()
+        for part in range(3):
+            copies[part].wait()
+            columns = slice(part * D, (part + 1) * D)
+            qkv[:, columns] = dot(value, w[:, columns]).astype(low)
+        for key_block, rows, key_rows, lane in head_parts(half, swapped):
+            query = two_heads(qkv[rows, lane : lane + 128], masks)
+            keys = qkv[key_rows, D + lane : D + lane + 128]
+            values = qkv[key_rows, 2 * D + lane : 2 * D + lane + 128]
+            shares = pair_softmax(query, keys, key_block, length_ref[0]).astype(low)
+            out = dot(shares, values)
+            mixed[rows, lane : lane + 128] = jnp.where(masks[2], out[:half], out[half:]).astype(low)
+        copies[3].wait()
+        first_sum[...] = hidden_ref[...] + dot(mixed[...], w[:, 3 * D : 4 * D])
+        copies[4].wait()
+        gains[...] = w[:, 4 * D :].astype(jnp.float32).T[:8]
+
+    return pl.pallas_call(
+        body,
+        in_specs=[SMEM_SPEC, VMEM_SPEC, ANY_SPEC],
+        out_specs=[VMEM_SPEC] * 5,
+        out_shape=shapes(
+            ((tokens, D), low),
+            ((tokens, 3 * D), low),
+            ((tokens, D), low),
+            ((tokens, D), jnp.float32),
+            ((8, D), jnp.float32),
+        ),
+        scratch_shapes=[pltpu.VMEM((D, 4 * D + PAD), low), pltpu.SemaphoreType.DMA((5,))],
+        cost_estimate=pl.CostEstimate(
+            flops=2 * tokens * D * 4 * D, bytes_accessed=9 << 20, transcendentals=0
+        ),
+        compiler_params=params(40),
+    )(lengths, hidden, weights)
+
+
+FF_TILE = D
+
+
+def ffn_forward(first_sum, gains, weights, start):
+    tokens = first_sum.shape[0]
+    low = jnp.bfloat16
+    steps = FF // FF_TILE
+    first = start // FF_TILE
+
+    def body(sum_ref, gain_ref, up, down, normed_low, activated, slope, second_sum, out, total):
+        step = pl.program_id(0)
+
+        @pl.when(step == 0)
+        def _():
+            normed = normalised(sum_ref[...])[0] * gain_ref[0:1]
+            normed_low[...] = normed.astype(low)
+            total[...] = normed
+
+        u = dot(normed_low[...], up[...])
+        inner = 0.7978845608028654 * (u + 0.044715 * (u * u * u))
+        wave = jnp.tanh(inner)
+        active = (0.5 * u * (1.0 + wave)).astype(low)
+        slope[...] = (
+            0.5 * (1.0 + wave)
+            + 0.5 * u * (1.0 - wave * wave) * (0.7978845608028654 * (1.0 + 0.134145 * (u * u)))
+        ).astype(low)
+        activated[...] = active
+        total[...] += dot_nt(active, down[...])
+
+        @pl.when(step == steps - 1)
+        def _():
+            second_sum[...] = total[...]
+            out[...] = normalised(total[...])[0] * gain_ref[1:2]
+
+    def fixed(shape):
+        return pl.BlockSpec(shape, lambda j: (0, 0))
+
+    wide = pl.BlockSpec((tokens, FF_TILE), lambda j: (0, j))
+    return pl.pallas_call(
+        body,
+        grid=(steps,),
+        in_specs=[
+            fixed((tokens, D)),
+            fixed((8, D)),
+            pl.BlockSpec((D, FF_TILE), lambda j: (0, first + j)),
+            pl.BlockSpec((D, FF_TILE), lambda j: (0, first + steps + j)),
+        ],
+        out_specs=[fixed((tokens, D)), wide, wide, fixed((tokens, D)), fixed((tokens, D))],
+        out_shape=shapes(
+            ((tokens, D), low),
+            ((tokens, FF), low),
+            ((tokens, FF), low),
+            ((tokens, D), jnp.float32),
+            ((tokens, D), jnp.float32),
+        ),
+        scratch_shapes=[pltpu.VMEM((tokens, D), jnp.float32)],
+        cost_estimate=pl.CostEstimate(
+            flops=4 * tokens * D * FF, bytes_accessed=15 << 20, transcendentals=tokens * FF
+        ),
+        compiler_params=params(40),
+    )(first_sum, gains, weights, weights)
+
+
+def second_norm_backward(grad, second_sum, gains):
+    tokens = grad.shape[0]
+
+    def body(grad_ref, sum_ref, gain_ref, out, low_out, gain_out):
+        result, gain_grad = norm_backward(sum_ref[...], gain_ref[1:2], grad_ref[...].astype(jnp.float32))
+        out[...] = result
+        low_out[...] = result.astype(jnp.bfloat16)
+        gain_out[...] = gain_grad
+
+    return pl.pallas_call(
+        body,
+        in_specs=[VMEM_SPEC] * 3,
+        out_specs=[VMEM_SPEC] * 3,
+        out_shape=shapes(
+            ((tokens, D), jnp.float32), ((tokens, D), jnp.bfloat16), ((1, D), jnp.float32)
+        ),
+        cost_estimate=pl.CostEstimate(flops=0, bytes_accessed=3 << 20, transcendentals=0),
+        compiler_params=params(16),
+    )(grad, second_sum, gains)
+
+
+def up_backward_kernel(grad_second, down_low, slope, weights, start):
+    tokens = grad_second.shape[0]
+    low = jnp.bfloat16
+    steps = FF // FF_TILE
+    first = start // FF_TILE
+
+    def body(grad_ref, low_ref, slope_ref, up, down, up_low, out):
+        step = pl.program_id(0)
+
+        @pl.when(step == 0)
+        def _():
+            out[...] = grad_ref[...]
+
+        piece = (dot(low_ref[...], down[...]) * slope_ref[...].astype(jnp.float32)).astype(low)
+        up_low[...] = piece
+        out[...] += dot_nt(piece, up[...])
+
+    def fixed(shape):
+        return pl.BlockSpec(shape, lambda j: (0, 0))
+
+    wide = pl.BlockSpec((tokens, FF_TILE), lambda j: (0, j))
+    return pl.pallas_call(
+        body,
+        grid=(steps,),
+        in_specs=[
+            fixed((tokens, D)),
+            fixed((tokens, D)),
+            wide,
+            pl.BlockSpec((D, FF_TILE), lambda j: (0, first + j)),
+            pl.BlockSpec((D, FF_TILE), lambda j: (0, first + steps + j)),
+        ],
+        out_specs=[wide, fixed((tokens, D))],
+        out_shape=shapes(((tokens, FF), low), ((tokens, D), jnp.float32)),
+        cost_estimate=pl.CostEstimate(
+            flops=4 * tokens * D * FF, bytes_accessed=14 << 20, transcendentals=0
+        ),
+        compiler_params=params(40),
+    )(grad_second, down_low, slope, weights, weights)
+
+
+def attention_backward_kernel(grad, first_sum, gains, qkv, lengths, weights, start, swapped):
+    tokens = grad.shape[0]
+    half = tokens // 2
+    low = jnp.bfloat16
+
+    def body(length_ref, grad_ref, sum_ref, gain_ref, qkv_ref, w_any, *rest):
+        attn_low, grad_qkv, grad_in, gain_out, grad_mixed, w, sems = rest
+        copies = attention_columns(w_any, start, w, sems)
+        masks = lane_masks()
+        result, gain_grad = norm_backward(sum_ref[...], gain_ref[0:1], grad_ref[...])
+        grad_in[...] = result
+        attn_low[...] = result.astype(low)
+        gain_out[...] = gain_grad
+        copies[3].wait()
+        grad_mixed[...] = dot_nt(attn_low[...], w[:, 3 * D : 4 * D]).astype(low)
+        for key_block, rows, key_rows, lane in head_parts(half, swapped):
+            query = two_heads(qkv_ref[rows, lane : lane + 128], masks)
+            keys = qkv_ref[key_rows, D + lane : D + lane + 128]
+            values = qkv_ref[key_rows, 2 * D + lane : 2 * D + lane + 128]
+            arriving = two_heads(grad_mixed[rows, lane : lane + 128], masks)
+            shares = pair_softmax(query, keys, key_block, length_ref[0])
+            grad_values = dot_tn(shares.astype(low), arriving)
+            grad_shares = dot_nt(arriving, values)
+            inner = jnp.sum(shares * grad_shares, axis=-1, keepdims=True)
+            grad_scores = (shares * (grad_shares - inner)).astype(low)
+            grad_query = dot(grad_scores, keys) * 0.125
+            grad_keys = dot_tn(grad_scores, query) * 0.125
+            grad_qkv[rows, lane : lane + 128] = jnp.where(
+                masks[2], grad_query[:half], grad_query[half:]
+            ).astype(low)
+            grad_qkv[key_rows, D + lane : D + lane + 128] = grad_keys.astype(low)
+            grad_qkv[key_rows, 2 * D + lane : 2 * D + lane + 128] = grad_values.astype(low)
+        for part in (0, 1, 2):
+            copies[part].wait()
+            columns = slice(part * D, (part + 1) * D)
+            grad_in[...] += dot_nt(grad_qkv[:, columns], w[:, columns])
+        copies[4].wait()
+
+    return pl.pallas_call(
+        body,
+        in_specs=[SMEM_SPEC] + [VMEM_SPEC] * 4 + [ANY_SPEC],
+        out_specs=[VMEM_SPEC] * 4,
+        out_shape=shapes(
+            ((tokens, D), low),
+            ((tokens, 3 * D), low),
+            ((tokens, D), jnp.float32),
+            ((1, D), jnp.float32),
+        ),
+        scratch_shapes=[
+            pltpu.VMEM((tokens, D), low),
+            pltpu.VMEM((D, 4 * D + PAD), low),
+            pltpu.SemaphoreType.DMA((5,)),
+        ],
+        cost_estimate=pl.CostEstimate(
+            flops=2 * tokens * D * 4 * D, bytes_accessed=10 << 20, transcendentals=0
+        ),
+        compiler_params=params(40),
+    )(lengths, grad, first_sum, gains, qkv, weights)
+
+
+def matrix_terms(left_t, right, unit):
+    tile = D
+
+    def body(la, lb, ra, rb, *outs):
+        value = (dot(la[...], ra[...]) + dot(lb[...], rb[...])).astype(jnp.bfloat16)
+        for (low, high), out in zip(ROWS, outs):
+            out[...] = value[low * unit : high * unit]
+
+    def whole(value):
+        return pl.BlockSpec(value.shape, lambda j: (0, 0))
+
+    tokens, width = right[0].shape
+    column = pl.BlockSpec((tokens, tile), lambda j: (0, j))
+    return pl.pallas_call(
+        body,
+        grid=(width // tile,),
+        in_specs=[whole(v) for v in left_t] + [column, column],
+        out_specs=[pl.BlockSpec(((b - a) * unit, tile), lambda j: (0, j)) for a, b in ROWS],
+        out_shape=[jax.ShapeDtypeStruct(((b - a) * unit, width), jnp.bfloat16) for a, b in ROWS],
+        cost_estimate=pl.CostEstimate(
+            flops=4 * tokens * 16 * unit * width, bytes_accessed=6 << 20, transcendentals=0
+        ),
+        compiler_params=pltpu.CompilerParams(vmem_limit_bytes=32 << 20),
+    )(*left_t, *right)
+
+
+def attention_terms(inputs_t, grad_qkv, mixed_t, attn_low, gains_t, unit, extra=()):
+    wide = extra[1][0].shape[1] if extra else 0
+    width = 4 * D + PAD + wide
+
+    def body(ia, ib, qa, qb, ma, mb, oa, ob, ga, gb, *refs):
+        outs = refs[4 if extra else 0 :]
+
+        def put(value, column):
+            value = value.astype(jnp.bfloat16)
+            for (low, high), out in zip(ROWS, outs):
+                out[:, column : column + value.shape[1]] = value[low * unit : high * unit]
+
+        for j in range(3):
+            part = slice(j * D, (j + 1) * D)
+            put(dot(ia[...], qa[:, part]) + dot(ib[...], qb[:, part]), j * D)
+        put(dot(ma[...], oa[...]) + dot(mb[...], ob[...]), 3 * D)
+        put(ga[...].astype(jnp.float32) + gb[...].astype(jnp.float32), 4 * D)
+        for j in range(wide // D):
+            la, lb, ra, rb = refs[:4]
+            part = slice(j * D, (j + 1) * D)
+            put(dot(la[...], ra[:, part]) + dot(lb[...], rb[:, part]), 4 * D + PAD + j * D)
+
+    operands = [*inputs_t, *grad_qkv, *mixed_t, *attn_low, *gains_t]
+    for pair in extra:
+        operands += pair
+    return pl.pallas_call(
+        body,
+        in_specs=[VMEM_SPEC] * len(operands),
+        out_specs=[VMEM_SPEC] * 5,
+        out_shape=shapes(*((((b - a) * unit, width), jnp.bfloat16) for a, b in ROWS)),
+        cost_estimate=pl.CostEstimate(
+            flops=2 * 512 * 16 * unit * width, bytes_accessed=12 << 20, transcendentals=0
+        ),
+        compiler_params=params(40),
+    )(*operands)
+
+
+def add(*values):
+    return sum(value.astype(jnp.float32) for value in values)
+
+
+class Reduction:
+    def __init__(self, pieces, grid, unit):
+        self.grid, self.unit, self.round, self.due = grid, unit, 0, False
+        self.out, self.kept = list(pieces[:2]), list(pieces[2:])
+
+    def state(self):
+        return (self.out, self.kept)
+
+    def restore(self, state):
+        self.out, self.kept = state
+
+    def send(self):
+        grid = self.grid
+        routes = (
+            (grid.along_x, grid.along_y),
+            (grid.along_x, grid.along_y),
+            (grid.inward,),
+            (grid.middle,),
+            (grid.pair,),
+        )[self.round]
+        self.out = [swap(value, route) for value, route in zip(self.out, routes)]
+        self.round += 1
+
+    def prepare(self):
+        low, unit, two = jnp.bfloat16, self.unit, 2 * self.unit
+        if self.round == 1:
+            (from_x, from_y), (to_x, to_y, own) = self.out, self.kept
+            to_x = jnp.concatenate([to_x[:two], add(to_x[two:], from_y).astype(low)], axis=0)
+            to_y = jnp.concatenate([add(to_y[:two], from_x).astype(low), to_y[two:]], axis=0)
+            self.out, self.kept = [to_x, to_y], [own]
+        elif self.round == 2:
+            (from_x, from_y), (own,) = self.out, self.kept
+            self.out = [add(own[two:], from_x[two:], from_y[two:]).astype(low)]
+            self.kept = [add(own[:two], from_x[:two], from_y[:two]).astype(low), self.out[0]]
+        elif self.round == 3:
+            near, far = self.kept
+            self.out, self.kept = [add(far, self.out[0]).astype(low)], [near]
+        else:
+            near = add(self.kept[0], self.out[0])
+            self.out, self.kept = [near[unit:].astype(low)], [near[:unit]]
+
+    def result(self):
+        return add(self.kept[0], self.out[0])
+
+
+def gate(values, *earlier):
+    return lax.optimization_barrier((values, earlier))[0]
+
+
+class Segments:
+    def __init__(self):
+        self.active = []
+
+    def run(self, sends, late, compute, values):
+        for reduction in sends:
+            if reduction not in self.active:
+                self.active.append(reduction)
+        waiting = [r for r in self.active if r not in sends and r not in late and r.due]
+        for reduction in sends:
+            reduction.send()
+            reduction.due = True
+        for reduction in late:
+            if reduction.due:
+                reduction.prepare()
+            reduction.send()
+            reduction.due = True
+        for reduction in waiting:
+            if reduction.round < 2:
+                reduction.prepare()
+                reduction.due = False
+        values = compute(values)
+        states = [reduction.state() for reduction in self.active]
+        states, values = lax.optimization_barrier((states, values))
+        for reduction, state in zip(self.active, states):
+            reduction.restore(state)
+        self.active = [r for r in self.active if r.round < 5]
+        return values
+
+
+class Gathering:
+    def __init__(self, block, grid):
+        self.pieces, self.grid, self.unit = [block], grid, block.shape[0]
+        self.steps = [self.pair, self.middle, self.outward, self.square, self.diagonal]
+
+    def advance(self):
+        self.pieces = list(self.steps.pop(0)(self.pieces, self.grid, 2 * self.unit))
+
+    @staticmethod
+    def pair(pieces, grid, two):
+        (block,) = pieces
+        return (jnp.concatenate([block, swap(block, grid.pair)], axis=0),)
+
+    @staticmethod
+    def middle(pieces, grid, two):
+        (near,) = pieces
+        return (near, swap(near, grid.middle))
+
+    @staticmethod
+    def outward(pieces, grid, two):
+        near, far = pieces
+        z = lax.axis_index("fsdp") // 2
+        far = jnp.where((z == 1) | (z == 2), far, swap(far, grid.outward))
+        return (jnp.concatenate([near, far], axis=0),)
+
+    @staticmethod
+    def square(pieces, grid, two):
+        (line,) = pieces
+        return (line, swap(line, grid.along_x), swap(line, grid.along_y))
+
+    @staticmethod
+    def diagonal(pieces, grid, two):
+        line, from_x, from_y = pieces
+        return (
+            swap(from_y[:two], grid.along_x),
+            swap(from_x[two:], grid.along_y),
+            from_x,
+            from_y,
+            line,
+        )
+
+    def result(self):
+        pieces = self.pieces
+        return place_blocks(pieces + [swap(piece, self.grid.core) for piece in pieces], self.unit)
+
+
+def place_blocks(pieces, unit):
+    width = pieces[0].shape[1]
+    dp, fsdp = lax.axis_index("dp"), lax.axis_index("fsdp")
+    x, core, z, y = dp // 2, dp % 2, fsdp // 2, fsdp % 2
+    dx, dy, s = (jnp.asarray(SLOTS[:, j], jnp.int32) for j in range(3))
+    place = jnp.where(s < 2, z ^ s, jnp.where(z < 2, s, 3 - s))
+    rows = jnp.concatenate(
+        [(((x ^ dx) * 2 + owner) * 4 + place) * 2 + (y ^ dy) for owner in (core, 1 - core)]
+    )
+
+    tiles = unit // 8
+
+    def body(rows_ref, *refs):
+        sources, target = refs[:10], refs[10]
+        for half in range(2):
+            for (low, high), source in zip(ROWS, sources[half * 5 : half * 5 + 5]):
+                for slot in range(low, high):
+                    row = rows_ref[half * 16 + slot] * tiles
+                    first = (slot - low) * tiles
+                    target[pl.ds(row, tiles)] = source[first : first + tiles]
+
+    placed = pl.pallas_call(
+        body,
+        in_specs=[pl.BlockSpec(memory_space=pltpu.SMEM)]
+        + [pl.BlockSpec(memory_space=pltpu.VMEM)] * 10,
+        out_specs=pl.BlockSpec(memory_space=pltpu.VMEM),
+        out_shape=jax.ShapeDtypeStruct((32 * tiles, 8, width), jnp.bfloat16),
+        cost_estimate=pl.CostEstimate(
+            flops=0, bytes_accessed=4 * 32 * unit * width, transcendentals=0
+        ),
+        compiler_params=pltpu.CompilerParams(vmem_limit_bytes=40 << 20),
+    )(rows, *(piece.reshape(-1, 8, width) for piece in pieces))
+    return placed.reshape(32 * unit, width)
 
 
 def per_device(
+    sizes,
     tokens,
     lengths,
     query_weight,
@@ -239,24 +888,171 @@
         down_weight,
         norm_gains,
     )
+    if sizes == (4, 8):
+        return grid_step(tokens, lengths, shards, cotangent)
     hidden = tokens[0].astype(jnp.float32)
     length = lengths[0]
-    weights_all = [unpack(collect(shards, layer)) for layer in range(LAYERS)]
+    weights_all = [
+        unpack(plain_gather(pack_attention(shards, j)), plain_gather(pack_ffn(shards, j)))
+        for j in range(LAYERS)
+    ]
     kept_all = []
     for layer in range(LAYERS):
         hidden, kept = layer_forward(hidden, length, weights_all[layer], layer % 2 == 1)
         kept_all.append(kept)
-    activations = hidden.astype(jnp.bfloat16)[None]
-    grad_hidden = cotangent[0].astype(jnp.float32)
-    layer_grads = [None] * LAYERS
+    grad = cotangent[0].astype(jnp.float32)
+    outputs = [None] * LAYERS
     for layer in reversed(range(LAYERS)):
-        grad_hidden, terms = layer_backward(
-            grad_hidden, kept_all[layer], weights_all[layer], layer % 2 == 1, length
+        kept, weights = kept_all[layer], weights_all[layer]
+        grad_second, down_low, gain_second = down_backward(grad, kept, weights)
+        grad_normed, up_low = up_backward(grad_second, down_low, kept, weights)
+        ffn = plain_scatter(plain_ffn_terms((kept[7], up_low, down_low, kept[9])))
+        grad_first, attn_low, grad_mixed, gain_first = mixed_backward(grad_normed, kept, weights)
+        grad_qkv = scores_backward(grad_mixed, kept, layer % 2 == 1, length)
+        grad = inputs_backward(grad_first, grad_qkv, weights)
+        gains = jnp.stack([gain_first, gain_second])
+        attention = plain_scatter(
+            plain_attention_terms((kept[0], grad_qkv, kept[5], attn_low), gains)
         )
-        summed = lax.psum_scatter(terms, ("dp", "fsdp"), scatter_dimension=0, tiled=True)
-        layer_grads[layer] = arrange(summed)
-    stacked = tuple((jnp.stack([entry[member] for entry in layer_grads]) for member in range(7)))
-    return (activations, grad_hidden[None], *stacked)
+        outputs[layer] = (attention_outputs(attention), ffn_outputs(ffn))
+    return finish(hidden, grad, outputs)
+
+
+def finish(hidden, grad, outputs):
+    layers = [(*attention[:4], *ffn, attention[4]) for attention, ffn in outputs]
+    stacked = tuple((jnp.stack([entry[member] for entry in layers]) for member in range(7)))
+    return (hidden.astype(jnp.bfloat16)[None], grad[None], *stacked)
+
+
+def gather_first_layer(blocks, grid):
+    attention, ffn = (Gathering(block, grid) for block in blocks)
+    for moves in (
+        (attention,),
+        (attention, ffn),
+        (attention, ffn),
+        (attention, ffn),
+        (attention,),
+    ):
+        for gathering in moves:
+            gathering.advance()
+        attention.pieces, ffn.pieces = lax.optimization_barrier((attention.pieces, ffn.pieces))
+    first = attention.result()
+    ffn.advance()
+    ffn.advance()
+    return first, ffn.result()
+
+
+def grid_step(tokens, lengths, shards, cotangent):
+    grid, unit = Grid(), shards[0].shape[1]
+    order = row_order(unit)
+
+    second = plain_gather(
+        jnp.concatenate([pack_ffn(shards, 1), pack_attention(shards, 1)], axis=1)
+    )
+    first = gather_first_layer((pack_attention(shards, 0), pack_ffn(shards, 0)), grid)
+    attention_at = ((first[0], 0, False), (second, 2 * FF, True))
+    ffn_at = ((first[1], 0), (second, 0))
+
+    hidden = tokens[0].astype(jnp.float32)
+    kept, left, right = [], [], []
+    for layer in range(LAYERS):
+        inputs_low, qkv, mixed, first_sum, gains = attention_forward(
+            hidden, lengths, *attention_at[layer]
+        )
+        normed_low, activated, slope, second_sum, hidden = ffn_forward(
+            first_sum, gains, *ffn_at[layer]
+        )
+        kept.append((qkv, first_sum, gains, slope, second_sum))
+        left.append(share_left((inputs_low, mixed, normed_low), order, grid))
+        right.append(both(activated, grid))
+
+    segments = Segments()
+
+    def norm_part(layer, grad):
+        qkv, first_sum, gains, slope, second_sum = kept[layer]
+        grad_second, down_low, gain_grad = second_norm_backward(grad, second_sum, gains)
+        return grad_second, down_low, gain_grad, *share_left((down_low,), order, grid)
+
+    def up_part(layer, grad_second, down_low):
+        up_low, grad = up_backward_kernel(grad_second, down_low, kept[layer][3], *ffn_at[layer])
+        return grad, up_low
+
+    def attention_part(layer, grad):
+        qkv, first_sum, gains, slope, second_sum = kept[layer]
+        return attention_backward_kernel(
+            grad, first_sum, gains, qkv, lengths, *attention_at[layer]
+        )
+
+    def attention_pieces(layer, attn_low, grad_qkv, gain_first, gain_second, extra=()):
+        gains = jnp.concatenate([gain_first, gain_second, jnp.zeros((6, D), jnp.float32)], axis=0)
+        inputs_t, mixed_t, _ = left[layer]
+        (gains_t,) = share_left((gains,), order, grid)
+        return attention_terms(
+            inputs_t, both(grad_qkv, grid), mixed_t, both(attn_low, grid), gains_t, unit, extra
+        )
+
+    grad_second, down_low, gain_second_1, down_t = norm_part(1, cotangent[0])
+    pieces = matrix_terms(down_t, right[1], unit)
+    grad_second, down_low, pieces = lax.optimization_barrier((grad_second, down_low, pieces))
+    down_1 = Reduction(pieces, grid, unit)
+
+    def work(values):
+        grad, up_low = up_part(1, *values)
+        return (grad, matrix_terms(left[1][2], both(up_low, grid), unit))
+
+    grad, pieces = segments.run([down_1], [], work, (grad_second, down_low))
+    up_1 = Reduction(pieces, grid, unit)
+
+    def work(values):
+        return attention_part(1, values)
+
+    attn_low, grad_qkv, grad, gain_first = segments.run([up_1], [], work, grad)
+
+    def work(values):
+        return norm_part(0, values)
+
+    grad_second, down_low, gain_second_0, down_t = segments.run([down_1], [], work, grad)
+
+    def work(values):
+        return attention_pieces(
+            1, attn_low, grad_qkv, gain_first, gain_second_1, (down_t, right[0])
+        )
+
+    pieces = segments.run([up_1], [down_1], work, ())
+    joined = Reduction(pieces, grid, unit)
+
+    def work(values):
+        grad, up_low = up_part(0, *values)
+        return (grad, matrix_terms(left[0][2], both(up_low, grid), unit))
+
+    grad, pieces = segments.run([joined], [down_1, up_1], work, (grad_second, down_low))
+    up_0 = Reduction(pieces, grid, unit)
+
+    def work(values):
+        attn_low, grad_qkv, grad, gain_first = attention_part(0, values)
+        return grad, attention_pieces(0, attn_low, grad_qkv, gain_first, gain_second_0)
+
+    grad, pieces = segments.run([], [joined, down_1, up_1], work, grad)
+    attention_0 = Reduction(pieces, grid, unit)
+
+    def nothing(values):
+        return values
+
+    segments.run([up_0], [up_1], nothing, ())
+    segments.run([attention_0], [], nothing, ())
+    segments.run([up_0], [joined], nothing, ())
+    segments.run([attention_0], [joined, up_0], nothing, ())
+    segments.run([], [attention_0, up_0], nothing, ())
+    segments.run([], [attention_0, joined, up_0], nothing, ())
+    segments.run([], [attention_0], nothing, ())
+
+    width = 4 * D + PAD
+    middle, down_0 = joined.result()[:, :width], joined.result()[:, width:]
+    outputs = [
+        (attention_outputs(attention_0.result()), (up_0.result(), down_0.T)),
+        (attention_outputs(middle), (up_1.result(), down_1.result().T)),
+    ]
+    return finish(hidden, grad, outputs)
 
 
 def solution(mesh):
@@ -273,7 +1069,7 @@
         P(("dp", "fsdp"), None, None),
     )
     return jax.shard_map(
-        per_device,
+        functools.partial(per_device, (mesh.shape["dp"], mesh.shape["fsdp"])),
         mesh=mesh,
         in_specs=placed,
         out_specs=(

time: 651 us -> 434 us (0.67)
  waiting for transfers between devices: 465 us -> 190 us
  matrix products: 91.8 us -> 0 us
  Pallas kernels: 0 us -> 85.2 us
  starting transfers between devices: 0.38 us -> 78.4 us
  local copies, waits for them, and re-layouts: 54.9 us -> 42.4 us
    unnamed x6 -> x1, waiting for transfers between devices: 275 us -> 0.02 us
    all_gather x2 -> x1, waiting for transfers between devices: 191 us -> 0.01 us  [plain_gather(): return lax.all_gather(block, ('dp', 'fsdp'), axis=0, tiled=True)]
    ppermute x0 -> x77, waiting for transfers between devices: none -> 190 us  [swap(): return lax.ppermute(value, ('dp', 'fsdp'), route)]
    dot_general x36 -> x0, matrix products: 91.8 us -> none  [the longest x8 29.8 us: product_right_t(): lax.dot_general(left, right, (((1,), (1,)), ((), ())), preferred_element_...]
    pallas_call x0 -> x23, Pallas kernels: none -> 85.2 us  [the longest x2 20.6 us: attention_backward_kernel(): pl.pallas_call(body, in_specs=[SMEM_SPEC] + [VMEM_SPEC] * 4 + [ANY_SPEC],...]
    ppermute x0 -> x77, starting transfers between devices: none -> 78.4 us  [swap(): return lax.ppermute(value, ('dp', 'fsdp'), route)]
    unnamed x197 -> x187, local copies, waits for them, and re-layouts: 22.8 us -> 38.1 us
    convert_element_type x13 -> x0, local copies, waits for them, and re-layouts: 14.2 us -> none  [the longest x1 4.23 us: layer_backward(): product_left_t(inputs_low, grad_qkv).astype(low)]
  transfers between devices with their start and end apart: 4 -> 78, of which waited for: 4 -> 31; matrix products, arithmetic and copies ran while one was open for 11% -> 4% of each run, Pallas kernels for 0% -> 15%
where the time goes in v3:
time: 434 us; the launch traced here: 429 us
  waiting for transfers between devices  190 us (44%)
  Pallas kernels  85.2 us (20%)
  starting transfers between devices  78.4 us (18%)
  local copies, waits for them, and re-layouts  42.4 us (10%)
  between operations  16.5 us (4%)
  other arithmetic  16.4 us (4%)
    ppermute x77, waiting for transfers between devices, swap(): return lax.ppermute(value, ('dp', 'fsdp'), route)  190 us
    ppermute x77, starting transfers between devices, swap(): return lax.ppermute(value, ('dp', 'fsdp'), route)  78.4 us
    unnamed x187, local copies, waits for them, and re-layouts  38.1 us
    pallas_call x2, Pallas kernels, attention_backward_kernel(): pl.pallas_call(body, in_specs=[SMEM_SPEC] + [VMEM_SPEC] * 4 + [ANY_SPEC],...  20.6 us
    pallas_call x2, Pallas kernels, ffn_forward(): pl.pallas_call(body, grid=(steps,), in_specs=[fixed((tokens, D)), fixed((...  15.6 us
    pallas_call x2, Pallas kernels, up_backward_kernel(): pl.pallas_call(body, grid=(steps,), in_specs=[fixed((tokens, D)), fixed((...  12 us
    pallas_call x2, Pallas kernels, attention_forward(): pl.pallas_call(body, in_specs=[SMEM_SPEC, VMEM_SPEC, ANY_SPEC], out_specs...  8.98 us
    pallas_call x3, Pallas kernels, matrix_terms(): pl.pallas_call(body, grid=(width // tile,), in_specs=[whole(v) for v in l...  8.7 us
  transfers between devices with their start and end apart: 78, of which 31 were waited for; matrix products, arithmetic and copies ran while one was open for 4% of the time, Pallas kernels for 15%

profile of v3, /device:TPU:0, one launch (start us, length us, event | category | flops | bytes accessed | tf_op | source)
XLA Modules:
  0.0 429.4 jit_solution(3973604093619602856)
XLA Ops:
  14.1 3.1 collective-permute-start
  17.2 3.9 collective-permute-done
  21.2 1.8 collective-permute-start.2
  23.6 8.8 %collective-permute-done.2 = bf16[24,6144]{1,0:T(8,128)(2,1)S(1)} collective-permute-done((bf16[24,6144]{1,0:T(8,128)(2,1)S(1)}, bf16[24,6144]{1,0:T(8,128)(2,1)S(1)}, u32[]{:S(2)}, u32[]{:S(2)}) %collective-permute-start.2) | collective-permute-done | bytes 294944 | tf_op jit(solution)/shard_map/ppermute | solution.py:270
  34.5 15.3 %collective-permute-done.3 = bf16[48,3200]{1,0:T(8,128)(2,1)S(1)} collective-permute-done((bf16[48,3200]{1,0:T(8,128)(2,1)S(1)}, bf16[48,3200]{1,0:T(8,128)(2,1)S(1)}, u32[]{:S(2)}, u32[]{:S(2)}) %collective-permute-start.3) | collective-permute-done | bytes 307232 | tf_op jit(solution)/shard_map/ppermute | solution.py:270
  51.2 1.6 collective-permute-start.5
  52.8 1.5 collective-permute-start.6
  54.3 32.3 %collective-permute-done.7 = bf16[48,6144]{1,0:T(8,128)(2,1)S(1)} collective-permute-done((bf16[48,6144]{1,0:T(8,128)(2,1)S(1)}, bf16[48,6144]{1,0:T(8,128)(2,1)S(1)}, u32[]{:S(2)}, u32[]{:S(2)}) %collective-permute-start.7) | collective-permute-done | bytes 589856 | tf_op jit(solution)/shard_map/ppermute | solution.py:270
  88.2 1.6 collective-permute-start.9
  89.8 12.9 %collective-permute-done.8 = bf16[48,3200]{1,0:T(8,128)(2,1)S(1)} collective-permute-done((bf16[48,3200]{1,0:T(8,128)(2,1)S(1)}, bf16[48,3200]{1,0:T(8,128)(2,1)S(1)}, u32[]{:S(2)}, u32[]{:S(2)}) %collective-permute-start.8) | collective-permute-done | bytes 307232 | tf_op jit(solution)/shard_map/ppermute | solution.py:270
  102.7 1.9 collective-permute-done.9
  104.6 1.8 collective-permute-start.15
  107.5 37.4 %collective-permute-done.15 = bf16[96,6144]{1,0:T(8,128)(2,1)S(1)} collective-permute-done((bf16[96,6144]{1,0:T(8,128)(2,1)S(1)}, bf16[96,6144]{1,0:T(8,128)(2,1)S(1)}, u32[]{:S(2)}, u32[]{:S(2)}) %collective-permute-start.15) | collective-permute-done | bytes 1179680 | tf_op jit(solution)/shard_map/ppermute | solution.py:270
  146.2 1.9 slice.368
  148.8 1.5 collective-permute-start.16
  154.7 9.8 %collective-permute-done.16 = bf16[48,6144]{1,0:T(8,128)(2,1)} collective-permute-done((bf16[48,6144]{1,0:T(8,128)(2,1)}, bf16[48,6144]{1,0:T(8,128)(2,1)}, u32[]{:S(2)}, u32[]{:S(2)}) %collective-permute-start.16) | collective-permute-done | bytes 589856 | tf_op jit(solution)/shard_map/ppermute | solution.py:270
  164.4 1.9 collective-permute-done.18
  175.3 4.1 shard_map.260
  182.0 7.0 %shard_map.261 = bf16[96,8,6144]{2,1,0:T(8,128)(2,1)} custom-call(s32[32]{0:T(128)S(1)} %pad_add_fusion.1.rows_ref, bf16[6,8,6144]{2,1,0:T(8,128)(2,1)} %bitcast.21.refs_0_, bf16[6,8,6144]{2,1,0:T(8,128)(2,1)} %bitcast.22.refs_1_, bf16[12,8,6144]{2,1,0:T(8,128)(2,1)} %bitcast.23.refs_2_, bf16[12,8,6144]{2,1,0:T(8,128)(2,1)S(1)} %bitcast.109, ...), custom_call_target="tpu_custom_call" | custom-call | bytes 18874368 | tf_op jit(solution)/shard_map/pallas_call | solution.py:855
  189.0 7.9 %shard_map.262 = (bf16[256,768]{1,0:T(8,128)(2,1)S(1)}, bf16[256,3072]{1,0:T(8,128)(2,1)S(1)}, bf16[256,3072]{1,0:T(8,128)(2,1)S(1)}, f32[256,768]{1,0:T(8,128)S(1)}, f32[256,768]{1,0:T(8,128)S(1)}) custom-call(f32[256,768]{1,0:T(8,128)S(1)} %get-tuple-element.261.sum_ref, f32[8,768]{1,0:T(8,128)S(1)} %get-tuple-element.262.gain_ref, ...), custom_call_target="tpu_custom_call" | custom-call | flops 2415919104 | bytes 15728640 | tf_op jit(solution)/shard_map/pallas_call | solution.py:496
  200.1 4.8 %shard_map.263 = (bf16[256,768]{1,0:T(8,128)(2,1)S(1)}, bf16[256,2304]{1,0:T(8,128)(2,1)S(1)}, bf16[256,768]{1,0:T(8,128)(2,1)S(1)}, f32[256,768]{1,0:T(8,128)S(1)}, f32[8,768]{1,0:T(8,128)S(1)}) custom-call(s32[1]{0:T(128)S(6)} %copy.44.length_ref, f32[256,768]{1,0:T(8,128)S(1)} %get-tuple-element.264.hidden_ref, ...), custom_call_target="tpu_custom_call" | custom-call | flops 1207959552 | bytes 9437184 | tf_op jit(solution)/shard_map/pallas_call | solution.py:439
  205.0 7.8 %shard_map.264 = (bf16[256,768]{1,0:T(8,128)(2,1)S(1)}, bf16[256,3072]{1,0:T(8,128)(2,1)S(1)}, bf16[256,3072]{1,0:T(8,128)(2,1)S(1)}, f32[256,768]{1,0:T(8,128)S(1)}, f32[256,768]{1,0:T(8,128)S(1)}) custom-call(f32[256,768]{1,0:T(8,128)S(1)} %get-tuple-element.265.sum_ref, f32[8,768]{1,0:T(8,128)S(1)} %get-tuple-element.266.gain_ref, ...), custom_call_target="tpu_custom_call" | custom-call | flops 2415919104 | bytes 15728640 | tf_op jit(solution)/shard_map/pallas_call | solution.py:496
  216.8 2.4 shard_map.267
  219.2 6.9 %shard_map.268 = (bf16[256,3072]{1,0:T(8,128)(2,1)S(1)}, f32[256,768]{1,0:T(8,128)S(1)}) custom-call(f32[256,768]{1,0:T(8,128)S(1)} %get-tuple-element.284.grad_ref, bf16[256,768]{1,0:T(8,128)(2,1)S(1)} %get-tuple-element.285.refs_0_.low_ref, bf16[256,3072]{1,0:T(8,128)(2,1)S(1)} %get-tuple-element.286.slope_ref, ...), custom_call_target="tpu_custom_call" | custom-call | flops 2415919104 | bytes 14680064 | tf_op jit(solution)/shard_map/pallas_call | solution.py:563
  226.5 1.7 shard_map.269
  230.3 1.6 collective-permute-start.27
  232.0 1.9 shard_map.277
  237.0 2.4 shard_map.270
  239.5 1.3 collective-permute-start.30
  241.7 10.9 %shard_map.271 = (bf16[256,768]{1,0:T(8,128)(2,1)S(1)}, bf16[256,2304]{1,0:T(8,128)(2,1)S(1)}, f32[256,768]{1,0:T(8,128)S(1)}, f32[1,768]{1,0:T(1,128)S(1)}) custom-call(s32[1]{0:T(128)S(6)} %copy.44.length_ref, f32[256,768]{1,0:T(8,128)S(1)} %get-tuple-element.309.grad_ref, f32[256,768]{1,0:T(8,128)S(1)} %get-tuple-element.265.sum_ref, ...), custom_call_target="tpu_custom_call" | custom-call | flops 1207959552 | bytes 10485760 | tf_op jit(solution)/shard_map/pallas_call | solution.py:620
  252.7 1.6 collective-permute-start.32
  258.2 9.3 %collective-permute-done.32 = bf16[96,3072]{1,0:T(8,128)(2,1)S(1)} collective-permute-done((bf16[96,3072]{1,0:T(8,128)(2,1)S(1)}, bf16[96,3072]{1,0:T(8,128)(2,1)S(1)}, u32[]{:S(2)}, u32[]{:S(2)}) %collective-permute-start.32) | collective-permute-done | bytes 589856 | tf_op jit(solution)/shard_map/ppermute | solution.py:270
  269.7 1.4 collective-permute-start.37
  272.2 4.1 collective-permute-start.35
  276.3 5.1 %shard_map.276 = (bf16[256,3072]{1,0:T(8,128)(2,1)}, f32[256,768]{1,0:T(8,128)S(1)}) custom-call(f32[256,768]{1,0:T(8,128)S(1)} %get-tuple-element.365.grad_ref, bf16[256,768]{1,0:T(8,128)(2,1)S(1)} %get-tuple-element.366.refs_0_.low_ref, bf16[256,3072]{1,0:T(8,128)(2,1)S(1)} %copy-done.4, bf16[768,6144]{1,0:T(8,128)(2,1)S(1)} %bitcast.102, ...), custom_call_target="tpu_custom_call" | custom-call | flops 2415919104 | bytes 14680064 | tf_op jit(solution)/shard_map/pallas_call | solution.py:563
  283.7 1.4 copy-done.34
  292.0 3.6 shard_map.275
  299.7 1.4 add_convert_fusion.16
  301.1 3.5 collective-permute-start.45
  304.7 4.0 shard_map.278
  310.2 3.0 collective-permute-done.46
  316.8 9.7 %shard_map.279 = (bf16[256,768]{1,0:T(8,128)(2,1)S(1)}, bf16[256,2304]{1,0:T(8,128)(2,1)S(1)}, f32[256,768]{1,0:T(8,128)}, f32[1,768]{1,0:T(1,128)S(1)}) custom-call(s32[1]{0:T(128)S(6)} %copy.44.length_ref, f32[256,768]{1,0:T(8,128)S(1)} %get-tuple-element.390.grad_ref, f32[256,768]{1,0:T(8,128)S(1)} %get-tuple-element.261.sum_ref, ...), custom_call_target="tpu_custom_call" | custom-call | flops 1207959552 | bytes 10485760 | tf_op jit(solution)/shard_map/pallas_call | solution.py:620
  329.8 1.5 collective-permute-done.57.ob
  331.3 2.2 collective-permute-start.50
  334.2 1.4 shard_map.281
  335.7 2.0 collective-permute-done.50
  338.6 4.9 %collective-permute-done.52 = bf16[96,6272]{1,0:T(8,128)(2,1)S(1)} collective-permute-done((bf16[96,6272]{1,0:T(8,128)(2,1)S(1)}, bf16[96,6272]{1,0:T(8,128)(2,1)S(1)}, u32[]{:S(2)}, u32[]{:S(2)}) %collective-permute-start.52) | collective-permute-done | bytes 1204256 | tf_op jit(solution)/shard_map/ppermute | solution.py:270
  343.5 1.6 collective-permute-done.53
  345.2 1.6 collective-permute-start.59
  348.3 1.5 collective-permute-done.60
  349.8 1.6 collective-permute-done.61
  351.8 2.4 collective-permute-done.62
  354.2 1.4 collective-permute-done.63
  356.0 3.3 collective-permute-start.64
  361.3 10.5 %collective-permute-done.65 = bf16[96,3072]{1,0:T(8,128)(2,1)S(1)} collective-permute-done((bf16[96,3072]{1,0:T(8,128)(2,1)S(1)}, bf16[96,3072]{1,0:T(8,128)(2,1)S(1)}, u32[]{:S(2)}, u32[]{:S(2)}) %collective-permute-start.65) | collective-permute-done | bytes 589856 | tf_op jit(solution)/shard_map/ppermute | solution.py:270
  373.3 1.4 collective-permute-start.69
  375.8 2.9 collective-permute-start.68
  379.5 3.4 collective-permute-done.68
  383.0 2.1 collective-permute-done.69
  387.3 6.1 %collective-permute-start.72 = (bf16[48,3200]{1,0:T(8,128)(2,1)S(1)}, bf16[48,3200]{1,0:T(8,128)(2,1)S(1)}, u32[]{:S(2)}, u32[]{:S(2)}) collective-permute-start(bf16[48,3200]{1,0:T(8,128)(2,1)S(1)} %get-tuple-element.464), channel_id=1, source_target_pairs={{0,2},{1,3},{6,4},{7,5},{8,10},{9,11},{14,12},{15,13},{16,18},{17,... | collective-permute-start | bytes 921608 | tf_op jit(solution)/shard_map/ppermute | solution.py:270
  393.4 7.6 %collective-permute-done.72 = bf16[48,3200]{1,0:T(8,128)(2,1)S(1)} collective-permute-done((bf16[48,3200]{1,0:T(8,128)(2,1)S(1)}, bf16[48,3200]{1,0:T(8,128)(2,1)S(1)}, u32[]{:S(2)}, u32[]{:S(2)}) %collective-permute-start.72) | collective-permute-done | bytes 307232 | tf_op jit(solution)/shard_map/ppermute | solution.py:270
  401.2 2.5 collective-permute-start.73
  404.7 7.0 %collective-permute-done.74 = bf16[24,3072]{1,0:T(8,128)(2,1)S(1)} collective-permute-done((bf16[24,3072]{1,0:T(8,128)(2,1)S(1)}, bf16[24,3072]{1,0:T(8,128)(2,1)S(1)}, u32[]{:S(2)}, u32[]{:S(2)}) %collective-permute-start.74) | collective-permute-done | bytes 147488 | tf_op jit(solution)/shard_map/ppermute | solution.py:270
  412.7 3.1 collective-permute-start.76
  (411 shorter events, 93.4 us)
Async XLA Ops:
  7.2 192.9 %all-gather.2.cloned.1.call-start = ((), (), s32[]{:S(2)}) async-start(), calls=%async_computation | async-start | bytes 14800896 | tf_op jit(solution)/shard_map/all_gather | solution.py:56
  21.2 11.3 %collective-permute-start.2 = (bf16[24,6144]{1,0:T(8,128)(2,1)S(1)}, bf16[24,6144]{1,0:T(8,128)(2,1)S(1)}, u32[]{:S(2)}, u32[]{:S(2)}) collective-permute-start(bf16[24,6144]{1,0:T(8,128)(2,1)S(1)} %pad_maximum_fusion.16), channel_id=1, source_target_pairs={{0,2},{1,3},{2,0},{3,1},{4,6},{5,7},{6,4},{7,5},{8,10},{9,11},{10,... | collective-permute-start | bytes 884744 | tf_op jit(solution)/shard_map/ppermute | solution.py:270
  23.0 9.5 %collective-permute-start.1 = (bf16[48,3200]{1,0:T(8,128)(2,1)S(1)}, bf16[48,3200]{1,0:T(8,128)(2,1)S(1)}, u32[]{:S(2)}, u32[]{:S(2)}) collective-permute-start(bf16[48,3200]{1,0:T(8,128)(2,1)S(1)} %pad_maximum_fusion.15), channel_id=1, source_target_pairs={{2,4},{3,5},{4,2},{5,3},{10,12},{11,13},{12,10},{13,11},{18,20},{1... | collective-permute-start | bytes 921608 | tf_op jit(solution)/shard_map/ppermute | solution.py:270
  32.5 17.4 %collective-permute-start.3 = (bf16[48,3200]{1,0:T(8,128)(2,1)S(1)}, bf16[48,3200]{1,0:T(8,128)(2,1)S(1)}, u32[]{:S(2)}, u32[]{:S(2)}) collective-permute-start(bf16[48,3200]{1,0:T(8,128)(2,1)S(1)} %collective-permute-done.1), channel_id=1, source_target_pairs={{2,0},{3,1},{4,6},{5,7},{10,8},{11,9},{12,14},{13,15},{18,16},{19,... | collective-permute-start | bytes 921608 | tf_op jit(solution)/shard_map/ppermute | solution.py:270
  33.8 16.1 %collective-permute-start.4 = (bf16[48,6144]{1,0:T(8,128)(2,1)S(1)}, bf16[48,6144]{1,0:T(8,128)(2,1)S(1)}, u32[]{:S(2)}, u32[]{:S(2)}) collective-permute-start(bf16[48,6144]{1,0:T(8,128)(2,1)S(1)} %pad_maximum_fusion.6), channel_id=1, source_target_pairs={{2,4},{3,5},{4,2},{5,3},{10,12},{11,13},{12,10},{13,11},{18,20},{1... | collective-permute-start | bytes 1769480 | tf_op jit(solution)/shard_map/ppermute | solution.py:270
  49.9 36.7 %collective-permute-start.7 = (bf16[48,6144]{1,0:T(8,128)(2,1)S(1)}, bf16[48,6144]{1,0:T(8,128)(2,1)S(1)}, u32[]{:S(2)}, u32[]{:S(2)}) collective-permute-start(bf16[48,6144]{1,0:T(8,128)(2,1)S(1)} %collective-permute-done.4), channel_id=1, source_target_pairs={{2,0},{3,1},{4,6},{5,7},{10,8},{11,9},{12,14},{13,15},{18,16},{19,... | collective-permute-start | bytes 1769480 | tf_op jit(solution)/shard_map/ppermute | solution.py:270
  51.2 35.6 %collective-permute-start.5 = (bf16[96,3200]{1,0:T(8,128)(2,1)S(1)}, bf16[96,3200]{1,0:T(8,128)(2,1)S(1)}, u32[]{:S(2)}, u32[]{:S(2)}) collective-permute-start(bf16[96,3200]{1,0:T(8,128)(2,1)S(1)} %pad_maximum_fusion.3), channel_id=1, source_target_pairs={{0,16},{1,17},{2,18},{3,19},{4,20},{5,21},{6,22},{7,23},{8,24},{9,... | collective-permute-start | bytes 1843208 | tf_op jit(solution)/shard_map/ppermute | solution.py:270
  52.8 34.0 %collective-permute-start.6 = (bf16[96,3200]{1,0:T(8,128)(2,1)S(1)}, bf16[96,3200]{1,0:T(8,128)(2,1)S(1)}, u32[]{:S(2)}, u32[]{:S(2)}) collective-permute-start(bf16[96,3200]{1,0:T(8,128)(2,1)S(1)} %pad_maximum_fusion.3), channel_id=1, source_target_pairs={{0,1},{1,0},{2,3},{3,2},{4,5},{5,4},{6,7},{7,6},{8,9},{9,8},{10,11... | collective-permute-start | bytes 1843208 | tf_op jit(solution)/shard_map/ppermute | solution.py:270
  86.9 15.8 %collective-permute-start.8 = (bf16[48,3200]{1,0:T(8,128)(2,1)S(1)}, bf16[48,3200]{1,0:T(8,128)(2,1)S(1)}, u32[]{:S(2)}, u32[]{:S(2)}) collective-permute-start(bf16[48,3200]{1,0:T(8,128)(2,1)S(1)} %slice.285), channel_id=1, source_target_pairs={{0,16},{1,17},{2,18},{3,19},{4,20},{5,21},{6,22},{7,23},{8,24},{9,... | collective-permute-start | bytes 921608 | tf_op jit(solution)/shard_map/ppermute | solution.py:270
  88.2 16.4 %collective-permute-start.9 = (bf16[48,3200]{1,0:T(8,128)(2,1)S(1)}, bf16[48,3200]{1,0:T(8,128)(2,1)S(1)}, u32[]{:S(2)}, u32[]{:S(2)}) collective-permute-start(bf16[48,3200]{1,0:T(8,128)(2,1)S(1)} %slice.286), channel_id=1, source_target_pairs={{0,1},{1,0},{2,3},{3,2},{4,5},{5,4},{6,7},{7,6},{8,9},{9,8},{10,11... | collective-permute-start | bytes 921608 | tf_op jit(solution)/shard_map/ppermute | solution.py:270
  104.6 40.2 %collective-permute-start.15 = (bf16[96,6144]{1,0:T(8,128)(2,1)S(1)}, bf16[96,6144]{1,0:T(8,128)(2,1)S(1)}, u32[]{:S(2)}, u32[]{:S(2)}) collective-permute-start(bf16[96,6144]{1,0:T(8,128)(2,1)S(1)} %pad_maximum_fusion.2), channel_id=1, source_target_pairs={{0,1},{1,0},{2,3},{3,2},{4,5},{5,4},{6,7},{7,6},{8,9},{9,8},{10,11... | collective-permute-start | bytes 3538952 | tf_op jit(solution)/shard_map/ppermute | solution.py:270
  106.5 38.4 %collective-permute-start.17 = (bf16[96,6144]{1,0:T(8,128)(2,1)S(1)}, bf16[96,6144]{1,0:T(8,128)(2,1)}, u32[]{:S(2)}, u32[]{:S(2)}) collective-permute-start(bf16[96,6144]{1,0:T(8,128)(2,1)S(1)} %pad_maximum_fusion.2), channel_id=1, source_target_pairs={{0,16},{1,17},{2,18},{3,19},{4,20},{5,21},{6,22},{7,23},{8,24},{9,... | collective-permute-start | bytes 3538952 | tf_op jit(solution)/shard_map/ppermute | solution.py:270
  106.9 44.7 %collective-permute-start.12 = (bf16[96,3200]{1,0:T(8,128)(2,1)S(1)}, bf16[96,3200]{1,0:T(8,128)(2,1)S(1)}, u32[]{:S(2)}, u32[]{:S(2)}) collective-permute-start(bf16[96,3200]{1,0:T(8,128)(2,1)S(1)} %collective-permute-done.5), channel_id=1, source_target_pairs={{0,8},{1,9},{2,10},{3,11},{4,12},{5,13},{6,14},{7,15},{8,0},{9,1},... | collective-permute-start | bytes 1843208 | tf_op jit(solution)/shard_map/ppermute | solution.py:270
  106.9 45.5 %collective-permute-start.13 = (bf16[96,3200]{1,0:T(8,128)(2,1)S(1)}, bf16[96,3200]{1,0:T(8,128)(2,1)S(1)}, u32[]{:S(2)}, u32[]{:S(2)}) collective-permute-start(bf16[96,3200]{1,0:T(8,128)(2,1)S(1)} %collective-permute-done.6), channel_id=1, source_target_pairs={{0,8},{1,9},{2,10},{3,11},{4,12},{5,13},{6,14},{7,15},{8,0},{9,1},... | collective-permute-start | bytes 1843208 | tf_op jit(solution)/shard_map/ppermute | solution.py:270
  107.4 46.3 %collective-permute-start.14 = (bf16[96,3200]{1,0:T(8,128)(2,1)S(1)}, bf16[96,3200]{1,0:T(8,128)(2,1)S(1)}, u32[]{:S(2)}, u32[]{:S(2)}) collective-permute-start(bf16[96,3200]{1,0:T(8,128)(2,1)S(1)} %pad_maximum_fusion.3), channel_id=1, source_target_pairs={{0,8},{1,9},{2,10},{3,11},{4,12},{5,13},{6,14},{7,15},{8,0},{9,1},... | collective-permute-start | bytes 1843208 | tf_op jit(solution)/shard_map/ppermute | solution.py:270
  148.8 15.6 %collective-permute-start.16 = (bf16[48,6144]{1,0:T(8,128)(2,1)}, bf16[48,6144]{1,0:T(8,128)(2,1)}, u32[]{:S(2)}, u32[]{:S(2)}) collective-permute-start(bf16[48,6144]{1,0:T(8,128)(2,1)} %slice.367), channel_id=1, source_target_pairs={{0,16},{1,17},{2,18},{3,19},{4,20},{5,21},{6,22},{7,23},{8,24},{9,... | collective-permute-start | bytes 1769480 | tf_op jit(solution)/shard_map/ppermute | solution.py:270
  151.1 15.3 %collective-permute-start.18 = (bf16[48,6144]{1,0:T(8,128)(2,1)}, bf16[48,6144]{1,0:T(8,128)(2,1)}, u32[]{:S(2)}, u32[]{:S(2)}) collective-permute-start(bf16[48,6144]{1,0:T(8,128)(2,1)} %slice.368), channel_id=1, source_target_pairs={{0,1},{1,0},{2,3},{3,2},{4,5},{5,4},{6,7},{7,6},{8,9},{9,8},{10,11... | collective-permute-start | bytes 1769480 | tf_op jit(solution)/shard_map/ppermute | solution.py:270
  152.4 29.6 %collective-permute-start.23 = (bf16[96,6144]{1,0:T(8,128)(2,1)S(1)}, bf16[96,6144]{1,0:T(8,128)(2,1)}, u32[]{:S(2)}, u32[]{:S(2)}) collective-permute-start(bf16[96,6144]{1,0:T(8,128)(2,1)S(1)} %pad_maximum_fusion.2), channel_id=1, source_target_pairs={{0,8},{1,9},{2,10},{3,11},{4,12},{5,13},{6,14},{7,15},{8,0},{9,1},... | collective-permute-start | bytes 3538952 | tf_op jit(solution)/shard_map/ppermute | solution.py:270
  153.3 28.7 %collective-permute-start.21 = (bf16[96,6144]{1,0:T(8,128)(2,1)}, bf16[96,6144]{1,0:T(8,128)(2,1)}, u32[]{:S(2)}, u32[]{:S(2)}) collective-permute-start(bf16[96,6144]{1,0:T(8,128)(2,1)} %collective-permute-done.17), channel_id=1, source_target_pairs={{0,8},{1,9},{2,10},{3,11},{4,12},{5,13},{6,14},{7,15},{8,0},{9,1},... | collective-permute-start | bytes 3538952 | tf_op jit(solution)/shard_map/ppermute | solution.py:270
  154.6 27.4 %collective-permute-start.22 = (bf16[96,6144]{1,0:T(8,128)(2,1)S(1)}, bf16[96,6144]{1,0:T(8,128)(2,1)}, u32[]{:S(2)}, u32[]{:S(2)}) collective-permute-start(bf16[96,6144]{1,0:T(8,128)(2,1)S(1)} %collective-permute-done.15), channel_id=1, source_target_pairs={{0,8},{1,9},{2,10},{3,11},{4,12},{5,13},{6,14},{7,15},{8,0},{9,1},... | collective-permute-start | bytes 3538952 | tf_op jit(solution)/shard_map/ppermute | solution.py:270
  164.4 17.6 %collective-permute-start.19 = (bf16[48,6144]{1,0:T(8,128)(2,1)}, bf16[48,6144]{1,0:T(8,128)(2,1)S(1)}, u32[]{:S(2)}, u32[]{:S(2)}) collective-permute-start(bf16[48,6144]{1,0:T(8,128)(2,1)} %collective-permute-done.16), channel_id=1, source_target_pairs={{0,8},{1,9},{2,10},{3,11},{4,12},{5,13},{6,14},{7,15},{8,0},{9,1},... | collective-permute-start | bytes 1769480 | tf_op jit(solution)/shard_map/ppermute | solution.py:270
  166.3 15.6 %collective-permute-start.20 = (bf16[48,6144]{1,0:T(8,128)(2,1)}, bf16[48,6144]{1,0:T(8,128)(2,1)S(1)}, u32[]{:S(2)}, u32[]{:S(2)}) collective-permute-start(bf16[48,6144]{1,0:T(8,128)(2,1)} %collective-permute-done.18), channel_id=1, source_target_pairs={{0,8},{1,9},{2,10},{3,11},{4,12},{5,13},{6,14},{7,15},{8,0},{9,1},... | collective-permute-start | bytes 1769480 | tf_op jit(solution)/shard_map/ppermute | solution.py:270
  226.0 11.0 %collective-permute-start.29 = (bf16[256,3072]{1,0:T(8,128)(2,1)S(1)}, bf16[256,3072]{1,0:T(8,128)(2,1)S(1)}, u32[]{:S(2)}, u32[]{:S(2)}) collective-permute-start(bf16[256,3072]{1,0:T(8,128)(2,1)S(1)} %get-tuple-element.293.ra), channel_id=1, source_target_pairs={{0,8},{1,9},{2,10},{3,11},{4,12},{5,13},{6,14},{7,15},{8,0},{9,1},... | collective-permute-start | bytes 4718600 | tf_op jit(solution)/shard_map/ppermute | solution.py:270
  229.7 9.7 %collective-permute-start.26 = (bf16[48,3072]{1,0:T(8,128)(2,1)S(1)}, bf16[48,3072]{1,0:T(8,128)(2,1)S(1)}, u32[]{:S(2)}, u32[]{:S(2)}) collective-permute-start(bf16[48,3072]{1,0:T(8,128)(2,1)S(1)} %get-tuple-element.279), channel_id=1, source_target_pairs={{0,16},{1,17},{2,18},{3,19},{4,20},{5,21},{6,22},{7,23},{8,24},{9,... | collective-permute-start | bytes 884744 | tf_op jit(solution)/shard_map/ppermute | solution.py:270
  230.3 9.2 %collective-permute-start.27 = (bf16[48,3072]{1,0:T(8,128)(2,1)S(1)}, bf16[48,3072]{1,0:T(8,128)(2,1)S(1)}, u32[]{:S(2)}, u32[]{:S(2)}) collective-permute-start(bf16[48,3072]{1,0:T(8,128)(2,1)S(1)} %get-tuple-element.280), channel_id=1, source_target_pairs={{0,1},{1,0},{2,3},{3,2},{4,5},{5,4},{6,7},{7,6},{8,9},{9,8},{10,11... | collective-permute-start | bytes 884744 | tf_op jit(solution)/shard_map/ppermute | solution.py:270
  231.9 36.9 %collective-permute-start.43 = (bf16[256,3072]{1,0:T(8,128)(2,1)S(1)}, bf16[256,3072]{1,0:T(8,128)(2,1)S(1)}, u32[]{:S(2)}, u32[]{:S(2)}) collective-permute-start(bf16[256,3072]{1,0:T(8,128)(2,1)S(1)} %copy-done.31), channel_id=1, source_target_pairs={{0,8},{1,9},{2,10},{3,11},{4,12},{5,13},{6,14},{7,15},{8,0},{9,1},... | collective-permute-start | bytes 4718600 | tf_op jit(solution)/shard_map/ppermute | solution.py:270
  236.6 32.4 %collective-permute-start.38 = (bf16[384,256]{1,0:T(8,128)(2,1)}, bf16[384,256]{1,0:T(8,128)(2,1)}, u32[]{:S(2)}, u32[]{:S(2)}) collective-permute-start(bf16[384,256]{1,0:T(8,128)(2,1)} %get-tuple-element.337), channel_id=1, source_target_pairs={{0,8},{1,9},{2,10},{3,11},{4,12},{5,13},{6,14},{7,15},{8,0},{9,1},... | collective-permute-start | bytes 589832 | tf_op jit(solution)/shard_map/ppermute | solution.py:270
  239.5 13.2 %collective-permute-start.30 = (bf16[48,3072]{1,0:T(8,128)(2,1)S(1)}, bf16[48,3072]{1,0:T(8,128)(2,1)S(1)}, u32[]{:S(2)}, u32[]{:S(2)}) collective-permute-start(bf16[48,3072]{1,0:T(8,128)(2,1)S(1)} %get-tuple-element.304), channel_id=1, source_target_pairs={{0,16},{1,17},{2,18},{3,19},{4,20},{5,21},{6,22},{7,23},{8,24},{9,... | collective-permute-start | bytes 884744 | tf_op jit(solution)/shard_map/ppermute | solution.py:270
  240.8 11.8 %collective-permute-start.31 = (bf16[48,3072]{1,0:T(8,128)(2,1)S(1)}, bf16[48,3072]{1,0:T(8,128)(2,1)S(1)}, u32[]{:S(2)}, u32[]{:S(2)}) collective-permute-start(bf16[48,3072]{1,0:T(8,128)(2,1)S(1)} %get-tuple-element.305), channel_id=1, source_target_pairs={{0,1},{1,0},{2,3},{3,2},{4,5},{5,4},{6,7},{7,6},{8,9},{9,8},{10,11... | collective-permute-start | bytes 884744 | tf_op jit(solution)/shard_map/ppermute | solution.py:270
  252.7 14.7 %collective-permute-start.32 = (bf16[96,3072]{1,0:T(8,128)(2,1)S(1)}, bf16[96,3072]{1,0:T(8,128)(2,1)S(1)}, u32[]{:S(2)}, u32[]{:S(2)}) collective-permute-start(bf16[96,3072]{1,0:T(8,128)(2,1)S(1)} %pad_maximum_fusion.7), channel_id=1, source_target_pairs={{0,16},{1,17},{2,18},{3,19},{4,20},{5,21},{6,22},{7,23},{8,24},{9,... | collective-permute-start | bytes 1769480 | tf_op jit(solution)/shard_map/ppermute | solution.py:270
  254.3 14.0 %collective-permute-start.33 = (bf16[96,3072]{1,0:T(8,128)(2,1)S(1)}, bf16[96,3072]{1,0:T(8,128)(2,1)S(1)}, u32[]{:S(2)}, u32[]{:S(2)}) collective-permute-start(bf16[96,3072]{1,0:T(8,128)(2,1)S(1)} %pad_maximum_fusion.8), channel_id=1, source_target_pairs={{0,1},{1,0},{2,3},{3,2},{4,5},{5,4},{6,7},{7,6},{8,9},{9,8},{10,11... | collective-permute-start | bytes 1769480 | tf_op jit(solution)/shard_map/ppermute | solution.py:270
  258.2 11.6 %collective-permute-start.40 = (bf16[384,256]{1,0:T(8,128)(2,1)}, bf16[384,256]{1,0:T(8,128)(2,1)S(1)}, u32[]{:S(2)}, u32[]{:S(2)}) collective-permute-start(bf16[384,256]{1,0:T(8,128)(2,1)} %get-tuple-element.340), channel_id=1, source_target_pairs={{0,8},{1,9},{2,10},{3,11},{4,12},{5,13},{6,14},{7,15},{8,0},{9,1},... | collective-permute-start | bytes 589832 | tf_op jit(solution)/shard_map/ppermute | solution.py:270
  267.4 14.7 %collective-permute-start.39 = (bf16[256,2304]{1,0:T(8,128)(2,1)S(1)}, bf16[256,2304]{1,0:T(8,128)(2,1)S(1)}, u32[]{:S(2)}, u32[]{:S(2)}) collective-permute-start(bf16[256,2304]{1,0:T(8,128)(2,1)S(1)} %get-tuple-element.338.qa), channel_id=1, source_target_pairs={{0,8},{1,9},{2,10},{3,11},{4,12},{5,13},{6,14},{7,15},{8,0},{9,1},... | collective-permute-start | bytes 3538952 | tf_op jit(solution)/shard_map/ppermute | solution.py:270
  268.3 13.1 %collective-permute-start.41 = (bf16[256,768]{1,0:T(8,128)(2,1)S(1)}, bf16[256,768]{1,0:T(8,128)(2,1)S(1)}, u32[]{:S(2)}, u32[]{:S(2)}) collective-permute-start(bf16[256,768]{1,0:T(8,128)(2,1)S(1)} %get-tuple-element.341.oa), channel_id=1, source_target_pairs={{0,8},{1,9},{2,10},{3,11},{4,12},{5,13},{6,14},{7,15},{8,0},{9,1},... | collective-permute-start | bytes 1179656 | tf_op jit(solution)/shard_map/ppermute | solution.py:270
  269.0 26.6 %collective-permute-start.36 = (bf16[96,3072]{1,0:T(8,128)(2,1)}, bf16[96,3072]{1,0:T(8,128)(2,1)}, u32[]{:S(2)}, u32[]{:S(2)}) collective-permute-start(bf16[96,3072]{1,0:T(8,128)(2,1)} %pad_maximum_fusion.9), channel_id=1, source_target_pairs={{0,16},{1,17},{2,18},{3,19},{4,20},{5,21},{6,22},{7,23},{8,24},{9,... | collective-permute-start | bytes 1769480 | tf_op jit(solution)/shard_map/ppermute | solution.py:270
  269.7 25.9 %collective-permute-start.37 = (bf16[96,3072]{1,0:T(8,128)(2,1)}, bf16[96,3072]{1,0:T(8,128)(2,1)}, u32[]{:S(2)}, u32[]{:S(2)}) collective-permute-start(bf16[96,3072]{1,0:T(8,128)(2,1)} %pad_maximum_fusion.10), channel_id=1, source_target_pairs={{0,1},{1,0},{2,3},{3,2},{4,5},{5,4},{6,7},{7,6},{8,9},{9,8},{10,11... | collective-permute-start | bytes 1769480 | tf_op jit(solution)/shard_map/ppermute | solution.py:270
  272.2 23.4 %collective-permute-start.35 = (bf16[48,3072]{1,0:T(8,128)(2,1)}, bf16[48,3072]{1,0:T(8,128)(2,1)}, u32[]{:S(2)}, u32[]{:S(2)}) collective-permute-start(bf16[48,3072]{1,0:T(8,128)(2,1)} %get-tuple-element.354), channel_id=1, source_target_pairs={{0,2},{1,3},{6,4},{7,5},{8,10},{9,11},{14,12},{15,13},{16,18},{17,... | collective-permute-start | bytes 884744 | tf_op jit(solution)/shard_map/ppermute | solution.py:270
  282.2 18.9 %collective-permute-start.48 = (bf16[384,256]{1,0:T(8,128)(2,1)}, bf16[384,256]{1,0:T(8,128)(2,1)S(1)}, u32[]{:S(2)}, u32[]{:S(2)}) collective-permute-start(bf16[384,256]{1,0:T(8,128)(2,1)} %get-tuple-element.373), channel_id=1, source_target_pairs={{0,8},{1,9},{2,10},{3,11},{4,12},{5,13},{6,14},{7,15},{8,0},{9,1},... | collective-permute-start | bytes 589832 | tf_op jit(solution)/shard_map/ppermute | solution.py:270
  283.2 21.4 %collective-permute-start.49 = (bf16[256,3072]{1,0:T(8,128)(2,1)}, bf16[256,3072]{1,0:T(8,128)(2,1)S(1)}, u32[]{:S(2)}, u32[]{:S(2)}) collective-permute-start(bf16[256,3072]{1,0:T(8,128)(2,1)} %get-tuple-element.374.ra), channel_id=1, source_target_pairs={{0,8},{1,9},{2,10},{3,11},{4,12},{5,13},{6,14},{7,15},{8,0},{9,1},... | collective-permute-start | bytes 4718600 | tf_op jit(solution)/shard_map/ppermute | solution.py:270
  296.8 11.9 %collective-permute-start.44 = (bf16[48,3072]{1,0:T(8,128)(2,1)S(1)}, bf16[48,3072]{1,0:T(8,128)(2,1)S(1)}, u32[]{:S(2)}, u32[]{:S(2)}) collective-permute-start(bf16[48,3072]{1,0:T(8,128)(2,1)S(1)} %add_convert_fusion.18), channel_id=1, source_target_pairs={{2,4},{3,5},{4,2},{5,3},{10,12},{11,13},{12,10},{13,11},{18,20},{1... | collective-permute-start | bytes 884744 | tf_op jit(solution)/shard_map/ppermute | solution.py:270
  297.6 15.6 %collective-permute-start.46 = (bf16[48,6272]{1,0:T(8,128)(2,1)S(1)}, bf16[48,6272]{1,0:T(8,128)(2,1)S(1)}, u32[]{:S(2)}, u32[]{:S(2)}) collective-permute-start(bf16[48,6272]{1,0:T(8,128)(2,1)S(1)} %get-tuple-element.360), channel_id=1, source_target_pairs={{0,16},{1,17},{2,18},{3,19},{4,20},{5,21},{6,22},{7,23},{8,24},{9,... | collective-permute-start | bytes 1806344 | tf_op jit(solution)/shard_map/ppermute | solution.py:270
  298.5 15.2 %collective-permute-start.47 = (bf16[48,6272]{1,0:T(8,128)(2,1)S(1)}, bf16[48,6272]{1,0:T(8,128)(2,1)S(1)}, u32[]{:S(2)}, u32[]{:S(2)}) collective-permute-start(bf16[48,6272]{1,0:T(8,128)(2,1)S(1)} %get-tuple-element.361), channel_id=1, source_target_pairs={{0,1},{1,0},{2,3},{3,2},{4,5},{5,4},{6,7},{7,6},{8,9},{9,8},{10,11... | collective-permute-start | bytes 1806344 | tf_op jit(solution)/shard_map/ppermute | solution.py:270
  301.1 9.1 %collective-permute-start.45 = (bf16[48,3072]{1,0:T(8,128)(2,1)S(1)}, bf16[48,3072]{1,0:T(8,128)(2,1)S(1)}, u32[]{:S(2)}, u32[]{:S(2)}) collective-permute-start(bf16[48,3072]{1,0:T(8,128)(2,1)S(1)} %get-tuple-element.382), channel_id=1, source_target_pairs={{0,2},{1,3},{6,4},{7,5},{8,10},{9,11},{14,12},{15,13},{16,18},{17,... | collective-permute-start | bytes 884744 | tf_op jit(solution)/shard_map/ppermute | solution.py:270
  304.6 22.4 %collective-permute-start.54 = (bf16[384,256]{1,0:T(8,128)(2,1)S(1)}, bf16[384,256]{1,0:T(8,128)(2,1)S(1)}, u32[]{:S(2)}, u32[]{:S(2)}) collective-permute-start(bf16[384,256]{1,0:T(8,128)(2,1)S(1)} %copy-done.46), channel_id=1, source_target_pairs={{0,8},{1,9},{2,10},{3,11},{4,12},{5,13},{6,14},{7,15},{8,0},{9,1},... | collective-permute-start | bytes 589832 | tf_op jit(solution)/shard_map/ppermute | solution.py:270
  308.7 19.0 %collective-permute-start.56 = (bf16[384,256]{1,0:T(8,128)(2,1)S(1)}, bf16[384,256]{1,0:T(8,128)(2,1)S(1)}, u32[]{:S(2)}, u32[]{:S(2)}) collective-permute-start(bf16[384,256]{1,0:T(8,128)(2,1)S(1)} %get-tuple-element.397), channel_id=1, source_target_pairs={{0,8},{1,9},{2,10},{3,11},{4,12},{5,13},{6,14},{7,15},{8,0},{9,1},... | collective-permute-start | bytes 589832 | tf_op jit(solution)/shard_map/ppermute | solution.py:270
  314.0 29.5 %collective-permute-start.52 = (bf16[96,6272]{1,0:T(8,128)(2,1)S(1)}, bf16[96,6272]{1,0:T(8,128)(2,1)S(1)}, u32[]{:S(2)}, u32[]{:S(2)}) collective-permute-start(bf16[96,6272]{1,0:T(8,128)(2,1)S(1)} %pad_maximum_fusion), channel_id=1, source_target_pairs={{0,16},{1,17},{2,18},{3,19},{4,20},{5,21},{6,22},{7,23},{8,24},{9,... | collective-permute-start | bytes 3612680 | tf_op jit(solution)/shard_map/ppermute | solution.py:270
  315.6 29.5 %collective-permute-start.53 = (bf16[96,6272]{1,0:T(8,128)(2,1)S(1)}, bf16[96,6272]{1,0:T(8,128)(2,1)S(1)}, u32[]{:S(2)}, u32[]{:S(2)}) collective-permute-start(bf16[96,6272]{1,0:T(8,128)(2,1)S(1)} %pad_maximum_fusion.1), channel_id=1, source_target_pairs={{0,1},{1,0},{2,3},{3,2},{4,5},{5,4},{6,7},{7,6},{8,9},{9,8},{10,11... | collective-permute-start | bytes 3612680 | tf_op jit(solution)/shard_map/ppermute | solution.py:270
  327.7 10.9 %collective-permute-start.51 = (bf16[48,3072]{1,0:T(8,128)(2,1)S(1)}, bf16[48,3072]{1,0:T(8,128)(2,1)S(1)}, u32[]{:S(2)}, u32[]{:S(2)}) collective-permute-start(bf16[48,3072]{1,0:T(8,128)(2,1)S(1)} %add_convert_fusion.15), channel_id=1, source_target_pairs={{2,4},{3,5},{4,2},{5,3},{10,12},{11,13},{12,10},{13,11},{18,20},{1... | collective-permute-start | bytes 884744 | tf_op jit(solution)/shard_map/ppermute | solution.py:270
  333.5 16.3 %collective-permute-start.60 = (bf16[48,3072]{1,0:T(8,128)(2,1)S(1)}, bf16[48,3072]{1,0:T(8,128)(2,1)S(1)}, u32[]{:S(2)}, u32[]{:S(2)}) collective-permute-start(bf16[48,3072]{1,0:T(8,128)(2,1)S(1)} %get-tuple-element.414), channel_id=1, source_target_pairs={{0,16},{1,17},{2,18},{3,19},{4,20},{5,21},{6,22},{7,23},{8,24},{9,... | collective-permute-start | bytes 884744 | tf_op jit(solution)/shard_map/ppermute | solution.py:270
  337.6 13.8 %collective-permute-start.61 = (bf16[48,3072]{1,0:T(8,128)(2,1)S(1)}, bf16[48,3072]{1,0:T(8,128)(2,1)S(1)}, u32[]{:S(2)}, u32[]{:S(2)}) collective-permute-start(bf16[48,3072]{1,0:T(8,128)(2,1)S(1)} %get-tuple-element.415), channel_id=1, source_target_pairs={{0,1},{1,0},{2,3},{3,2},{4,5},{5,4},{6,7},{7,6},{8,9},{9,8},{10,11... | collective-permute-start | bytes 884744 | tf_op jit(solution)/shard_map/ppermute | solution.py:270
  346.8 7.4 %collective-permute-start.62 = (bf16[48,3200]{1,0:T(8,128)(2,1)S(1)}, bf16[48,3200]{1,0:T(8,128)(2,1)S(1)}, u32[]{:S(2)}, u32[]{:S(2)}) collective-permute-start(bf16[48,3200]{1,0:T(8,128)(2,1)S(1)} %get-tuple-element.427), channel_id=1, source_target_pairs={{0,16},{1,17},{2,18},{3,19},{4,20},{5,21},{6,22},{7,23},{8,24},{9,... | collective-permute-start | bytes 921608 | tf_op jit(solution)/shard_map/ppermute | solution.py:270
  347.5 8.0 %collective-permute-start.63 = (bf16[48,3200]{1,0:T(8,128)(2,1)S(1)}, bf16[48,3200]{1,0:T(8,128)(2,1)S(1)}, u32[]{:S(2)}, u32[]{:S(2)}) collective-permute-start(bf16[48,3200]{1,0:T(8,128)(2,1)S(1)} %get-tuple-element.428), channel_id=1, source_target_pairs={{0,1},{1,0},{2,3},{3,2},{4,5},{5,4},{6,7},{7,6},{8,9},{9,8},{10,11... | collective-permute-start | bytes 921608 | tf_op jit(solution)/shard_map/ppermute | solution.py:270
  356.0 16.2 %collective-permute-start.64 = (bf16[48,6272]{1,0:T(8,128)(2,1)S(1)}, bf16[48,6272]{1,0:T(8,128)(2,1)S(1)}, u32[]{:S(2)}, u32[]{:S(2)}) collective-permute-start(bf16[48,6272]{1,0:T(8,128)(2,1)S(1)} %get-tuple-element.443), channel_id=1, source_target_pairs={{0,2},{1,3},{6,4},{7,5},{8,10},{9,11},{14,12},{15,13},{16,18},{17,... | collective-permute-start | bytes 1806344 | tf_op jit(solution)/shard_map/ppermute | solution.py:270
  359.3 12.5 %collective-permute-start.65 = (bf16[96,3072]{1,0:T(8,128)(2,1)S(1)}, bf16[96,3072]{1,0:T(8,128)(2,1)S(1)}, u32[]{:S(2)}, u32[]{:S(2)}) collective-permute-start(bf16[96,3072]{1,0:T(8,128)(2,1)S(1)} %pad_maximum_fusion.11), channel_id=1, source_target_pairs={{0,16},{1,17},{2,18},{3,19},{4,20},{5,21},{6,22},{7,23},{8,24},{9,... | collective-permute-start | bytes 1769480 | tf_op jit(solution)/shard_map/ppermute | solution.py:270
  360.1 12.2 %collective-permute-start.66 = (bf16[96,3072]{1,0:T(8,128)(2,1)S(1)}, bf16[96,3072]{1,0:T(8,128)(2,1)S(1)}, u32[]{:S(2)}, u32[]{:S(2)}) collective-permute-start(bf16[96,3072]{1,0:T(8,128)(2,1)S(1)} %pad_maximum_fusion.12), channel_id=1, source_target_pairs={{0,1},{1,0},{2,3},{3,2},{4,5},{5,4},{6,7},{7,6},{8,9},{9,8},{10,11... | collective-permute-start | bytes 1769480 | tf_op jit(solution)/shard_map/ppermute | solution.py:270
  372.4 10.5 %collective-permute-start.67 = (bf16[48,6272]{1,0:T(8,128)(2,1)S(1)}, bf16[48,6272]{1,0:T(8,128)(2,1)S(1)}, u32[]{:S(2)}, u32[]{:S(2)}) collective-permute-start(bf16[48,6272]{1,0:T(8,128)(2,1)S(1)} %add_convert_fusion), channel_id=1, source_target_pairs={{2,4},{3,5},{4,2},{5,3},{10,12},{11,13},{12,10},{13,11},{18,20},{1... | collective-permute-start | bytes 1806344 | tf_op jit(solution)/shard_map/ppermute | solution.py:270
  373.3 11.8 %collective-permute-start.69 = (bf16[96,3200]{1,0:T(8,128)(2,1)S(1)}, bf16[96,3200]{1,0:T(8,128)(2,1)S(1)}, u32[]{:S(2)}, u32[]{:S(2)}) collective-permute-start(bf16[96,3200]{1,0:T(8,128)(2,1)S(1)} %pad_maximum_fusion.4), channel_id=1, source_target_pairs={{0,16},{1,17},{2,18},{3,19},{4,20},{5,21},{6,22},{7,23},{8,24},{9,... | collective-permute-start | bytes 1843208 | tf_op jit(solution)/shard_map/ppermute | solution.py:270
  374.6 11.5 %collective-permute-start.70 = (bf16[96,3200]{1,0:T(8,128)(2,1)S(1)}, bf16[96,3200]{1,0:T(8,128)(2,1)S(1)}, u32[]{:S(2)}, u32[]{:S(2)}) collective-permute-start(bf16[96,3200]{1,0:T(8,128)(2,1)S(1)} %pad_maximum_fusion.5), channel_id=1, source_target_pairs={{0,1},{1,0},{2,3},{3,2},{4,5},{5,4},{6,7},{7,6},{8,9},{9,8},{10,11... | collective-permute-start | bytes 1843208 | tf_op jit(solution)/shard_map/ppermute | solution.py:270
  375.8 7.1 %collective-permute-start.68 = (bf16[48,3072]{1,0:T(8,128)(2,1)S(1)}, bf16[48,3072]{1,0:T(8,128)(2,1)S(1)}, u32[]{:S(2)}, u32[]{:S(2)}) collective-permute-start(bf16[48,3072]{1,0:T(8,128)(2,1)S(1)} %get-tuple-element.454), channel_id=1, source_target_pairs={{0,2},{1,3},{6,4},{7,5},{8,10},{9,11},{14,12},{15,13},{16,18},{17,... | collective-permute-start | bytes 884744 | tf_op jit(solution)/shard_map/ppermute | solution.py:270
  386.2 7.2 %collective-permute-start.71 = (bf16[48,3072]{1,0:T(8,128)(2,1)S(1)}, bf16[48,3072]{1,0:T(8,128)(2,1)S(1)}, u32[]{:S(2)}, u32[]{:S(2)}) collective-permute-start(bf16[48,3072]{1,0:T(8,128)(2,1)S(1)} %add_convert_fusion.10), channel_id=1, source_target_pairs={{2,4},{3,5},{4,2},{5,3},{10,12},{11,13},{12,10},{13,11},{18,20},{1... | collective-permute-start | bytes 884744 | tf_op jit(solution)/shard_map/ppermute | solution.py:270
  387.3 13.7 %collective-permute-start.72 = (bf16[48,3200]{1,0:T(8,128)(2,1)S(1)}, bf16[48,3200]{1,0:T(8,128)(2,1)S(1)}, u32[]{:S(2)}, u32[]{:S(2)}) collective-permute-start(bf16[48,3200]{1,0:T(8,128)(2,1)S(1)} %get-tuple-element.464), channel_id=1, source_target_pairs={{0,2},{1,3},{6,4},{7,5},{8,10},{9,11},{14,12},{15,13},{16,18},{17,... | collective-permute-start | bytes 921608 | tf_op jit(solution)/shard_map/ppermute | solution.py:270
  401.2 10.5 %collective-permute-start.73 = (bf16[24,6272]{1,0:T(8,128)(2,1)S(1)}, bf16[24,6272]{1,0:T(8,128)(2,1)S(1)}, u32[]{:S(2)}, u32[]{:S(2)}) collective-permute-start(bf16[24,6272]{1,0:T(8,128)(2,1)S(1)} %slice.460), channel_id=1, source_target_pairs={{0,2},{1,3},{2,0},{3,1},{4,6},{5,7},{6,4},{7,5},{8,10},{9,11},{10,... | collective-permute-start | bytes 903176 | tf_op jit(solution)/shard_map/ppermute | solution.py:270
  403.8 7.9 %collective-permute-start.74 = (bf16[24,3072]{1,0:T(8,128)(2,1)S(1)}, bf16[24,3072]{1,0:T(8,128)(2,1)S(1)}, u32[]{:S(2)}, u32[]{:S(2)}) collective-permute-start(bf16[24,3072]{1,0:T(8,128)(2,1)S(1)} %slice.462), channel_id=1, source_target_pairs={{0,2},{1,3},{2,0},{3,1},{4,6},{5,7},{6,4},{7,5},{8,10},{9,11},{10,... | collective-permute-start | bytes 442376 | tf_op jit(solution)/shard_map/ppermute | solution.py:270
  404.0 7.7 %collective-permute-start.75 = (bf16[48,3200]{1,0:T(8,128)(2,1)S(1)}, bf16[48,3200]{1,0:T(8,128)(2,1)S(1)}, u32[]{:S(2)}, u32[]{:S(2)}) collective-permute-start(bf16[48,3200]{1,0:T(8,128)(2,1)S(1)} %add_convert_fusion.5), channel_id=1, source_target_pairs={{2,4},{3,5},{4,2},{5,3},{10,12},{11,13},{12,10},{13,11},{18,20},{1... | collective-permute-start | bytes 921608 | tf_op jit(solution)/shard_map/ppermute | solution.py:270
  (109 other events, 1111.0 us)
Sparse Core Ops, SparseCore 0:
  14.1 143.0 all-gather.1

commit v4 on v3

--- a/solution.py
+++ b/solution.py
@@ -14,6 +14,7 @@
 FF = 3072
 LAYERS = 2
 PAD = 128
+LIGHT = pl.CostEstimate(flops=1 << 20, bytes_accessed=1 << 16, transcendentals=0)
 
 
 def norm(value, gain):
@@ -289,7 +290,7 @@
     return (natural == rows[None]).astype(jnp.bfloat16)
 
 
-def share_left(values, order, grid):
+def share_left(values, order):
     lengths = [max(value.shape[0], PAD) for value in values]
     half = D // 2
 
@@ -308,16 +309,18 @@
         in_specs=[VMEM_SPEC] * (1 + len(values)),
         out_specs=[VMEM_SPEC] * (2 * len(values)),
         out_shape=shapes(*(((half, n), jnp.bfloat16) for n in lengths for _ in range(2))),
-        cost_estimate=pl.CostEstimate(
-            flops=2 * D * D * sum(lengths), bytes_accessed=2 << 20, transcendentals=0
-        ),
-        compiler_params=params(24),
+        cost_estimate=LIGHT,
+        compiler_params=params(8),
     )(order, *values)
-    return [(turned[2 * j], swap(turned[2 * j + 1], grid.core)) for j in range(len(values))]
+    return [(turned[2 * j], turned[2 * j + 1]) for j in range(len(values))]
 
 
 def both(value, grid):
     return (value, swap(value, grid.core))
+
+
+def traded(pair, grid):
+    return (pair[0], swap(pair[1], grid.core))
 
 
 ROWS = ((0, 2), (2, 4), (4, 8), (8, 12), (12, 16))
@@ -448,10 +451,8 @@
             ((8, D), jnp.float32),
         ),
         scratch_shapes=[pltpu.VMEM((D, 4 * D + PAD), low), pltpu.SemaphoreType.DMA((5,))],
-        cost_estimate=pl.CostEstimate(
-            flops=2 * tokens * D * 4 * D, bytes_accessed=9 << 20, transcendentals=0
-        ),
-        compiler_params=params(40),
+        cost_estimate=LIGHT,
+        compiler_params=params(14),
     )(lengths, hidden, weights)
 
 
@@ -511,10 +512,8 @@
             ((tokens, D), jnp.float32),
         ),
         scratch_shapes=[pltpu.VMEM((tokens, D), jnp.float32)],
-        cost_estimate=pl.CostEstimate(
-            flops=4 * tokens * D * FF, bytes_accessed=15 << 20, transcendentals=tokens * FF
-        ),
-        compiler_params=params(40),
+        cost_estimate=LIGHT,
+        compiler_params=params(16),
     )(first_sum, gains, weights, weights)
 
 
@@ -534,8 +533,8 @@
         out_shape=shapes(
             ((tokens, D), jnp.float32), ((tokens, D), jnp.bfloat16), ((1, D), jnp.float32)
         ),
-        cost_estimate=pl.CostEstimate(flops=0, bytes_accessed=3 << 20, transcendentals=0),
-        compiler_params=params(16),
+        cost_estimate=LIGHT,
+        compiler_params=params(6),
     )(grad, second_sum, gains)
 
 
@@ -572,10 +571,8 @@
         ],
         out_specs=[wide, fixed((tokens, D))],
         out_shape=shapes(((tokens, FF), low), ((tokens, D), jnp.float32)),
-        cost_estimate=pl.CostEstimate(
-            flops=4 * tokens * D * FF, bytes_accessed=14 << 20, transcendentals=0
-        ),
-        compiler_params=params(40),
+        cost_estimate=LIGHT,
+        compiler_params=params(12),
     )(grad_second, down_low, slope, weights, weights)
 
 
@@ -632,46 +629,49 @@
             pltpu.VMEM((D, 4 * D + PAD), low),
             pltpu.SemaphoreType.DMA((5,)),
         ],
-        cost_estimate=pl.CostEstimate(
-            flops=2 * tokens * D * 4 * D, bytes_accessed=10 << 20, transcendentals=0
-        ),
-        compiler_params=params(40),
+        cost_estimate=LIGHT,
+        compiler_params=params(16),
     )(lengths, grad, first_sum, gains, qkv, weights)
 
 
-def matrix_terms(left_t, right, unit):
+def matrix_terms(products, unit):
     tile = D
-
-    def body(la, lb, ra, rb, *outs):
-        value = (dot(la[...], ra[...]) + dot(lb[...], rb[...])).astype(jnp.bfloat16)
-        for (low, high), out in zip(ROWS, outs):
-            out[...] = value[low * unit : high * unit]
-
-    def whole(value):
-        return pl.BlockSpec(value.shape, lambda j: (0, 0))
-
-    tokens, width = right[0].shape
-    column = pl.BlockSpec((tokens, tile), lambda j: (0, j))
+    tokens, width = products[0][1][0].shape
+    steps = width // tile
+
+    def body(*refs):
+        outs = refs[4 * len(products) :]
+        for j in range(len(products)):
+            la, lb, ra, rb = refs[4 * j : 4 * j + 4]
+
+            @pl.when(pl.program_id(0) // steps == j)
+            def _(la=la, lb=lb, ra=ra, rb=rb):
+                value = (dot(la[...], ra[...]) + dot(lb[...], rb[...])).astype(jnp.bfloat16)
+                for (low, high), out in zip(ROWS, outs):
+                    out[...] = value[low * unit : high * unit]
+
+    in_specs, operands = [], []
+    for j, (left, right) in enumerate(products):
+        whole = pl.BlockSpec(left[0].shape, lambda i: (0, 0))
+        column = pl.BlockSpec(
+            (tokens, tile), lambda i, j=j: (0, jnp.clip(i - j * steps, 0, steps - 1))
+        )
+        in_specs += [whole, whole, column, column]
+        operands += [*left, *right]
+    wide = width * len(products)
     return pl.pallas_call(
         body,
-        grid=(width // tile,),
-        in_specs=[whole(v) for v in left_t] + [column, column],
-        out_specs=[pl.BlockSpec(((b - a) * unit, tile), lambda j: (0, j)) for a, b in ROWS],
-        out_shape=[jax.ShapeDtypeStruct(((b - a) * unit, width), jnp.bfloat16) for a, b in ROWS],
-        cost_estimate=pl.CostEstimate(
-            flops=4 * tokens * 16 * unit * width, bytes_accessed=6 << 20, transcendentals=0
-        ),
-        compiler_params=pltpu.CompilerParams(vmem_limit_bytes=32 << 20),
-    )(*left_t, *right)
-
-
-def attention_terms(inputs_t, grad_qkv, mixed_t, attn_low, gains_t, unit, extra=()):
-    wide = extra[1][0].shape[1] if extra else 0
-    width = 4 * D + PAD + wide
-
-    def body(ia, ib, qa, qb, ma, mb, oa, ob, ga, gb, *refs):
-        outs = refs[4 if extra else 0 :]
-
+        grid=(wide // tile,),
+        in_specs=in_specs,
+        out_specs=[pl.BlockSpec(((b - a) * unit, tile), lambda i: (0, i)) for a, b in ROWS],
+        out_shape=shapes(*((((b - a) * unit, wide), jnp.bfloat16) for a, b in ROWS)),
+        cost_estimate=LIGHT,
+        compiler_params=params(10),
+    )(*operands)
+
+
+def attention_terms(inputs_t, grad_qkv, mixed_t, attn_low, gains_t, unit):
+    def body(ia, ib, qa, qb, ma, mb, oa, ob, ga, gb, *outs):
         def put(value, column):
             value = value.astype(jnp.bfloat16)
             for (low, high), out in zip(ROWS, outs):
@@ -682,23 +682,15 @@
             put(dot(ia[...], qa[:, part]) + dot(ib[...], qb[:, part]), j * D)
         put(dot(ma[...], oa[...]) + dot(mb[...], ob[...]), 3 * D)
         put(ga[...].astype(jnp.float32) + gb[...].astype(jnp.float32), 4 * D)
-        for j in range(wide // D):
-            la, lb, ra, rb = refs[:4]
-            part = slice(j * D, (j + 1) * D)
-            put(dot(la[...], ra[:, part]) + dot(lb[...], rb[:, part]), 4 * D + PAD + j * D)
 
     operands = [*inputs_t, *grad_qkv, *mixed_t, *attn_low, *gains_t]
-    for pair in extra:
-        operands += pair
     return pl.pallas_call(
         body,
         in_specs=[VMEM_SPEC] * len(operands),
         out_specs=[VMEM_SPEC] * 5,
-        out_shape=shapes(*((((b - a) * unit, width), jnp.bfloat16) for a, b in ROWS)),
-        cost_estimate=pl.CostEstimate(
-            flops=2 * 512 * 16 * unit * width, bytes_accessed=12 << 20, transcendentals=0
-        ),
-        compiler_params=params(40),
+        out_shape=shapes(*((((b - a) * unit, 4 * D + PAD), jnp.bfloat16) for a, b in ROWS)),
+        cost_estimate=LIGHT,
+        compiler_params=params(12),
     )(*operands)
 
 
@@ -708,7 +700,7 @@
 
 class Reduction:
     def __init__(self, pieces, grid, unit):
-        self.grid, self.unit, self.round, self.due = grid, unit, 0, False
+        self.grid, self.unit, self.round = grid, unit, 0
         self.out, self.kept = list(pieces[:2]), list(pieces[2:])
 
     def state(self):
@@ -759,24 +751,15 @@
     def __init__(self):
         self.active = []
 
-    def run(self, sends, late, compute, values):
+    def run(self, sends, compute=None, values=()):
         for reduction in sends:
             if reduction not in self.active:
                 self.active.append(reduction)
-        waiting = [r for r in self.active if r not in sends and r not in late and r.due]
-        for reduction in sends:
-            reduction.send()
-            reduction.due = True
-        for reduction in late:
-            if reduction.due:
+            if reduction.round:
                 reduction.prepare()
             reduction.send()
-            reduction.due = True
-        for reduction in waiting:
-            if reduction.round < 2:
-                reduction.prepare()
-                reduction.due = False
-        values = compute(values)
+        if compute:
+            values = compute(*values)
         states = [reduction.state() for reduction in self.active]
         states, values = lax.optimization_barrier((states, values))
         for reduction, state in zip(self.active, states):
@@ -858,10 +841,8 @@
         + [pl.BlockSpec(memory_space=pltpu.VMEM)] * 10,
         out_specs=pl.BlockSpec(memory_space=pltpu.VMEM),
         out_shape=jax.ShapeDtypeStruct((32 * tiles, 8, width), jnp.bfloat16),
-        cost_estimate=pl.CostEstimate(
-            flops=0, bytes_accessed=4 * 32 * unit * width, transcendentals=0
-        ),
-        compiler_params=pltpu.CompilerParams(vmem_limit_bytes=40 << 20),
+        cost_estimate=LIGHT,
+        compiler_params=params(22),
     )(rows, *(piece.reshape(-1, 8, width) for piece in pieces))
     return placed.reshape(32 * unit, width)
 
@@ -924,133 +905,142 @@
     return (hidden.astype(jnp.bfloat16)[None], grad[None], *stacked)
 
 
-def gather_first_layer(blocks, grid):
+def gather_first_layer(blocks, grid, attend):
     attention, ffn = (Gathering(block, grid) for block in blocks)
     for moves in (
         (attention,),
         (attention, ffn),
+        (attention,),
         (attention, ffn),
         (attention, ffn),
-        (attention,),
     ):
         for gathering in moves:
             gathering.advance()
         attention.pieces, ffn.pieces = lax.optimization_barrier((attention.pieces, ffn.pieces))
-    first = attention.result()
     ffn.advance()
+    weights = attention.result()
+    attended = attend(weights)
+    ffn.pieces, attended = lax.optimization_barrier((ffn.pieces, attended))
     ffn.advance()
-    return first, ffn.result()
+    return weights, ffn.result(), attended
 
 
 def grid_step(tokens, lengths, shards, cotangent):
     grid, unit = Grid(), shards[0].shape[1]
     order = row_order(unit)
+    hidden = tokens[0].astype(jnp.float32)
 
     second = plain_gather(
         jnp.concatenate([pack_ffn(shards, 1), pack_attention(shards, 1)], axis=1)
     )
-    first = gather_first_layer((pack_attention(shards, 0), pack_ffn(shards, 0)), grid)
-    attention_at = ((first[0], 0, False), (second, 2 * FF, True))
-    ffn_at = ((first[1], 0), (second, 0))
-
-    hidden = tokens[0].astype(jnp.float32)
+
+    def attend(weights):
+        return attention_forward(hidden, lengths, weights, 0, False)
+
+    attention, ffn, attended = gather_first_layer(
+        (pack_attention(shards, 0), pack_ffn(shards, 0)), grid, attend
+    )
+    attention_at = ((attention, 0, False), (second, 2 * FF, True))
+    ffn_at = ((ffn, 0), (second, 0))
+
     kept, left, right = [], [], []
     for layer in range(LAYERS):
-        inputs_low, qkv, mixed, first_sum, gains = attention_forward(
-            hidden, lengths, *attention_at[layer]
-        )
+        if layer:
+            attended = attention_forward(hidden, lengths, *attention_at[layer])
+        inputs_low, qkv, mixed, first_sum, gains = attended
         normed_low, activated, slope, second_sum, hidden = ffn_forward(
             first_sum, gains, *ffn_at[layer]
         )
         kept.append((qkv, first_sum, gains, slope, second_sum))
-        left.append(share_left((inputs_low, mixed, normed_low), order, grid))
+        left.append(share_left((inputs_low, mixed, normed_low), order))
         right.append(both(activated, grid))
 
-    segments = Segments()
-
     def norm_part(layer, grad):
-        qkv, first_sum, gains, slope, second_sum = kept[layer]
-        grad_second, down_low, gain_grad = second_norm_backward(grad, second_sum, gains)
-        return grad_second, down_low, gain_grad, *share_left((down_low,), order, grid)
+        grad_second, down_low, gain_grad = second_norm_backward(
+            grad, kept[layer][4], kept[layer][2]
+        )
+        return grad_second, down_low, gain_grad, share_left((down_low,), order)[0]
 
     def up_part(layer, grad_second, down_low):
         up_low, grad = up_backward_kernel(grad_second, down_low, kept[layer][3], *ffn_at[layer])
         return grad, up_low
 
     def attention_part(layer, grad):
-        qkv, first_sum, gains, slope, second_sum = kept[layer]
-        return attention_backward_kernel(
+        qkv, first_sum, gains = kept[layer][:3]
+        attn_low, grad_qkv, grad, gain_first = attention_backward_kernel(
             grad, first_sum, gains, qkv, lengths, *attention_at[layer]
         )
-
-    def attention_pieces(layer, attn_low, grad_qkv, gain_first, gain_second, extra=()):
+        return grad, grad_qkv, attn_low, gain_first
+
+    def attention_pieces(layer, grad_qkv, attn_low, gain_first, gain_second):
         gains = jnp.concatenate([gain_first, gain_second, jnp.zeros((6, D), jnp.float32)], axis=0)
-        inputs_t, mixed_t, _ = left[layer]
-        (gains_t,) = share_left((gains,), order, grid)
+        inputs_t, mixed_t, gains_t = (
+            traded(pair, grid) for pair in (*left[layer][:2], share_left((gains,), order)[0])
+        )
         return attention_terms(
-            inputs_t, both(grad_qkv, grid), mixed_t, both(attn_low, grid), gains_t, unit, extra
+            inputs_t, both(grad_qkv, grid), mixed_t, both(attn_low, grid), gains_t, unit
         )
 
-    grad_second, down_low, gain_second_1, down_t = norm_part(1, cotangent[0])
-    pieces = matrix_terms(down_t, right[1], unit)
+    def up_product(layer, up_low):
+        return traded(left[layer][2], grid), both(up_low, grid)
+
+    segments = Segments()
+    grad_second, down_low, gain_second, down_t = norm_part(1, cotangent[0])
+    pieces = matrix_terms([(traded(down_t, grid), right[1])], unit)
     grad_second, down_low, pieces = lax.optimization_barrier((grad_second, down_low, pieces))
     down_1 = Reduction(pieces, grid, unit)
 
-    def work(values):
-        grad, up_low = up_part(1, *values)
-        return (grad, matrix_terms(left[1][2], both(up_low, grid), unit))
-
-    grad, pieces = segments.run([down_1], [], work, (grad_second, down_low))
+    def work(grad_second, down_low):
+        return up_part(1, grad_second, down_low)
+
+    grad, up_low = segments.run([down_1], work, (grad_second, down_low))
+
+    def work(grad, up_low):
+        return attention_part(1, grad), matrix_terms([up_product(1, up_low)], unit)
+
+    (grad, *rest), pieces = segments.run([down_1], work, (grad, up_low))
     up_1 = Reduction(pieces, grid, unit)
 
-    def work(values):
-        return attention_part(1, values)
-
-    attn_low, grad_qkv, grad, gain_first = segments.run([up_1], [], work, grad)
-
-    def work(values):
-        return norm_part(0, values)
-
-    grad_second, down_low, gain_second_0, down_t = segments.run([down_1], [], work, grad)
-
-    def work(values):
-        return attention_pieces(
-            1, attn_low, grad_qkv, gain_first, gain_second_1, (down_t, right[0])
-        )
-
-    pieces = segments.run([up_1], [down_1], work, ())
-    joined = Reduction(pieces, grid, unit)
-
-    def work(values):
-        grad, up_low = up_part(0, *values)
-        return (grad, matrix_terms(left[0][2], both(up_low, grid), unit))
-
-    grad, pieces = segments.run([joined], [down_1, up_1], work, (grad_second, down_low))
-    up_0 = Reduction(pieces, grid, unit)
-
-    def work(values):
-        attn_low, grad_qkv, grad, gain_first = attention_part(0, values)
-        return grad, attention_pieces(0, attn_low, grad_qkv, gain_first, gain_second_0)
-
-    grad, pieces = segments.run([], [joined, down_1, up_1], work, grad)
+    def work(grad, *rest):
+        return norm_part(0, grad), attention_pieces(1, *rest, gain_second)
+
+    (grad_second, down_low, gain_second_0, down_t), pieces = segments.run(
+        [up_1, down_1], work, (grad, *rest)
+    )
+    attention_1 = Reduction(pieces, grid, unit)
+
+    def work(grad_second, down_low):
+        return up_part(0, grad_second, down_low)
+
+    grad, up_low = segments.run([up_1, down_1], work, (grad_second, down_low))
+
+    def work(up_low, down_t):
+        return matrix_terms([(traded(down_t, grid), right[0]), up_product(0, up_low)], unit)
+
+    pieces = segments.run([attention_1, down_1, up_1], work, (up_low, down_t))
+    ffn_0 = Reduction(pieces, grid, unit)
+
+    def work(grad):
+        return attention_part(0, grad)
+
+    grad, *rest = segments.run([attention_1, up_1], work, (grad,))
+
+    def work(*rest):
+        return attention_pieces(0, *rest, gain_second_0)
+
+    pieces = segments.run([ffn_0, up_1, attention_1], work, rest)
     attention_0 = Reduction(pieces, grid, unit)
-
-    def nothing(values):
-        return values
-
-    segments.run([up_0], [up_1], nothing, ())
-    segments.run([attention_0], [], nothing, ())
-    segments.run([up_0], [joined], nothing, ())
-    segments.run([attention_0], [joined, up_0], nothing, ())
-    segments.run([], [attention_0, up_0], nothing, ())
-    segments.run([], [attention_0, joined, up_0], nothing, ())
-    segments.run([], [attention_0], nothing, ())
-
-    width = 4 * D + PAD
-    middle, down_0 = joined.result()[:, :width], joined.result()[:, width:]
+    segments.run([ffn_0, attention_1])
+    segments.run([attention_0, attention_1])
+    segments.run([attention_0, ffn_0])
+    segments.run([attention_0, ffn_0])
+    segments.run([attention_0, ffn_0])
+    segments.run([attention_0])
+
+    summed = ffn_0.result()
     outputs = [
-        (attention_outputs(attention_0.result()), (up_0.result(), down_0.T)),
-        (attention_outputs(middle), (up_1.result(), down_1.result().T)),
+        (attention_outputs(attention_0.result()), (summed[:, FF:], summed[:, :FF].T)),
+        (attention_outputs(attention_1.result()), (up_1.result(), down_1.result().T)),
     ]
     return finish(hidden, grad, outputs)
 

time: 434 us -> 399 us (0.919)
  local copies, waits for them, and re-layouts: 42.4 us -> 25.9 us
  Pallas kernels: 85.2 us -> 71.4 us
  other arithmetic: 16.4 us -> 11.4 us
    unnamed x187 -> x99, local copies, waits for them, and re-layouts: 38.1 us -> 20.4 us
  transfers between devices with their start and end apart: 78 -> 78, of which waited for: 31 -> 41; matrix products, arithmetic and copies ran while one was open for 4% -> 3% of each run, Pallas kernels for 15% -> 15%
where the time goes in v4:
time: 399 us; the launch traced here: 395 us
  waiting for transfers between devices  193 us (48%)
  starting transfers between devices  77.3 us (19%)
  Pallas kernels  71.4 us (18%)
  local copies, waits for them, and re-layouts  25.9 us (6%)
  between operations  16.4 us (4%)
  other arithmetic  11.4 us (3%)
    ppermute x77, waiting for transfers between devices, swap(): return lax.ppermute(value, ('dp', 'fsdp'), route)  193 us
    ppermute x77, starting transfers between devices, swap(): return lax.ppermute(value, ('dp', 'fsdp'), route)  77.2 us
    unnamed x99, local copies, waits for them, and re-layouts  20.4 us
    pallas_call x2, Pallas kernels, attention_backward_kernel(): pl.pallas_call(body, in_specs=[SMEM_SPEC] + [VMEM_SPEC] * 4 + [ANY_SPEC],...  18.6 us
    pallas_call x2, Pallas kernels, ffn_forward(): pl.pallas_call(body, grid=(steps,), in_specs=[fixed((tokens, D)), fixed((...  12.9 us
    pallas_call x3, Pallas kernels, matrix_terms(): pl.pallas_call(body, grid=(wide // tile,), in_specs=in_specs, out_specs=[...  10.3 us
    pallas_call x2, Pallas kernels, up_backward_kernel(): pl.pallas_call(body, grid=(steps,), in_specs=[fixed((tokens, D)), fixed((...  9.29 us
    pallas_call x2, Pallas kernels, attention_forward(): pl.pallas_call(body, in_specs=[SMEM_SPEC, VMEM_SPEC, ANY_SPEC], out_specs...  8.12 us
  transfers between devices with their start and end apart: 78, of which 41 were waited for; matrix products, arithmetic and copies ran while one was open for 3% of the time, Pallas kernels for 15%

profile of v4, /device:TPU:0, one launch (start us, length us, event | category | flops | bytes accessed | tf_op | source)
XLA Modules:
  0.0 395.2 jit_solution(7781236995623902084)
XLA Ops:
  14.0 3.1 collective-permute-start
  17.2 3.9 collective-permute-done
  21.1 1.8 collective-permute-start.2
  23.6 8.8 %collective-permute-done.2 = bf16[24,6144]{1,0:T(8,128)(2,1)S(1)} collective-permute-done((bf16[24,6144]{1,0:T(8,128)(2,1)S(1)}, bf16[24,6144]{1,0:T(8,128)(2,1)S(1)}, u32[]{:S(2)}, u32[]{:S(2)}) %collective-permute-start.2) | collective-permute-done | bytes 294944 | tf_op jit(solution)/shard_map/ppermute | solution.py:271
  32.4 1.3 collective-permute-start.3
  33.7 16.0 %collective-permute-done.3 = bf16[48,3200]{1,0:T(8,128)(2,1)S(1)} collective-permute-done((bf16[48,3200]{1,0:T(8,128)(2,1)S(1)}, bf16[48,3200]{1,0:T(8,128)(2,1)S(1)}, u32[]{:S(2)}, u32[]{:S(2)}) %collective-permute-start.3) | collective-permute-done | bytes 307232 | tf_op jit(solution)/shard_map/ppermute | solution.py:271
  49.9 1.6 collective-permute-start.4
  51.4 1.5 collective-permute-start.5
  53.7 20.7 %collective-permute-done.4 = bf16[96,3200]{1,0:T(8,128)(2,1)} collective-permute-done((bf16[96,3200]{1,0:T(8,128)(2,1)S(1)}, bf16[96,3200]{1,0:T(8,128)(2,1)}, u32[]{:S(2)}, u32[]{:S(2)}) %collective-permute-start.4) | collective-permute-done | bytes 614432 | tf_op jit(solution)/shard_map/ppermute | solution.py:271
  74.3 1.3 collective-permute-start.9
  76.6 1.4 collective-permute-start.7
  79.0 1.6 collective-permute-start.8
  80.6 22.7 %collective-permute-done.9 = bf16[48,6144]{1,0:T(8,128)(2,1)S(1)} collective-permute-done((bf16[48,6144]{1,0:T(8,128)(2,1)S(1)}, bf16[48,6144]{1,0:T(8,128)(2,1)S(1)}, u32[]{:S(2)}, u32[]{:S(2)}) %collective-permute-start.9) | collective-permute-done | bytes 589856 | tf_op jit(solution)/shard_map/ppermute | solution.py:271
  103.6 1.4 collective-permute-start.10
  105.0 1.5 collective-permute-start.11
  112.3 2.2 shard_map.259
  114.4 4.1 %shard_map.260 = (bf16[256,768]{1,0:T(8,128)(2,1)S(1)}, bf16[256,2304]{1,0:T(8,128)(2,1)S(1)}, bf16[256,768]{1,0:T(8,128)(2,1)S(1)}, f32[256,768]{1,0:T(8,128)S(1)}, f32[8,768]{1,0:T(8,128)S(1)}) custom-call(s32[1]{0:T(128)S(6)} %copy.44.length_ref, f32[256,768]{1,0:T(8,128)S(1)} %bitcast_convert_fusion.hidden_ref, bf16[768,3200]{1,0:T(8,128)(2,1)S(1)} %bitcast.104), custom_call_target="tpu_custom_call" | custom-call | flops 1048576 | bytes 65536 | tf_op jit(solution)/shard_map/pallas_call | solution.py:442
  118.6 23.4 %collective-permute-done.10 = bf16[96,6144]{1,0:T(8,128)(2,1)S(1)} collective-permute-done((bf16[96,6144]{1,0:T(8,128)(2,1)S(1)}, bf16[96,6144]{1,0:T(8,128)(2,1)S(1)}, u32[]{:S(2)}, u32[]{:S(2)}) %collective-permute-start.10) | collective-permute-done | bytes 1179680 | tf_op jit(solution)/shard_map/ppermute | solution.py:271
  143.3 1.5 collective-permute-start.17
  146.1 11.7 %collective-permute-done.17 = bf16[48,6144]{1,0:T(8,128)(2,1)S(1)} collective-permute-done((bf16[48,6144]{1,0:T(8,128)(2,1)S(1)}, bf16[48,6144]{1,0:T(8,128)(2,1)S(1)}, u32[]{:S(2)}, u32[]{:S(2)}) %collective-permute-start.17) | collective-permute-done | bytes 589856 | tf_op jit(solution)/shard_map/ppermute | solution.py:271
  157.7 1.3 collective-permute-done.18
  159.7 1.3 collective-permute-done.20
  161.0 1.9 shard_map.261
  162.9 6.2 %shard_map.262 = (bf16[256,768]{1,0:T(8,128)(2,1)S(1)}, bf16[256,3072]{1,0:T(8,128)(2,1)S(1)}, bf16[256,3072]{1,0:T(8,128)(2,1)S(1)}, f32[256,768]{1,0:T(8,128)S(1)}, f32[256,768]{1,0:T(8,128)S(1)}) custom-call(f32[256,768]{1,0:T(8,128)S(1)} %get-tuple-element.263.sum_ref, f32[8,768]{1,0:T(8,128)S(1)} %get-tuple-element.264.gain_ref, ...), custom_call_target="tpu_custom_call" | custom-call | flops 1048576 | bytes 65536 | tf_op jit(solution)/shard_map/pallas_call | solution.py:497
  169.2 3.6 copy-done.2
  174.9 5.1 %copy-done = bf16[768,9344]{1,0:T(8,128)(2,1)S(1)} copy-done((bf16[768,9344]{1,0:T(8,128)(2,1)S(1)}, bf16[768,9344]{1,0:T(8,128)(2,1)}, u32[]{:S(2)}) %copy-start) | copy-done | bytes 14352408
  179.9 4.0 %shard_map.263 = (bf16[256,768]{1,0:T(8,128)(2,1)S(1)}, bf16[256,2304]{1,0:T(8,128)(2,1)S(1)}, bf16[256,768]{1,0:T(8,128)(2,1)S(1)}, f32[256,768]{1,0:T(8,128)S(1)}, f32[8,768]{1,0:T(8,128)S(1)}) custom-call(s32[1]{0:T(128)S(6)} %copy.44.length_ref, f32[256,768]{1,0:T(8,128)S(1)} %get-tuple-element.268.hidden_ref, bf16[768,9344]{1,0:T(8,128)(2,1)S(1)} %copy-done), custom_call_target="tpu_custom_call" | custom-call | flops 1048576 | bytes 65536 | tf_op jit(solution)/shard_map/pallas_call | solution.py:442
  185.1 6.6 %shard_map.264 = (bf16[256,768]{1,0:T(8,128)(2,1)S(1)}, bf16[256,3072]{1,0:T(8,128)(2,1)S(1)}, bf16[256,3072]{1,0:T(8,128)(2,1)S(1)}, f32[256,768]{1,0:T(8,128)S(1)}, f32[256,768]{1,0:T(8,128)S(1)}) custom-call(f32[256,768]{1,0:T(8,128)S(1)} %get-tuple-element.269.sum_ref, f32[8,768]{1,0:T(8,128)S(1)} %get-tuple-element.270.gain_ref, ...), custom_call_target="tpu_custom_call" | custom-call | flops 1048576 | bytes 65536 | tf_op jit(solution)/shard_map/pallas_call | solution.py:497
  194.0 1.4 collective-permute-done.24.refs_1_
  195.5 2.4 shard_map.267
  199.9 4.7 %shard_map.268 = (bf16[256,3072]{1,0:T(8,128)(2,1)S(1)}, f32[256,768]{1,0:T(8,128)S(1)}) custom-call(f32[256,768]{1,0:T(8,128)S(1)} %get-tuple-element.288.grad_ref, bf16[256,768]{1,0:T(8,128)(2,1)S(1)} %get-tuple-element.289.refs_0_.low_ref, bf16[256,3072]{1,0:T(8,128)(2,1)S(1)} %get-tuple-element.290.slope_ref, bf16[768,9344]{1,0:T(8,128)(2,1)S(1)} %copy-done.1, ...), custom_call_target="tpu_custom_call" | custom-call | flops 1048576 | bytes 65536 | tf_op jit(solution)/shard_map/pallas_call | solution.py:562
  204.6 2.4 collective-permute-done.26
  212.0 8.8 %shard_map.269 = (bf16[256,768]{1,0:T(8,128)(2,1)S(1)}, bf16[256,2304]{1,0:T(8,128)(2,1)S(1)}, f32[256,768]{1,0:T(8,128)S(1)}, f32[1,768]{1,0:T(1,128)S(1)}) custom-call(s32[1]{0:T(128)S(6)} %copy.44.length_ref, f32[256,768]{1,0:T(8,128)S(1)} %get-tuple-element.298.grad_ref, f32[256,768]{1,0:T(8,128)S(1)} %get-tuple-element.269.sum_ref, ...), custom_call_target="tpu_custom_call" | custom-call | flops 1048576 | bytes 65536 | tf_op jit(solution)/shard_map/pallas_call | solution.py:617
  221.1 2.8 shard_map.271
  226.3 4.4 %collective-permute-start.32 = (bf16[48,3072]{1,0:T(8,128)(2,1)S(1)}, bf16[48,3072]{1,0:T(8,128)(2,1)S(1)}, u32[]{:S(2)}, u32[]{:S(2)}) collective-permute-start(bf16[48,3072]{1,0:T(8,128)(2,1)S(1)} %get-tuple-element.345), channel_id=1, source_target_pairs={{0,2},{1,3},{6,4},{7,5},{8,10},{9,11},{14,12},{15,13},{16,18},{17,... | collective-permute-start | bytes 884744 | tf_op jit(solution)/shard_map/ppermute | solution.py:271
  233.6 1.4 shard_map.275
  235.0 2.4 collective-permute-done.32
  237.5 2.3 collective-permute-done.33
  243.4 4.6 %shard_map.276 = (bf16[256,3072]{1,0:T(8,128)(2,1)S(1)}, f32[256,768]{1,0:T(8,128)S(1)}) custom-call(f32[256,768]{1,0:T(8,128)S(1)} %get-tuple-element.353.grad_ref, bf16[256,768]{1,0:T(8,128)(2,1)S(1)} %get-tuple-element.354.refs_0_.low_ref, bf16[256,3072]{1,0:T(8,128)(2,1)S(1)} %copy-done.5, bf16[768,6144]{1,0:T(8,128)(2,1)S(1)} %bitcast.102, ...), custom_call_target="tpu_custom_call" | custom-call | flops 1048576 | bytes 65536 | tf_op jit(solution)/shard_map/pallas_call | solution.py:562
  247.9 6.9 %collective-permute-done.41 = bf16[96,3072]{1,0:T(8,128)(2,1)S(1)} collective-permute-done((bf16[96,3072]{1,0:T(8,128)(2,1)S(1)}, bf16[96,3072]{1,0:T(8,128)(2,1)S(1)}, u32[]{:S(2)}, u32[]{:S(2)}) %collective-permute-start.41) | collective-permute-done | bytes 589856 | tf_op jit(solution)/shard_map/ppermute | solution.py:271
  259.7 2.2 collective-permute-start.44
  262.1 5.1 %shard_map.278 = (bf16[48,6144]{1,0:T(8,128)(2,1)S(1)}, bf16[48,6144]{1,0:T(8,128)(2,1)S(1)}, bf16[96,6144]{1,0:T(8,128)(2,1)S(1)}, bf16[96,6144]{1,0:T(8,128)(2,1)S(1)}, bf16[96,6144]{1,0:T(8,128)(2,1)S(1)}) custom-call(bf16[384,256]{1,0:T(8,128)(2,1)S(1)} %get-tuple-element.368.refs_0_, bf16[384,256]{1,0:T(8,128)(2,1)S(1)} %collective-permute-done.47.refs_1_, ...), custom_call_target="tpu_custom_call" | custom-call | flops 1048576 | bytes 65536 | tf_op jit(solution)/shard_map/pallas_call | solution.py:662
  267.5 4.0 %collective-permute-done.43 = bf16[24,3072]{1,0:T(8,128)(2,1)S(1)} collective-permute-done((bf16[24,3072]{1,0:T(8,128)(2,1)S(1)}, bf16[24,3072]{1,0:T(8,128)(2,1)S(1)}, u32[]{:S(2)}, u32[]{:S(2)}) %collective-permute-start.43) | collective-permute-done | bytes 147488 | tf_op jit(solution)/shard_map/ppermute | solution.py:271
  273.0 1.4 collective-permute-start.53
  275.8 9.8 %shard_map.279 = (bf16[256,768]{1,0:T(8,128)(2,1)S(1)}, bf16[256,2304]{1,0:T(8,128)(2,1)S(1)}, f32[256,768]{1,0:T(8,128)}, f32[1,768]{1,0:T(1,128)S(1)}) custom-call(s32[1]{0:T(128)S(6)} %copy.44.length_ref, f32[256,768]{1,0:T(8,128)S(1)} %get-tuple-element.390.grad_ref, f32[256,768]{1,0:T(8,128)S(1)} %get-tuple-element.263.sum_ref, ...), custom_call_target="tpu_custom_call" | custom-call | flops 1048576 | bytes 65536 | tf_op jit(solution)/shard_map/pallas_call | solution.py:617
  289.1 1.6 collective-permute-start.57
  290.7 4.5 %collective-permute-start.55 = (bf16[48,3200]{1,0:T(8,128)(2,1)S(1)}, bf16[48,3200]{1,0:T(8,128)(2,1)S(1)}, u32[]{:S(2)}, u32[]{:S(2)}) collective-permute-start(bf16[48,3200]{1,0:T(8,128)(2,1)S(1)} %get-tuple-element.422), channel_id=1, source_target_pairs={{0,2},{1,3},{6,4},{7,5},{8,10},{9,11},{14,12},{15,13},{16,18},{17,... | collective-permute-start | bytes 921608 | tf_op jit(solution)/shard_map/ppermute | solution.py:271
  295.4 1.6 collective-permute-done.61.ob
  297.0 1.4 shard_map.281
  298.4 2.6 collective-permute-done.56
  301.0 3.4 collective-permute-done.57
  311.1 22.9 %collective-permute-done.64 = bf16[96,6144]{1,0:T(8,128)(2,1)S(1)} collective-permute-done((bf16[96,6144]{1,0:T(8,128)(2,1)S(1)}, bf16[96,6144]{1,0:T(8,128)(2,1)S(1)}, u32[]{:S(2)}, u32[]{:S(2)}) %collective-permute-start.64) | collective-permute-done | bytes 1179680 | tf_op jit(solution)/shard_map/ppermute | solution.py:271
  334.0 1.4 collective-permute-done.65
  335.5 2.5 collective-permute-start.66
  339.5 1.7 collective-permute-done.66
  341.7 4.0 %collective-permute-start.69 = (bf16[48,6144]{1,0:T(8,128)(2,1)S(1)}, bf16[48,6144]{1,0:T(8,128)(2,1)S(1)}, u32[]{:S(2)}, u32[]{:S(2)}) collective-permute-start(bf16[48,6144]{1,0:T(8,128)(2,1)S(1)} %get-tuple-element.448), channel_id=1, source_target_pairs={{0,2},{1,3},{6,4},{7,5},{8,10},{9,11},{14,12},{15,13},{16,18},{17,... | collective-permute-start | bytes 1769480 | tf_op jit(solution)/shard_map/ppermute | solution.py:271
  347.1 1.4 collective-permute-start.71
  348.5 6.7 %collective-permute-done.69 = bf16[48,6144]{1,0:T(8,128)(2,1)S(1)} collective-permute-done((bf16[48,6144]{1,0:T(8,128)(2,1)S(1)}, bf16[48,6144]{1,0:T(8,128)(2,1)S(1)}, u32[]{:S(2)}, u32[]{:S(2)}) %collective-permute-start.69) | collective-permute-done | bytes 589856 | tf_op jit(solution)/shard_map/ppermute | solution.py:271
  355.1 3.0 collective-permute-done.70
  360.5 4.8 %collective-permute-start.73 = (bf16[48,3200]{1,0:T(8,128)(2,1)S(1)}, bf16[48,3200]{1,0:T(8,128)(2,1)S(1)}, u32[]{:S(2)}, u32[]{:S(2)}) collective-permute-start(bf16[48,3200]{1,0:T(8,128)(2,1)S(1)} %get-tuple-element.456), channel_id=1, source_target_pairs={{0,2},{1,3},{6,4},{7,5},{8,10},{9,11},{14,12},{15,13},{16,18},{17,... | collective-permute-start | bytes 921608 | tf_op jit(solution)/shard_map/ppermute | solution.py:271
  365.3 5.0 %collective-permute-done.73 = bf16[48,3200]{1,0:T(8,128)(2,1)S(1)} collective-permute-done((bf16[48,3200]{1,0:T(8,128)(2,1)S(1)}, bf16[48,3200]{1,0:T(8,128)(2,1)S(1)}, u32[]{:S(2)}, u32[]{:S(2)}) %collective-permute-start.73) | collective-permute-done | bytes 307232 | tf_op jit(solution)/shard_map/ppermute | solution.py:271
  371.2 2.5 collective-permute-start.74
  374.6 5.5 %collective-permute-done.74 = bf16[24,6144]{1,0:T(8,128)(2,1)} collective-permute-done((bf16[24,6144]{1,0:T(8,128)(2,1)}, bf16[24,6144]{1,0:T(8,128)(2,1)}, u32[]{:S(2)}, u32[]{:S(2)}) %collective-permute-start.74) | collective-permute-done | bytes 294944 | tf_op jit(solution)/shard_map/ppermute | solution.py:271
  380.3 2.5 collective-permute-start.76
  (321 shorter events, 71.1 us)
Async XLA Ops:
  7.2 167.7 %all-gather.2.cloned.1.call-start = ((), (), s32[]{:S(2)}) async-start(), calls=%async_computation | async-start | bytes 14800896 | tf_op jit(solution)/shard_map/all_gather | solution.py:57
  14.0 7.1 %collective-permute-start = (bf16[24,3200]{1,0:T(8,128)(2,1)S(1)}, bf16[24,3200]{1,0:T(8,128)(2,1)S(1)}, u32[]{:S(2)}, u32[]{:S(2)}) collective-permute-start(bf16[24,3200]{1,0:T(8,128)(2,1)S(1)} %constant_dynamic-update-slice_fusion), channel_id=1, source_target_pairs={{0,2},{1,3},{2,0},{3,1},{4,6},{5,7},{6,4},{7,5},{8,10},{9,11},{10,... | collective-permute-start | bytes 460808 | tf_op jit(solution)/shard_map/ppermute | solution.py:271
  21.1 11.3 %collective-permute-start.2 = (bf16[24,6144]{1,0:T(8,128)(2,1)S(1)}, bf16[24,6144]{1,0:T(8,128)(2,1)S(1)}, u32[]{:S(2)}, u32[]{:S(2)}) collective-permute-start(bf16[24,6144]{1,0:T(8,128)(2,1)S(1)} %pad_maximum_fusion.16), channel_id=1, source_target_pairs={{0,2},{1,3},{2,0},{3,1},{4,6},{5,7},{6,4},{7,5},{8,10},{9,11},{10,... | collective-permute-start | bytes 884744 | tf_op jit(solution)/shard_map/ppermute | solution.py:271
  22.9 9.5 %collective-permute-start.1 = (bf16[48,3200]{1,0:T(8,128)(2,1)S(1)}, bf16[48,3200]{1,0:T(8,128)(2,1)S(1)}, u32[]{:S(2)}, u32[]{:S(2)}) collective-permute-start(bf16[48,3200]{1,0:T(8,128)(2,1)S(1)} %pad_maximum_fusion.15), channel_id=1, source_target_pairs={{2,4},{3,5},{4,2},{5,3},{10,12},{11,13},{12,10},{13,11},{18,20},{1... | collective-permute-start | bytes 921608 | tf_op jit(solution)/shard_map/ppermute | solution.py:271
  32.4 17.4 %collective-permute-start.3 = (bf16[48,3200]{1,0:T(8,128)(2,1)S(1)}, bf16[48,3200]{1,0:T(8,128)(2,1)S(1)}, u32[]{:S(2)}, u32[]{:S(2)}) collective-permute-start(bf16[48,3200]{1,0:T(8,128)(2,1)S(1)} %collective-permute-done.1), channel_id=1, source_target_pairs={{2,0},{3,1},{4,6},{5,7},{10,8},{11,9},{12,14},{13,15},{18,16},{19,... | collective-permute-start | bytes 921608 | tf_op jit(solution)/shard_map/ppermute | solution.py:271
  49.9 24.4 %collective-permute-start.4 = (bf16[96,3200]{1,0:T(8,128)(2,1)S(1)}, bf16[96,3200]{1,0:T(8,128)(2,1)}, u32[]{:S(2)}, u32[]{:S(2)}) collective-permute-start(bf16[96,3200]{1,0:T(8,128)(2,1)S(1)} %pad_maximum_fusion.3), channel_id=1, source_target_pairs={{0,16},{1,17},{2,18},{3,19},{4,20},{5,21},{6,22},{7,23},{8,24},{9,... | collective-permute-start | bytes 1843208 | tf_op jit(solution)/shard_map/ppermute | solution.py:271
  51.4 22.9 %collective-permute-start.5 = (bf16[96,3200]{1,0:T(8,128)(2,1)S(1)}, bf16[96,3200]{1,0:T(8,128)(2,1)}, u32[]{:S(2)}, u32[]{:S(2)}) collective-permute-start(bf16[96,3200]{1,0:T(8,128)(2,1)S(1)} %pad_maximum_fusion.3), channel_id=1, source_target_pairs={{0,1},{1,0},{2,3},{3,2},{4,5},{5,4},{6,7},{7,6},{8,9},{9,8},{10,11... | collective-permute-start | bytes 1843208 | tf_op jit(solution)/shard_map/ppermute | solution.py:271
  74.3 29.1 %collective-permute-start.9 = (bf16[48,6144]{1,0:T(8,128)(2,1)S(1)}, bf16[48,6144]{1,0:T(8,128)(2,1)S(1)}, u32[]{:S(2)}, u32[]{:S(2)}) collective-permute-start(bf16[48,6144]{1,0:T(8,128)(2,1)S(1)} %collective-permute-done.6), channel_id=1, source_target_pairs={{2,0},{3,1},{4,6},{5,7},{10,8},{11,9},{12,14},{13,15},{18,16},{19,... | collective-permute-start | bytes 1769480 | tf_op jit(solution)/shard_map/ppermute | solution.py:271
  76.6 27.0 %collective-permute-start.7 = (bf16[48,3200]{1,0:T(8,128)(2,1)S(1)}, bf16[48,3200]{1,0:T(8,128)(2,1)S(1)}, u32[]{:S(2)}, u32[]{:S(2)}) collective-permute-start(bf16[48,3200]{1,0:T(8,128)(2,1)S(1)} %slice.282), channel_id=1, source_target_pairs={{0,16},{1,17},{2,18},{3,19},{4,20},{5,21},{6,22},{7,23},{8,24},{9,... | collective-permute-start | bytes 921608 | tf_op jit(solution)/shard_map/ppermute | solution.py:271
  79.0 24.6 %collective-permute-start.8 = (bf16[48,3200]{1,0:T(8,128)(2,1)S(1)}, bf16[48,3200]{1,0:T(8,128)(2,1)S(1)}, u32[]{:S(2)}, u32[]{:S(2)}) collective-permute-start(bf16[48,3200]{1,0:T(8,128)(2,1)S(1)} %slice.283), channel_id=1, source_target_pairs={{0,1},{1,0},{2,3},{3,2},{4,5},{5,4},{6,7},{7,6},{8,9},{9,8},{10,11... | collective-permute-start | bytes 921608 | tf_op jit(solution)/shard_map/ppermute | solution.py:271
  103.6 38.5 %collective-permute-start.10 = (bf16[96,6144]{1,0:T(8,128)(2,1)S(1)}, bf16[96,6144]{1,0:T(8,128)(2,1)S(1)}, u32[]{:S(2)}, u32[]{:S(2)}) collective-permute-start(bf16[96,6144]{1,0:T(8,128)(2,1)S(1)} %pad_maximum_fusion), channel_id=1, source_target_pairs={{0,16},{1,17},{2,18},{3,19},{4,20},{5,21},{6,22},{7,23},{8,24},{9,... | collective-permute-start | bytes 3538952 | tf_op jit(solution)/shard_map/ppermute | solution.py:271
  105.0 37.2 %collective-permute-start.11 = (bf16[96,6144]{1,0:T(8,128)(2,1)S(1)}, bf16[96,6144]{1,0:T(8,128)(2,1)}, u32[]{:S(2)}, u32[]{:S(2)}) collective-permute-start(bf16[96,6144]{1,0:T(8,128)(2,1)S(1)} %pad_maximum_fusion), channel_id=1, source_target_pairs={{0,1},{1,0},{2,3},{3,2},{4,5},{5,4},{6,7},{7,6},{8,9},{9,8},{10,11... | collective-permute-start | bytes 3538952 | tf_op jit(solution)/shard_map/ppermute | solution.py:271
  143.3 14.4 %collective-permute-start.17 = (bf16[48,6144]{1,0:T(8,128)(2,1)S(1)}, bf16[48,6144]{1,0:T(8,128)(2,1)S(1)}, u32[]{:S(2)}, u32[]{:S(2)}) collective-permute-start(bf16[48,6144]{1,0:T(8,128)(2,1)S(1)} %slice.284), channel_id=1, source_target_pairs={{0,16},{1,17},{2,18},{3,19},{4,20},{5,21},{6,22},{7,23},{8,24},{9,... | collective-permute-start | bytes 1769480 | tf_op jit(solution)/shard_map/ppermute | solution.py:271
  144.9 14.1 %collective-permute-start.18 = (bf16[48,6144]{1,0:T(8,128)(2,1)S(1)}, bf16[48,6144]{1,0:T(8,128)(2,1)S(1)}, u32[]{:S(2)}, u32[]{:S(2)}) collective-permute-start(bf16[48,6144]{1,0:T(8,128)(2,1)S(1)} %slice.285), channel_id=1, source_target_pairs={{0,1},{1,0},{2,3},{3,2},{4,5},{5,4},{6,7},{7,6},{8,9},{9,8},{10,11... | collective-permute-start | bytes 1769480 | tf_op jit(solution)/shard_map/ppermute | solution.py:271
  145.5 15.4 %collective-permute-start.21 = (bf16[96,6144]{1,0:T(8,128)(2,1)S(1)}, bf16[96,6144]{1,0:T(8,128)(2,1)S(1)}, u32[]{:S(2)}, u32[]{:S(2)}) collective-permute-start(bf16[96,6144]{1,0:T(8,128)(2,1)S(1)} %collective-permute-done.10), channel_id=1, source_target_pairs={{0,8},{1,9},{2,10},{3,11},{4,12},{5,13},{6,14},{7,15},{8,0},{9,1},... | collective-permute-start | bytes 3538952 | tf_op jit(solution)/shard_map/ppermute | solution.py:271
  145.5 15.4 %collective-permute-start.22 = (bf16[96,6144]{1,0:T(8,128)(2,1)}, bf16[96,6144]{1,0:T(8,128)(2,1)S(1)}, u32[]{:S(2)}, u32[]{:S(2)}) collective-permute-start(bf16[96,6144]{1,0:T(8,128)(2,1)} %collective-permute-done.11), channel_id=1, source_target_pairs={{0,8},{1,9},{2,10},{3,11},{4,12},{5,13},{6,14},{7,15},{8,0},{9,1},... | collective-permute-start | bytes 3538952 | tf_op jit(solution)/shard_map/ppermute | solution.py:271
  146.1 14.9 %collective-permute-start.23 = (bf16[96,6144]{1,0:T(8,128)(2,1)S(1)}, bf16[96,6144]{1,0:T(8,128)(2,1)S(1)}, u32[]{:S(2)}, u32[]{:S(2)}) collective-permute-start(bf16[96,6144]{1,0:T(8,128)(2,1)S(1)} %pad_maximum_fusion), channel_id=1, source_target_pairs={{0,8},{1,9},{2,10},{3,11},{4,12},{5,13},{6,14},{7,15},{8,0},{9,1},... | collective-permute-start | bytes 3538952 | tf_op jit(solution)/shard_map/ppermute | solution.py:271
  197.9 9.1 %collective-permute-start.26 = (bf16[48,3072]{1,0:T(8,128)(2,1)S(1)}, bf16[48,3072]{1,0:T(8,128)(2,1)S(1)}, u32[]{:S(2)}, u32[]{:S(2)}) collective-permute-start(bf16[48,3072]{1,0:T(8,128)(2,1)S(1)} %get-tuple-element.283), channel_id=1, source_target_pairs={{0,16},{1,17},{2,18},{3,19},{4,20},{5,21},{6,22},{7,23},{8,24},{9,... | collective-permute-start | bytes 884744 | tf_op jit(solution)/shard_map/ppermute | solution.py:271
  199.0 8.8 %collective-permute-start.27 = (bf16[48,3072]{1,0:T(8,128)(2,1)S(1)}, bf16[48,3072]{1,0:T(8,128)(2,1)S(1)}, u32[]{:S(2)}, u32[]{:S(2)}) collective-permute-start(bf16[48,3072]{1,0:T(8,128)(2,1)S(1)} %get-tuple-element.284), channel_id=1, source_target_pairs={{0,1},{1,0},{2,3},{3,2},{4,5},{5,4},{6,7},{7,6},{8,9},{9,8},{10,11... | collective-permute-start | bytes 884744 | tf_op jit(solution)/shard_map/ppermute | solution.py:271
  207.9 16.0 %collective-permute-start.28 = (bf16[96,3072]{1,0:T(8,128)(2,1)S(1)}, bf16[96,3072]{1,0:T(8,128)(2,1)S(1)}, u32[]{:S(2)}, u32[]{:S(2)}) collective-permute-start(bf16[96,3072]{1,0:T(8,128)(2,1)S(1)} %pad_maximum_fusion.9), channel_id=1, source_target_pairs={{0,16},{1,17},{2,18},{3,19},{4,20},{5,21},{6,22},{7,23},{8,24},{9,... | collective-permute-start | bytes 1769480 | tf_op jit(solution)/shard_map/ppermute | solution.py:271
  209.0 12.1 %collective-permute-start.31 = (bf16[256,3072]{1,0:T(8,128)(2,1)S(1)}, bf16[256,3072]{1,0:T(8,128)(2,1)S(1)}, u32[]{:S(2)}, u32[]{:S(2)}) collective-permute-start(bf16[256,3072]{1,0:T(8,128)(2,1)S(1)} %get-tuple-element.309.refs_2_), channel_id=1, source_target_pairs={{0,8},{1,9},{2,10},{3,11},{4,12},{5,13},{6,14},{7,15},{8,0},{9,1},... | collective-permute-start | bytes 4718600 | tf_op jit(solution)/shard_map/ppermute | solution.py:271
  209.2 15.8 %collective-permute-start.29 = (bf16[96,3072]{1,0:T(8,128)(2,1)S(1)}, bf16[96,3072]{1,0:T(8,128)(2,1)S(1)}, u32[]{:S(2)}, u32[]{:S(2)}) collective-permute-start(bf16[96,3072]{1,0:T(8,128)(2,1)S(1)} %pad_maximum_fusion.10), channel_id=1, source_target_pairs={{0,1},{1,0},{2,3},{3,2},{4,5},{5,4},{6,7},{7,6},{8,9},{9,8},{10,11... | collective-permute-start | bytes 1769480 | tf_op jit(solution)/shard_map/ppermute | solution.py:271
  211.3 9.4 %collective-permute-start.30 = (bf16[384,256]{1,0:T(8,128)(2,1)S(1)}, bf16[384,256]{1,0:T(8,128)(2,1)S(1)}, u32[]{:S(2)}, u32[]{:S(2)}) collective-permute-start(bf16[384,256]{1,0:T(8,128)(2,1)S(1)} %get-tuple-element.308), channel_id=1, source_target_pairs={{0,8},{1,9},{2,10},{3,11},{4,12},{5,13},{6,14},{7,15},{8,0},{9,1},... | collective-permute-start | bytes 589832 | tf_op jit(solution)/shard_map/ppermute | solution.py:271
  211.7 14.6 %collective-permute-start.35 = (bf16[384,256]{1,0:T(8,128)(2,1)S(1)}, bf16[384,256]{1,0:T(8,128)(2,1)S(1)}, u32[]{:S(2)}, u32[]{:S(2)}) collective-permute-start(bf16[384,256]{1,0:T(8,128)(2,1)S(1)} %get-tuple-element.331), channel_id=1, source_target_pairs={{0,8},{1,9},{2,10},{3,11},{4,12},{5,13},{6,14},{7,15},{8,0},{9,1},... | collective-permute-start | bytes 589832 | tf_op jit(solution)/shard_map/ppermute | solution.py:271
  220.8 9.9 %collective-permute-start.37 = (bf16[384,256]{1,0:T(8,128)(2,1)S(1)}, bf16[384,256]{1,0:T(8,128)(2,1)S(1)}, u32[]{:S(2)}, u32[]{:S(2)}) collective-permute-start(bf16[384,256]{1,0:T(8,128)(2,1)S(1)} %get-tuple-element.334), channel_id=1, source_target_pairs={{0,8},{1,9},{2,10},{3,11},{4,12},{5,13},{6,14},{7,15},{8,0},{9,1},... | collective-permute-start | bytes 589832 | tf_op jit(solution)/shard_map/ppermute | solution.py:271
  225.0 8.6 %collective-permute-start.36 = (bf16[256,2304]{1,0:T(8,128)(2,1)S(1)}, bf16[256,2304]{1,0:T(8,128)(2,1)S(1)}, u32[]{:S(2)}, u32[]{:S(2)}) collective-permute-start(bf16[256,2304]{1,0:T(8,128)(2,1)S(1)} %get-tuple-element.332.qa), channel_id=1, source_target_pairs={{0,8},{1,9},{2,10},{3,11},{4,12},{5,13},{6,14},{7,15},{8,0},{9,1},... | collective-permute-start | bytes 3538952 | tf_op jit(solution)/shard_map/ppermute | solution.py:271
  225.0 8.5 %collective-permute-start.38 = (bf16[256,768]{1,0:T(8,128)(2,1)S(1)}, bf16[256,768]{1,0:T(8,128)(2,1)S(1)}, u32[]{:S(2)}, u32[]{:S(2)}) collective-permute-start(bf16[256,768]{1,0:T(8,128)(2,1)S(1)} %get-tuple-element.335.oa), channel_id=1, source_target_pairs={{0,8},{1,9},{2,10},{3,11},{4,12},{5,13},{6,14},{7,15},{8,0},{9,1},... | collective-permute-start | bytes 1179656 | tf_op jit(solution)/shard_map/ppermute | solution.py:271
  226.0 5.8 %collective-permute-start.39 = (bf16[384,128]{1,0:T(8,128)(2,1)S(1)}, bf16[384,128]{1,0:T(8,128)(2,1)S(1)}, u32[]{:S(2)}, u32[]{:S(2)}) collective-permute-start(bf16[384,128]{1,0:T(8,128)(2,1)S(1)} %get-tuple-element.339), channel_id=1, source_target_pairs={{0,8},{1,9},{2,10},{3,11},{4,12},{5,13},{6,14},{7,15},{8,0},{9,1},... | collective-permute-start | bytes 294920 | tf_op jit(solution)/shard_map/ppermute | solution.py:271
  226.3 11.1 %collective-permute-start.32 = (bf16[48,3072]{1,0:T(8,128)(2,1)S(1)}, bf16[48,3072]{1,0:T(8,128)(2,1)S(1)}, u32[]{:S(2)}, u32[]{:S(2)}) collective-permute-start(bf16[48,3072]{1,0:T(8,128)(2,1)S(1)} %get-tuple-element.345), channel_id=1, source_target_pairs={{0,2},{1,3},{6,4},{7,5},{8,10},{9,11},{14,12},{15,13},{16,18},{17,... | collective-permute-start | bytes 884744 | tf_op jit(solution)/shard_map/ppermute | solution.py:271
  230.7 9.0 %collective-permute-start.33 = (bf16[48,3072]{1,0:T(8,128)(2,1)S(1)}, bf16[48,3072]{1,0:T(8,128)(2,1)S(1)}, u32[]{:S(2)}, u32[]{:S(2)}) collective-permute-start(bf16[48,3072]{1,0:T(8,128)(2,1)S(1)} %get-tuple-element.318), channel_id=1, source_target_pairs={{0,16},{1,17},{2,18},{3,19},{4,20},{5,21},{6,22},{7,23},{8,24},{9,... | collective-permute-start | bytes 884744 | tf_op jit(solution)/shard_map/ppermute | solution.py:271
  231.8 8.7 %collective-permute-start.34 = (bf16[48,3072]{1,0:T(8,128)(2,1)S(1)}, bf16[48,3072]{1,0:T(8,128)(2,1)S(1)}, u32[]{:S(2)}, u32[]{:S(2)}) collective-permute-start(bf16[48,3072]{1,0:T(8,128)(2,1)S(1)} %get-tuple-element.319), channel_id=1, source_target_pairs={{0,1},{1,0},{2,3},{3,2},{4,5},{5,4},{6,7},{7,6},{8,9},{9,8},{10,11... | collective-permute-start | bytes 884744 | tf_op jit(solution)/shard_map/ppermute | solution.py:271
  233.5 26.1 %collective-permute-start.48 = (bf16[256,3072]{1,0:T(8,128)(2,1)S(1)}, bf16[256,3072]{1,0:T(8,128)(2,1)S(1)}, u32[]{:S(2)}, u32[]{:S(2)}) collective-permute-start(bf16[256,3072]{1,0:T(8,128)(2,1)S(1)} %get-tuple-element.370.refs_2_), channel_id=1, source_target_pairs={{0,8},{1,9},{2,10},{3,11},{4,12},{5,13},{6,14},{7,15},{8,0},{9,1},... | collective-permute-start | bytes 4718600 | tf_op jit(solution)/shard_map/ppermute | solution.py:271
  240.6 14.2 %collective-permute-start.41 = (bf16[96,3072]{1,0:T(8,128)(2,1)S(1)}, bf16[96,3072]{1,0:T(8,128)(2,1)S(1)}, u32[]{:S(2)}, u32[]{:S(2)}) collective-permute-start(bf16[96,3072]{1,0:T(8,128)(2,1)S(1)} %pad_maximum_fusion.11), channel_id=1, source_target_pairs={{0,16},{1,17},{2,18},{3,19},{4,20},{5,21},{6,22},{7,23},{8,24},{9,... | collective-permute-start | bytes 1769480 | tf_op jit(solution)/shard_map/ppermute | solution.py:271
  241.9 13.9 %collective-permute-start.42 = (bf16[96,3072]{1,0:T(8,128)(2,1)S(1)}, bf16[96,3072]{1,0:T(8,128)(2,1)S(1)}, u32[]{:S(2)}, u32[]{:S(2)}) collective-permute-start(bf16[96,3072]{1,0:T(8,128)(2,1)S(1)} %pad_maximum_fusion.12), channel_id=1, source_target_pairs={{0,1},{1,0},{2,3},{3,2},{4,5},{5,4},{6,7},{7,6},{8,9},{9,8},{10,11... | collective-permute-start | bytes 1769480 | tf_op jit(solution)/shard_map/ppermute | solution.py:271
  242.6 5.3 %collective-permute-start.40 = (bf16[48,3072]{1,0:T(8,128)(2,1)S(1)}, bf16[48,3072]{1,0:T(8,128)(2,1)S(1)}, u32[]{:S(2)}, u32[]{:S(2)}) collective-permute-start(bf16[48,3072]{1,0:T(8,128)(2,1)S(1)} %add_convert_fusion.20), channel_id=1, source_target_pairs={{2,4},{3,5},{4,2},{5,3},{10,12},{11,13},{12,10},{13,11},{18,20},{1... | collective-permute-start | bytes 884744 | tf_op jit(solution)/shard_map/ppermute | solution.py:271
  255.8 6.3 %collective-permute-start.50 = (bf16[256,3072]{1,0:T(8,128)(2,1)S(1)}, bf16[256,3072]{1,0:T(8,128)(2,1)S(1)}, u32[]{:S(2)}, u32[]{:S(2)}) collective-permute-start(bf16[256,3072]{1,0:T(8,128)(2,1)S(1)} %get-tuple-element.376.refs_6_), channel_id=1, source_target_pairs={{0,8},{1,9},{2,10},{3,11},{4,12},{5,13},{6,14},{7,15},{8,0},{9,1},... | collective-permute-start | bytes 4718600 | tf_op jit(solution)/shard_map/ppermute | solution.py:271
  257.6 9.6 %collective-permute-start.45 = (bf16[48,3200]{1,0:T(8,128)(2,1)S(1)}, bf16[48,3200]{1,0:T(8,128)(2,1)S(1)}, u32[]{:S(2)}, u32[]{:S(2)}) collective-permute-start(bf16[48,3200]{1,0:T(8,128)(2,1)S(1)} %get-tuple-element.363), channel_id=1, source_target_pairs={{0,16},{1,17},{2,18},{3,19},{4,20},{5,21},{6,22},{7,23},{8,24},{9,... | collective-permute-start | bytes 921608 | tf_op jit(solution)/shard_map/ppermute | solution.py:271
  258.6 9.0 %collective-permute-start.46 = (bf16[48,3200]{1,0:T(8,128)(2,1)S(1)}, bf16[48,3200]{1,0:T(8,128)(2,1)S(1)}, u32[]{:S(2)}, u32[]{:S(2)}) collective-permute-start(bf16[48,3200]{1,0:T(8,128)(2,1)S(1)} %get-tuple-element.364), channel_id=1, source_target_pairs={{0,1},{1,0},{2,3},{3,2},{4,5},{5,4},{6,7},{7,6},{8,9},{9,8},{10,11... | collective-permute-start | bytes 921608 | tf_op jit(solution)/shard_map/ppermute | solution.py:271
  259.7 11.9 %collective-permute-start.44 = (bf16[48,3072]{1,0:T(8,128)(2,1)S(1)}, bf16[48,3072]{1,0:T(8,128)(2,1)S(1)}, u32[]{:S(2)}, u32[]{:S(2)}) collective-permute-start(bf16[48,3072]{1,0:T(8,128)(2,1)S(1)} %get-tuple-element.382), channel_id=1, source_target_pairs={{0,2},{1,3},{6,4},{7,5},{8,10},{9,11},{14,12},{15,13},{16,18},{17,... | collective-permute-start | bytes 884744 | tf_op jit(solution)/shard_map/ppermute | solution.py:271
  262.0 9.5 %collective-permute-start.43 = (bf16[24,3072]{1,0:T(8,128)(2,1)S(1)}, bf16[24,3072]{1,0:T(8,128)(2,1)S(1)}, u32[]{:S(2)}, u32[]{:S(2)}) collective-permute-start(bf16[24,3072]{1,0:T(8,128)(2,1)S(1)} %slice.462), channel_id=1, source_target_pairs={{0,2},{1,3},{2,0},{3,1},{4,6},{5,7},{6,4},{7,5},{8,10},{9,11},{10,... | collective-permute-start | bytes 442376 | tf_op jit(solution)/shard_map/ppermute | solution.py:271
  271.7 15.1 %collective-permute-start.52 = (bf16[96,3200]{1,0:T(8,128)(2,1)S(1)}, bf16[96,3200]{1,0:T(8,128)(2,1)S(1)}, u32[]{:S(2)}, u32[]{:S(2)}) collective-permute-start(bf16[96,3200]{1,0:T(8,128)(2,1)S(1)} %pad_maximum_fusion.4), channel_id=1, source_target_pairs={{0,16},{1,17},{2,18},{3,19},{4,20},{5,21},{6,22},{7,23},{8,24},{9,... | collective-permute-start | bytes 1843208 | tf_op jit(solution)/shard_map/ppermute | solution.py:271
  273.0 14.8 %collective-permute-start.53 = (bf16[96,3200]{1,0:T(8,128)(2,1)S(1)}, bf16[96,3200]{1,0:T(8,128)(2,1)S(1)}, u32[]{:S(2)}, u32[]{:S(2)}) collective-permute-start(bf16[96,3200]{1,0:T(8,128)(2,1)S(1)} %pad_maximum_fusion.5), channel_id=1, source_target_pairs={{0,1},{1,0},{2,3},{3,2},{4,5},{5,4},{6,7},{7,6},{8,9},{9,8},{10,11... | collective-permute-start | bytes 1843208 | tf_op jit(solution)/shard_map/ppermute | solution.py:271
  274.5 11.1 %collective-permute-start.51 = (bf16[48,3072]{1,0:T(8,128)(2,1)S(1)}, bf16[48,3072]{1,0:T(8,128)(2,1)S(1)}, u32[]{:S(2)}, u32[]{:S(2)}) collective-permute-start(bf16[48,3072]{1,0:T(8,128)(2,1)S(1)} %add_convert_fusion.15), channel_id=1, source_target_pairs={{2,4},{3,5},{4,2},{5,3},{10,12},{11,13},{12,10},{13,11},{18,20},{1... | collective-permute-start | bytes 884744 | tf_op jit(solution)/shard_map/ppermute | solution.py:271
  275.2 13.9 %collective-permute-start.58 = (bf16[384,256]{1,0:T(8,128)(2,1)S(1)}, bf16[384,256]{1,0:T(8,128)(2,1)S(1)}, u32[]{:S(2)}, u32[]{:S(2)}) collective-permute-start(bf16[384,256]{1,0:T(8,128)(2,1)S(1)} %get-tuple-element.408), channel_id=1, source_target_pairs={{0,8},{1,9},{2,10},{3,11},{4,12},{5,13},{6,14},{7,15},{8,0},{9,1},... | collective-permute-start | bytes 589832 | tf_op jit(solution)/shard_map/ppermute | solution.py:271
  275.3 15.4 %collective-permute-start.60 = (bf16[384,256]{1,0:T(8,128)(2,1)S(1)}, bf16[384,256]{1,0:T(8,128)(2,1)S(1)}, u32[]{:S(2)}, u32[]{:S(2)}) collective-permute-start(bf16[384,256]{1,0:T(8,128)(2,1)S(1)} %get-tuple-element.411), channel_id=1, source_target_pairs={{0,8},{1,9},{2,10},{3,11},{4,12},{5,13},{6,14},{7,15},{8,0},{9,1},... | collective-permute-start | bytes 589832 | tf_op jit(solution)/shard_map/ppermute | solution.py:271
  285.7 15.4 %collective-permute-start.56 = (bf16[48,6144]{1,0:T(8,128)(2,1)S(1)}, bf16[48,6144]{1,0:T(8,128)(2,1)S(1)}, u32[]{:S(2)}, u32[]{:S(2)}) collective-permute-start(bf16[48,6144]{1,0:T(8,128)(2,1)S(1)} %get-tuple-element.402), channel_id=1, source_target_pairs={{0,16},{1,17},{2,18},{3,19},{4,20},{5,21},{6,22},{7,23},{8,24},{9,... | collective-permute-start | bytes 1769480 | tf_op jit(solution)/shard_map/ppermute | solution.py:271
  287.8 9.2 %collective-permute-start.59 = (bf16[256,2304]{1,0:T(8,128)(2,1)S(1)}, bf16[256,2304]{1,0:T(8,128)(2,1)S(1)}, u32[]{:S(2)}, u32[]{:S(2)}) collective-permute-start(bf16[256,2304]{1,0:T(8,128)(2,1)S(1)} %get-tuple-element.409.qa), channel_id=1, source_target_pairs={{0,8},{1,9},{2,10},{3,11},{4,12},{5,13},{6,14},{7,15},{8,0},{9,1},... | collective-permute-start | bytes 3538952 | tf_op jit(solution)/shard_map/ppermute | solution.py:271
  288.3 6.9 %collective-permute-start.62 = (bf16[384,128]{1,0:T(8,128)(2,1)S(1)}, bf16[384,128]{1,0:T(8,128)(2,1)S(1)}, u32[]{:S(2)}, u32[]{:S(2)}) collective-permute-start(bf16[384,128]{1,0:T(8,128)(2,1)S(1)} %get-tuple-element.416), channel_id=1, source_target_pairs={{0,8},{1,9},{2,10},{3,11},{4,12},{5,13},{6,14},{7,15},{8,0},{9,1},... | collective-permute-start | bytes 294920 | tf_op jit(solution)/shard_map/ppermute | solution.py:271
  289.1 15.3 %collective-permute-start.57 = (bf16[48,6144]{1,0:T(8,128)(2,1)S(1)}, bf16[48,6144]{1,0:T(8,128)(2,1)S(1)}, u32[]{:S(2)}, u32[]{:S(2)}) collective-permute-start(bf16[48,6144]{1,0:T(8,128)(2,1)S(1)} %get-tuple-element.403), channel_id=1, source_target_pairs={{0,1},{1,0},{2,3},{3,2},{4,5},{5,4},{6,7},{7,6},{8,9},{9,8},{10,11... | collective-permute-start | bytes 1769480 | tf_op jit(solution)/shard_map/ppermute | solution.py:271
  290.7 14.1 %collective-permute-start.55 = (bf16[48,3200]{1,0:T(8,128)(2,1)S(1)}, bf16[48,3200]{1,0:T(8,128)(2,1)S(1)}, u32[]{:S(2)}, u32[]{:S(2)}) collective-permute-start(bf16[48,3200]{1,0:T(8,128)(2,1)S(1)} %get-tuple-element.422), channel_id=1, source_target_pairs={{0,2},{1,3},{6,4},{7,5},{8,10},{9,11},{14,12},{15,13},{16,18},{17,... | collective-permute-start | bytes 921608 | tf_op jit(solution)/shard_map/ppermute | solution.py:271
  297.0 7.8 %collective-permute-start.54 = (bf16[24,3072]{1,0:T(8,128)(2,1)S(1)}, bf16[24,3072]{1,0:T(8,128)(2,1)S(1)}, u32[]{:S(2)}, u32[]{:S(2)}) collective-permute-start(bf16[24,3072]{1,0:T(8,128)(2,1)S(1)} %slice.461), channel_id=1, source_target_pairs={{0,2},{1,3},{2,0},{3,1},{4,6},{5,7},{6,4},{7,5},{8,10},{9,11},{10,... | collective-permute-start | bytes 442376 | tf_op jit(solution)/shard_map/ppermute | solution.py:271
  305.1 29.0 %collective-permute-start.64 = (bf16[96,6144]{1,0:T(8,128)(2,1)S(1)}, bf16[96,6144]{1,0:T(8,128)(2,1)S(1)}, u32[]{:S(2)}, u32[]{:S(2)}) collective-permute-start(bf16[96,6144]{1,0:T(8,128)(2,1)S(1)} %pad_maximum_fusion.1), channel_id=1, source_target_pairs={{0,16},{1,17},{2,18},{3,19},{4,20},{5,21},{6,22},{7,23},{8,24},{9,... | collective-permute-start | bytes 3538952 | tf_op jit(solution)/shard_map/ppermute | solution.py:271
  306.4 29.0 %collective-permute-start.65 = (bf16[96,6144]{1,0:T(8,128)(2,1)S(1)}, bf16[96,6144]{1,0:T(8,128)(2,1)S(1)}, u32[]{:S(2)}, u32[]{:S(2)}) collective-permute-start(bf16[96,6144]{1,0:T(8,128)(2,1)S(1)} %pad_maximum_fusion.2), channel_id=1, source_target_pairs={{0,1},{1,0},{2,3},{3,2},{4,5},{5,4},{6,7},{7,6},{8,9},{9,8},{10,11... | collective-permute-start | bytes 3538952 | tf_op jit(solution)/shard_map/ppermute | solution.py:271
  309.2 29.2 %collective-permute-start.67 = (bf16[48,3200]{1,0:T(8,128)(2,1)S(1)}, bf16[48,3200]{1,0:T(8,128)(2,1)S(1)}, u32[]{:S(2)}, u32[]{:S(2)}) collective-permute-start(bf16[48,3200]{1,0:T(8,128)(2,1)S(1)} %get-tuple-element.435), channel_id=1, source_target_pairs={{0,16},{1,17},{2,18},{3,19},{4,20},{5,21},{6,22},{7,23},{8,24},{9,... | collective-permute-start | bytes 921608 | tf_op jit(solution)/shard_map/ppermute | solution.py:271
  310.2 29.3 %collective-permute-start.68 = (bf16[48,3200]{1,0:T(8,128)(2,1)S(1)}, bf16[48,3200]{1,0:T(8,128)(2,1)S(1)}, u32[]{:S(2)}, u32[]{:S(2)}) collective-permute-start(bf16[48,3200]{1,0:T(8,128)(2,1)S(1)} %get-tuple-element.436), channel_id=1, source_target_pairs={{0,1},{1,0},{2,3},{3,2},{4,5},{5,4},{6,7},{7,6},{8,9},{9,8},{10,11... | collective-permute-start | bytes 921608 | tf_op jit(solution)/shard_map/ppermute | solution.py:271
  335.5 5.7 %collective-permute-start.66 = (bf16[24,3200]{1,0:T(8,128)(2,1)S(1)}, bf16[24,3200]{1,0:T(8,128)(2,1)S(1)}, u32[]{:S(2)}, u32[]{:S(2)}) collective-permute-start(bf16[24,3200]{1,0:T(8,128)(2,1)S(1)} %slice.460), channel_id=1, source_target_pairs={{0,2},{1,3},{2,0},{3,1},{4,6},{5,7},{6,4},{7,5},{8,10},{9,11},{10,... | collective-permute-start | bytes 460808 | tf_op jit(solution)/shard_map/ppermute | solution.py:271
  341.7 13.4 %collective-permute-start.69 = (bf16[48,6144]{1,0:T(8,128)(2,1)S(1)}, bf16[48,6144]{1,0:T(8,128)(2,1)S(1)}, u32[]{:S(2)}, u32[]{:S(2)}) collective-permute-start(bf16[48,6144]{1,0:T(8,128)(2,1)S(1)} %get-tuple-element.448), channel_id=1, source_target_pairs={{0,2},{1,3},{6,4},{7,5},{8,10},{9,11},{14,12},{15,13},{16,18},{17,... | collective-permute-start | bytes 1769480 | tf_op jit(solution)/shard_map/ppermute | solution.py:271
  345.8 12.3 %collective-permute-start.70 = (bf16[96,3200]{1,0:T(8,128)(2,1)S(1)}, bf16[96,3200]{1,0:T(8,128)(2,1)S(1)}, u32[]{:S(2)}, u32[]{:S(2)}) collective-permute-start(bf16[96,3200]{1,0:T(8,128)(2,1)S(1)} %pad_maximum_fusion.6), channel_id=1, source_target_pairs={{0,16},{1,17},{2,18},{3,19},{4,20},{5,21},{6,22},{7,23},{8,24},{9,... | collective-permute-start | bytes 1843208 | tf_op jit(solution)/shard_map/ppermute | solution.py:271
  347.1 12.1 %collective-permute-start.71 = (bf16[96,3200]{1,0:T(8,128)(2,1)S(1)}, bf16[96,3200]{1,0:T(8,128)(2,1)S(1)}, u32[]{:S(2)}, u32[]{:S(2)}) collective-permute-start(bf16[96,3200]{1,0:T(8,128)(2,1)S(1)} %pad_maximum_fusion.7), channel_id=1, source_target_pairs={{0,1},{1,0},{2,3},{3,2},{4,5},{5,4},{6,7},{7,6},{8,9},{9,8},{10,11... | collective-permute-start | bytes 1843208 | tf_op jit(solution)/shard_map/ppermute | solution.py:271
  359.4 10.9 %collective-permute-start.72 = (bf16[48,6144]{1,0:T(8,128)(2,1)S(1)}, bf16[48,6144]{1,0:T(8,128)(2,1)S(1)}, u32[]{:S(2)}, u32[]{:S(2)}) collective-permute-start(bf16[48,6144]{1,0:T(8,128)(2,1)S(1)} %add_convert_fusion), channel_id=1, source_target_pairs={{2,4},{3,5},{4,2},{5,3},{10,12},{11,13},{12,10},{13,11},{18,20},{1... | collective-permute-start | bytes 1769480 | tf_op jit(solution)/shard_map/ppermute | solution.py:271
  360.5 9.8 %collective-permute-start.73 = (bf16[48,3200]{1,0:T(8,128)(2,1)S(1)}, bf16[48,3200]{1,0:T(8,128)(2,1)S(1)}, u32[]{:S(2)}, u32[]{:S(2)}) collective-permute-start(bf16[48,3200]{1,0:T(8,128)(2,1)S(1)} %get-tuple-element.456), channel_id=1, source_target_pairs={{0,2},{1,3},{6,4},{7,5},{8,10},{9,11},{14,12},{15,13},{16,18},{17,... | collective-permute-start | bytes 921608 | tf_op jit(solution)/shard_map/ppermute | solution.py:271
  371.2 8.9 %collective-permute-start.74 = (bf16[24,6144]{1,0:T(8,128)(2,1)}, bf16[24,6144]{1,0:T(8,128)(2,1)}, u32[]{:S(2)}, u32[]{:S(2)}) collective-permute-start(bf16[24,6144]{1,0:T(8,128)(2,1)} %slice.458), channel_id=1, source_target_pairs={{0,2},{1,3},{2,0},{3,1},{4,6},{5,7},{6,4},{7,5},{8,10},{9,11},{10,... | collective-permute-start | bytes 884744 | tf_op jit(solution)/shard_map/ppermute | solution.py:271
  373.8 6.4 %collective-permute-start.75 = (bf16[48,3200]{1,0:T(8,128)(2,1)S(1)}, bf16[48,3200]{1,0:T(8,128)(2,1)S(1)}, u32[]{:S(2)}, u32[]{:S(2)}) collective-permute-start(bf16[48,3200]{1,0:T(8,128)(2,1)S(1)} %add_convert_fusion.5), channel_id=1, source_target_pairs={{2,4},{3,5},{4,2},{5,3},{10,12},{11,13},{12,10},{13,11},{18,20},{1... | collective-permute-start | bytes 921608 | tf_op jit(solution)/shard_map/ppermute | solution.py:271
  380.3 5.6 %collective-permute-start.76 = (bf16[24,3200]{1,0:T(8,128)(2,1)S(1)}, bf16[24,3200]{1,0:T(8,128)(2,1)S(1)}, u32[]{:S(2)}, u32[]{:S(2)}) collective-permute-start(bf16[24,3200]{1,0:T(8,128)(2,1)S(1)} %slice.459), channel_id=1, source_target_pairs={{0,2},{1,3},{2,0},{3,1},{4,6},{5,7},{6,4},{7,5},{8,10},{9,11},{10,... | collective-permute-start | bytes 460808 | tf_op jit(solution)/shard_map/ppermute | solution.py:271
  (64 other events, 464.0 us)
Sparse Core Ops, SparseCore 0:
  14.0 136.3 all-gather.1

commit v5 on v4

--- a/solution.py
+++ b/solution.py
@@ -259,32 +259,43 @@
             ]
 
         self.core = route(lambda x, core, z, y: (x, 1 - core, z, y))
-        self.along_x = route(lambda x, core, z, y: (1 - x, core, z, y))
-        self.along_y = route(lambda x, core, z, y: (x, core, z, 1 - y))
+        self.first = route(
+            lambda x, core, z, y: (x, core, z, 1 - y) if core else (1 - x, core, z, y)
+        )
+        self.second = route(
+            lambda x, core, z, y: (1 - x, core, z, y) if core else (x, core, z, 1 - y)
+        )
         self.pair = route(lambda x, core, z, y: (x, core, z ^ 1, y))
         self.middle = route(lambda x, core, z, y: (x, core, 3 - z, y), (1, 2))
         self.outward = route(lambda x, core, z, y: (x, core, z ^ 1, y), (1, 2))
-        self.inward = route(lambda x, core, z, y: (x, core, z ^ 1, y), (0, 3))
+        self.line = [route(lambda x, core, z, y, s=s: (x, core, z ^ s, y)) for s in (1, 2, 3)]
 
 
 def swap(value, route):
     return lax.ppermute(value, ("dp", "fsdp"), route)
 
 
-SLOTS = np.array([(dx, dy, s) for dx, dy in ((1, 1), (1, 0), (0, 1), (0, 0)) for s in range(4)])
+SLOTS = np.array([(far, near, s) for far, near in ((1, 1), (1, 0), (0, 1), (0, 0)) for s in range(4)])
+ROWS = ((0, 2), (2, 4), (4, 8), (8, 12), (12, 16))
+TERM_SLOTS = SLOTS[[0, 1, 4, 5, 2, 3, 10, 11, 6, 7, 8, 9, 12, 13, 14, 15]]
+TERM_ROWS = ((0, 4), (4, 8), (8, 10), (10, 12), (12, 16))
+
+
+def slot_rows(slots, place, x, y, owner):
+    first, second = (jnp.asarray(slots[:, j], jnp.int32) for j in range(2))
+    along_x = jnp.where(owner == 0, first, second)
+    along_y = jnp.where(owner == 0, second, first)
+    return (((x ^ along_x) * 2 + owner) * 4 + place) * 2 + (y ^ along_y)
 
 
 def row_order(unit):
     dp, fsdp = lax.axis_index("dp"), lax.axis_index("fsdp")
     x, core, z, y = dp // 2, dp % 2, fsdp // 2, fsdp % 2
-    dx, dy, s = (jnp.asarray(np.repeat(SLOTS[:, j], unit), jnp.int32) for j in range(3))
+    slots = np.repeat(TERM_SLOTS, unit, axis=0)
+    place = z ^ jnp.asarray(slots[:, 2], jnp.int32)
     offset = jnp.asarray(np.tile(np.arange(unit), 16), jnp.int32)
-    place = jnp.where(s < 2, z ^ s, jnp.where(z < 2, s, 3 - s))
     rows = jnp.concatenate(
-        [
-            ((((x ^ dx) * 2 + owner) * 4 + place) * 2 + (y ^ dy)) * unit + offset
-            for owner in (core, 1 - core)
-        ]
+        [slot_rows(slots, place, x, y, owner) * unit + offset for owner in (core, 1 - core)]
     )
     natural = lax.broadcasted_iota(jnp.int32, (32 * unit, 32 * unit), 0)
     return (natural == rows[None]).astype(jnp.bfloat16)
@@ -295,24 +306,26 @@
     half = D // 2
 
     def body(order_ref, *refs):
-        for j, value_ref in enumerate(refs[: len(values)]):
+        mine, other = refs[len(values) :]
+        start = 0
+        for length, value_ref in zip(lengths, refs):
             ordered = dot(value_ref[...].astype(jnp.bfloat16), order_ref[...])
-            short = lengths[j] - ordered.shape[0]
+            short = length - ordered.shape[0]
             if short:
                 ordered = jnp.concatenate([ordered, jnp.zeros((short, D), jnp.float32)], axis=0)
             turned = ordered.T.astype(jnp.bfloat16)
-            refs[len(values) + 2 * j][...] = turned[:half]
-            refs[len(values) + 2 * j + 1][...] = turned[half:]
-
-    turned = pl.pallas_call(
+            mine[:, start : start + length] = turned[:half]
+            other[:, start : start + length] = turned[half:]
+            start += length
+
+    return pl.pallas_call(
         body,
         in_specs=[VMEM_SPEC] * (1 + len(values)),
-        out_specs=[VMEM_SPEC] * (2 * len(values)),
-        out_shape=shapes(*(((half, n), jnp.bfloat16) for n in lengths for _ in range(2))),
+        out_specs=[VMEM_SPEC] * 2,
+        out_shape=shapes(*[((half, sum(lengths)), jnp.bfloat16)] * 2),
         cost_estimate=LIGHT,
         compiler_params=params(8),
     )(order, *values)
-    return [(turned[2 * j], turned[2 * j + 1]) for j in range(len(values))]
 
 
 def both(value, grid):
@@ -321,9 +334,6 @@
 
 def traded(pair, grid):
     return (pair[0], swap(pair[1], grid.core))
-
-
-ROWS = ((0, 2), (2, 4), (4, 8), (8, 12), (12, 16))
 
 
 def dot(left, right):
@@ -353,12 +363,11 @@
 
 
 def pair_softmax(query_pair, keys, key_block, length):
-    half = keys.shape[0]
-    scores = dot_nt(query_pair, keys) * 0.125
-    position = lax.broadcasted_iota(jnp.int32, scores.shape, 1) + key_block * half
+    scores = dot_nt(keys, query_pair) * 0.125
+    position = lax.broadcasted_iota(jnp.int32, scores.shape, 0) + key_block * keys.shape[0]
     scores = jnp.where(position < length, scores, -1e30)
-    raised = jnp.exp(scores - jnp.max(scores, axis=-1, keepdims=True))
-    return raised / jnp.sum(raised, axis=-1, keepdims=True)
+    raised = jnp.exp(scores - jnp.max(scores, axis=0, keepdims=True))
+    return raised / jnp.sum(raised, axis=0, keepdims=True)
 
 
 def normalised(value):
@@ -432,7 +441,7 @@
             keys = qkv[key_rows, D + lane : D + lane + 128]
             values = qkv[key_rows, 2 * D + lane : 2 * D + lane + 128]
             shares = pair_softmax(query, keys, key_block, length_ref[0]).astype(low)
-            out = dot(shares, values)
+            out = dot_tn(shares, values)
             mixed[rows, lane : lane + 128] = jnp.where(masks[2], out[:half], out[half:]).astype(low)
         copies[3].wait()
         first_sum[...] = hidden_ref[...] + dot(mixed[...], w[:, 3 * D : 4 * D])
@@ -582,45 +591,44 @@
     low = jnp.bfloat16
 
     def body(length_ref, grad_ref, sum_ref, gain_ref, qkv_ref, w_any, *rest):
-        attn_low, grad_qkv, grad_in, gain_out, grad_mixed, w, sems = rest
+        grads, grad_in, gain_out, grad_mixed, w, sems = rest
         copies = attention_columns(w_any, start, w, sems)
         masks = lane_masks()
         result, gain_grad = norm_backward(sum_ref[...], gain_ref[0:1], grad_ref[...])
         grad_in[...] = result
-        attn_low[...] = result.astype(low)
+        grads[:, 3 * D :] = result.astype(low)
         gain_out[...] = gain_grad
         copies[3].wait()
-        grad_mixed[...] = dot_nt(attn_low[...], w[:, 3 * D : 4 * D]).astype(low)
+        grad_mixed[...] = dot_nt(grads[:, 3 * D :], w[:, 3 * D : 4 * D]).astype(low)
         for key_block, rows, key_rows, lane in head_parts(half, swapped):
             query = two_heads(qkv_ref[rows, lane : lane + 128], masks)
             keys = qkv_ref[key_rows, D + lane : D + lane + 128]
             values = qkv_ref[key_rows, 2 * D + lane : 2 * D + lane + 128]
             arriving = two_heads(grad_mixed[rows, lane : lane + 128], masks)
             shares = pair_softmax(query, keys, key_block, length_ref[0])
-            grad_values = dot_tn(shares.astype(low), arriving)
-            grad_shares = dot_nt(arriving, values)
-            inner = jnp.sum(shares * grad_shares, axis=-1, keepdims=True)
+            grad_values = dot(shares.astype(low), arriving)
+            grad_shares = dot_nt(values, arriving)
+            inner = jnp.sum(shares * grad_shares, axis=0, keepdims=True)
             grad_scores = (shares * (grad_shares - inner)).astype(low)
-            grad_query = dot(grad_scores, keys) * 0.125
-            grad_keys = dot_tn(grad_scores, query) * 0.125
-            grad_qkv[rows, lane : lane + 128] = jnp.where(
+            grad_query = dot_tn(grad_scores, keys) * 0.125
+            grad_keys = dot(grad_scores, query) * 0.125
+            grads[rows, lane : lane + 128] = jnp.where(
                 masks[2], grad_query[:half], grad_query[half:]
             ).astype(low)
-            grad_qkv[key_rows, D + lane : D + lane + 128] = grad_keys.astype(low)
-            grad_qkv[key_rows, 2 * D + lane : 2 * D + lane + 128] = grad_values.astype(low)
+            grads[key_rows, D + lane : D + lane + 128] = grad_keys.astype(low)
+            grads[key_rows, 2 * D + lane : 2 * D + lane + 128] = grad_values.astype(low)
         for part in (0, 1, 2):
             copies[part].wait()
             columns = slice(part * D, (part + 1) * D)
-            grad_in[...] += dot_nt(grad_qkv[:, columns], w[:, columns])
+            grad_in[...] += dot_nt(grads[:, columns], w[:, columns])
         copies[4].wait()
 
     return pl.pallas_call(
         body,
         in_specs=[SMEM_SPEC] + [VMEM_SPEC] * 4 + [ANY_SPEC],
-        out_specs=[VMEM_SPEC] * 4,
+        out_specs=[VMEM_SPEC] * 3,
         out_shape=shapes(
-            ((tokens, D), low),
-            ((tokens, 3 * D), low),
+            ((tokens, 4 * D), low),
             ((tokens, D), jnp.float32),
             ((1, D), jnp.float32),
         ),
@@ -636,62 +644,124 @@
 
 def matrix_terms(products, unit):
     tile = D
-    tokens, width = products[0][1][0].shape
+    tokens, width = products[0][2][0].shape
     steps = width // tile
 
     def body(*refs):
-        outs = refs[4 * len(products) :]
+        outs = refs[starts[-1] :]
         for j in range(len(products)):
-            la, lb, ra, rb = refs[4 * j : 4 * j + 4]
-
-            @pl.when(pl.program_id(0) // steps == j)
-            def _(la=la, lb=lb, ra=ra, rb=rb):
-                value = (dot(la[...], ra[...]) + dot(lb[...], rb[...])).astype(jnp.bfloat16)
-                for (low, high), out in zip(ROWS, outs):
-                    out[...] = value[low * unit : high * unit]
-
-    in_specs, operands = [], []
-    for j, (left, right) in enumerate(products):
-        whole = pl.BlockSpec(left[0].shape, lambda i: (0, 0))
+            la, lb, ra, *received = refs[starts[j] : starts[j + 1]]
+            for step in range(steps if len(received) > 1 else 1):
+                rb = received[step]
+                place = pl.program_id(0) - j * steps
+                here = place == step if len(received) > 1 else place // steps == 0
+
+                @pl.when(here)
+                def _(la=la, lb=lb, ra=ra, rb=rb):
+                    value = (dot(la[...], ra[...]) + dot(lb[...], rb[...])).astype(jnp.bfloat16)
+                    for (low, high), out in zip(TERM_ROWS, outs):
+                        out[...] = value[low * unit : high * unit]
+
+    in_specs, operands, starts = [], [], [0]
+    for j, (left, part, right) in enumerate(products):
+        block = pl.BlockSpec((16 * unit, tokens), lambda i, part=part: (0, part))
         column = pl.BlockSpec(
             (tokens, tile), lambda i, j=j: (0, jnp.clip(i - j * steps, 0, steps - 1))
         )
-        in_specs += [whole, whole, column, column]
-        operands += [*left, *right]
+        own, received = right
+        if isinstance(received, list):
+            whole = pl.BlockSpec((tokens, tile), lambda i: (0, 0))
+            in_specs += [block, block, column] + [whole] * steps
+            operands += [*left, own, *received]
+        else:
+            in_specs += [block, block, column, column]
+            operands += [*left, own, received]
+        starts.append(len(operands))
     wide = width * len(products)
     return pl.pallas_call(
         body,
         grid=(wide // tile,),
         in_specs=in_specs,
-        out_specs=[pl.BlockSpec(((b - a) * unit, tile), lambda i: (0, i)) for a, b in ROWS],
-        out_shape=shapes(*((((b - a) * unit, wide), jnp.bfloat16) for a, b in ROWS)),
+        out_specs=[pl.BlockSpec(((b - a) * unit, tile), lambda i: (0, i)) for a, b in TERM_ROWS],
+        out_shape=shapes(*((((b - a) * unit, wide), jnp.bfloat16) for a, b in TERM_ROWS)),
         cost_estimate=LIGHT,
         compiler_params=params(10),
     )(*operands)
 
 
-def attention_terms(inputs_t, grad_qkv, mixed_t, attn_low, gains_t, unit):
-    def body(ia, ib, qa, qb, ma, mb, oa, ob, ga, gb, *outs):
+def attention_terms(left, grads, gains, start, unit):
+    tokens = grads[0].shape[0]
+
+    def body(la, lb, ra, rb, ga, gb, *outs):
         def put(value, column):
             value = value.astype(jnp.bfloat16)
-            for (low, high), out in zip(ROWS, outs):
+            for (low, high), out in zip(TERM_ROWS, outs):
                 out[:, column : column + value.shape[1]] = value[low * unit : high * unit]
 
-        for j in range(3):
+        for j in range(4):
             part = slice(j * D, (j + 1) * D)
-            put(dot(ia[...], qa[:, part]) + dot(ib[...], qb[:, part]), j * D)
-        put(dot(ma[...], oa[...]) + dot(mb[...], ob[...]), 3 * D)
-        put(ga[...].astype(jnp.float32) + gb[...].astype(jnp.float32), 4 * D)
-
-    operands = [*inputs_t, *grad_qkv, *mixed_t, *attn_low, *gains_t]
+            from_left = slice(0, tokens) if j < 3 else slice(tokens, 2 * tokens)
+            put(
+                dot(la[:, from_left], ra[:, part]) + dot(lb[:, from_left], rb[:, part]),
+                j * D,
+            )
+        gain = slice(start, start + PAD)
+        put(ga[:, gain].astype(jnp.float32) + gb[:, gain].astype(jnp.float32), 4 * D)
+
     return pl.pallas_call(
         body,
-        in_specs=[VMEM_SPEC] * len(operands),
+        in_specs=[VMEM_SPEC] * 6,
         out_specs=[VMEM_SPEC] * 5,
-        out_shape=shapes(*((((b - a) * unit, 4 * D + PAD), jnp.bfloat16) for a, b in ROWS)),
+        out_shape=shapes(*((((b - a) * unit, 4 * D + PAD), jnp.bfloat16) for a, b in TERM_ROWS)),
         cost_estimate=LIGHT,
         compiler_params=params(12),
-    )(*operands)
+    )(*left, *grads, *gains)
+
+
+def square_sums(came_first, came_second, later_first, later_second):
+    rows, width = later_first.shape
+
+    def body(one, other, first, second, first_out, second_out):
+        first_out[...] = add(first[...], other[:rows]).astype(jnp.bfloat16)
+        second_out[...] = add(second[...], one[:rows]).astype(jnp.bfloat16)
+
+    return pl.pallas_call(
+        body,
+        in_specs=[VMEM_SPEC] * 4,
+        out_specs=[VMEM_SPEC] * 2,
+        out_shape=shapes(*[((rows, width), jnp.bfloat16)] * 2),
+        cost_estimate=LIGHT,
+        compiler_params=params(8),
+    )(came_first, came_second, later_first, later_second)
+
+
+def line_sums(groups, unit):
+    two = 2 * unit
+    widths = [group[0].shape[1] for group in groups]
+
+    def body(*refs):
+        outs = refs[5 * len(groups) :]
+        start = 0
+        for j, width in enumerate(widths):
+            own, one, other, last_first, last_second = refs[5 * j : 5 * j + 5]
+            columns = slice(start, start + width)
+            near = add(own[:two], one[two:], last_second[...])
+            far = add(own[two:], other[two:], last_first[...])
+            outs[0][:, columns] = near[:unit]
+            outs[1][:, columns] = near[unit:].astype(jnp.bfloat16)
+            outs[2][:, columns] = far[:unit].astype(jnp.bfloat16)
+            outs[3][:, columns] = far[unit:].astype(jnp.bfloat16)
+            start += width
+
+    low = ((unit, sum(widths)), jnp.bfloat16)
+    return pl.pallas_call(
+        body,
+        in_specs=[VMEM_SPEC] * (5 * len(groups)),
+        out_specs=[VMEM_SPEC] * 4,
+        out_shape=shapes(((unit, sum(widths)), jnp.float32), low, low, low),
+        cost_estimate=LIGHT,
+        compiler_params=params(14),
+    )(*(value for group in groups for value in group))
 
 
 def add(*values):
@@ -700,47 +770,37 @@
 
 class Reduction:
     def __init__(self, pieces, grid, unit):
-        self.grid, self.unit, self.round = grid, unit, 0
+        self.grid, self.unit, self.round, self.joined = grid, unit, 0, False
         self.out, self.kept = list(pieces[:2]), list(pieces[2:])
 
-    def state(self):
-        return (self.out, self.kept)
+    def state(self, pending):
+        return ([] if pending else self.out, self.kept)
 
     def restore(self, state):
-        self.out, self.kept = state
+        out, self.kept = state
+        self.out = out or self.out
 
     def send(self):
         grid = self.grid
-        routes = (
-            (grid.along_x, grid.along_y),
-            (grid.along_x, grid.along_y),
-            (grid.inward,),
-            (grid.middle,),
-            (grid.pair,),
-        )[self.round]
+        routes = grid.line if self.round == 2 else (grid.first, grid.second)
         self.out = [swap(value, route) for value, route in zip(self.out, routes)]
         self.round += 1
 
     def prepare(self):
-        low, unit, two = jnp.bfloat16, self.unit, 2 * self.unit
         if self.round == 1:
-            (from_x, from_y), (to_x, to_y, own) = self.out, self.kept
-            to_x = jnp.concatenate([to_x[:two], add(to_x[two:], from_y).astype(low)], axis=0)
-            to_y = jnp.concatenate([add(to_y[:two], from_x).astype(low), to_y[two:]], axis=0)
-            self.out, self.kept = [to_x, to_y], [own]
-        elif self.round == 2:
-            (from_x, from_y), (own,) = self.out, self.kept
-            self.out = [add(own[two:], from_x[two:], from_y[two:]).astype(low)]
-            self.kept = [add(own[:two], from_x[:two], from_y[:two]).astype(low), self.out[0]]
-        elif self.round == 3:
-            near, far = self.kept
-            self.out, self.kept = [add(far, self.out[0]).astype(low)], [near]
-        else:
-            near = add(self.kept[0], self.out[0])
-            self.out, self.kept = [near[unit:].astype(low)], [near[:unit]]
+            later_first, later_second, own = self.kept
+            self.kept = [own, *self.out]
+            self.out = list(square_sums(*self.out, later_first, later_second))
+        elif not self.joined:
+            self.join()
+
+    def join(self, *others):
+        groups = [(*reduction.kept, *reduction.out) for reduction in (self, *others)]
+        own, *self.out = line_sums(groups, self.unit)
+        self.kept, self.joined = [own], True
 
     def result(self):
-        return add(self.kept[0], self.out[0])
+        return add(self.kept[0], *self.out)
 
 
 def gate(values, *earlier):
@@ -751,7 +811,11 @@
     def __init__(self):
         self.active = []
 
-    def run(self, sends, compute=None, values=()):
+    def join(self, reduction, *others):
+        reduction.join(*others)
+        self.active = [r for r in self.active if r not in others]
+
+    def run(self, sends, compute=None, values=(), pending=()):
         for reduction in sends:
             if reduction not in self.active:
                 self.active.append(reduction)
@@ -760,11 +824,11 @@
             reduction.send()
         if compute:
             values = compute(*values)
-        states = [reduction.state() for reduction in self.active]
+        states = [reduction.state(reduction in pending) for reduction in self.active]
         states, values = lax.optimization_barrier((states, values))
         for reduction, state in zip(self.active, states):
             reduction.restore(state)
-        self.active = [r for r in self.active if r.round < 5]
+        self.active = [r for r in self.active if r.round < 3 or r in pending]
         return values
 
 
@@ -796,18 +860,13 @@
     @staticmethod
     def square(pieces, grid, two):
         (line,) = pieces
-        return (line, swap(line, grid.along_x), swap(line, grid.along_y))
+        return (line, swap(line, grid.first), swap(line, grid.second))
 
     @staticmethod
     def diagonal(pieces, grid, two):
-        line, from_x, from_y = pieces
-        return (
-            swap(from_y[:two], grid.along_x),
-            swap(from_x[two:], grid.along_y),
-            from_x,
-            from_y,
-            line,
-        )
+        line, one, other = pieces
+        late = swap(one[two:], grid.second)
+        return (swap(other[:two], grid.first), late, one, other, line)
 
     def result(self):
         pieces = self.pieces
@@ -818,12 +877,9 @@
     width = pieces[0].shape[1]
     dp, fsdp = lax.axis_index("dp"), lax.axis_index("fsdp")
     x, core, z, y = dp // 2, dp % 2, fsdp // 2, fsdp % 2
-    dx, dy, s = (jnp.asarray(SLOTS[:, j], jnp.int32) for j in range(3))
+    s = jnp.asarray(SLOTS[:, 2], jnp.int32)
     place = jnp.where(s < 2, z ^ s, jnp.where(z < 2, s, 3 - s))
-    rows = jnp.concatenate(
-        [(((x ^ dx) * 2 + owner) * 4 + place) * 2 + (y ^ dy) for owner in (core, 1 - core)]
-    )
-
+    rows = jnp.concatenate([slot_rows(SLOTS, place, x, y, owner) for owner in (core, 1 - core)])
     tiles = unit // 8
 
     def body(rows_ref, *refs):
@@ -905,24 +961,40 @@
     return (hidden.astype(jnp.bfloat16)[None], grad[None], *stacked)
 
 
-def gather_first_layer(blocks, grid, attend):
+def gather_first_layer(blocks, second, order, grid, attend):
     attention, ffn = (Gathering(block, grid) for block in blocks)
-    for moves in (
-        (attention,),
-        (attention, ffn),
-        (attention,),
-        (attention, ffn),
-        (attention, ffn),
-    ):
-        for gathering in moves:
-            gathering.advance()
-        attention.pieces, ffn.pieces = lax.optimization_barrier((attention.pieces, ffn.pieces))
+
+    def hold(*gatherings):
+        pieces = [g.pieces[:2] if len(g.pieces) == 3 else g.pieces for g in gatherings]
+        pieces = lax.optimization_barrier(pieces)
+        for g, held in zip(gatherings, pieces):
+            g.pieces = [*held, *g.pieces[len(held) :]]
+
+    attention.advance()
+    hold(attention)
+    ffn.pieces = gate(ffn.pieces, attention.pieces)
+    attention.advance()
     ffn.advance()
+    hold(attention, ffn)
+    attention.advance()
+    ffn.advance()
+    order, ffn.pieces = lax.optimization_barrier((order, ffn.pieces))
+    hold(attention, ffn)
+    attention.advance()
+    ffn.advance()
+    hold(attention, ffn)
+    attention.advance()
+    ffn.pieces = gate(ffn.pieces, attention.pieces[1])
+    ffn.advance()
+    hold(attention)
     weights = attention.result()
     attended = attend(weights)
-    ffn.pieces, attended = lax.optimization_barrier((ffn.pieces, attended))
+    held, attended = lax.optimization_barrier((ffn.pieces[:2], attended))
+    ffn.pieces = [*held, *ffn.pieces[2:]]
     ffn.advance()
-    return weights, ffn.result(), attended
+    pieces, second = lax.optimization_barrier((ffn.pieces, second))
+    ffn.pieces = list(pieces)
+    return weights, ffn.result(), second, order, attended
 
 
 def grid_step(tokens, lengths, shards, cotangent):
@@ -937,8 +1009,8 @@
     def attend(weights):
         return attention_forward(hidden, lengths, weights, 0, False)
 
-    attention, ffn, attended = gather_first_layer(
-        (pack_attention(shards, 0), pack_ffn(shards, 0)), grid, attend
+    attention, ffn, second, order, attended = gather_first_layer(
+        (pack_attention(shards, 0), pack_ffn(shards, 0)), second, order, grid, attend
     )
     attention_at = ((attention, 0, False), (second, 2 * FF, True))
     ffn_at = ((ffn, 0), (second, 0))
@@ -952,14 +1024,11 @@
             first_sum, gains, *ffn_at[layer]
         )
         kept.append((qkv, first_sum, gains, slope, second_sum))
-        left.append(share_left((inputs_low, mixed, normed_low), order))
+        left.append(traded(share_left((inputs_low, mixed, normed_low), order), grid))
         right.append(both(activated, grid))
 
     def norm_part(layer, grad):
-        grad_second, down_low, gain_grad = second_norm_backward(
-            grad, kept[layer][4], kept[layer][2]
-        )
-        return grad_second, down_low, gain_grad, share_left((down_low,), order)[0]
+        return second_norm_backward(grad, kept[layer][4], kept[layer][2])
 
     def up_part(layer, grad_second, down_low):
         up_low, grad = up_backward_kernel(grad_second, down_low, kept[layer][3], *ffn_at[layer])
@@ -967,80 +1036,74 @@
 
     def attention_part(layer, grad):
         qkv, first_sum, gains = kept[layer][:3]
-        attn_low, grad_qkv, grad, gain_first = attention_backward_kernel(
+        return attention_backward_kernel(
             grad, first_sum, gains, qkv, lengths, *attention_at[layer]
         )
-        return grad, grad_qkv, attn_low, gain_first
-
-    def attention_pieces(layer, grad_qkv, attn_low, gain_first, gain_second):
-        gains = jnp.concatenate([gain_first, gain_second, jnp.zeros((6, D), jnp.float32)], axis=0)
-        inputs_t, mixed_t, gains_t = (
-            traded(pair, grid) for pair in (*left[layer][:2], share_left((gains,), order)[0])
-        )
-        return attention_terms(
-            inputs_t, both(grad_qkv, grid), mixed_t, both(attn_low, grid), gains_t, unit
-        )
+
+    def gain_rows(first, second):
+        return jnp.concatenate([first, second, jnp.zeros((6, D), jnp.float32)], axis=0)
 
     def up_product(layer, up_low):
-        return traded(left[layer][2], grid), both(up_low, grid)
+        return left[layer], 2, both(up_low, grid)
+
+    def up_product_in_tiles(layer, up_low):
+        received = [swap(up_low[:, j : j + D], grid.core) for j in range(0, FF, D)]
+        return left[layer], 2, (up_low, received)
 
     segments = Segments()
-    grad_second, down_low, gain_second, down_t = norm_part(1, cotangent[0])
-    pieces = matrix_terms([(traded(down_t, grid), right[1])], unit)
+    grad_second, down_low, gain_second = norm_part(1, cotangent[0])
+    down_t = traded(share_left((down_low,), order), grid)
+    pieces = matrix_terms([(down_t, 0, right[1])], unit)
     grad_second, down_low, pieces = lax.optimization_barrier((grad_second, down_low, pieces))
     down_1 = Reduction(pieces, grid, unit)
 
     def work(grad_second, down_low):
-        return up_part(1, grad_second, down_low)
-
-    grad, up_low = segments.run([down_1], work, (grad_second, down_low))
-
-    def work(grad, up_low):
-        return attention_part(1, grad), matrix_terms([up_product(1, up_low)], unit)
-
-    (grad, *rest), pieces = segments.run([down_1], work, (grad, up_low))
+        grad, up_low = up_part(1, grad_second, down_low)
+        pieces = matrix_terms([up_product_in_tiles(1, up_low)], unit)
+        return attention_part(1, grad), pieces
+
+    (grads, grad, gain_first), pieces = segments.run([down_1], work, (grad_second, down_low))
     up_1 = Reduction(pieces, grid, unit)
-
-    def work(grad, *rest):
-        return norm_part(0, grad), attention_pieces(1, *rest, gain_second)
-
-    (grad_second, down_low, gain_second_0, down_t), pieces = segments.run(
-        [up_1, down_1], work, (grad, *rest)
+    gains_1 = gain_rows(gain_first, gain_second)
+
+    def work(grad, grads, gains):
+        grads = both(grads, grid)
+        grad_second, down_low, gain_second = norm_part(0, grad)
+        shared = traded(share_left((down_low, gains), order), grid)
+        grad, up_low = up_part(0, grad_second, down_low)
+        pieces = attention_terms(left[1], grads, shared, grads[0].shape[0], unit)
+        return grad, up_low, gain_second, shared, pieces
+
+    grad, up_low, gain_second, shared, pieces = segments.run(
+        [up_1, down_1], work, (grad, grads, gains_1)
     )
     attention_1 = Reduction(pieces, grid, unit)
 
-    def work(grad_second, down_low):
-        return up_part(0, grad_second, down_low)
-
-    grad, up_low = segments.run([up_1, down_1], work, (grad_second, down_low))
-
-    def work(up_low, down_t):
-        return matrix_terms([(traded(down_t, grid), right[0]), up_product(0, up_low)], unit)
-
-    pieces = segments.run([attention_1, down_1, up_1], work, (up_low, down_t))
+    def work(grad, up_low, shared):
+        pieces = matrix_terms([(shared, 0, right[0]), up_product(0, up_low)], unit)
+        return attention_part(0, grad), pieces
+
+    (grads, grad, gain_first), pieces = segments.run(
+        [attention_1, up_1], work, (grad, up_low, shared)
+    )
     ffn_0 = Reduction(pieces, grid, unit)
 
-    def work(grad):
-        return attention_part(0, grad)
-
-    grad, *rest = segments.run([attention_1, up_1], work, (grad,))
-
-    def work(*rest):
-        return attention_pieces(0, *rest, gain_second_0)
-
-    pieces = segments.run([ffn_0, up_1, attention_1], work, rest)
+    def work(grads, gain_first):
+        gains = traded(share_left((gain_rows(gain_first, gain_second),), order), grid)
+        return attention_terms(left[0], both(grads, grid), gains, 0, unit)
+
+    segments.join(down_1, up_1)
+    pieces = segments.run([ffn_0, attention_1, down_1], work, (grads, gain_first))
     attention_0 = Reduction(pieces, grid, unit)
-    segments.run([ffn_0, attention_1])
-    segments.run([attention_0, attention_1])
-    segments.run([attention_0, ffn_0])
-    segments.run([attention_0, ffn_0])
-    segments.run([attention_0, ffn_0])
+    segments.run([ffn_0, attention_0, attention_1], pending=[attention_0])
+    segments.run([ffn_0], pending=[ffn_0])
+    segments.run([attention_0], pending=[ffn_0])
     segments.run([attention_0])
 
-    summed = ffn_0.result()
+    summed_0, summed_1 = ffn_0.result(), down_1.result()
     outputs = [
-        (attention_outputs(attention_0.result()), (summed[:, FF:], summed[:, :FF].T)),
-        (attention_outputs(attention_1.result()), (up_1.result(), down_1.result().T)),
+        (attention_outputs(attention.result()), (summed[:, FF:], summed[:, :FF].T))
+        for attention, summed in ((attention_0, summed_0), (attention_1, summed_1))
     ]
     return finish(hidden, grad, outputs)
 

time: 399 us -> 381 us (0.955)
  local copies, waits for them, and re-layouts: 25.9 us -> 17 us
  starting transfers between devices: 77.3 us -> 71.4 us
  waiting for transfers between devices: 193 us -> 189 us
    unnamed x99 -> x89, local copies, waits for them, and re-layouts: 20.4 us -> 11.4 us
    ppermute x77 -> x70, starting transfers between devices: 77.2 us -> 71.4 us  [swap(): return lax.ppermute(value, ('dp', 'fsdp'), route)]
    ppermute x77 -> x70, waiting for transfers between devices: 193 us -> 189 us  [swap(): return lax.ppermute(value, ('dp', 'fsdp'), route)]
  transfers between devices with their start and end apart: 78 -> 71, of which waited for: 41 -> 27; matrix products, arithmetic and copies ran while one was open for 3% -> 2% of each run, Pallas kernels for 15% -> 14%
where the time goes in v5:
time: 381 us; the launch traced here: 377 us
  waiting for transfers between devices  189 us (50%)
  Pallas kernels  74.5 us (20%)
  starting transfers between devices  71.4 us (19%)
  local copies, waits for them, and re-layouts  17 us (4%)
  between operations  15.9 us (4%)
  other arithmetic  8.93 us (2%)
    ppermute x70, waiting for transfers between devices, swap(): return lax.ppermute(value, ('dp', 'fsdp'), route)  189 us
    ppermute x70, starting transfers between devices, swap(): return lax.ppermute(value, ('dp', 'fsdp'), route)  71.4 us
    pallas_call x2, Pallas kernels, attention_backward_kernel(): pl.pallas_call(body, in_specs=[SMEM_SPEC] + [VMEM_SPEC] * 4 + [ANY_SPEC],...  15.3 us
    pallas_call x2, Pallas kernels, ffn_forward(): pl.pallas_call(body, grid=(steps,), in_specs=[fixed((tokens, D)), fixed((...  13.5 us
    pallas_call x3, Pallas kernels, matrix_terms(): pl.pallas_call(body, grid=(wide // tile,), in_specs=in_specs, out_specs=[...  11.9 us
    unnamed x89, local copies, waits for them, and re-layouts  11.4 us
    pallas_call x2, Pallas kernels, up_backward_kernel(): pl.pallas_call(body, grid=(steps,), in_specs=[fixed((tokens, D)), fixed((...  9.38 us
    pallas_call x2, Pallas kernels, attention_forward(): pl.pallas_call(body, in_specs=[SMEM_SPEC, VMEM_SPEC, ANY_SPEC], out_specs...  7.83 us
  transfers between devices with their start and end apart: 71, of which 27 were waited for; matrix products, arithmetic and copies ran while one was open for 2% of the time, Pallas kernels for 14%

profile of v5, /device:TPU:0, one launch (start us, length us, event | category | flops | bytes accessed | tf_op | source)
XLA Modules:
  0.0 376.7 jit_solution(8130661230414982249)
XLA Ops:
  14.1 3.1 collective-permute-start
  17.3 3.9 %collective-permute-done = bf16[24,3200]{1,0:T(8,128)(2,1)S(1)} collective-permute-done((bf16[24,3200]{1,0:T(8,128)(2,1)S(1)}, bf16[24,3200]{1,0:T(8,128)(2,1)S(1)}, u32[]{:S(2)}, u32[]{:S(2)}) %collective-permute-start) | collective-permute-done | bytes 153632 | tf_op jit(solution)/shard_map/ppermute | solution.py:275
  21.2 1.8 collective-permute-start.2
  23.7 8.7 %collective-permute-done.2 = bf16[24,6144]{1,0:T(8,128)(2,1)S(1)} collective-permute-done((bf16[24,6144]{1,0:T(8,128)(2,1)S(1)}, bf16[24,6144]{1,0:T(8,128)(2,1)S(1)}, u32[]{:S(2)}, u32[]{:S(2)}) %collective-permute-start.2) | collective-permute-done | bytes 294944 | tf_op jit(solution)/shard_map/ppermute | solution.py:275
  32.5 1.3 collective-permute-start.3
  35.0 14.9 %collective-permute-done.3 = bf16[48,3200]{1,0:T(8,128)(2,1)S(1)} collective-permute-done((bf16[48,3200]{1,0:T(8,128)(2,1)S(1)}, bf16[48,3200]{1,0:T(8,128)(2,1)S(1)}, u32[]{:S(2)}, u32[]{:S(2)}) %collective-permute-start.3) | collective-permute-done | bytes 307232 | tf_op jit(solution)/shard_map/ppermute | solution.py:275
  50.0 1.4 collective-permute-start.6
  51.5 1.6 collective-permute-start.5
  53.0 1.5 collective-permute-start.9
  54.5 33.1 %collective-permute-done.6 = bf16[48,6144]{1,0:T(8,128)(2,1)S(1)} collective-permute-done((bf16[48,6144]{1,0:T(8,128)(2,1)S(1)}, bf16[48,6144]{1,0:T(8,128)(2,1)S(1)}, u32[]{:S(2)}, u32[]{:S(2)}) %collective-permute-start.6) | collective-permute-done | bytes 589856 | tf_op jit(solution)/shard_map/ppermute | solution.py:275
  90.6 1.9 collective-permute-start.10
  92.5 13.3 %collective-permute-done.7 = bf16[48,3200]{1,0:T(8,128)(2,1)S(1)} collective-permute-done((bf16[48,3200]{1,0:T(8,128)(2,1)S(1)}, bf16[48,3200]{1,0:T(8,128)(2,1)S(1)}, u32[]{:S(2)}, u32[]{:S(2)}) %collective-permute-start.7) | collective-permute-done | bytes 307232 | tf_op jit(solution)/shard_map/ppermute | solution.py:275
  106.7 1.4 collective-permute-start.16
  114.1 2.2 shard_map.313
  116.3 4.0 %shard_map.314 = (bf16[256,768]{1,0:T(8,128)(2,1)S(1)}, bf16[256,2304]{1,0:T(8,128)(2,1)S(1)}, bf16[256,768]{1,0:T(8,128)(2,1)S(1)}, f32[256,768]{1,0:T(8,128)S(1)}, f32[8,768]{1,0:T(8,128)S(1)}) custom-call(s32[1]{0:T(128)S(6)} %copy.50.length_ref, f32[256,768]{1,0:T(8,128)S(1)} %bitcast_convert_fusion.hidden_ref, bf16[768,3200]{1,0:T(8,128)(2,1)S(1)} %bitcast.104), custom_call_target="tpu_custom_call" | custom-call | flops 1048576 | bytes 65536 | tf_op jit(solution)/shard_map/pallas_call | solution.py:451
  122.8 22.1 %collective-permute-done.8 = bf16[96,6144]{1,0:T(8,128)(2,1)} collective-permute-done((bf16[96,6144]{1,0:T(8,128)(2,1)S(1)}, bf16[96,6144]{1,0:T(8,128)(2,1)}, u32[]{:S(2)}, u32[]{:S(2)}) %collective-permute-start.8) | collective-permute-done | bytes 1179680 | tf_op jit(solution)/shard_map/ppermute | solution.py:275
  147.0 1.8 collective-permute-start.17
  150.3 11.2 %collective-permute-done.17 = bf16[48,6144]{1,0:T(8,128)(2,1)} collective-permute-done((bf16[48,6144]{1,0:T(8,128)(2,1)S(1)}, bf16[48,6144]{1,0:T(8,128)(2,1)}, u32[]{:S(2)}, u32[]{:S(2)}) %collective-permute-start.17) | collective-permute-done | bytes 589856 | tf_op jit(solution)/shard_map/ppermute | solution.py:275
  162.5 6.2 %collective-permute-done.19 = bf16[48,6144]{1,0:T(8,128)(2,1)S(1)} collective-permute-done((bf16[48,6144]{1,0:T(8,128)(2,1)}, bf16[48,6144]{1,0:T(8,128)(2,1)S(1)}, u32[]{:S(2)}, u32[]{:S(2)}) %collective-permute-start.19) | collective-permute-done | bytes 589856 | tf_op jit(solution)/shard_map/ppermute | solution.py:275
  169.6 2.8 shard_map.315
  172.4 6.9 %shard_map.316 = (bf16[256,768]{1,0:T(8,128)(2,1)S(1)}, bf16[256,3072]{1,0:T(8,128)(2,1)}, bf16[256,3072]{1,0:T(8,128)(2,1)S(1)}, f32[256,768]{1,0:T(8,128)S(1)}, f32[256,768]{1,0:T(8,128)S(1)}) custom-call(f32[256,768]{1,0:T(8,128)S(1)} %get-tuple-element.275.sum_ref, f32[8,768]{1,0:T(8,128)S(1)} %copy-done.17, bf16[768,6144]{1,0:T(8,128)(2,1)S(1)} %bitcast.100, ...), custom_call_target="tpu_custom_call" | custom-call | flops 1048576 | bytes 65536 | tf_op jit(solution)/shard_map/pallas_call | solution.py:506
  179.3 3.8 %shard_map.317 = (bf16[256,768]{1,0:T(8,128)(2,1)S(1)}, bf16[256,2304]{1,0:T(8,128)(2,1)S(1)}, bf16[256,768]{1,0:T(8,128)(2,1)S(1)}, f32[256,768]{1,0:T(8,128)S(1)}, f32[8,768]{1,0:T(8,128)S(1)}) custom-call(s32[1]{0:T(128)S(6)} %copy.50.length_ref, f32[256,768]{1,0:T(8,128)S(1)} %get-tuple-element.284.hidden_ref, bf16[768,9344]{1,0:T(8,128)(2,1)S(1)} %bitcast.99), custom_call_target="tpu_custom_call" | custom-call | flops 1048576 | bytes 65536 | tf_op jit(solution)/shard_map/pallas_call | solution.py:451
  183.2 6.6 %shard_map.318 = (bf16[256,768]{1,0:T(8,128)(2,1)S(1)}, bf16[256,3072]{1,0:T(8,128)(2,1)S(1)}, bf16[256,3072]{1,0:T(8,128)(2,1)S(1)}, f32[256,768]{1,0:T(8,128)S(1)}, f32[256,768]{1,0:T(8,128)S(1)}) custom-call(f32[256,768]{1,0:T(8,128)S(1)} %get-tuple-element.286.sum_ref, f32[8,768]{1,0:T(8,128)S(1)} %get-tuple-element.287.gain_ref, ...), custom_call_target="tpu_custom_call" | custom-call | flops 1048576 | bytes 65536 | tf_op jit(solution)/shard_map/pallas_call | solution.py:506
  193.6 2.4 shard_map.321
  196.1 4.8 %shard_map.322 = (bf16[256,3072]{1,0:T(8,128)(2,1)S(1)}, f32[256,768]{1,0:T(8,128)S(1)}) custom-call(f32[256,768]{1,0:T(8,128)S(1)} %get-tuple-element.306.grad_ref, bf16[256,768]{1,0:T(8,128)(2,1)S(1)} %get-tuple-element.307.refs_0_.low_ref, bf16[256,3072]{1,0:T(8,128)(2,1)S(1)} %get-tuple-element.308.slope_ref, bf16[768,9344]{1,0:T(8,128)(2,1)S(1)} %bitcast.99, ...), custom_call_target="tpu_custom_call" | custom-call | flops 1048576 | bytes 65536 | tf_op jit(solution)/shard_map/pallas_call | solution.py:571
  201.8 1.8 collective-permute-start.27
  204.1 7.2 %shard_map.323 = (bf16[256,3072]{1,0:T(8,128)(2,1)S(1)}, f32[256,768]{1,0:T(8,128)S(1)}, f32[1,768]{1,0:T(1,128)S(1)}) custom-call(s32[1]{0:T(128)S(6)} %copy.50.length_ref, f32[256,768]{1,0:T(8,128)S(1)} %get-tuple-element.309.grad_ref, f32[256,768]{1,0:T(8,128)S(1)} %get-tuple-element.286.sum_ref, f32[8,768]{1,0:T(8,128)S(1)} %get-tuple-element.287.gain_ref, ...), custom_call_target="tpu_custom_call" | custom-call | flops 1048576 | bytes 65536 | tf_op jit(solution)/shard_map/pallas_call | solution.py:626
  211.4 2.9 shard_map.325
  214.3 2.9 collective-permute-done.26.one.refs_1_
  219.4 1.8 collective-permute-start.36
  221.8 1.6 collective-permute-start.34
  223.4 4.6 %shard_map.328 = (bf16[256,3072]{1,0:T(8,128)(2,1)S(1)}, f32[256,768]{1,0:T(8,128)S(1)}) custom-call(f32[256,768]{1,0:T(8,128)S(1)} %get-tuple-element.339.grad_ref, bf16[256,768]{1,0:T(8,128)(2,1)S(1)} %get-tuple-element.340.low_ref.refs_0_, bf16[256,3072]{1,0:T(8,128)(2,1)S(1)} %get-tuple-element.341.slope_ref, bf16[768,6144]{1,0:T(8,128)(2,1)S(1)} %bitcast.102, ...), custom_call_target="tpu_custom_call" | custom-call | flops 1048576 | bytes 65536 | tf_op jit(solution)/shard_map/pallas_call | solution.py:571
  228.0 1.4 shard_map.330
  229.5 11.6 %collective-permute-done.33.refs_3_ = bf16[48,3072]{1,0:T(8,128)(2,1)S(1)} collective-permute-done((bf16[48,3072]{1,0:T(8,128)(2,1)S(1)}, bf16[48,3072]{1,0:T(8,128)(2,1)S(1)}, u32[]{:S(2)}, u32[]{:S(2)}) %collective-permute-start.33) | collective-permute-done | bytes 294944 | tf_op jit(solution)/shard_map/ppermute | solution.py:275
  243.2 1.7 collective-permute-start.42
  245.7 1.7 collective-permute-start.40
  247.5 8.1 %shard_map.332 = (bf16[256,3072]{1,0:T(8,128)(2,1)S(1)}, f32[256,768]{1,0:T(8,128)}, f32[1,768]{1,0:T(1,128)S(1)}) custom-call(s32[1]{0:T(128)S(6)} %copy.50.length_ref, f32[256,768]{1,0:T(8,128)S(1)} %get-tuple-element.372.grad_ref, f32[256,768]{1,0:T(8,128)S(1)} %get-tuple-element.275.sum_ref, f32[8,768]{1,0:T(8,128)S(1)} %copy-done.17, ...), custom_call_target="tpu_custom_call" | custom-call | flops 1048576 | bytes 65536 | tf_op jit(solution)/shard_map/pallas_call | solution.py:626
  255.6 6.6 %shard_map.334 = (bf16[96,6144]{1,0:T(8,128)(2,1)S(1)}, bf16[96,6144]{1,0:T(8,128)(2,1)S(1)}, bf16[48,6144]{1,0:T(8,128)(2,1)S(1)}, bf16[48,6144]{1,0:T(8,128)(2,1)S(1)}, bf16[96,6144]{1,0:T(8,128)(2,1)S(1)}) custom-call(bf16[384,384]{1,0:T(8,128)(2,1)S(1)} %get-tuple-element.377.ga.refs_0_, bf16[384,384]{1,0:T(8,128)(2,1)S(1)} %collective-permute-done.37.gb.refs_1_, ...), custom_call_target="tpu_custom_call" | custom-call | flops 1048576 | bytes 65536 | tf_op jit(solution)/shard_map/pallas_call | solution.py:681
  262.2 3.3 collective-permute-done.39.refs_8_
  266.1 1.4 collective-permute-start.52
  268.5 1.6 collective-permute-start.46
  270.0 3.5 collective-permute-start.47
  273.7 10.6 %collective-permute-done.46 = bf16[24,6144]{1,0:T(8,128)(2,1)S(1)} collective-permute-done((bf16[24,6144]{1,0:T(8,128)(2,1)S(1)}, bf16[24,6144]{1,0:T(8,128)(2,1)S(1)}, u32[]{:S(2)}, u32[]{:S(2)}) %collective-permute-start.46) | collective-permute-done | bytes 294944 | tf_op jit(solution)/shard_map/ppermute | solution.py:275
  285.0 1.4 collective-permute-start.50
  286.4 5.6 %collective-permute-start.48 = (bf16[24,6144]{1,0:T(8,128)(2,1)S(1)}, bf16[24,6144]{1,0:T(8,128)(2,1)S(1)}, u32[]{:S(2)}, u32[]{:S(2)}) collective-permute-start(bf16[24,6144]{1,0:T(8,128)(2,1)S(1)} %get-tuple-element.404), channel_id=1, source_target_pairs={{0,6},{1,7},{2,4},{3,5},{4,2},{5,3},{6,0},{7,1},{8,14},{9,15},{10,... | collective-permute-start | bytes 884744 | tf_op jit(solution)/shard_map/ppermute | solution.py:275
  292.0 1.4 shard_map.338
  293.4 3.9 %collective-permute-done.48 = bf16[24,6144]{1,0:T(8,128)(2,1)S(1)} collective-permute-done((bf16[24,6144]{1,0:T(8,128)(2,1)S(1)}, bf16[24,6144]{1,0:T(8,128)(2,1)S(1)}, u32[]{:S(2)}, u32[]{:S(2)}) %collective-permute-start.48) | collective-permute-done | bytes 294944 | tf_op jit(solution)/shard_map/ppermute | solution.py:275
  297.3 3.8 collective-permute-done.49.refs_3_
  301.3 2.5 collective-permute-start.55
  305.6 1.4 collective-permute-start.57
  307.3 1.8 collective-permute-start.58
  309.1 1.4 collective-permute-start.59
  311.3 6.4 %collective-permute-done.56 = bf16[24,3200]{1,0:T(8,128)(2,1)S(1)} collective-permute-done((bf16[24,3200]{1,0:T(8,128)(2,1)S(1)}, bf16[24,3200]{1,0:T(8,128)(2,1)S(1)}, u32[]{:S(2)}, u32[]{:S(2)}) %collective-permute-start.56) | collective-permute-done | bytes 153632 | tf_op jit(solution)/shard_map/ppermute | solution.py:275
  317.7 1.8 collective-permute-start.64
  320.4 3.1 collective-permute-done.58.refs_3_
  323.5 1.9 collective-permute-done.59.refs_4_
  327.5 2.0 collective-permute-start.61
  329.5 1.4 collective-permute-start.62
  330.9 5.2 %collective-permute-done.63.one.refs_1_ = bf16[96,3200]{1,0:T(8,128)(2,1)S(1)} collective-permute-done((bf16[96,3200]{1,0:T(8,128)(2,1)S(1)}, bf16[96,3200]{1,0:T(8,128)(2,1)S(1)}, u32[]{:S(2)}, u32[]{:S(2)}) %collective-permute-start.63) | collective-permute-done | bytes 614432 | tf_op jit(solution)/shard_map/ppermute | solution.py:275
  337.0 1.7 collective-permute-start.65
  340.2 5.8 %collective-permute-done.65.refs_3_ = bf16[48,3200]{1,0:T(8,128)(2,1)S(1)} collective-permute-done((bf16[48,3200]{1,0:T(8,128)(2,1)}, bf16[48,3200]{1,0:T(8,128)(2,1)S(1)}, u32[]{:S(2)}, u32[]{:S(2)}) %collective-permute-start.65) | collective-permute-done | bytes 307232 | tf_op jit(solution)/shard_map/ppermute | solution.py:275
  346.9 3.0 collective-permute-start.68
  350.7 1.8 collective-permute-done.67
  352.5 11.8 %collective-permute-done.68 = bf16[24,3200]{1,0:T(8,128)(2,1)S(1)} collective-permute-done((bf16[24,3200]{1,0:T(8,128)(2,1)S(1)}, bf16[24,3200]{1,0:T(8,128)(2,1)S(1)}, u32[]{:S(2)}, u32[]{:S(2)}) %collective-permute-start.68) | collective-permute-done | bytes 153632 | tf_op jit(solution)/shard_map/ppermute | solution.py:275
  (246 shorter events, 55.1 us)
Async XLA Ops:
  7.2 154.2 %all-gather.2.cloned.1.call-start = ((), (), s32[]{:S(2)}) async-start(), calls=%async_computation | async-start | bytes 14800896 | tf_op jit(solution)/shard_map/all_gather | solution.py:57
  14.1 7.1 %collective-permute-start = (bf16[24,3200]{1,0:T(8,128)(2,1)S(1)}, bf16[24,3200]{1,0:T(8,128)(2,1)S(1)}, u32[]{:S(2)}, u32[]{:S(2)}) collective-permute-start(bf16[24,3200]{1,0:T(8,128)(2,1)S(1)} %constant_dynamic-update-slice_fusion), channel_id=1, source_target_pairs={{0,2},{1,3},{2,0},{3,1},{4,6},{5,7},{6,4},{7,5},{8,10},{9,11},{10,... | collective-permute-start | bytes 460808 | tf_op jit(solution)/shard_map/ppermute | solution.py:275
  21.2 11.3 %collective-permute-start.2 = (bf16[24,6144]{1,0:T(8,128)(2,1)S(1)}, bf16[24,6144]{1,0:T(8,128)(2,1)S(1)}, u32[]{:S(2)}, u32[]{:S(2)}) collective-permute-start(bf16[24,6144]{1,0:T(8,128)(2,1)S(1)} %pad_maximum_fusion.6), channel_id=1, source_target_pairs={{0,2},{1,3},{2,0},{3,1},{4,6},{5,7},{6,4},{7,5},{8,10},{9,11},{10,... | collective-permute-start | bytes 884744 | tf_op jit(solution)/shard_map/ppermute | solution.py:275
  23.0 9.5 %collective-permute-start.1 = (bf16[48,3200]{1,0:T(8,128)(2,1)S(1)}, bf16[48,3200]{1,0:T(8,128)(2,1)S(1)}, u32[]{:S(2)}, u32[]{:S(2)}) collective-permute-start(bf16[48,3200]{1,0:T(8,128)(2,1)S(1)} %pad_maximum_fusion.5), channel_id=1, source_target_pairs={{2,4},{3,5},{4,2},{5,3},{10,12},{11,13},{12,10},{13,11},{18,20},{1... | collective-permute-start | bytes 921608 | tf_op jit(solution)/shard_map/ppermute | solution.py:275
  32.5 17.4 %collective-permute-start.3 = (bf16[48,3200]{1,0:T(8,128)(2,1)S(1)}, bf16[48,3200]{1,0:T(8,128)(2,1)S(1)}, u32[]{:S(2)}, u32[]{:S(2)}) collective-permute-start(bf16[48,3200]{1,0:T(8,128)(2,1)S(1)} %collective-permute-done.1), channel_id=1, source_target_pairs={{2,0},{3,1},{4,6},{5,7},{10,8},{11,9},{12,14},{13,15},{18,16},{19,... | collective-permute-start | bytes 921608 | tf_op jit(solution)/shard_map/ppermute | solution.py:275
  34.3 15.8 %collective-permute-start.4 = (bf16[48,6144]{1,0:T(8,128)(2,1)S(1)}, bf16[48,6144]{1,0:T(8,128)(2,1)S(1)}, u32[]{:S(2)}, u32[]{:S(2)}) collective-permute-start(bf16[48,6144]{1,0:T(8,128)(2,1)S(1)} %pad_maximum_fusion.2), channel_id=1, source_target_pairs={{2,4},{3,5},{4,2},{5,3},{10,12},{11,13},{12,10},{13,11},{18,20},{1... | collective-permute-start | bytes 1769480 | tf_op jit(solution)/shard_map/ppermute | solution.py:275
  50.0 37.7 %collective-permute-start.6 = (bf16[48,6144]{1,0:T(8,128)(2,1)S(1)}, bf16[48,6144]{1,0:T(8,128)(2,1)S(1)}, u32[]{:S(2)}, u32[]{:S(2)}) collective-permute-start(bf16[48,6144]{1,0:T(8,128)(2,1)S(1)} %collective-permute-done.4), channel_id=1, source_target_pairs={{2,0},{3,1},{4,6},{5,7},{10,8},{11,9},{12,14},{13,15},{18,16},{19,... | collective-permute-start | bytes 1769480 | tf_op jit(solution)/shard_map/ppermute | solution.py:275
  51.5 36.5 %collective-permute-start.5 = (bf16[96,3200]{1,0:T(8,128)(2,1)S(1)}, bf16[96,3200]{1,0:T(8,128)(2,1)}, u32[]{:S(2)}, u32[]{:S(2)}) collective-permute-start(bf16[96,3200]{1,0:T(8,128)(2,1)S(1)} %pad_maximum_fusion.1), channel_id=1, source_target_pairs={{0,16},{1,17},{2,18},{3,19},{4,20},{5,21},{6,22},{7,23},{8,9},{9,8... | collective-permute-start | bytes 1843208 | tf_op jit(solution)/shard_map/ppermute | solution.py:275
  53.0 36.6 %collective-permute-start.9 = (bf16[96,3200]{1,0:T(8,128)(2,1)S(1)}, bf16[96,3200]{1,0:T(8,128)(2,1)}, u32[]{:S(2)}, u32[]{:S(2)}) collective-permute-start(bf16[96,3200]{1,0:T(8,128)(2,1)S(1)} %pad_maximum_fusion.1), channel_id=1, source_target_pairs={{0,1},{1,0},{2,3},{3,2},{4,5},{5,4},{6,7},{7,6},{8,24},{9,25},{10,... | collective-permute-start | bytes 1843208 | tf_op jit(solution)/shard_map/ppermute | solution.py:275
  89.0 16.8 %collective-permute-start.7 = (bf16[48,3200]{1,0:T(8,128)(2,1)S(1)}, bf16[48,3200]{1,0:T(8,128)(2,1)S(1)}, u32[]{:S(2)}, u32[]{:S(2)}) collective-permute-start(bf16[48,3200]{1,0:T(8,128)(2,1)S(1)} %slice.115), channel_id=1, source_target_pairs={{0,1},{1,0},{2,3},{3,2},{4,5},{5,4},{6,7},{7,6},{8,24},{9,25},{10,... | collective-permute-start | bytes 921608 | tf_op jit(solution)/shard_map/ppermute | solution.py:275
  90.6 17.5 %collective-permute-start.10 = (bf16[48,3200]{1,0:T(8,128)(2,1)S(1)}, bf16[48,3200]{1,0:T(8,128)(2,1)S(1)}, u32[]{:S(2)}, u32[]{:S(2)}) collective-permute-start(bf16[48,3200]{1,0:T(8,128)(2,1)S(1)} %slice.144), channel_id=1, source_target_pairs={{0,16},{1,17},{2,18},{3,19},{4,20},{5,21},{6,22},{7,23},{8,9},{9,8... | collective-permute-start | bytes 921608 | tf_op jit(solution)/shard_map/ppermute | solution.py:275
  105.8 39.1 %collective-permute-start.8 = (bf16[96,6144]{1,0:T(8,128)(2,1)S(1)}, bf16[96,6144]{1,0:T(8,128)(2,1)}, u32[]{:S(2)}, u32[]{:S(2)}) collective-permute-start(bf16[96,6144]{1,0:T(8,128)(2,1)S(1)} %pad_maximum_fusion), channel_id=1, source_target_pairs={{0,16},{1,17},{2,18},{3,19},{4,20},{5,21},{6,22},{7,23},{8,9},{9,8... | collective-permute-start | bytes 3538952 | tf_op jit(solution)/shard_map/ppermute | solution.py:275
  106.7 39.2 %collective-permute-start.16 = (bf16[96,6144]{1,0:T(8,128)(2,1)S(1)}, bf16[96,6144]{1,0:T(8,128)(2,1)}, u32[]{:S(2)}, u32[]{:S(2)}) collective-permute-start(bf16[96,6144]{1,0:T(8,128)(2,1)S(1)} %pad_maximum_fusion), channel_id=1, source_target_pairs={{0,1},{1,0},{2,3},{3,2},{4,5},{5,4},{6,7},{7,6},{8,24},{9,25},{10,... | collective-permute-start | bytes 3538952 | tf_op jit(solution)/shard_map/ppermute | solution.py:275
  109.4 4.7 %collective-permute-start.13 = (bf16[96,3200]{1,0:T(8,128)(2,1)}, bf16[96,3200]{1,0:T(8,128)(2,1)}, u32[]{:S(2)}, u32[]{:S(2)}) collective-permute-start(bf16[96,3200]{1,0:T(8,128)(2,1)} %collective-permute-done.5), channel_id=1, source_target_pairs={{0,8},{1,9},{2,10},{3,11},{4,12},{5,13},{6,14},{7,15},{8,0},{9,1},... | collective-permute-start | bytes 1843208 | tf_op jit(solution)/shard_map/ppermute | solution.py:275
  110.5 3.6 collective-permute-start.14
  147.0 14.4 %collective-permute-start.17 = (bf16[48,6144]{1,0:T(8,128)(2,1)S(1)}, bf16[48,6144]{1,0:T(8,128)(2,1)}, u32[]{:S(2)}, u32[]{:S(2)}) collective-permute-start(bf16[48,6144]{1,0:T(8,128)(2,1)S(1)} %slice.145), channel_id=1, source_target_pairs={{0,16},{1,17},{2,18},{3,19},{4,20},{5,21},{6,22},{7,23},{8,9},{9,8... | collective-permute-start | bytes 1769480 | tf_op jit(solution)/shard_map/ppermute | solution.py:275
  149.9 11.5 %collective-permute-start.18 = (bf16[48,6144]{1,0:T(8,128)(2,1)S(1)}, bf16[48,6144]{1,0:T(8,128)(2,1)}, u32[]{:S(2)}, u32[]{:S(2)}) collective-permute-start(bf16[48,6144]{1,0:T(8,128)(2,1)S(1)} %slice.118), channel_id=1, source_target_pairs={{0,1},{1,0},{2,3},{3,2},{4,5},{5,4},{6,7},{7,6},{8,24},{9,25},{10,... | collective-permute-start | bytes 1769480 | tf_op jit(solution)/shard_map/ppermute | solution.py:275
  161.4 8.1 %collective-permute-start.21 = (bf16[96,6144]{1,0:T(8,128)(2,1)}, bf16[96,6144]{1,0:T(8,128)(2,1)S(1)}, u32[]{:S(2)}, u32[]{:S(2)}) collective-permute-start(bf16[96,6144]{1,0:T(8,128)(2,1)} %collective-permute-done.8), channel_id=1, source_target_pairs={{0,8},{1,9},{2,10},{3,11},{4,12},{5,13},{6,14},{7,15},{8,0},{9,1},... | collective-permute-start | bytes 3538952 | tf_op jit(solution)/shard_map/ppermute | solution.py:275
  161.4 8.1 %collective-permute-start.22 = (bf16[96,6144]{1,0:T(8,128)(2,1)}, bf16[96,6144]{1,0:T(8,128)(2,1)S(1)}, u32[]{:S(2)}, u32[]{:S(2)}) collective-permute-start(bf16[96,6144]{1,0:T(8,128)(2,1)} %collective-permute-done.16), channel_id=1, source_target_pairs={{0,8},{1,9},{2,10},{3,11},{4,12},{5,13},{6,14},{7,15},{8,0},{9,1},... | collective-permute-start | bytes 3538952 | tf_op jit(solution)/shard_map/ppermute | solution.py:275
  162.0 7.6 %collective-permute-start.23 = (bf16[96,6144]{1,0:T(8,128)(2,1)S(1)}, bf16[96,6144]{1,0:T(8,128)(2,1)S(1)}, u32[]{:S(2)}, u32[]{:S(2)}) collective-permute-start(bf16[96,6144]{1,0:T(8,128)(2,1)S(1)} %pad_maximum_fusion), channel_id=1, source_target_pairs={{0,8},{1,9},{2,10},{3,11},{4,12},{5,13},{6,14},{7,15},{8,0},{9,1},... | collective-permute-start | bytes 3538952 | tf_op jit(solution)/shard_map/ppermute | solution.py:275
  162.0 6.7 %collective-permute-start.19 = (bf16[48,6144]{1,0:T(8,128)(2,1)}, bf16[48,6144]{1,0:T(8,128)(2,1)S(1)}, u32[]{:S(2)}, u32[]{:S(2)}) collective-permute-start(bf16[48,6144]{1,0:T(8,128)(2,1)} %collective-permute-done.17), channel_id=1, source_target_pairs={{0,8},{1,9},{2,10},{3,11},{4,12},{5,13},{6,14},{7,15},{8,0},{9,1},... | collective-permute-start | bytes 1769480 | tf_op jit(solution)/shard_map/ppermute | solution.py:275
  162.5 7.1 %collective-permute-start.20 = (bf16[48,6144]{1,0:T(8,128)(2,1)}, bf16[48,6144]{1,0:T(8,128)(2,1)S(1)}, u32[]{:S(2)}, u32[]{:S(2)}) collective-permute-start(bf16[48,6144]{1,0:T(8,128)(2,1)} %collective-permute-done.18), channel_id=1, source_target_pairs={{0,8},{1,9},{2,10},{3,11},{4,12},{5,13},{6,14},{7,15},{8,0},{9,1},... | collective-permute-start | bytes 1769480 | tf_op jit(solution)/shard_map/ppermute | solution.py:275
  189.8 3.8 collective-permute-start.25
  192.8 10.7 %collective-permute-start.28 = (bf16[384,768]{1,0:T(8,128)(2,1)S(1)}, bf16[384,768]{1,0:T(8,128)(2,1)S(1)}, u32[]{:S(2)}, u32[]{:S(2)}) collective-permute-start(bf16[384,768]{1,0:T(8,128)(2,1)S(1)} %get-tuple-element.318), channel_id=1, source_target_pairs={{0,8},{1,9},{2,10},{3,11},{4,12},{5,13},{6,14},{7,15},{8,0},{9,1},... | collective-permute-start | bytes 1769480 | tf_op jit(solution)/shard_map/ppermute | solution.py:275
  201.2 15.9 %collective-permute-start.26 = (bf16[96,3072]{1,0:T(8,128)(2,1)S(1)}, bf16[96,3072]{1,0:T(8,128)(2,1)S(1)}, u32[]{:S(2)}, u32[]{:S(2)}) collective-permute-start(bf16[96,3072]{1,0:T(8,128)(2,1)S(1)} %get-tuple-element.301), channel_id=1, source_target_pairs={{0,16},{1,17},{2,18},{3,19},{4,20},{5,21},{6,22},{7,23},{8,9},{9,8... | collective-permute-start | bytes 1769480 | tf_op jit(solution)/shard_map/ppermute | solution.py:275
  201.8 15.3 %collective-permute-start.27 = (bf16[96,3072]{1,0:T(8,128)(2,1)S(1)}, bf16[96,3072]{1,0:T(8,128)(2,1)S(1)}, u32[]{:S(2)}, u32[]{:S(2)}) collective-permute-start(bf16[96,3072]{1,0:T(8,128)(2,1)S(1)} %get-tuple-element.302), channel_id=1, source_target_pairs={{0,1},{1,0},{2,3},{3,2},{4,5},{5,4},{6,7},{7,6},{8,24},{9,25},{10,... | collective-permute-start | bytes 1769480 | tf_op jit(solution)/shard_map/ppermute | solution.py:275
  203.5 7.8 %collective-permute-start.30 = (bf16[256,768]{1,0:T(8,128)(2,1)S(1)}, bf16[256,768]{1,0:T(8,128)(2,1)S(1)}, u32[]{:S(2)}, u32[]{:S(2)}) collective-permute-start(bf16[256,768]{1,0:T(8,128)(2,1)S(1)} %get-tuple-element.497), channel_id=1, source_target_pairs={{0,8},{1,9},{2,10},{3,11},{4,12},{5,13},{6,14},{7,15},{8,0},{9,1},... | collective-permute-start | bytes 1179656 | tf_op jit(solution)/shard_map/ppermute | solution.py:275
  203.5 7.8 %collective-permute-start.31 = (bf16[256,768]{1,0:T(8,128)(2,1)S(1)}, bf16[256,768]{1,0:T(8,128)(2,1)S(1)}, u32[]{:S(2)}, u32[]{:S(2)}) collective-permute-start(bf16[256,768]{1,0:T(8,128)(2,1)S(1)} %get-tuple-element.496), channel_id=1, source_target_pairs={{0,8},{1,9},{2,10},{3,11},{4,12},{5,13},{6,14},{7,15},{8,0},{9,1},... | collective-permute-start | bytes 1179656 | tf_op jit(solution)/shard_map/ppermute | solution.py:275
  204.1 7.3 %collective-permute-start.32 = (bf16[256,768]{1,0:T(8,128)(2,1)S(1)}, bf16[256,768]{1,0:T(8,128)(2,1)S(1)}, u32[]{:S(2)}, u32[]{:S(2)}) collective-permute-start(bf16[256,768]{1,0:T(8,128)(2,1)S(1)} %get-tuple-element.495), channel_id=1, source_target_pairs={{0,8},{1,9},{2,10},{3,11},{4,12},{5,13},{6,14},{7,15},{8,0},{9,1},... | collective-permute-start | bytes 1179656 | tf_op jit(solution)/shard_map/ppermute | solution.py:275
  217.1 6.3 %collective-permute-start.38 = (bf16[256,3072]{1,0:T(8,128)(2,1)S(1)}, bf16[256,3072]{1,0:T(8,128)(2,1)S(1)}, u32[]{:S(2)}, u32[]{:S(2)}) collective-permute-start(bf16[256,3072]{1,0:T(8,128)(2,1)S(1)} %get-tuple-element.349.ra), channel_id=1, source_target_pairs={{0,8},{1,9},{2,10},{3,11},{4,12},{5,13},{6,14},{7,15},{8,0},{9,1},... | collective-permute-start | bytes 4718600 | tf_op jit(solution)/shard_map/ppermute | solution.py:275
  218.6 3.2 collective-permute-start.37
  219.1 22.0 %collective-permute-start.35 = (bf16[96,3072]{1,0:T(8,128)(2,1)S(1)}, bf16[96,3072]{1,0:T(8,128)(2,1)S(1)}, u32[]{:S(2)}, u32[]{:S(2)}) collective-permute-start(bf16[96,3072]{1,0:T(8,128)(2,1)S(1)} %get-tuple-element.332), channel_id=1, source_target_pairs={{0,16},{1,17},{2,18},{3,19},{4,20},{5,21},{6,22},{7,23},{8,9},{9,8... | collective-permute-start | bytes 1769480 | tf_op jit(solution)/shard_map/ppermute | solution.py:275
  219.4 21.7 %collective-permute-start.36 = (bf16[96,3072]{1,0:T(8,128)(2,1)S(1)}, bf16[96,3072]{1,0:T(8,128)(2,1)S(1)}, u32[]{:S(2)}, u32[]{:S(2)}) collective-permute-start(bf16[96,3072]{1,0:T(8,128)(2,1)S(1)} %get-tuple-element.333), channel_id=1, source_target_pairs={{0,1},{1,0},{2,3},{3,2},{4,5},{5,4},{6,7},{7,6},{8,24},{9,25},{10,... | collective-permute-start | bytes 1769480 | tf_op jit(solution)/shard_map/ppermute | solution.py:275
  221.3 19.8 %collective-permute-start.33 = (bf16[48,3072]{1,0:T(8,128)(2,1)S(1)}, bf16[48,3072]{1,0:T(8,128)(2,1)S(1)}, u32[]{:S(2)}, u32[]{:S(2)}) collective-permute-start(bf16[48,3072]{1,0:T(8,128)(2,1)S(1)} %get-tuple-element.329), channel_id=1, source_target_pairs={{0,16},{1,17},{2,18},{3,19},{4,20},{5,21},{6,22},{7,23},{8,9},{9,8... | collective-permute-start | bytes 884744 | tf_op jit(solution)/shard_map/ppermute | solution.py:275
  221.8 19.3 %collective-permute-start.34 = (bf16[48,3072]{1,0:T(8,128)(2,1)S(1)}, bf16[48,3072]{1,0:T(8,128)(2,1)S(1)}, u32[]{:S(2)}, u32[]{:S(2)}) collective-permute-start(bf16[48,3072]{1,0:T(8,128)(2,1)S(1)} %get-tuple-element.330), channel_id=1, source_target_pairs={{0,1},{1,0},{2,3},{3,2},{4,5},{5,4},{6,7},{7,6},{8,24},{9,25},{10,... | collective-permute-start | bytes 884744 | tf_op jit(solution)/shard_map/ppermute | solution.py:275
  223.4 22.3 %collective-permute-start.43 = (bf16[256,3072]{1,0:T(8,128)(2,1)}, bf16[256,3072]{1,0:T(8,128)(2,1)S(1)}, u32[]{:S(2)}, u32[]{:S(2)}) collective-permute-start(bf16[256,3072]{1,0:T(8,128)(2,1)} %get-tuple-element.379.refs_2_), channel_id=1, source_target_pairs={{0,8},{1,9},{2,10},{3,11},{4,12},{5,13},{6,14},{7,15},{8,0},{9,1},... | collective-permute-start | bytes 4718600 | tf_op jit(solution)/shard_map/ppermute | solution.py:275
  241.1 14.5 %collective-permute-start.45 = (bf16[256,3072]{1,0:T(8,128)(2,1)S(1)}, bf16[256,3072]{1,0:T(8,128)(2,1)S(1)}, u32[]{:S(2)}, u32[]{:S(2)}) collective-permute-start(bf16[256,3072]{1,0:T(8,128)(2,1)S(1)} %get-tuple-element.385.refs_6_), channel_id=1, source_target_pairs={{0,8},{1,9},{2,10},{3,11},{4,12},{5,13},{6,14},{7,15},{8,0},{9,1},... | collective-permute-start | bytes 4718600 | tf_op jit(solution)/shard_map/ppermute | solution.py:275
  243.0 22.5 %collective-permute-start.41 = (bf16[96,3200]{1,0:T(8,128)(2,1)S(1)}, bf16[96,3200]{1,0:T(8,128)(2,1)S(1)}, u32[]{:S(2)}, u32[]{:S(2)}) collective-permute-start(bf16[96,3200]{1,0:T(8,128)(2,1)S(1)} %get-tuple-element.367), channel_id=1, source_target_pairs={{0,16},{1,17},{2,18},{3,19},{4,20},{5,21},{6,22},{7,23},{8,9},{9,8... | collective-permute-start | bytes 1843208 | tf_op jit(solution)/shard_map/ppermute | solution.py:275
  243.2 22.2 %collective-permute-start.42 = (bf16[96,3200]{1,0:T(8,128)(2,1)S(1)}, bf16[96,3200]{1,0:T(8,128)(2,1)S(1)}, u32[]{:S(2)}, u32[]{:S(2)}) collective-permute-start(bf16[96,3200]{1,0:T(8,128)(2,1)S(1)} %get-tuple-element.368), channel_id=1, source_target_pairs={{0,1},{1,0},{2,3},{3,2},{4,5},{5,4},{6,7},{7,6},{8,24},{9,25},{10,... | collective-permute-start | bytes 1843208 | tf_op jit(solution)/shard_map/ppermute | solution.py:275
  245.4 20.0 %collective-permute-start.39 = (bf16[48,3072]{1,0:T(8,128)(2,1)S(1)}, bf16[48,3072]{1,0:T(8,128)(2,1)S(1)}, u32[]{:S(2)}, u32[]{:S(2)}) collective-permute-start(bf16[48,3072]{1,0:T(8,128)(2,1)S(1)} %get-tuple-element.364), channel_id=1, source_target_pairs={{0,16},{1,17},{2,18},{3,19},{4,20},{5,21},{6,22},{7,23},{8,9},{9,8... | collective-permute-start | bytes 884744 | tf_op jit(solution)/shard_map/ppermute | solution.py:275
  245.7 19.7 %collective-permute-start.40 = (bf16[48,3072]{1,0:T(8,128)(2,1)S(1)}, bf16[48,3072]{1,0:T(8,128)(2,1)S(1)}, u32[]{:S(2)}, u32[]{:S(2)}) collective-permute-start(bf16[48,3072]{1,0:T(8,128)(2,1)S(1)} %get-tuple-element.365), channel_id=1, source_target_pairs={{0,1},{1,0},{2,3},{3,2},{4,5},{5,4},{6,7},{7,6},{8,24},{9,25},{10,... | collective-permute-start | bytes 884744 | tf_op jit(solution)/shard_map/ppermute | solution.py:275
  265.5 21.0 %collective-permute-start.53 = (bf16[256,3072]{1,0:T(8,128)(2,1)S(1)}, bf16[256,3072]{1,0:T(8,128)(2,1)S(1)}, u32[]{:S(2)}, u32[]{:S(2)}) collective-permute-start(bf16[256,3072]{1,0:T(8,128)(2,1)S(1)} %get-tuple-element.418.ra), channel_id=1, source_target_pairs={{0,8},{1,9},{2,10},{3,11},{4,12},{5,13},{6,14},{7,15},{8,0},{9,1},... | collective-permute-start | bytes 4718600 | tf_op jit(solution)/shard_map/ppermute | solution.py:275
  265.6 35.5 %collective-permute-start.51 = (bf16[96,6144]{1,0:T(8,128)(2,1)S(1)}, bf16[96,6144]{1,0:T(8,128)(2,1)S(1)}, u32[]{:S(2)}, u32[]{:S(2)}) collective-permute-start(bf16[96,6144]{1,0:T(8,128)(2,1)S(1)} %get-tuple-element.413), channel_id=1, source_target_pairs={{0,16},{1,17},{2,18},{3,19},{4,20},{5,21},{6,22},{7,23},{8,9},{9,8... | collective-permute-start | bytes 3538952 | tf_op jit(solution)/shard_map/ppermute | solution.py:275
  266.1 34.9 %collective-permute-start.52 = (bf16[96,6144]{1,0:T(8,128)(2,1)S(1)}, bf16[96,6144]{1,0:T(8,128)(2,1)S(1)}, u32[]{:S(2)}, u32[]{:S(2)}) collective-permute-start(bf16[96,6144]{1,0:T(8,128)(2,1)S(1)} %get-tuple-element.414), channel_id=1, source_target_pairs={{0,1},{1,0},{2,3},{3,2},{4,5},{5,4},{6,7},{7,6},{8,24},{9,25},{10,... | collective-permute-start | bytes 3538952 | tf_op jit(solution)/shard_map/ppermute | solution.py:275
  268.5 15.8 %collective-permute-start.46 = (bf16[24,6144]{1,0:T(8,128)(2,1)S(1)}, bf16[24,6144]{1,0:T(8,128)(2,1)S(1)}, u32[]{:S(2)}, u32[]{:S(2)}) collective-permute-start(bf16[24,6144]{1,0:T(8,128)(2,1)S(1)} %get-tuple-element.402), channel_id=1, source_target_pairs={{0,2},{1,3},{2,0},{3,1},{4,6},{5,7},{6,4},{7,5},{8,10},{9,11},{10,... | collective-permute-start | bytes 884744 | tf_op jit(solution)/shard_map/ppermute | solution.py:275
  270.0 15.0 %collective-permute-start.47 = (bf16[24,6144]{1,0:T(8,128)(2,1)S(1)}, bf16[24,6144]{1,0:T(8,128)(2,1)S(1)}, u32[]{:S(2)}, u32[]{:S(2)}) collective-permute-start(bf16[24,6144]{1,0:T(8,128)(2,1)S(1)} %get-tuple-element.403), channel_id=1, source_target_pairs={{0,4},{1,5},{2,6},{3,7},{4,0},{5,1},{6,2},{7,3},{8,12},{9,13},{10,... | collective-permute-start | bytes 884744 | tf_op jit(solution)/shard_map/ppermute | solution.py:275
  284.2 16.8 %collective-permute-start.49 = (bf16[48,3200]{1,0:T(8,128)(2,1)S(1)}, bf16[48,3200]{1,0:T(8,128)(2,1)S(1)}, u32[]{:S(2)}, u32[]{:S(2)}) collective-permute-start(bf16[48,3200]{1,0:T(8,128)(2,1)S(1)} %get-tuple-element.410), channel_id=1, source_target_pairs={{0,16},{1,17},{2,18},{3,19},{4,20},{5,21},{6,22},{7,23},{8,9},{9,8... | collective-permute-start | bytes 921608 | tf_op jit(solution)/shard_map/ppermute | solution.py:275
  285.0 16.0 %collective-permute-start.50 = (bf16[48,3200]{1,0:T(8,128)(2,1)S(1)}, bf16[48,3200]{1,0:T(8,128)(2,1)S(1)}, u32[]{:S(2)}, u32[]{:S(2)}) collective-permute-start(bf16[48,3200]{1,0:T(8,128)(2,1)S(1)} %get-tuple-element.411), channel_id=1, source_target_pairs={{0,1},{1,0},{2,3},{3,2},{4,5},{5,4},{6,7},{7,6},{8,24},{9,25},{10,... | collective-permute-start | bytes 921608 | tf_op jit(solution)/shard_map/ppermute | solution.py:275
  286.4 10.8 %collective-permute-start.48 = (bf16[24,6144]{1,0:T(8,128)(2,1)S(1)}, bf16[24,6144]{1,0:T(8,128)(2,1)S(1)}, u32[]{:S(2)}, u32[]{:S(2)}) collective-permute-start(bf16[24,6144]{1,0:T(8,128)(2,1)S(1)} %get-tuple-element.404), channel_id=1, source_target_pairs={{0,6},{1,7},{2,4},{3,5},{4,2},{5,3},{6,0},{7,1},{8,14},{9,15},{10,... | collective-permute-start | bytes 884744 | tf_op jit(solution)/shard_map/ppermute | solution.py:275
  301.3 9.2 %collective-permute-start.55 = (bf16[24,3200]{1,0:T(8,128)(2,1)S(1)}, bf16[24,3200]{1,0:T(8,128)(2,1)S(1)}, u32[]{:S(2)}, u32[]{:S(2)}) collective-permute-start(bf16[24,3200]{1,0:T(8,128)(2,1)S(1)} %get-tuple-element.433), channel_id=1, source_target_pairs={{0,2},{1,3},{2,0},{3,1},{4,6},{5,7},{6,4},{7,5},{8,10},{9,11},{10,... | collective-permute-start | bytes 460808 | tf_op jit(solution)/shard_map/ppermute | solution.py:275
  303.8 13.9 %collective-permute-start.56 = (bf16[24,3200]{1,0:T(8,128)(2,1)S(1)}, bf16[24,3200]{1,0:T(8,128)(2,1)S(1)}, u32[]{:S(2)}, u32[]{:S(2)}) collective-permute-start(bf16[24,3200]{1,0:T(8,128)(2,1)S(1)} %get-tuple-element.434), channel_id=1, source_target_pairs={{0,4},{1,5},{2,6},{3,7},{4,0},{5,1},{6,2},{7,3},{8,12},{9,13},{10,... | collective-permute-start | bytes 460808 | tf_op jit(solution)/shard_map/ppermute | solution.py:275
  305.6 14.8 %collective-permute-start.57 = (bf16[24,3200]{1,0:T(8,128)(2,1)S(1)}, bf16[24,3200]{1,0:T(8,128)(2,1)S(1)}, u32[]{:S(2)}, u32[]{:S(2)}) collective-permute-start(bf16[24,3200]{1,0:T(8,128)(2,1)S(1)} %get-tuple-element.435), channel_id=1, source_target_pairs={{0,6},{1,7},{2,4},{3,5},{4,2},{5,3},{6,0},{7,1},{8,14},{9,15},{10,... | collective-permute-start | bytes 460808 | tf_op jit(solution)/shard_map/ppermute | solution.py:275
  307.3 16.2 %collective-permute-start.58 = (bf16[48,6144]{1,0:T(8,128)(2,1)S(1)}, bf16[48,6144]{1,0:T(8,128)(2,1)S(1)}, u32[]{:S(2)}, u32[]{:S(2)}) collective-permute-start(bf16[48,6144]{1,0:T(8,128)(2,1)S(1)} %get-tuple-element.441), channel_id=1, source_target_pairs={{0,16},{1,17},{2,18},{3,19},{4,20},{5,21},{6,22},{7,23},{8,9},{9,8... | collective-permute-start | bytes 1769480 | tf_op jit(solution)/shard_map/ppermute | solution.py:275
  309.1 16.3 %collective-permute-start.59 = (bf16[48,6144]{1,0:T(8,128)(2,1)S(1)}, bf16[48,6144]{1,0:T(8,128)(2,1)S(1)}, u32[]{:S(2)}, u32[]{:S(2)}) collective-permute-start(bf16[48,6144]{1,0:T(8,128)(2,1)S(1)} %get-tuple-element.442), channel_id=1, source_target_pairs={{0,1},{1,0},{2,3},{3,2},{4,5},{5,4},{6,7},{7,6},{8,24},{9,25},{10,... | collective-permute-start | bytes 1769480 | tf_op jit(solution)/shard_map/ppermute | solution.py:275
  310.4 25.6 %collective-permute-start.63 = (bf16[96,3200]{1,0:T(8,128)(2,1)S(1)}, bf16[96,3200]{1,0:T(8,128)(2,1)S(1)}, u32[]{:S(2)}, u32[]{:S(2)}) collective-permute-start(bf16[96,3200]{1,0:T(8,128)(2,1)S(1)} %get-tuple-element.456), channel_id=1, source_target_pairs={{0,16},{1,17},{2,18},{3,19},{4,20},{5,21},{6,22},{7,23},{8,9},{9,8... | collective-permute-start | bytes 1843208 | tf_op jit(solution)/shard_map/ppermute | solution.py:275
  317.7 18.4 %collective-permute-start.64 = (bf16[96,3200]{1,0:T(8,128)(2,1)S(1)}, bf16[96,3200]{1,0:T(8,128)(2,1)S(1)}, u32[]{:S(2)}, u32[]{:S(2)}) collective-permute-start(bf16[96,3200]{1,0:T(8,128)(2,1)S(1)} %get-tuple-element.457), channel_id=1, source_target_pairs={{0,1},{1,0},{2,3},{3,2},{4,5},{5,4},{6,7},{7,6},{8,24},{9,25},{10,... | collective-permute-start | bytes 1843208 | tf_op jit(solution)/shard_map/ppermute | solution.py:275
  326.5 23.4 %collective-permute-start.60 = (bf16[24,6144]{1,0:T(8,128)(2,1)}, bf16[24,6144]{1,0:T(8,128)(2,1)S(1)}, u32[]{:S(2)}, u32[]{:S(2)}) collective-permute-start(bf16[24,6144]{1,0:T(8,128)(2,1)} %get-tuple-element.452), channel_id=1, source_target_pairs={{0,2},{1,3},{2,0},{3,1},{4,6},{5,7},{6,4},{7,5},{8,10},{9,11},{10,... | collective-permute-start | bytes 884744 | tf_op jit(solution)/shard_map/ppermute | solution.py:275
  327.5 23.2 %collective-permute-start.61 = (bf16[24,6144]{1,0:T(8,128)(2,1)}, bf16[24,6144]{1,0:T(8,128)(2,1)}, u32[]{:S(2)}, u32[]{:S(2)}) collective-permute-start(bf16[24,6144]{1,0:T(8,128)(2,1)} %get-tuple-element.453), channel_id=1, source_target_pairs={{0,4},{1,5},{2,6},{3,7},{4,0},{5,1},{6,2},{7,3},{8,12},{9,13},{10,... | collective-permute-start | bytes 884744 | tf_op jit(solution)/shard_map/ppermute | solution.py:275
  329.5 21.2 %collective-permute-start.62 = (bf16[24,6144]{1,0:T(8,128)(2,1)}, bf16[24,6144]{1,0:T(8,128)(2,1)}, u32[]{:S(2)}, u32[]{:S(2)}) collective-permute-start(bf16[24,6144]{1,0:T(8,128)(2,1)} %get-tuple-element.454), channel_id=1, source_target_pairs={{0,6},{1,7},{2,4},{3,5},{4,2},{5,3},{6,0},{7,1},{8,14},{9,15},{10,... | collective-permute-start | bytes 884744 | tf_op jit(solution)/shard_map/ppermute | solution.py:275
  337.0 9.0 %collective-permute-start.65 = (bf16[48,3200]{1,0:T(8,128)(2,1)}, bf16[48,3200]{1,0:T(8,128)(2,1)S(1)}, u32[]{:S(2)}, u32[]{:S(2)}) collective-permute-start(bf16[48,3200]{1,0:T(8,128)(2,1)} %get-tuple-element.466), channel_id=1, source_target_pairs={{0,16},{1,17},{2,18},{3,19},{4,20},{5,21},{6,22},{7,23},{8,9},{9,8... | collective-permute-start | bytes 921608 | tf_op jit(solution)/shard_map/ppermute | solution.py:275
  338.7 7.3 %collective-permute-start.66 = (bf16[48,3200]{1,0:T(8,128)(2,1)}, bf16[48,3200]{1,0:T(8,128)(2,1)S(1)}, u32[]{:S(2)}, u32[]{:S(2)}) collective-permute-start(bf16[48,3200]{1,0:T(8,128)(2,1)} %get-tuple-element.467), channel_id=1, source_target_pairs={{0,1},{1,0},{2,3},{3,2},{4,5},{5,4},{6,7},{7,6},{8,24},{9,25},{10,... | collective-permute-start | bytes 921608 | tf_op jit(solution)/shard_map/ppermute | solution.py:275
  346.2 6.3 %collective-permute-start.67 = (bf16[24,3200]{1,0:T(8,128)(2,1)S(1)}, bf16[24,3200]{1,0:T(8,128)(2,1)S(1)}, u32[]{:S(2)}, u32[]{:S(2)}) collective-permute-start(bf16[24,3200]{1,0:T(8,128)(2,1)S(1)} %get-tuple-element.475), channel_id=1, source_target_pairs={{0,2},{1,3},{2,0},{3,1},{4,6},{5,7},{6,4},{7,5},{8,10},{9,11},{10,... | collective-permute-start | bytes 460808 | tf_op jit(solution)/shard_map/ppermute | solution.py:275
  346.9 17.5 %collective-permute-start.68 = (bf16[24,3200]{1,0:T(8,128)(2,1)S(1)}, bf16[24,3200]{1,0:T(8,128)(2,1)S(1)}, u32[]{:S(2)}, u32[]{:S(2)}) collective-permute-start(bf16[24,3200]{1,0:T(8,128)(2,1)S(1)} %get-tuple-element.476), channel_id=1, source_target_pairs={{0,4},{1,5},{2,6},{3,7},{4,0},{5,1},{6,2},{7,3},{8,12},{9,13},{10,... | collective-permute-start | bytes 460808 | tf_op jit(solution)/shard_map/ppermute | solution.py:275
  349.9 14.5 %collective-permute-start.69 = (bf16[24,3200]{1,0:T(8,128)(2,1)S(1)}, bf16[24,3200]{1,0:T(8,128)(2,1)S(1)}, u32[]{:S(2)}, u32[]{:S(2)}) collective-permute-start(bf16[24,3200]{1,0:T(8,128)(2,1)S(1)} %get-tuple-element.477), channel_id=1, source_target_pairs={{0,6},{1,7},{2,4},{3,5},{4,2},{5,3},{6,0},{7,1},{8,14},{9,15},{10,... | collective-permute-start | bytes 460808 | tf_op jit(solution)/shard_map/ppermute | solution.py:275
  (48 other events, 418.4 us)
Sparse Core Ops, SparseCore 0:
  14.1 143.3 all-gather.1

commit v6 on v5

--- a/solution.py
+++ b/solution.py
@@ -276,7 +276,7 @@
 
 
 SLOTS = np.array([(far, near, s) for far, near in ((1, 1), (1, 0), (0, 1), (0, 0)) for s in range(4)])
-ROWS = ((0, 2), (2, 4), (4, 8), (8, 12), (12, 16))
+ROWS = tuple((j, j + 2) for j in range(0, 16, 2))
 TERM_SLOTS = SLOTS[[0, 1, 4, 5, 2, 3, 10, 11, 6, 7, 8, 9, 12, 13, 14, 15]]
 TERM_ROWS = ((0, 4), (4, 8), (8, 10), (10, 12), (12, 16))
 
@@ -764,6 +764,32 @@
     )(*(value for group in groups for value in group))
 
 
+def stack_attention(layers):
+    rows, width = layers[0][0].shape
+    starts = [0]
+    for layer in layers:
+        starts.append(starts[-1] + len(layer))
+
+    def body(*refs):
+        outs = refs[starts[-1] :]
+        for layer in range(len(layers)):
+            total = add(*(ref[...] for ref in refs[starts[layer] : starts[layer + 1]]))
+            for j, out in enumerate(outs):
+                out[layer] = total[:, j * D : min((j + 1) * D, width)]
+
+    return pl.pallas_call(
+        body,
+        in_specs=[VMEM_SPEC] * starts[-1],
+        out_specs=[VMEM_SPEC] * 5,
+        out_shape=shapes(
+            *[((len(layers), rows, D), jnp.float32)] * 4,
+            ((len(layers), rows, PAD), jnp.float32),
+        ),
+        cost_estimate=LIGHT,
+        compiler_params=params(8),
+    )(*(value for layer in layers for value in layer))
+
+
 def add(*values):
     return sum(value.astype(jnp.float32) for value in values)
 
@@ -854,19 +880,33 @@
     def outward(pieces, grid, two):
         near, far = pieces
         z = lax.axis_index("fsdp") // 2
-        far = jnp.where((z == 1) | (z == 2), far, swap(far, grid.outward))
-        return (jnp.concatenate([near, far], axis=0),)
+        return (near, jnp.where((z == 1) | (z == 2), far, swap(far, grid.outward)))
 
     @staticmethod
     def square(pieces, grid, two):
-        (line,) = pieces
-        return (line, swap(line, grid.first), swap(line, grid.second))
+        near, far = pieces
+        return (
+            swap(far, grid.first),
+            swap(near, grid.second),
+            swap(near, grid.first),
+            swap(far, grid.second),
+            near,
+            far,
+        )
 
     @staticmethod
     def diagonal(pieces, grid, two):
-        line, one, other = pieces
-        late = swap(one[two:], grid.second)
-        return (swap(other[:two], grid.first), late, one, other, line)
+        first_far, second_near, first_near, second_far, near, far = pieces
+        return (
+            swap(second_near, grid.first),
+            swap(first_far, grid.second),
+            first_near,
+            first_far,
+            second_near,
+            second_far,
+            near,
+            far,
+        )
 
     def result(self):
         pieces = self.pieces
@@ -883,9 +923,9 @@
     tiles = unit // 8
 
     def body(rows_ref, *refs):
-        sources, target = refs[:10], refs[10]
+        sources, target = refs[:16], refs[16]
         for half in range(2):
-            for (low, high), source in zip(ROWS, sources[half * 5 : half * 5 + 5]):
+            for (low, high), source in zip(ROWS, sources[half * 8 : half * 8 + 8]):
                 for slot in range(low, high):
                     row = rows_ref[half * 16 + slot] * tiles
                     first = (slot - low) * tiles
@@ -894,7 +934,7 @@
     placed = pl.pallas_call(
         body,
         in_specs=[pl.BlockSpec(memory_space=pltpu.SMEM)]
-        + [pl.BlockSpec(memory_space=pltpu.VMEM)] * 10,
+        + [pl.BlockSpec(memory_space=pltpu.VMEM)] * 16,
         out_specs=pl.BlockSpec(memory_space=pltpu.VMEM),
         out_shape=jax.ShapeDtypeStruct((32 * tiles, 8, width), jnp.bfloat16),
         cost_estimate=LIGHT,
@@ -965,7 +1005,7 @@
     attention, ffn = (Gathering(block, grid) for block in blocks)
 
     def hold(*gatherings):
-        pieces = [g.pieces[:2] if len(g.pieces) == 3 else g.pieces for g in gatherings]
+        pieces = [g.pieces[:2] if len(g.pieces) == 6 else g.pieces for g in gatherings]
         pieces = lax.optimization_barrier(pieces)
         for g, held in zip(gatherings, pieces):
             g.pieces = [*held, *g.pieces[len(held) :]]
@@ -984,7 +1024,7 @@
     ffn.advance()
     hold(attention, ffn)
     attention.advance()
-    ffn.pieces = gate(ffn.pieces, attention.pieces[1])
+    ffn.pieces = gate(ffn.pieces, attention.pieces[3])
     ffn.advance()
     hold(attention)
     weights = attention.result()
@@ -992,8 +1032,8 @@
     held, attended = lax.optimization_barrier((ffn.pieces[:2], attended))
     ffn.pieces = [*held, *ffn.pieces[2:]]
     ffn.advance()
-    pieces, second = lax.optimization_barrier((ffn.pieces, second))
-    ffn.pieces = list(pieces)
+    held, second = lax.optimization_barrier((ffn.pieces[6:], second))
+    ffn.pieces = [*ffn.pieces[:6], *held]
     return weights, ffn.result(), second, order, attended
 
 
@@ -1096,16 +1136,20 @@
     pieces = segments.run([ffn_0, attention_1, down_1], work, (grads, gain_first))
     attention_0 = Reduction(pieces, grid, unit)
     segments.run([ffn_0, attention_0, attention_1], pending=[attention_0])
-    segments.run([ffn_0], pending=[ffn_0])
-    segments.run([attention_0], pending=[ffn_0])
+    segments.run([attention_0, ffn_0])
     segments.run([attention_0])
 
-    summed_0, summed_1 = ffn_0.result(), down_1.result()
-    outputs = [
-        (attention_outputs(attention.result()), (summed[:, FF:], summed[:, :FF].T))
-        for attention, summed in ((attention_0, summed_0), (attention_1, summed_1))
-    ]
-    return finish(hidden, grad, outputs)
+    summed = [reduction.result() for reduction in (ffn_0, down_1)]
+    done = attention_1.result()
+    *attention, gains = stack_attention([(*attention_0.kept, *attention_0.out), (done,)])
+    return (
+        hidden.astype(jnp.bfloat16)[None],
+        grad[None],
+        *attention,
+        jnp.stack([value[:, FF:] for value in summed]),
+        jnp.stack([value[:, :FF].T for value in summed]),
+        jnp.swapaxes(gains[:, :, :2], 1, 2),
+    )
 
 
 def solution(mesh):

time: 381 us -> 375 us (0.984)
  waiting for transfers between devices: 189 us -> 171 us
  starting transfers between devices: 71.4 us -> 87.8 us
  other arithmetic: 8.93 us -> 4.82 us
    ppermute x70 -> x80, waiting for transfers between devices: 189 us -> 171 us  [swap(): return lax.ppermute(value, ('dp', 'fsdp'), route)]
    ppermute x70 -> x80, starting transfers between devices: 71.4 us -> 87.7 us  [swap(): return lax.ppermute(value, ('dp', 'fsdp'), route)]
    slice x4 -> x0, local copies, waits for them, and re-layouts: 4.27 us -> none  [the longest x2 2.18 us: diagonal(): late = swap(one[two:], grid.second)]
    unnamed x89 -> x76, local copies, waits for them, and re-layouts: 11.4 us -> 14.4 us
  transfers between devices with their start and end apart: 71 -> 81, of which waited for: 27 -> 28; matrix products, arithmetic and copies ran while one was open for 2% -> 1% of each run, Pallas kernels for 14% -> 14%
where the time goes in v6:
time: 375 us; the launch traced here: 369 us
  waiting for transfers between devices  171 us (46%)
  starting transfers between devices  87.8 us (23%)
  Pallas kernels  74 us (20%)
  between operations  15.7 us (4%)
  local copies, waits for them, and re-layouts  15.5 us (4%)
  other arithmetic  4.82 us (1%)
    ppermute x80, waiting for transfers between devices, swap(): return lax.ppermute(value, ('dp', 'fsdp'), route)  171 us
    ppermute x80, starting transfers between devices, swap(): return lax.ppermute(value, ('dp', 'fsdp'), route)  87.7 us
    pallas_call x2, Pallas kernels, attention_backward_kernel(): pl.pallas_call(body, in_specs=[SMEM_SPEC] + [VMEM_SPEC] * 4 + [ANY_SPEC],...  15.3 us
    unnamed x76, local copies, waits for them, and re-layouts  14.4 us
    pallas_call x2, Pallas kernels, ffn_forward(): pl.pallas_call(body, grid=(steps,), in_specs=[fixed((tokens, D)), fixed((...  13.5 us
    pallas_call x3, Pallas kernels, matrix_terms(): pl.pallas_call(body, grid=(wide // tile,), in_specs=in_specs, out_specs=[...  11.9 us
    pallas_call x2, Pallas kernels, up_backward_kernel(): pl.pallas_call(body, grid=(steps,), in_specs=[fixed((tokens, D)), fixed((...  9.38 us
    pallas_call x2, Pallas kernels, attention_forward(): pl.pallas_call(body, in_specs=[SMEM_SPEC, VMEM_SPEC, ANY_SPEC], out_specs...  7.85 us
  transfers between devices with their start and end apart: 81, of which 28 were waited for; matrix products, arithmetic and copies ran while one was open for 1% of the time, Pallas kernels for 14%

profile of v6, /device:TPU:0, one launch (start us, length us, event | category | flops | bytes accessed | tf_op | source)
XLA Modules:
  0.0 369.2 jit_solution(4112139379395215631)
XLA Ops:
  14.1 3.1 collective-permute-start
  17.3 3.9 %collective-permute-done = bf16[24,3200]{1,0:T(8,128)(2,1)S(1)} collective-permute-done((bf16[24,3200]{1,0:T(8,128)(2,1)S(1)}, bf16[24,3200]{1,0:T(8,128)(2,1)S(1)}, u32[]{:S(2)}, u32[]{:S(2)}) %collective-permute-start) | collective-permute-done | bytes 153632 | tf_op jit(solution)/shard_map/ppermute | solution.py:275
  21.2 1.8 collective-permute-start.2
  23.7 8.7 %collective-permute-done.2 = bf16[24,6144]{1,0:T(8,128)(2,1)S(1)} collective-permute-done((bf16[24,6144]{1,0:T(8,128)(2,1)S(1)}, bf16[24,6144]{1,0:T(8,128)(2,1)S(1)}, u32[]{:S(2)}, u32[]{:S(2)}) %collective-permute-start.2) | collective-permute-done | bytes 294944 | tf_op jit(solution)/shard_map/ppermute | solution.py:275
  32.5 1.3 collective-permute-start.3
  35.2 14.8 %collective-permute-done.3 = bf16[48,3200]{1,0:T(8,128)(2,1)S(1)} collective-permute-done((bf16[48,3200]{1,0:T(8,128)(2,1)S(1)}, bf16[48,3200]{1,0:T(8,128)(2,1)S(1)}, u32[]{:S(2)}, u32[]{:S(2)}) %collective-permute-start.3) | collective-permute-done | bytes 307232 | tf_op jit(solution)/shard_map/ppermute | solution.py:275
  50.0 1.3 collective-permute-start.7
  51.3 1.6 collective-permute-start.6
  52.9 1.5 collective-permute-start.12
  55.4 32.9 %collective-permute-done.7 = bf16[48,6144]{1,0:T(8,128)(2,1)S(1)} collective-permute-done((bf16[48,6144]{1,0:T(8,128)(2,1)S(1)}, bf16[48,6144]{1,0:T(8,128)(2,1)S(1)}, u32[]{:S(2)}, u32[]{:S(2)}) %collective-permute-start.7) | collective-permute-done | bytes 589856 | tf_op jit(solution)/shard_map/ppermute | solution.py:275
  89.2 1.6 collective-permute-start.11
  90.9 11.1 %collective-permute-done.10 = bf16[48,3200]{1,0:T(8,128)(2,1)S(1)} collective-permute-done((bf16[48,3200]{1,0:T(8,128)(2,1)S(1)}, bf16[48,3200]{1,0:T(8,128)(2,1)S(1)}, u32[]{:S(2)}, u32[]{:S(2)}) %collective-permute-start.10) | collective-permute-done | bytes 307232 | tf_op jit(solution)/shard_map/ppermute | solution.py:275
  102.0 4.2 %collective-permute-done.11 = bf16[48,3200]{1,0:T(8,128)(2,1)} collective-permute-done((bf16[48,3200]{1,0:T(8,128)(2,1)}, bf16[48,3200]{1,0:T(8,128)(2,1)}, u32[]{:S(2)}, u32[]{:S(2)}) %collective-permute-start.11) | collective-permute-done | bytes 307232 | tf_op jit(solution)/shard_map/ppermute | solution.py:275
  108.0 13.0 %collective-permute-done.24 = bf16[48,6144]{1,0:T(8,128)(2,1)S(1)} collective-permute-done((bf16[48,6144]{1,0:T(8,128)(2,1)S(1)}, bf16[48,6144]{1,0:T(8,128)(2,1)S(1)}, u32[]{:S(2)}, u32[]{:S(2)}) %collective-permute-start.24) | collective-permute-done | bytes 589856 | tf_op jit(solution)/shard_map/ppermute | solution.py:275
  123.6 1.7 collective-permute-start.8
  125.2 1.3 collective-permute-start.25
  131.3 2.1 shard_map.313
  133.4 4.0 %shard_map.314 = (bf16[256,768]{1,0:T(8,128)(2,1)S(1)}, bf16[256,2304]{1,0:T(8,128)(2,1)S(1)}, bf16[256,768]{1,0:T(8,128)(2,1)S(1)}, f32[256,768]{1,0:T(8,128)S(1)}, f32[8,768]{1,0:T(8,128)S(1)}) custom-call(s32[1]{0:T(128)S(6)} %copy.49.length_ref, f32[256,768]{1,0:T(8,128)S(1)} %bitcast_convert_fusion.hidden_ref, bf16[768,3200]{1,0:T(8,128)(2,1)S(1)} %bitcast.96), custom_call_target="tpu_custom_call" | custom-call | flops 1048576 | bytes 65536 | tf_op jit(solution)/shard_map/pallas_call | solution.py:451
  140.0 1.7 collective-permute-start.22
  141.6 1.3 collective-permute-start.23
  142.9 5.4 %collective-permute-done.25 = bf16[48,6144]{1,0:T(8,128)(2,1)} collective-permute-done((bf16[48,6144]{1,0:T(8,128)(2,1)S(1)}, bf16[48,6144]{1,0:T(8,128)(2,1)}, u32[]{:S(2)}, u32[]{:S(2)}) %collective-permute-start.25) | collective-permute-done | bytes 589856 | tf_op jit(solution)/shard_map/ppermute | solution.py:275
  148.8 7.7 %collective-permute-done.22 = bf16[48,6144]{1,0:T(8,128)(2,1)} collective-permute-done((bf16[48,6144]{1,0:T(8,128)(2,1)}, bf16[48,6144]{1,0:T(8,128)(2,1)}, u32[]{:S(2)}, u32[]{:S(2)}) %collective-permute-start.22) | collective-permute-done | bytes 589856 | tf_op jit(solution)/shard_map/ppermute | solution.py:275
  156.5 1.7 collective-permute-done.23
  158.9 2.4 collective-permute-done.27
  163.0 3.1 shard_map.315
  166.1 6.9 %shard_map.316 = (bf16[256,768]{1,0:T(8,128)(2,1)S(1)}, bf16[256,3072]{1,0:T(8,128)(2,1)}, bf16[256,3072]{1,0:T(8,128)(2,1)S(1)}, f32[256,768]{1,0:T(8,128)S(1)}, f32[256,768]{1,0:T(8,128)S(1)}) custom-call(f32[256,768]{1,0:T(8,128)S(1)} %get-tuple-element.282.sum_ref, f32[8,768]{1,0:T(8,128)S(1)} %copy-done.15, bf16[768,6144]{1,0:T(8,128)(2,1)S(1)} %bitcast.92, ...), custom_call_target="tpu_custom_call" | custom-call | flops 1048576 | bytes 65536 | tf_op jit(solution)/shard_map/pallas_call | solution.py:506
  173.1 3.9 %shard_map.317 = (bf16[256,768]{1,0:T(8,128)(2,1)S(1)}, bf16[256,2304]{1,0:T(8,128)(2,1)S(1)}, bf16[256,768]{1,0:T(8,128)(2,1)S(1)}, f32[256,768]{1,0:T(8,128)S(1)}, f32[8,768]{1,0:T(8,128)S(1)}) custom-call(s32[1]{0:T(128)S(6)} %copy.49.length_ref, f32[256,768]{1,0:T(8,128)S(1)} %get-tuple-element.288.hidden_ref, bf16[768,9344]{1,0:T(8,128)(2,1)S(1)} %bitcast.91), custom_call_target="tpu_custom_call" | custom-call | flops 1048576 | bytes 65536 | tf_op jit(solution)/shard_map/pallas_call | solution.py:451
  176.9 6.6 %shard_map.318 = (bf16[256,768]{1,0:T(8,128)(2,1)S(1)}, bf16[256,3072]{1,0:T(8,128)(2,1)S(1)}, bf16[256,3072]{1,0:T(8,128)(2,1)S(1)}, f32[256,768]{1,0:T(8,128)S(1)}, f32[256,768]{1,0:T(8,128)S(1)}) custom-call(f32[256,768]{1,0:T(8,128)S(1)} %get-tuple-element.290.sum_ref, f32[8,768]{1,0:T(8,128)S(1)} %get-tuple-element.291.gain_ref, ...), custom_call_target="tpu_custom_call" | custom-call | flops 1048576 | bytes 65536 | tf_op jit(solution)/shard_map/pallas_call | solution.py:506
  187.3 2.4 shard_map.321
  189.8 4.8 %shard_map.322 = (bf16[256,3072]{1,0:T(8,128)(2,1)S(1)}, f32[256,768]{1,0:T(8,128)S(1)}) custom-call(f32[256,768]{1,0:T(8,128)S(1)} %get-tuple-element.310.grad_ref, bf16[256,768]{1,0:T(8,128)(2,1)S(1)} %get-tuple-element.311.refs_0_.low_ref, bf16[256,3072]{1,0:T(8,128)(2,1)S(1)} %get-tuple-element.312.slope_ref, bf16[768,9344]{1,0:T(8,128)(2,1)S(1)} %bitcast.91, ...), custom_call_target="tpu_custom_call" | custom-call | flops 1048576 | bytes 65536 | tf_op jit(solution)/shard_map/pallas_call | solution.py:571
  195.7 1.3 collective-permute-start.37
  197.5 7.2 %shard_map.323 = (bf16[256,3072]{1,0:T(8,128)(2,1)S(1)}, f32[256,768]{1,0:T(8,128)S(1)}, f32[1,768]{1,0:T(1,128)S(1)}) custom-call(s32[1]{0:T(128)S(6)} %copy.49.length_ref, f32[256,768]{1,0:T(8,128)S(1)} %get-tuple-element.313.grad_ref, f32[256,768]{1,0:T(8,128)S(1)} %get-tuple-element.290.sum_ref, f32[8,768]{1,0:T(8,128)S(1)} %get-tuple-element.291.gain_ref, ...), custom_call_target="tpu_custom_call" | custom-call | flops 1048576 | bytes 65536 | tf_op jit(solution)/shard_map/pallas_call | solution.py:626
  204.8 2.9 shard_map.325
  207.7 3.2 collective-permute-done.36.one.refs_1_
  213.6 1.5 collective-permute-start.46
  217.1 4.6 %shard_map.328 = (bf16[256,3072]{1,0:T(8,128)(2,1)S(1)}, f32[256,768]{1,0:T(8,128)S(1)}) custom-call(f32[256,768]{1,0:T(8,128)S(1)} %get-tuple-element.343.grad_ref, bf16[256,768]{1,0:T(8,128)(2,1)S(1)} %get-tuple-element.344.low_ref.refs_0_, bf16[256,3072]{1,0:T(8,128)(2,1)S(1)} %get-tuple-element.345.slope_ref, bf16[768,6144]{1,0:T(8,128)(2,1)S(1)} %bitcast.94, ...), custom_call_target="tpu_custom_call" | custom-call | flops 1048576 | bytes 65536 | tf_op jit(solution)/shard_map/pallas_call | solution.py:571
  221.8 1.4 shard_map.330
  223.2 11.9 %collective-permute-done.43.refs_3_ = bf16[48,3072]{1,0:T(8,128)(2,1)S(1)} collective-permute-done((bf16[48,3072]{1,0:T(8,128)(2,1)S(1)}, bf16[48,3072]{1,0:T(8,128)(2,1)S(1)}, u32[]{:S(2)}, u32[]{:S(2)}) %collective-permute-start.43) | collective-permute-done | bytes 294944 | tf_op jit(solution)/shard_map/ppermute | solution.py:275
  241.4 8.1 %shard_map.332 = (bf16[256,3072]{1,0:T(8,128)(2,1)S(1)}, f32[256,768]{1,0:T(8,128)}, f32[1,768]{1,0:T(1,128)S(1)}) custom-call(s32[1]{0:T(128)S(6)} %copy.49.length_ref, f32[256,768]{1,0:T(8,128)S(1)} %get-tuple-element.376.grad_ref, f32[256,768]{1,0:T(8,128)S(1)} %get-tuple-element.282.sum_ref, f32[8,768]{1,0:T(8,128)S(1)} %copy-done.15, ...), custom_call_target="tpu_custom_call" | custom-call | flops 1048576 | bytes 65536 | tf_op jit(solution)/shard_map/pallas_call | solution.py:626
  249.5 6.6 %shard_map.334 = (bf16[96,6144]{1,0:T(8,128)(2,1)S(1)}, bf16[96,6144]{1,0:T(8,128)(2,1)S(1)}, bf16[48,6144]{1,0:T(8,128)(2,1)S(1)}, bf16[48,6144]{1,0:T(8,128)(2,1)S(1)}, bf16[96,6144]{1,0:T(8,128)(2,1)S(1)}) custom-call(bf16[384,384]{1,0:T(8,128)(2,1)S(1)} %get-tuple-element.381.ga.refs_0_, bf16[384,384]{1,0:T(8,128)(2,1)S(1)} %collective-permute-done.47.gb.refs_1_, ...), custom_call_target="tpu_custom_call" | custom-call | flops 1048576 | bytes 65536 | tf_op jit(solution)/shard_map/pallas_call | solution.py:681
  256.1 3.9 %collective-permute-done.49.refs_8_ = bf16[48,3072]{1,0:T(8,128)(2,1)S(1)} collective-permute-done((bf16[48,3072]{1,0:T(8,128)(2,1)S(1)}, bf16[48,3072]{1,0:T(8,128)(2,1)S(1)}, u32[]{:S(2)}, u32[]{:S(2)}) %collective-permute-start.49) | collective-permute-done | bytes 294944 | tf_op jit(solution)/shard_map/ppermute | solution.py:275
  262.7 5.1 %collective-permute-start.56 = (bf16[24,6144]{1,0:T(8,128)(2,1)S(1)}, bf16[24,6144]{1,0:T(8,128)(2,1)S(1)}, u32[]{:S(2)}, u32[]{:S(2)}) collective-permute-start(bf16[24,6144]{1,0:T(8,128)(2,1)S(1)} %get-tuple-element.406), channel_id=1, source_target_pairs={{0,2},{1,3},{2,0},{3,1},{4,6},{5,7},{6,4},{7,5},{8,10},{9,11},{10,... | collective-permute-start | bytes 884744 | tf_op jit(solution)/shard_map/ppermute | solution.py:275
  267.8 2.8 collective-permute-start.57
  270.7 11.1 %collective-permute-done.56 = bf16[24,6144]{1,0:T(8,128)(2,1)S(1)} collective-permute-done((bf16[24,6144]{1,0:T(8,128)(2,1)S(1)}, bf16[24,6144]{1,0:T(8,128)(2,1)S(1)}, u32[]{:S(2)}, u32[]{:S(2)}) %collective-permute-start.56) | collective-permute-done | bytes 294944 | tf_op jit(solution)/shard_map/ppermute | solution.py:275
  282.8 1.4 collective-permute-start.60
  284.2 4.6 %collective-permute-start.58 = (bf16[24,6144]{1,0:T(8,128)(2,1)S(1)}, bf16[24,6144]{1,0:T(8,128)(2,1)S(1)}, u32[]{:S(2)}, u32[]{:S(2)}) collective-permute-start(bf16[24,6144]{1,0:T(8,128)(2,1)S(1)} %get-tuple-element.408), channel_id=1, source_target_pairs={{0,6},{1,7},{2,4},{3,5},{4,2},{5,3},{6,0},{7,1},{8,14},{9,15},{10,... | collective-permute-start | bytes 884744 | tf_op jit(solution)/shard_map/ppermute | solution.py:275
  288.7 1.4 shard_map.338
  290.1 4.2 %collective-permute-done.58 = bf16[24,6144]{1,0:T(8,128)(2,1)S(1)} collective-permute-done((bf16[24,6144]{1,0:T(8,128)(2,1)S(1)}, bf16[24,6144]{1,0:T(8,128)(2,1)S(1)}, u32[]{:S(2)}, u32[]{:S(2)}) %collective-permute-start.58) | collective-permute-done | bytes 294944 | tf_op jit(solution)/shard_map/ppermute | solution.py:275
  295.7 5.2 %collective-permute-start.65 = (bf16[24,3200]{1,0:T(8,128)(2,1)S(1)}, bf16[24,3200]{1,0:T(8,128)(2,1)S(1)}, u32[]{:S(2)}, u32[]{:S(2)}) collective-permute-start(bf16[24,3200]{1,0:T(8,128)(2,1)S(1)} %get-tuple-element.437), channel_id=1, source_target_pairs={{0,2},{1,3},{2,0},{3,1},{4,6},{5,7},{6,4},{7,5},{8,10},{9,11},{10,... | collective-permute-start | bytes 460808 | tf_op jit(solution)/shard_map/ppermute | solution.py:275
  300.8 1.2 collective-permute-start.66
  302.9 1.4 collective-permute-start.67
  304.5 1.6 collective-permute-start.68
  307.4 1.4 collective-permute-start.73
  308.8 7.3 %collective-permute-start.74 = (bf16[96,3200]{1,0:T(8,128)(2,1)S(1)}, bf16[96,3200]{1,0:T(8,128)(2,1)S(1)}, u32[]{:S(2)}, u32[]{:S(2)}) collective-permute-start(bf16[96,3200]{1,0:T(8,128)(2,1)S(1)} %get-tuple-element.461), channel_id=1, source_target_pairs={{0,1},{1,0},{2,3},{3,2},{4,5},{5,4},{6,7},{7,6},{8,24},{9,25},{10,... | collective-permute-start | bytes 1843208 | tf_op jit(solution)/shard_map/ppermute | solution.py:275
  316.3 4.5 %collective-permute-done.68.refs_3_ = bf16[48,6144]{1,0:T(8,128)(2,1)S(1)} collective-permute-done((bf16[48,6144]{1,0:T(8,128)(2,1)S(1)}, bf16[48,6144]{1,0:T(8,128)(2,1)S(1)}, u32[]{:S(2)}, u32[]{:S(2)}) %collective-permute-start.68) | collective-permute-done | bytes 589856 | tf_op jit(solution)/shard_map/ppermute | solution.py:275
  320.8 1.6 collective-permute-done.69.refs_4_
  323.9 1.9 collective-permute-start.71
  325.8 1.5 collective-permute-start.72
  327.2 5.5 %collective-permute-done.73.one.refs_1_ = bf16[96,3200]{1,0:T(8,128)(2,1)S(1)} collective-permute-done((bf16[96,3200]{1,0:T(8,128)(2,1)S(1)}, bf16[96,3200]{1,0:T(8,128)(2,1)S(1)}, u32[]{:S(2)}, u32[]{:S(2)}) %collective-permute-start.73) | collective-permute-done | bytes 614432 | tf_op jit(solution)/shard_map/ppermute | solution.py:275
  332.9 1.8 collective-permute-start.75
  336.0 8.9 %collective-permute-done.71 = bf16[24,6144]{1,0:T(8,128)(2,1)S(1)} collective-permute-done((bf16[24,6144]{1,0:T(8,128)(2,1)S(1)}, bf16[24,6144]{1,0:T(8,128)(2,1)S(1)}, u32[]{:S(2)}, u32[]{:S(2)}) %collective-permute-start.71) | collective-permute-done | bytes 294944 | tf_op jit(solution)/shard_map/ppermute | solution.py:275
  345.1 3.8 %collective-permute-start.77 = (bf16[24,3200]{1,0:T(8,128)(2,1)S(1)}, bf16[24,3200]{1,0:T(8,128)(2,1)S(1)}, u32[]{:S(2)}, u32[]{:S(2)}) collective-permute-start(bf16[24,3200]{1,0:T(8,128)(2,1)S(1)} %get-tuple-element.472), channel_id=1, source_target_pairs={{0,2},{1,3},{2,0},{3,1},{4,6},{5,7},{6,4},{7,5},{8,10},{9,11},{10,... | collective-permute-start | bytes 460808 | tf_op jit(solution)/shard_map/ppermute | solution.py:275
  349.9 1.4 collective-permute-start.79
  353.3 7.3 %collective-permute-done.78.refs_2_ = bf16[24,3200]{1,0:T(8,128)(2,1)S(1)} collective-permute-done((bf16[24,3200]{1,0:T(8,128)(2,1)S(1)}, bf16[24,3200]{1,0:T(8,128)(2,1)S(1)}, u32[]{:S(2)}, u32[]{:S(2)}) %collective-permute-start.78) | collective-permute-done | bytes 153632 | tf_op jit(solution)/shard_map/ppermute | solution.py:275
  (239 shorter events, 56.8 us)
Async XLA Ops:
  7.2 141.6 %all-gather.2.cloned.1.call-start = ((), (), s32[]{:S(2)}) async-start(), calls=%async_computation | async-start | bytes 14800896 | tf_op jit(solution)/shard_map/all_gather | solution.py:57
  21.2 11.3 %collective-permute-start.2 = (bf16[24,6144]{1,0:T(8,128)(2,1)S(1)}, bf16[24,6144]{1,0:T(8,128)(2,1)S(1)}, u32[]{:S(2)}, u32[]{:S(2)}) collective-permute-start(bf16[24,6144]{1,0:T(8,128)(2,1)S(1)} %pad_maximum_fusion.4), channel_id=1, source_target_pairs={{0,2},{1,3},{2,0},{3,1},{4,6},{5,7},{6,4},{7,5},{8,10},{9,11},{10,... | collective-permute-start | bytes 884744 | tf_op jit(solution)/shard_map/ppermute | solution.py:275
  23.0 9.5 %collective-permute-start.1 = (bf16[48,3200]{1,0:T(8,128)(2,1)S(1)}, bf16[48,3200]{1,0:T(8,128)(2,1)S(1)}, u32[]{:S(2)}, u32[]{:S(2)}) collective-permute-start(bf16[48,3200]{1,0:T(8,128)(2,1)S(1)} %pad_maximum_fusion.3), channel_id=1, source_target_pairs={{2,4},{3,5},{4,2},{5,3},{10,12},{11,13},{12,10},{13,11},{18,20},{1... | collective-permute-start | bytes 921608 | tf_op jit(solution)/shard_map/ppermute | solution.py:275
  32.5 17.4 %collective-permute-start.3 = (bf16[48,3200]{1,0:T(8,128)(2,1)S(1)}, bf16[48,3200]{1,0:T(8,128)(2,1)S(1)}, u32[]{:S(2)}, u32[]{:S(2)}) collective-permute-start(bf16[48,3200]{1,0:T(8,128)(2,1)S(1)} %collective-permute-done.1), channel_id=1, source_target_pairs={{2,0},{3,1},{4,6},{5,7},{10,8},{11,9},{12,14},{13,15},{18,16},{19,... | collective-permute-start | bytes 921608 | tf_op jit(solution)/shard_map/ppermute | solution.py:275
  34.3 15.6 %collective-permute-start.4 = (bf16[48,6144]{1,0:T(8,128)(2,1)S(1)}, bf16[48,6144]{1,0:T(8,128)(2,1)S(1)}, u32[]{:S(2)}, u32[]{:S(2)}) collective-permute-start(bf16[48,6144]{1,0:T(8,128)(2,1)S(1)} %pad_maximum_fusion), channel_id=1, source_target_pairs={{2,4},{3,5},{4,2},{5,3},{10,12},{11,13},{12,10},{13,11},{18,20},{1... | collective-permute-start | bytes 1769480 | tf_op jit(solution)/shard_map/ppermute | solution.py:275
  50.0 38.3 %collective-permute-start.7 = (bf16[48,6144]{1,0:T(8,128)(2,1)S(1)}, bf16[48,6144]{1,0:T(8,128)(2,1)S(1)}, u32[]{:S(2)}, u32[]{:S(2)}) collective-permute-start(bf16[48,6144]{1,0:T(8,128)(2,1)S(1)} %collective-permute-done.4), channel_id=1, source_target_pairs={{2,0},{3,1},{4,6},{5,7},{10,8},{11,9},{12,14},{13,15},{18,16},{19,... | collective-permute-start | bytes 1769480 | tf_op jit(solution)/shard_map/ppermute | solution.py:275
  51.3 37.1 %collective-permute-start.6 = (bf16[48,3200]{1,0:T(8,128)(2,1)S(1)}, bf16[48,3200]{1,0:T(8,128)(2,1)S(1)}, u32[]{:S(2)}, u32[]{:S(2)}) collective-permute-start(bf16[48,3200]{1,0:T(8,128)(2,1)S(1)} %pad_maximum_fusion.3), channel_id=1, source_target_pairs={{0,1},{1,0},{2,3},{3,2},{4,5},{5,4},{6,7},{7,6},{8,24},{9,25},{10,... | collective-permute-start | bytes 921608 | tf_op jit(solution)/shard_map/ppermute | solution.py:275
  52.9 38.0 %collective-permute-start.12 = (bf16[48,3200]{1,0:T(8,128)(2,1)S(1)}, bf16[48,3200]{1,0:T(8,128)(2,1)}, u32[]{:S(2)}, u32[]{:S(2)}) collective-permute-start(bf16[48,3200]{1,0:T(8,128)(2,1)S(1)} %pad_maximum_fusion.3), channel_id=1, source_target_pairs={{0,16},{1,17},{2,18},{3,19},{4,20},{5,21},{6,22},{7,23},{8,9},{9,8... | collective-permute-start | bytes 921608 | tf_op jit(solution)/shard_map/ppermute | solution.py:275
  54.3 34.0 %collective-permute-start.5 = (bf16[48,3200]{1,0:T(8,128)(2,1)S(1)}, bf16[48,3200]{1,0:T(8,128)(2,1)}, u32[]{:S(2)}, u32[]{:S(2)}) collective-permute-start(bf16[48,3200]{1,0:T(8,128)(2,1)S(1)} %broadcast_select_fusion.1), channel_id=1, source_target_pairs={{0,16},{1,17},{2,18},{3,19},{4,20},{5,21},{6,22},{7,23},{8,9},{9,8... | collective-permute-start | bytes 921608 | tf_op jit(solution)/shard_map/ppermute | solution.py:275
  54.9 36.0 %collective-permute-start.13 = (bf16[48,3200]{1,0:T(8,128)(2,1)S(1)}, bf16[48,3200]{1,0:T(8,128)(2,1)}, u32[]{:S(2)}, u32[]{:S(2)}) collective-permute-start(bf16[48,3200]{1,0:T(8,128)(2,1)S(1)} %broadcast_select_fusion.1), channel_id=1, source_target_pairs={{0,1},{1,0},{2,3},{3,2},{4,5},{5,4},{6,7},{7,6},{8,24},{9,25},{10,... | collective-permute-start | bytes 921608 | tf_op jit(solution)/shard_map/ppermute | solution.py:275
  88.4 13.6 %collective-permute-start.10 = (bf16[48,3200]{1,0:T(8,128)(2,1)S(1)}, bf16[48,3200]{1,0:T(8,128)(2,1)S(1)}, u32[]{:S(2)}, u32[]{:S(2)}) collective-permute-start(bf16[48,3200]{1,0:T(8,128)(2,1)S(1)} %collective-permute-done.6), channel_id=1, source_target_pairs={{0,16},{1,17},{2,18},{3,19},{4,20},{5,21},{6,22},{7,23},{8,9},{9,8... | collective-permute-start | bytes 921608 | tf_op jit(solution)/shard_map/ppermute | solution.py:275
  89.2 17.0 %collective-permute-start.11 = (bf16[48,3200]{1,0:T(8,128)(2,1)}, bf16[48,3200]{1,0:T(8,128)(2,1)}, u32[]{:S(2)}, u32[]{:S(2)}) collective-permute-start(bf16[48,3200]{1,0:T(8,128)(2,1)} %collective-permute-done.5), channel_id=1, source_target_pairs={{0,1},{1,0},{2,3},{3,2},{4,5},{5,4},{6,7},{7,6},{8,24},{9,25},{10,... | collective-permute-start | bytes 921608 | tf_op jit(solution)/shard_map/ppermute | solution.py:275
  90.8 30.1 %collective-permute-start.24 = (bf16[48,6144]{1,0:T(8,128)(2,1)S(1)}, bf16[48,6144]{1,0:T(8,128)(2,1)S(1)}, u32[]{:S(2)}, u32[]{:S(2)}) collective-permute-start(bf16[48,6144]{1,0:T(8,128)(2,1)S(1)} %pad_maximum_fusion), channel_id=1, source_target_pairs={{0,16},{1,17},{2,18},{3,19},{4,20},{5,21},{6,22},{7,23},{8,9},{9,8... | collective-permute-start | bytes 1769480 | tf_op jit(solution)/shard_map/ppermute | solution.py:275
  106.2 15.5 %collective-permute-start.14 = (bf16[48,3200]{1,0:T(8,128)(2,1)S(1)}, bf16[48,3200]{1,0:T(8,128)(2,1)S(1)}, u32[]{:S(2)}, u32[]{:S(2)}) collective-permute-start(bf16[48,3200]{1,0:T(8,128)(2,1)S(1)} %collective-permute-done.10), channel_id=1, source_target_pairs={{0,8},{1,9},{2,10},{3,11},{4,12},{5,13},{6,14},{7,15},{8,0},{9,1},... | collective-permute-start | bytes 921608 | tf_op jit(solution)/shard_map/ppermute | solution.py:275
  106.9 16.1 %collective-permute-start.15 = (bf16[48,3200]{1,0:T(8,128)(2,1)}, bf16[48,3200]{1,0:T(8,128)(2,1)}, u32[]{:S(2)}, u32[]{:S(2)}) collective-permute-start(bf16[48,3200]{1,0:T(8,128)(2,1)} %collective-permute-done.11), channel_id=1, source_target_pairs={{0,8},{1,9},{2,10},{3,11},{4,12},{5,13},{6,14},{7,15},{8,0},{9,1},... | collective-permute-start | bytes 921608 | tf_op jit(solution)/shard_map/ppermute | solution.py:275
  107.4 16.1 %collective-permute-start.16 = (bf16[48,3200]{1,0:T(8,128)(2,1)}, bf16[48,3200]{1,0:T(8,128)(2,1)}, u32[]{:S(2)}, u32[]{:S(2)}) collective-permute-start(bf16[48,3200]{1,0:T(8,128)(2,1)} %collective-permute-done.12), channel_id=1, source_target_pairs={{0,8},{1,9},{2,10},{3,11},{4,12},{5,13},{6,14},{7,15},{8,0},{9,1},... | collective-permute-start | bytes 921608 | tf_op jit(solution)/shard_map/ppermute | solution.py:275
  107.5 17.8 %collective-permute-start.17 = (bf16[48,3200]{1,0:T(8,128)(2,1)}, bf16[48,3200]{1,0:T(8,128)(2,1)}, u32[]{:S(2)}, u32[]{:S(2)}) collective-permute-start(bf16[48,3200]{1,0:T(8,128)(2,1)} %collective-permute-done.5), channel_id=1, source_target_pairs={{0,8},{1,9},{2,10},{3,11},{4,12},{5,13},{6,14},{7,15},{8,0},{9,1},... | collective-permute-start | bytes 921608 | tf_op jit(solution)/shard_map/ppermute | solution.py:275
  123.0 17.0 %collective-permute-start.9 = (bf16[48,6144]{1,0:T(8,128)(2,1)S(1)}, bf16[48,6144]{1,0:T(8,128)(2,1)}, u32[]{:S(2)}, u32[]{:S(2)}) collective-permute-start(bf16[48,6144]{1,0:T(8,128)(2,1)S(1)} %pad_maximum_fusion), channel_id=1, source_target_pairs={{0,1},{1,0},{2,3},{3,2},{4,5},{5,4},{6,7},{7,6},{8,24},{9,25},{10,... | collective-permute-start | bytes 1769480 | tf_op jit(solution)/shard_map/ppermute | solution.py:275
  123.6 16.4 %collective-permute-start.8 = (bf16[48,6144]{1,0:T(8,128)(2,1)S(1)}, bf16[48,6144]{1,0:T(8,128)(2,1)}, u32[]{:S(2)}, u32[]{:S(2)}) collective-permute-start(bf16[48,6144]{1,0:T(8,128)(2,1)S(1)} %broadcast_select_fusion), channel_id=1, source_target_pairs={{0,16},{1,17},{2,18},{3,19},{4,20},{5,21},{6,22},{7,23},{8,9},{9,8... | collective-permute-start | bytes 1769480 | tf_op jit(solution)/shard_map/ppermute | solution.py:275
  125.2 23.0 %collective-permute-start.25 = (bf16[48,6144]{1,0:T(8,128)(2,1)S(1)}, bf16[48,6144]{1,0:T(8,128)(2,1)}, u32[]{:S(2)}, u32[]{:S(2)}) collective-permute-start(bf16[48,6144]{1,0:T(8,128)(2,1)S(1)} %broadcast_select_fusion), channel_id=1, source_target_pairs={{0,1},{1,0},{2,3},{3,2},{4,5},{5,4},{6,7},{7,6},{8,24},{9,25},{10,... | collective-permute-start | bytes 1769480 | tf_op jit(solution)/shard_map/ppermute | solution.py:275
  129.0 19.8 %collective-permute-start.28 = (bf16[48,6144]{1,0:T(8,128)(2,1)}, bf16[48,6144]{1,0:T(8,128)(2,1)}, u32[]{:S(2)}, u32[]{:S(2)}) collective-permute-start(bf16[48,6144]{1,0:T(8,128)(2,1)} %copy-done.5), channel_id=1, source_target_pairs={{0,8},{1,9},{2,10},{3,11},{4,12},{5,13},{6,14},{7,15},{8,0},{9,1},... | collective-permute-start | bytes 1769480 | tf_op jit(solution)/shard_map/ppermute | solution.py:275
  140.0 16.6 %collective-permute-start.22 = (bf16[48,6144]{1,0:T(8,128)(2,1)}, bf16[48,6144]{1,0:T(8,128)(2,1)}, u32[]{:S(2)}, u32[]{:S(2)}) collective-permute-start(bf16[48,6144]{1,0:T(8,128)(2,1)} %collective-permute-done.9), channel_id=1, source_target_pairs={{0,16},{1,17},{2,18},{3,19},{4,20},{5,21},{6,22},{7,23},{8,9},{9,8... | collective-permute-start | bytes 1769480 | tf_op jit(solution)/shard_map/ppermute | solution.py:275
  141.6 16.7 %collective-permute-start.23 = (bf16[48,6144]{1,0:T(8,128)(2,1)}, bf16[48,6144]{1,0:T(8,128)(2,1)}, u32[]{:S(2)}, u32[]{:S(2)}) collective-permute-start(bf16[48,6144]{1,0:T(8,128)(2,1)} %collective-permute-done.8), channel_id=1, source_target_pairs={{0,1},{1,0},{2,3},{3,2},{4,5},{5,4},{6,7},{7,6},{8,24},{9,25},{10,... | collective-permute-start | bytes 1769480 | tf_op jit(solution)/shard_map/ppermute | solution.py:275
  148.3 10.0 %collective-permute-start.31 = (bf16[48,6144]{1,0:T(8,128)(2,1)}, bf16[48,6144]{1,0:T(8,128)(2,1)}, u32[]{:S(2)}, u32[]{:S(2)}) collective-permute-start(bf16[48,6144]{1,0:T(8,128)(2,1)} %collective-permute-done.25), channel_id=1, source_target_pairs={{0,8},{1,9},{2,10},{3,11},{4,12},{5,13},{6,14},{7,15},{8,0},{9,1},... | collective-permute-start | bytes 1769480 | tf_op jit(solution)/shard_map/ppermute | solution.py:275
  148.3 10.5 %collective-permute-start.29 = (bf16[48,6144]{1,0:T(8,128)(2,1)}, bf16[48,6144]{1,0:T(8,128)(2,1)}, u32[]{:S(2)}, u32[]{:S(2)}) collective-permute-start(bf16[48,6144]{1,0:T(8,128)(2,1)} %collective-permute-done.8), channel_id=1, source_target_pairs={{0,8},{1,9},{2,10},{3,11},{4,12},{5,13},{6,14},{7,15},{8,0},{9,1},... | collective-permute-start | bytes 1769480 | tf_op jit(solution)/shard_map/ppermute | solution.py:275
  148.8 10.1 %collective-permute-start.30 = (bf16[48,6144]{1,0:T(8,128)(2,1)}, bf16[48,6144]{1,0:T(8,128)(2,1)S(1)}, u32[]{:S(2)}, u32[]{:S(2)}) collective-permute-start(bf16[48,6144]{1,0:T(8,128)(2,1)} %collective-permute-done.9), channel_id=1, source_target_pairs={{0,8},{1,9},{2,10},{3,11},{4,12},{5,13},{6,14},{7,15},{8,0},{9,1},... | collective-permute-start | bytes 1769480 | tf_op jit(solution)/shard_map/ppermute | solution.py:275
  186.5 10.4 %collective-permute-start.38 = (bf16[384,768]{1,0:T(8,128)(2,1)S(1)}, bf16[384,768]{1,0:T(8,128)(2,1)S(1)}, u32[]{:S(2)}, u32[]{:S(2)}) collective-permute-start(bf16[384,768]{1,0:T(8,128)(2,1)S(1)} %get-tuple-element.322), channel_id=1, source_target_pairs={{0,8},{1,9},{2,10},{3,11},{4,12},{5,13},{6,14},{7,15},{8,0},{9,1},... | collective-permute-start | bytes 1769480 | tf_op jit(solution)/shard_map/ppermute | solution.py:275
  194.9 16.0 %collective-permute-start.36 = (bf16[96,3072]{1,0:T(8,128)(2,1)S(1)}, bf16[96,3072]{1,0:T(8,128)(2,1)S(1)}, u32[]{:S(2)}, u32[]{:S(2)}) collective-permute-start(bf16[96,3072]{1,0:T(8,128)(2,1)S(1)} %get-tuple-element.305), channel_id=1, source_target_pairs={{0,16},{1,17},{2,18},{3,19},{4,20},{5,21},{6,22},{7,23},{8,9},{9,8... | collective-permute-start | bytes 1769480 | tf_op jit(solution)/shard_map/ppermute | solution.py:275
  195.7 15.2 %collective-permute-start.37 = (bf16[96,3072]{1,0:T(8,128)(2,1)S(1)}, bf16[96,3072]{1,0:T(8,128)(2,1)S(1)}, u32[]{:S(2)}, u32[]{:S(2)}) collective-permute-start(bf16[96,3072]{1,0:T(8,128)(2,1)S(1)} %get-tuple-element.306), channel_id=1, source_target_pairs={{0,1},{1,0},{2,3},{3,2},{4,5},{5,4},{6,7},{7,6},{8,24},{9,25},{10,... | collective-permute-start | bytes 1769480 | tf_op jit(solution)/shard_map/ppermute | solution.py:275
  196.9 7.8 %collective-permute-start.40 = (bf16[256,768]{1,0:T(8,128)(2,1)S(1)}, bf16[256,768]{1,0:T(8,128)(2,1)S(1)}, u32[]{:S(2)}, u32[]{:S(2)}) collective-permute-start(bf16[256,768]{1,0:T(8,128)(2,1)S(1)} %get-tuple-element.508), channel_id=1, source_target_pairs={{0,8},{1,9},{2,10},{3,11},{4,12},{5,13},{6,14},{7,15},{8,0},{9,1},... | collective-permute-start | bytes 1179656 | tf_op jit(solution)/shard_map/ppermute | solution.py:275
  196.9 7.8 %collective-permute-start.41 = (bf16[256,768]{1,0:T(8,128)(2,1)S(1)}, bf16[256,768]{1,0:T(8,128)(2,1)S(1)}, u32[]{:S(2)}, u32[]{:S(2)}) collective-permute-start(bf16[256,768]{1,0:T(8,128)(2,1)S(1)} %get-tuple-element.507), channel_id=1, source_target_pairs={{0,8},{1,9},{2,10},{3,11},{4,12},{5,13},{6,14},{7,15},{8,0},{9,1},... | collective-permute-start | bytes 1179656 | tf_op jit(solution)/shard_map/ppermute | solution.py:275
  212.9 22.2 %collective-permute-start.45 = (bf16[96,3072]{1,0:T(8,128)(2,1)S(1)}, bf16[96,3072]{1,0:T(8,128)(2,1)S(1)}, u32[]{:S(2)}, u32[]{:S(2)}) collective-permute-start(bf16[96,3072]{1,0:T(8,128)(2,1)S(1)} %get-tuple-element.336), channel_id=1, source_target_pairs={{0,16},{1,17},{2,18},{3,19},{4,20},{5,21},{6,22},{7,23},{8,9},{9,8... | collective-permute-start | bytes 1769480 | tf_op jit(solution)/shard_map/ppermute | solution.py:275
  213.6 21.5 %collective-permute-start.46 = (bf16[96,3072]{1,0:T(8,128)(2,1)S(1)}, bf16[96,3072]{1,0:T(8,128)(2,1)S(1)}, u32[]{:S(2)}, u32[]{:S(2)}) collective-permute-start(bf16[96,3072]{1,0:T(8,128)(2,1)S(1)} %get-tuple-element.337), channel_id=1, source_target_pairs={{0,1},{1,0},{2,3},{3,2},{4,5},{5,4},{6,7},{7,6},{8,24},{9,25},{10,... | collective-permute-start | bytes 1769480 | tf_op jit(solution)/shard_map/ppermute | solution.py:275
  215.2 19.9 %collective-permute-start.43 = (bf16[48,3072]{1,0:T(8,128)(2,1)S(1)}, bf16[48,3072]{1,0:T(8,128)(2,1)S(1)}, u32[]{:S(2)}, u32[]{:S(2)}) collective-permute-start(bf16[48,3072]{1,0:T(8,128)(2,1)S(1)} %get-tuple-element.333), channel_id=1, source_target_pairs={{0,16},{1,17},{2,18},{3,19},{4,20},{5,21},{6,22},{7,23},{8,9},{9,8... | collective-permute-start | bytes 884744 | tf_op jit(solution)/shard_map/ppermute | solution.py:275
  215.9 19.2 %collective-permute-start.44 = (bf16[48,3072]{1,0:T(8,128)(2,1)S(1)}, bf16[48,3072]{1,0:T(8,128)(2,1)S(1)}, u32[]{:S(2)}, u32[]{:S(2)}) collective-permute-start(bf16[48,3072]{1,0:T(8,128)(2,1)S(1)} %get-tuple-element.334), channel_id=1, source_target_pairs={{0,1},{1,0},{2,3},{3,2},{4,5},{5,4},{6,7},{7,6},{8,24},{9,25},{10,... | collective-permute-start | bytes 884744 | tf_op jit(solution)/shard_map/ppermute | solution.py:275
  217.1 23.2 %collective-permute-start.53 = (bf16[256,3072]{1,0:T(8,128)(2,1)}, bf16[256,3072]{1,0:T(8,128)(2,1)S(1)}, u32[]{:S(2)}, u32[]{:S(2)}) collective-permute-start(bf16[256,3072]{1,0:T(8,128)(2,1)} %get-tuple-element.383.refs_2_), channel_id=1, source_target_pairs={{0,8},{1,9},{2,10},{3,11},{4,12},{5,13},{6,14},{7,15},{8,0},{9,1},... | collective-permute-start | bytes 4718600 | tf_op jit(solution)/shard_map/ppermute | solution.py:275
  235.1 14.4 %collective-permute-start.55 = (bf16[256,3072]{1,0:T(8,128)(2,1)S(1)}, bf16[256,3072]{1,0:T(8,128)(2,1)S(1)}, u32[]{:S(2)}, u32[]{:S(2)}) collective-permute-start(bf16[256,3072]{1,0:T(8,128)(2,1)S(1)} %get-tuple-element.389.refs_6_), channel_id=1, source_target_pairs={{0,8},{1,9},{2,10},{3,11},{4,12},{5,13},{6,14},{7,15},{8,0},{9,1},... | collective-permute-start | bytes 4718600 | tf_op jit(solution)/shard_map/ppermute | solution.py:275
  236.9 23.0 %collective-permute-start.51 = (bf16[96,3200]{1,0:T(8,128)(2,1)S(1)}, bf16[96,3200]{1,0:T(8,128)(2,1)S(1)}, u32[]{:S(2)}, u32[]{:S(2)}) collective-permute-start(bf16[96,3200]{1,0:T(8,128)(2,1)S(1)} %get-tuple-element.371), channel_id=1, source_target_pairs={{0,16},{1,17},{2,18},{3,19},{4,20},{5,21},{6,22},{7,23},{8,9},{9,8... | collective-permute-start | bytes 1843208 | tf_op jit(solution)/shard_map/ppermute | solution.py:275
  237.7 22.3 %collective-permute-start.52 = (bf16[96,3200]{1,0:T(8,128)(2,1)S(1)}, bf16[96,3200]{1,0:T(8,128)(2,1)S(1)}, u32[]{:S(2)}, u32[]{:S(2)}) collective-permute-start(bf16[96,3200]{1,0:T(8,128)(2,1)S(1)} %get-tuple-element.372), channel_id=1, source_target_pairs={{0,1},{1,0},{2,3},{3,2},{4,5},{5,4},{6,7},{7,6},{8,24},{9,25},{10,... | collective-permute-start | bytes 1843208 | tf_op jit(solution)/shard_map/ppermute | solution.py:275
  239.4 20.5 %collective-permute-start.49 = (bf16[48,3072]{1,0:T(8,128)(2,1)S(1)}, bf16[48,3072]{1,0:T(8,128)(2,1)S(1)}, u32[]{:S(2)}, u32[]{:S(2)}) collective-permute-start(bf16[48,3072]{1,0:T(8,128)(2,1)S(1)} %get-tuple-element.368), channel_id=1, source_target_pairs={{0,16},{1,17},{2,18},{3,19},{4,20},{5,21},{6,22},{7,23},{8,9},{9,8... | collective-permute-start | bytes 884744 | tf_op jit(solution)/shard_map/ppermute | solution.py:275
  240.3 19.6 %collective-permute-start.50 = (bf16[48,3072]{1,0:T(8,128)(2,1)S(1)}, bf16[48,3072]{1,0:T(8,128)(2,1)S(1)}, u32[]{:S(2)}, u32[]{:S(2)}) collective-permute-start(bf16[48,3072]{1,0:T(8,128)(2,1)S(1)} %get-tuple-element.369), channel_id=1, source_target_pairs={{0,1},{1,0},{2,3},{3,2},{4,5},{5,4},{6,7},{7,6},{8,24},{9,25},{10,... | collective-permute-start | bytes 884744 | tf_op jit(solution)/shard_map/ppermute | solution.py:275
  259.9 24.2 %collective-permute-start.63 = (bf16[256,3072]{1,0:T(8,128)(2,1)S(1)}, bf16[256,3072]{1,0:T(8,128)(2,1)S(1)}, u32[]{:S(2)}, u32[]{:S(2)}) collective-permute-start(bf16[256,3072]{1,0:T(8,128)(2,1)S(1)} %get-tuple-element.422.ra), channel_id=1, source_target_pairs={{0,8},{1,9},{2,10},{3,11},{4,12},{5,13},{6,14},{7,15},{8,0},{9,1},... | collective-permute-start | bytes 4718600 | tf_op jit(solution)/shard_map/ppermute | solution.py:275
  260.0 35.4 %collective-permute-start.61 = (bf16[96,6144]{1,0:T(8,128)(2,1)S(1)}, bf16[96,6144]{1,0:T(8,128)(2,1)S(1)}, u32[]{:S(2)}, u32[]{:S(2)}) collective-permute-start(bf16[96,6144]{1,0:T(8,128)(2,1)S(1)} %get-tuple-element.417), channel_id=1, source_target_pairs={{0,16},{1,17},{2,18},{3,19},{4,20},{5,21},{6,22},{7,23},{8,9},{9,8... | collective-permute-start | bytes 3538952 | tf_op jit(solution)/shard_map/ppermute | solution.py:275
  260.8 34.6 %collective-permute-start.62 = (bf16[96,6144]{1,0:T(8,128)(2,1)S(1)}, bf16[96,6144]{1,0:T(8,128)(2,1)S(1)}, u32[]{:S(2)}, u32[]{:S(2)}) collective-permute-start(bf16[96,6144]{1,0:T(8,128)(2,1)S(1)} %get-tuple-element.418), channel_id=1, source_target_pairs={{0,1},{1,0},{2,3},{3,2},{4,5},{5,4},{6,7},{7,6},{8,24},{9,25},{10,... | collective-permute-start | bytes 3538952 | tf_op jit(solution)/shard_map/ppermute | solution.py:275
  262.7 19.1 %collective-permute-start.56 = (bf16[24,6144]{1,0:T(8,128)(2,1)S(1)}, bf16[24,6144]{1,0:T(8,128)(2,1)S(1)}, u32[]{:S(2)}, u32[]{:S(2)}) collective-permute-start(bf16[24,6144]{1,0:T(8,128)(2,1)S(1)} %get-tuple-element.406), channel_id=1, source_target_pairs={{0,2},{1,3},{2,0},{3,1},{4,6},{5,7},{6,4},{7,5},{8,10},{9,11},{10,... | collective-permute-start | bytes 884744 | tf_op jit(solution)/shard_map/ppermute | solution.py:275
  267.8 15.0 %collective-permute-start.57 = (bf16[24,6144]{1,0:T(8,128)(2,1)S(1)}, bf16[24,6144]{1,0:T(8,128)(2,1)S(1)}, u32[]{:S(2)}, u32[]{:S(2)}) collective-permute-start(bf16[24,6144]{1,0:T(8,128)(2,1)S(1)} %get-tuple-element.407), channel_id=1, source_target_pairs={{0,4},{1,5},{2,6},{3,7},{4,0},{5,1},{6,2},{7,3},{8,12},{9,13},{10,... | collective-permute-start | bytes 884744 | tf_op jit(solution)/shard_map/ppermute | solution.py:275
  281.8 13.6 %collective-permute-start.59 = (bf16[48,3200]{1,0:T(8,128)(2,1)S(1)}, bf16[48,3200]{1,0:T(8,128)(2,1)S(1)}, u32[]{:S(2)}, u32[]{:S(2)}) collective-permute-start(bf16[48,3200]{1,0:T(8,128)(2,1)S(1)} %get-tuple-element.414), channel_id=1, source_target_pairs={{0,16},{1,17},{2,18},{3,19},{4,20},{5,21},{6,22},{7,23},{8,9},{9,8... | collective-permute-start | bytes 921608 | tf_op jit(solution)/shard_map/ppermute | solution.py:275
  282.8 12.6 %collective-permute-start.60 = (bf16[48,3200]{1,0:T(8,128)(2,1)S(1)}, bf16[48,3200]{1,0:T(8,128)(2,1)S(1)}, u32[]{:S(2)}, u32[]{:S(2)}) collective-permute-start(bf16[48,3200]{1,0:T(8,128)(2,1)S(1)} %get-tuple-element.415), channel_id=1, source_target_pairs={{0,1},{1,0},{2,3},{3,2},{4,5},{5,4},{6,7},{7,6},{8,24},{9,25},{10,... | collective-permute-start | bytes 921608 | tf_op jit(solution)/shard_map/ppermute | solution.py:275
  284.2 10.2 %collective-permute-start.58 = (bf16[24,6144]{1,0:T(8,128)(2,1)S(1)}, bf16[24,6144]{1,0:T(8,128)(2,1)S(1)}, u32[]{:S(2)}, u32[]{:S(2)}) collective-permute-start(bf16[24,6144]{1,0:T(8,128)(2,1)S(1)} %get-tuple-element.408), channel_id=1, source_target_pairs={{0,6},{1,7},{2,4},{3,5},{4,2},{5,3},{6,0},{7,1},{8,14},{9,15},{10,... | collective-permute-start | bytes 884744 | tf_op jit(solution)/shard_map/ppermute | solution.py:275
  295.7 11.8 %collective-permute-start.65 = (bf16[24,3200]{1,0:T(8,128)(2,1)S(1)}, bf16[24,3200]{1,0:T(8,128)(2,1)S(1)}, u32[]{:S(2)}, u32[]{:S(2)}) collective-permute-start(bf16[24,3200]{1,0:T(8,128)(2,1)S(1)} %get-tuple-element.437), channel_id=1, source_target_pairs={{0,2},{1,3},{2,0},{3,1},{4,6},{5,7},{6,4},{7,5},{8,10},{9,11},{10,... | collective-permute-start | bytes 460808 | tf_op jit(solution)/shard_map/ppermute | solution.py:275
  300.8 8.0 %collective-permute-start.66 = (bf16[24,3200]{1,0:T(8,128)(2,1)S(1)}, bf16[24,3200]{1,0:T(8,128)(2,1)S(1)}, u32[]{:S(2)}, u32[]{:S(2)}) collective-permute-start(bf16[24,3200]{1,0:T(8,128)(2,1)S(1)} %get-tuple-element.438), channel_id=1, source_target_pairs={{0,4},{1,5},{2,6},{3,7},{4,0},{5,1},{6,2},{7,3},{8,12},{9,13},{10,... | collective-permute-start | bytes 460808 | tf_op jit(solution)/shard_map/ppermute | solution.py:275
  302.9 13.4 %collective-permute-start.67 = (bf16[24,3200]{1,0:T(8,128)(2,1)S(1)}, bf16[24,3200]{1,0:T(8,128)(2,1)S(1)}, u32[]{:S(2)}, u32[]{:S(2)}) collective-permute-start(bf16[24,3200]{1,0:T(8,128)(2,1)S(1)} %get-tuple-element.439), channel_id=1, source_target_pairs={{0,6},{1,7},{2,4},{3,5},{4,2},{5,3},{6,0},{7,1},{8,14},{9,15},{10,... | collective-permute-start | bytes 460808 | tf_op jit(solution)/shard_map/ppermute | solution.py:275
  304.5 16.3 %collective-permute-start.68 = (bf16[48,6144]{1,0:T(8,128)(2,1)S(1)}, bf16[48,6144]{1,0:T(8,128)(2,1)S(1)}, u32[]{:S(2)}, u32[]{:S(2)}) collective-permute-start(bf16[48,6144]{1,0:T(8,128)(2,1)S(1)} %get-tuple-element.445), channel_id=1, source_target_pairs={{0,16},{1,17},{2,18},{3,19},{4,20},{5,21},{6,22},{7,23},{8,9},{9,8... | collective-permute-start | bytes 1769480 | tf_op jit(solution)/shard_map/ppermute | solution.py:275
  306.1 16.3 %collective-permute-start.69 = (bf16[48,6144]{1,0:T(8,128)(2,1)S(1)}, bf16[48,6144]{1,0:T(8,128)(2,1)S(1)}, u32[]{:S(2)}, u32[]{:S(2)}) collective-permute-start(bf16[48,6144]{1,0:T(8,128)(2,1)S(1)} %get-tuple-element.446), channel_id=1, source_target_pairs={{0,1},{1,0},{2,3},{3,2},{4,5},{5,4},{6,7},{7,6},{8,24},{9,25},{10,... | collective-permute-start | bytes 1769480 | tf_op jit(solution)/shard_map/ppermute | solution.py:275
  307.4 25.3 %collective-permute-start.73 = (bf16[96,3200]{1,0:T(8,128)(2,1)S(1)}, bf16[96,3200]{1,0:T(8,128)(2,1)S(1)}, u32[]{:S(2)}, u32[]{:S(2)}) collective-permute-start(bf16[96,3200]{1,0:T(8,128)(2,1)S(1)} %get-tuple-element.460), channel_id=1, source_target_pairs={{0,16},{1,17},{2,18},{3,19},{4,20},{5,21},{6,22},{7,23},{8,9},{9,8... | collective-permute-start | bytes 1843208 | tf_op jit(solution)/shard_map/ppermute | solution.py:275
  308.8 24.0 %collective-permute-start.74 = (bf16[96,3200]{1,0:T(8,128)(2,1)S(1)}, bf16[96,3200]{1,0:T(8,128)(2,1)S(1)}, u32[]{:S(2)}, u32[]{:S(2)}) collective-permute-start(bf16[96,3200]{1,0:T(8,128)(2,1)S(1)} %get-tuple-element.461), channel_id=1, source_target_pairs={{0,1},{1,0},{2,3},{3,2},{4,5},{5,4},{6,7},{7,6},{8,24},{9,25},{10,... | collective-permute-start | bytes 1843208 | tf_op jit(solution)/shard_map/ppermute | solution.py:275
  322.8 13.2 %collective-permute-start.70 = (bf16[24,6144]{1,0:T(8,128)(2,1)S(1)}, bf16[24,6144]{1,0:T(8,128)(2,1)S(1)}, u32[]{:S(2)}, u32[]{:S(2)}) collective-permute-start(bf16[24,6144]{1,0:T(8,128)(2,1)S(1)} %get-tuple-element.456), channel_id=1, source_target_pairs={{0,2},{1,3},{2,0},{3,1},{4,6},{5,7},{6,4},{7,5},{8,10},{9,11},{10,... | collective-permute-start | bytes 884744 | tf_op jit(solution)/shard_map/ppermute | solution.py:275
  323.9 21.0 %collective-permute-start.71 = (bf16[24,6144]{1,0:T(8,128)(2,1)S(1)}, bf16[24,6144]{1,0:T(8,128)(2,1)S(1)}, u32[]{:S(2)}, u32[]{:S(2)}) collective-permute-start(bf16[24,6144]{1,0:T(8,128)(2,1)S(1)} %get-tuple-element.457), channel_id=1, source_target_pairs={{0,4},{1,5},{2,6},{3,7},{4,0},{5,1},{6,2},{7,3},{8,12},{9,13},{10,... | collective-permute-start | bytes 884744 | tf_op jit(solution)/shard_map/ppermute | solution.py:275
  325.8 19.1 %collective-permute-start.72 = (bf16[24,6144]{1,0:T(8,128)(2,1)S(1)}, bf16[24,6144]{1,0:T(8,128)(2,1)S(1)}, u32[]{:S(2)}, u32[]{:S(2)}) collective-permute-start(bf16[24,6144]{1,0:T(8,128)(2,1)S(1)} %get-tuple-element.458), channel_id=1, source_target_pairs={{0,6},{1,7},{2,4},{3,5},{4,2},{5,3},{6,0},{7,1},{8,14},{9,15},{10,... | collective-permute-start | bytes 884744 | tf_op jit(solution)/shard_map/ppermute | solution.py:275
  332.9 12.0 %collective-permute-start.75 = (bf16[48,3200]{1,0:T(8,128)(2,1)S(1)}, bf16[48,3200]{1,0:T(8,128)(2,1)S(1)}, u32[]{:S(2)}, u32[]{:S(2)}) collective-permute-start(bf16[48,3200]{1,0:T(8,128)(2,1)S(1)} %get-tuple-element.464), channel_id=1, source_target_pairs={{0,16},{1,17},{2,18},{3,19},{4,20},{5,21},{6,22},{7,23},{8,9},{9,8... | collective-permute-start | bytes 921608 | tf_op jit(solution)/shard_map/ppermute | solution.py:275
  334.7 10.2 %collective-permute-start.76 = (bf16[48,3200]{1,0:T(8,128)(2,1)S(1)}, bf16[48,3200]{1,0:T(8,128)(2,1)S(1)}, u32[]{:S(2)}, u32[]{:S(2)}) collective-permute-start(bf16[48,3200]{1,0:T(8,128)(2,1)S(1)} %get-tuple-element.465), channel_id=1, source_target_pairs={{0,1},{1,0},{2,3},{3,2},{4,5},{5,4},{6,7},{7,6},{8,24},{9,25},{10,... | collective-permute-start | bytes 921608 | tf_op jit(solution)/shard_map/ppermute | solution.py:275
  345.1 8.2 %collective-permute-start.77 = (bf16[24,3200]{1,0:T(8,128)(2,1)S(1)}, bf16[24,3200]{1,0:T(8,128)(2,1)S(1)}, u32[]{:S(2)}, u32[]{:S(2)}) collective-permute-start(bf16[24,3200]{1,0:T(8,128)(2,1)S(1)} %get-tuple-element.472), channel_id=1, source_target_pairs={{0,2},{1,3},{2,0},{3,1},{4,6},{5,7},{6,4},{7,5},{8,10},{9,11},{10,... | collective-permute-start | bytes 460808 | tf_op jit(solution)/shard_map/ppermute | solution.py:275
  348.9 11.7 %collective-permute-start.78 = (bf16[24,3200]{1,0:T(8,128)(2,1)S(1)}, bf16[24,3200]{1,0:T(8,128)(2,1)S(1)}, u32[]{:S(2)}, u32[]{:S(2)}) collective-permute-start(bf16[24,3200]{1,0:T(8,128)(2,1)S(1)} %get-tuple-element.473), channel_id=1, source_target_pairs={{0,4},{1,5},{2,6},{3,7},{4,0},{5,1},{6,2},{7,3},{8,12},{9,13},{10,... | collective-permute-start | bytes 460808 | tf_op jit(solution)/shard_map/ppermute | solution.py:275
  349.9 10.7 %collective-permute-start.79 = (bf16[24,3200]{1,0:T(8,128)(2,1)S(1)}, bf16[24,3200]{1,0:T(8,128)(2,1)S(1)}, u32[]{:S(2)}, u32[]{:S(2)}) collective-permute-start(bf16[24,3200]{1,0:T(8,128)(2,1)S(1)} %get-tuple-element.474), channel_id=1, source_target_pairs={{0,6},{1,7},{2,4},{3,5},{4,2},{5,3},{6,0},{7,1},{8,14},{9,15},{10,... | collective-permute-start | bytes 460808 | tf_op jit(solution)/shard_map/ppermute | solution.py:275
  (51 other events, 745.5 us)
Sparse Core Ops, SparseCore 0:
  14.1 131.6 all-gather.1

commit v7 on v6

--- a/solution.py
+++ b/solution.py
@@ -14,7 +14,7 @@
 FF = 3072
 LAYERS = 2
 PAD = 128
-LIGHT = pl.CostEstimate(flops=1 << 20, bytes_accessed=1 << 16, transcendentals=0)
+LIGHT = pl.CostEstimate(flops=1 << 30, bytes_accessed=1 << 22, transcendentals=0)
 
 
 def norm(value, gain):
@@ -1032,8 +1032,8 @@
     held, attended = lax.optimization_barrier((ffn.pieces[:2], attended))
     ffn.pieces = [*held, *ffn.pieces[2:]]
     ffn.advance()
-    held, second = lax.optimization_barrier((ffn.pieces[6:], second))
-    ffn.pieces = [*ffn.pieces[:6], *held]
+    held, second = lax.optimization_barrier((ffn.pieces[7:], second))
+    ffn.pieces = [*ffn.pieces[:7], *held]
     return weights, ffn.result(), second, order, attended
 
 

time: 375 us -> 373 us (level)
    unnamed x76 -> x88, local copies, waits for them, and re-layouts: 14.4 us -> 15.4 us
where the time goes in v7:
time: 373 us; the launch traced here: 368 us
  waiting for transfers between devices  174 us (47%)
  starting transfers between devices  85 us (23%)
  Pallas kernels  72.1 us (19%)
  local copies, waits for them, and re-layouts  16.5 us (4%)
  between operations  15.8 us (4%)
  other arithmetic  4.82 us (1%)
    ppermute x80, waiting for transfers between devices, swap(): return lax.ppermute(value, ('dp', 'fsdp'), route)  174 us
    ppermute x80, starting transfers between devices, swap(): return lax.ppermute(value, ('dp', 'fsdp'), route)  85 us
    unnamed x88, local copies, waits for them, and re-layouts  15.4 us
    pallas_call x2, Pallas kernels, attention_backward_kernel(): pl.pallas_call(body, in_specs=[SMEM_SPEC] + [VMEM_SPEC] * 4 + [ANY_SPEC],...  15.2 us
    pallas_call x2, Pallas kernels, ffn_forward(): pl.pallas_call(body, grid=(steps,), in_specs=[fixed((tokens, D)), fixed((...  12.9 us
    pallas_call x3, Pallas kernels, matrix_terms(): pl.pallas_call(body, grid=(wide // tile,), in_specs=in_specs, out_specs=[...  10.8 us
    pallas_call x2, Pallas kernels, up_backward_kernel(): pl.pallas_call(body, grid=(steps,), in_specs=[fixed((tokens, D)), fixed((...  9.29 us
    pallas_call x2, Pallas kernels, attention_forward(): pl.pallas_call(body, in_specs=[SMEM_SPEC, VMEM_SPEC, ANY_SPEC], out_specs...  7.84 us
  transfers between devices with their start and end apart: 81, of which 28 were waited for; matrix products, arithmetic and copies ran while one was open for 1% of the time, Pallas kernels for 14%

profile of v7, /device:TPU:0, one launch (start us, length us, event | category | flops | bytes accessed | tf_op | source)
XLA Modules:
  0.0 368.0 jit_solution(6836534321661857263)
XLA Ops:
  14.1 3.1 collective-permute-start
  17.3 3.9 %collective-permute-done = bf16[24,3200]{1,0:T(8,128)(2,1)S(1)} collective-permute-done((bf16[24,3200]{1,0:T(8,128)(2,1)S(1)}, bf16[24,3200]{1,0:T(8,128)(2,1)S(1)}, u32[]{:S(2)}, u32[]{:S(2)}) %collective-permute-start) | collective-permute-done | bytes 153632 | tf_op jit(solution)/shard_map/ppermute | solution.py:275
  21.2 1.8 collective-permute-start.2
  23.7 8.7 %collective-permute-done.2 = bf16[24,6144]{1,0:T(8,128)(2,1)S(1)} collective-permute-done((bf16[24,6144]{1,0:T(8,128)(2,1)S(1)}, bf16[24,6144]{1,0:T(8,128)(2,1)S(1)}, u32[]{:S(2)}, u32[]{:S(2)}) %collective-permute-start.2) | collective-permute-done | bytes 294944 | tf_op jit(solution)/shard_map/ppermute | solution.py:275
  32.5 1.3 collective-permute-start.3
  35.2 14.8 %collective-permute-done.3 = bf16[48,3200]{1,0:T(8,128)(2,1)S(1)} collective-permute-done((bf16[48,3200]{1,0:T(8,128)(2,1)S(1)}, bf16[48,3200]{1,0:T(8,128)(2,1)S(1)}, u32[]{:S(2)}, u32[]{:S(2)}) %collective-permute-start.3) | collective-permute-done | bytes 307232 | tf_op jit(solution)/shard_map/ppermute | solution.py:275
  50.0 1.3 collective-permute-start.7
  51.3 1.6 collective-permute-start.6
  52.8 1.5 collective-permute-start.12
  55.4 32.9 %collective-permute-done.7 = bf16[48,6144]{1,0:T(8,128)(2,1)S(1)} collective-permute-done((bf16[48,6144]{1,0:T(8,128)(2,1)S(1)}, bf16[48,6144]{1,0:T(8,128)(2,1)S(1)}, u32[]{:S(2)}, u32[]{:S(2)}) %collective-permute-start.7) | collective-permute-done | bytes 589856 | tf_op jit(solution)/shard_map/ppermute | solution.py:275
  89.2 1.6 collective-permute-start.11
  90.9 11.1 %collective-permute-done.10 = bf16[48,3200]{1,0:T(8,128)(2,1)S(1)} collective-permute-done((bf16[48,3200]{1,0:T(8,128)(2,1)S(1)}, bf16[48,3200]{1,0:T(8,128)(2,1)S(1)}, u32[]{:S(2)}, u32[]{:S(2)}) %collective-permute-start.10) | collective-permute-done | bytes 307232 | tf_op jit(solution)/shard_map/ppermute | solution.py:275
  102.0 4.2 %collective-permute-done.11 = bf16[48,3200]{1,0:T(8,128)(2,1)} collective-permute-done((bf16[48,3200]{1,0:T(8,128)(2,1)}, bf16[48,3200]{1,0:T(8,128)(2,1)}, u32[]{:S(2)}, u32[]{:S(2)}) %collective-permute-start.11) | collective-permute-done | bytes 307232 | tf_op jit(solution)/shard_map/ppermute | solution.py:275
  108.0 13.0 %collective-permute-done.24 = bf16[48,6144]{1,0:T(8,128)(2,1)S(1)} collective-permute-done((bf16[48,6144]{1,0:T(8,128)(2,1)S(1)}, bf16[48,6144]{1,0:T(8,128)(2,1)S(1)}, u32[]{:S(2)}, u32[]{:S(2)}) %collective-permute-start.24) | collective-permute-done | bytes 589856 | tf_op jit(solution)/shard_map/ppermute | solution.py:275
  123.6 1.6 collective-permute-start.8
  125.3 1.3 collective-permute-start.25
  131.5 2.1 shard_map.313
  133.6 4.0 %shard_map.314 = (bf16[256,768]{1,0:T(8,128)(2,1)S(1)}, bf16[256,2304]{1,0:T(8,128)(2,1)S(1)}, bf16[256,768]{1,0:T(8,128)(2,1)S(1)}, f32[256,768]{1,0:T(8,128)S(1)}, f32[8,768]{1,0:T(8,128)S(1)}) custom-call(s32[1]{0:T(128)S(6)} %copy.49.length_ref, f32[256,768]{1,0:T(8,128)S(1)} %bitcast_convert_fusion.hidden_ref, bf16[768,3200]{1,0:T(8,128)(2,1)S(1)} %bitcast.96), custom_call_target="tpu_custom_call" | custom-call | flops 1073741824 | bytes 4194304 | tf_op jit(solution)/shard_map/pallas_call | solution.py:451
  140.2 1.5 collective-permute-start.22
  141.6 1.3 collective-permute-start.23
  142.9 5.0 %collective-permute-done.25 = bf16[48,6144]{1,0:T(8,128)(2,1)} collective-permute-done((bf16[48,6144]{1,0:T(8,128)(2,1)S(1)}, bf16[48,6144]{1,0:T(8,128)(2,1)}, u32[]{:S(2)}, u32[]{:S(2)}) %collective-permute-start.25) | collective-permute-done | bytes 589856 | tf_op jit(solution)/shard_map/ppermute | solution.py:275
  148.5 8.3 %collective-permute-done.22 = bf16[48,6144]{1,0:T(8,128)(2,1)} collective-permute-done((bf16[48,6144]{1,0:T(8,128)(2,1)}, bf16[48,6144]{1,0:T(8,128)(2,1)}, u32[]{:S(2)}, u32[]{:S(2)}) %collective-permute-start.22) | collective-permute-done | bytes 589856 | tf_op jit(solution)/shard_map/ppermute | solution.py:275
  156.8 1.5 collective-permute-done.23
  159.0 2.3 collective-permute-done.27
  162.3 3.1 shard_map.315
  165.4 6.2 %shard_map.316 = (bf16[256,768]{1,0:T(8,128)(2,1)S(1)}, bf16[256,3072]{1,0:T(8,128)(2,1)S(1)}, bf16[256,3072]{1,0:T(8,128)(2,1)S(1)}, f32[256,768]{1,0:T(8,128)S(1)}, f32[256,768]{1,0:T(8,128)S(1)}) custom-call(f32[256,768]{1,0:T(8,128)S(1)} %get-tuple-element.281.sum_ref, f32[8,768]{1,0:T(8,128)S(1)} %get-tuple-element.282.gain_ref, ...), custom_call_target="tpu_custom_call" | custom-call | flops 1073741824 | bytes 4194304 | tf_op jit(solution)/shard_map/pallas_call | solution.py:506
  171.8 3.8 %shard_map.317 = (bf16[256,768]{1,0:T(8,128)(2,1)S(1)}, bf16[256,2304]{1,0:T(8,128)(2,1)S(1)}, bf16[256,768]{1,0:T(8,128)(2,1)S(1)}, f32[256,768]{1,0:T(8,128)S(1)}, f32[8,768]{1,0:T(8,128)S(1)}) custom-call(s32[1]{0:T(128)S(6)} %copy.49.length_ref, f32[256,768]{1,0:T(8,128)S(1)} %get-tuple-element.286.hidden_ref, bf16[768,9344]{1,0:T(8,128)(2,1)S(1)} %bitcast.91), custom_call_target="tpu_custom_call" | custom-call | flops 1073741824 | bytes 4194304 | tf_op jit(solution)/shard_map/pallas_call | solution.py:451
  175.6 6.6 %shard_map.318 = (bf16[256,768]{1,0:T(8,128)(2,1)S(1)}, bf16[256,3072]{1,0:T(8,128)(2,1)S(1)}, bf16[256,3072]{1,0:T(8,128)(2,1)S(1)}, f32[256,768]{1,0:T(8,128)S(1)}, f32[256,768]{1,0:T(8,128)S(1)}) custom-call(f32[256,768]{1,0:T(8,128)S(1)} %get-tuple-element.288.sum_ref, f32[8,768]{1,0:T(8,128)S(1)} %get-tuple-element.289.gain_ref, ...), custom_call_target="tpu_custom_call" | custom-call | flops 1073741824 | bytes 4194304 | tf_op jit(solution)/shard_map/pallas_call | solution.py:506
  186.0 2.4 shard_map.321
  188.5 4.7 %shard_map.322 = (bf16[256,3072]{1,0:T(8,128)(2,1)S(1)}, f32[256,768]{1,0:T(8,128)S(1)}) custom-call(f32[256,768]{1,0:T(8,128)S(1)} %get-tuple-element.308.grad_ref, bf16[256,768]{1,0:T(8,128)(2,1)S(1)} %get-tuple-element.309.refs_0_.low_ref, bf16[256,3072]{1,0:T(8,128)(2,1)S(1)} %get-tuple-element.310.slope_ref, bf16[768,9344]{1,0:T(8,128)(2,1)S(1)} %bitcast.91, ...), custom_call_target="tpu_custom_call" | custom-call | flops 1073741824 | bytes 4194304 | tf_op jit(solution)/shard_map/pallas_call | solution.py:571
  194.2 1.5 collective-permute-start.37
  196.2 7.2 %shard_map.323 = (bf16[256,3072]{1,0:T(8,128)(2,1)S(1)}, f32[256,768]{1,0:T(8,128)S(1)}, f32[1,768]{1,0:T(1,128)S(1)}) custom-call(s32[1]{0:T(128)S(6)} %copy.49.length_ref, f32[256,768]{1,0:T(8,128)S(1)} %get-tuple-element.311.grad_ref, f32[256,768]{1,0:T(8,128)S(1)} %get-tuple-element.288.sum_ref, f32[8,768]{1,0:T(8,128)S(1)} %get-tuple-element.289.gain_ref, ...), custom_call_target="tpu_custom_call" | custom-call | flops 1073741824 | bytes 4194304 | tf_op jit(solution)/shard_map/pallas_call | solution.py:626
  203.4 2.9 shard_map.325
  206.3 3.0 collective-permute-done.36.one.refs_1_
  211.9 1.7 collective-permute-start.46
  215.7 4.5 %shard_map.328 = (bf16[256,3072]{1,0:T(8,128)(2,1)S(1)}, f32[256,768]{1,0:T(8,128)S(1)}) custom-call(f32[256,768]{1,0:T(8,128)S(1)} %get-tuple-element.341.grad_ref, bf16[256,768]{1,0:T(8,128)(2,1)S(1)} %get-tuple-element.342.low_ref.refs_0_, bf16[256,3072]{1,0:T(8,128)(2,1)S(1)} %get-tuple-element.343.slope_ref, bf16[768,6144]{1,0:T(8,128)(2,1)S(1)} %bitcast.94, ...), custom_call_target="tpu_custom_call" | custom-call | flops 1073741824 | bytes 4194304 | tf_op jit(solution)/shard_map/pallas_call | solution.py:571
  220.3 1.4 shard_map.330
  221.7 11.8 %collective-permute-done.43.refs_3_ = bf16[48,3072]{1,0:T(8,128)(2,1)S(1)} collective-permute-done((bf16[48,3072]{1,0:T(8,128)(2,1)S(1)}, bf16[48,3072]{1,0:T(8,128)(2,1)S(1)}, u32[]{:S(2)}, u32[]{:S(2)}) %collective-permute-start.43) | collective-permute-done | bytes 294944 | tf_op jit(solution)/shard_map/ppermute | solution.py:275
  235.8 1.5 collective-permute-start.52
  239.8 8.1 %shard_map.332 = (bf16[256,3072]{1,0:T(8,128)(2,1)S(1)}, f32[256,768]{1,0:T(8,128)}, f32[1,768]{1,0:T(1,128)S(1)}) custom-call(s32[1]{0:T(128)S(6)} %copy.49.length_ref, f32[256,768]{1,0:T(8,128)S(1)} %get-tuple-element.374.grad_ref, f32[256,768]{1,0:T(8,128)S(1)} %get-tuple-element.281.sum_ref, f32[8,768]{1,0:T(8,128)S(1)} %get-tuple-element.282.gain_ref, ...), custom_call_target="tpu_custom_call" | custom-call | flops 1073741824 | bytes 4194304 | tf_op jit(solution)/shard_map/pallas_call | solution.py:626
  247.9 5.5 %shard_map.334 = (bf16[96,6144]{1,0:T(8,128)(2,1)S(1)}, bf16[96,6144]{1,0:T(8,128)(2,1)S(1)}, bf16[48,6144]{1,0:T(8,128)(2,1)S(1)}, bf16[48,6144]{1,0:T(8,128)(2,1)S(1)}, bf16[96,6144]{1,0:T(8,128)(2,1)S(1)}) custom-call(bf16[384,384]{1,0:T(8,128)(2,1)S(1)} %get-tuple-element.379.ga.refs_0_, bf16[384,384]{1,0:T(8,128)(2,1)S(1)} %collective-permute-done.47.gb.refs_1_, ...), custom_call_target="tpu_custom_call" | custom-call | flops 1073741824 | bytes 4194304 | tf_op jit(solution)/shard_map/pallas_call | solution.py:681
  253.4 4.9 %collective-permute-done.49.refs_8_ = bf16[48,3072]{1,0:T(8,128)(2,1)S(1)} collective-permute-done((bf16[48,3072]{1,0:T(8,128)(2,1)S(1)}, bf16[48,3072]{1,0:T(8,128)(2,1)S(1)}, u32[]{:S(2)}, u32[]{:S(2)}) %collective-permute-start.49) | collective-permute-done | bytes 294944 | tf_op jit(solution)/shard_map/ppermute | solution.py:275
  258.7 1.3 collective-permute-start.62
  261.8 5.4 %collective-permute-start.56 = (bf16[24,6144]{1,0:T(8,128)(2,1)S(1)}, bf16[24,6144]{1,0:T(8,128)(2,1)S(1)}, u32[]{:S(2)}, u32[]{:S(2)}) collective-permute-start(bf16[24,6144]{1,0:T(8,128)(2,1)S(1)} %get-tuple-element.404), channel_id=1, source_target_pairs={{0,2},{1,3},{2,0},{3,1},{4,6},{5,7},{6,4},{7,5},{8,10},{9,11},{10,... | collective-permute-start | bytes 884744 | tf_op jit(solution)/shard_map/ppermute | solution.py:275
  267.2 1.9 collective-permute-start.57
  269.2 11.2 %collective-permute-done.56 = bf16[24,6144]{1,0:T(8,128)(2,1)S(1)} collective-permute-done((bf16[24,6144]{1,0:T(8,128)(2,1)S(1)}, bf16[24,6144]{1,0:T(8,128)(2,1)S(1)}, u32[]{:S(2)}, u32[]{:S(2)}) %collective-permute-start.56) | collective-permute-done | bytes 294944 | tf_op jit(solution)/shard_map/ppermute | solution.py:275
  281.5 2.9 collective-permute-start.60
  284.4 2.5 collective-permute-start.58
  286.9 1.4 shard_map.338
  288.3 4.7 %collective-permute-done.58 = bf16[24,6144]{1,0:T(8,128)(2,1)S(1)} collective-permute-done((bf16[24,6144]{1,0:T(8,128)(2,1)S(1)}, bf16[24,6144]{1,0:T(8,128)(2,1)S(1)}, u32[]{:S(2)}, u32[]{:S(2)}) %collective-permute-start.58) | collective-permute-done | bytes 294944 | tf_op jit(solution)/shard_map/ppermute | solution.py:275
  294.1 5.0 %collective-permute-start.65 = (bf16[24,3200]{1,0:T(8,128)(2,1)S(1)}, bf16[24,3200]{1,0:T(8,128)(2,1)S(1)}, u32[]{:S(2)}, u32[]{:S(2)}) collective-permute-start(bf16[24,3200]{1,0:T(8,128)(2,1)S(1)} %get-tuple-element.435), channel_id=1, source_target_pairs={{0,2},{1,3},{2,0},{3,1},{4,6},{5,7},{6,4},{7,5},{8,10},{9,11},{10,... | collective-permute-start | bytes 460808 | tf_op jit(solution)/shard_map/ppermute | solution.py:275
  299.1 1.5 collective-permute-start.66
  301.4 1.4 collective-permute-start.67
  304.0 1.4 collective-permute-start.69
  306.8 7.5 %collective-permute-start.74 = (bf16[96,3200]{1,0:T(8,128)(2,1)S(1)}, bf16[96,3200]{1,0:T(8,128)(2,1)S(1)}, u32[]{:S(2)}, u32[]{:S(2)}) collective-permute-start(bf16[96,3200]{1,0:T(8,128)(2,1)S(1)} %get-tuple-element.459), channel_id=1, source_target_pairs={{0,1},{1,0},{2,3},{3,2},{4,5},{5,4},{6,7},{7,6},{8,24},{9,25},{10,... | collective-permute-start | bytes 1843208 | tf_op jit(solution)/shard_map/ppermute | solution.py:275
  314.5 4.9 %collective-permute-done.68.refs_3_ = bf16[48,6144]{1,0:T(8,128)(2,1)S(1)} collective-permute-done((bf16[48,6144]{1,0:T(8,128)(2,1)S(1)}, bf16[48,6144]{1,0:T(8,128)(2,1)S(1)}, u32[]{:S(2)}, u32[]{:S(2)}) %collective-permute-start.68) | collective-permute-done | bytes 589856 | tf_op jit(solution)/shard_map/ppermute | solution.py:275
  321.8 1.7 collective-permute-start.71
  323.5 1.6 collective-permute-start.72
  325.1 6.3 %collective-permute-done.73.one.refs_1_ = bf16[96,3200]{1,0:T(8,128)(2,1)S(1)} collective-permute-done((bf16[96,3200]{1,0:T(8,128)(2,1)S(1)}, bf16[96,3200]{1,0:T(8,128)(2,1)S(1)}, u32[]{:S(2)}, u32[]{:S(2)}) %collective-permute-start.73) | collective-permute-done | bytes 614432 | tf_op jit(solution)/shard_map/ppermute | solution.py:275
  331.5 1.6 collective-permute-start.75
  333.9 9.9 %collective-permute-done.71 = bf16[24,6144]{1,0:T(8,128)(2,1)S(1)} collective-permute-done((bf16[24,6144]{1,0:T(8,128)(2,1)S(1)}, bf16[24,6144]{1,0:T(8,128)(2,1)S(1)}, u32[]{:S(2)}, u32[]{:S(2)}) %collective-permute-start.71) | collective-permute-done | bytes 294944 | tf_op jit(solution)/shard_map/ppermute | solution.py:275
  344.0 3.8 %collective-permute-start.77 = (bf16[24,3200]{1,0:T(8,128)(2,1)S(1)}, bf16[24,3200]{1,0:T(8,128)(2,1)S(1)}, u32[]{:S(2)}, u32[]{:S(2)}) collective-permute-start(bf16[24,3200]{1,0:T(8,128)(2,1)S(1)} %get-tuple-element.470), channel_id=1, source_target_pairs={{0,2},{1,3},{2,0},{3,1},{4,6},{5,7},{6,4},{7,5},{8,10},{9,11},{10,... | collective-permute-start | bytes 460808 | tf_op jit(solution)/shard_map/ppermute | solution.py:275
  348.6 1.6 collective-permute-start.79
  352.2 7.3 %collective-permute-done.78.refs_2_ = bf16[24,3200]{1,0:T(8,128)(2,1)S(1)} collective-permute-done((bf16[24,3200]{1,0:T(8,128)(2,1)S(1)}, bf16[24,3200]{1,0:T(8,128)(2,1)S(1)}, u32[]{:S(2)}, u32[]{:S(2)}) %collective-permute-start.78) | collective-permute-done | bytes 153632 | tf_op jit(solution)/shard_map/ppermute | solution.py:275
  (251 shorter events, 55.0 us)
Async XLA Ops:
  7.2 140.7 %all-gather.2.cloned.1.call-start = ((), (), s32[]{:S(2)}) async-start(), calls=%async_computation | async-start | bytes 14800896 | tf_op jit(solution)/shard_map/all_gather | solution.py:57
  21.2 11.3 %collective-permute-start.2 = (bf16[24,6144]{1,0:T(8,128)(2,1)S(1)}, bf16[24,6144]{1,0:T(8,128)(2,1)S(1)}, u32[]{:S(2)}, u32[]{:S(2)}) collective-permute-start(bf16[24,6144]{1,0:T(8,128)(2,1)S(1)} %pad_maximum_fusion.4), channel_id=1, source_target_pairs={{0,2},{1,3},{2,0},{3,1},{4,6},{5,7},{6,4},{7,5},{8,10},{9,11},{10,... | collective-permute-start | bytes 884744 | tf_op jit(solution)/shard_map/ppermute | solution.py:275
  23.0 9.5 %collective-permute-start.1 = (bf16[48,3200]{1,0:T(8,128)(2,1)S(1)}, bf16[48,3200]{1,0:T(8,128)(2,1)S(1)}, u32[]{:S(2)}, u32[]{:S(2)}) collective-permute-start(bf16[48,3200]{1,0:T(8,128)(2,1)S(1)} %pad_maximum_fusion.3), channel_id=1, source_target_pairs={{2,4},{3,5},{4,2},{5,3},{10,12},{11,13},{12,10},{13,11},{18,20},{1... | collective-permute-start | bytes 921608 | tf_op jit(solution)/shard_map/ppermute | solution.py:275
  32.5 17.4 %collective-permute-start.3 = (bf16[48,3200]{1,0:T(8,128)(2,1)S(1)}, bf16[48,3200]{1,0:T(8,128)(2,1)S(1)}, u32[]{:S(2)}, u32[]{:S(2)}) collective-permute-start(bf16[48,3200]{1,0:T(8,128)(2,1)S(1)} %collective-permute-done.1), channel_id=1, source_target_pairs={{2,0},{3,1},{4,6},{5,7},{10,8},{11,9},{12,14},{13,15},{18,16},{19,... | collective-permute-start | bytes 921608 | tf_op jit(solution)/shard_map/ppermute | solution.py:275
  34.3 15.6 %collective-permute-start.4 = (bf16[48,6144]{1,0:T(8,128)(2,1)S(1)}, bf16[48,6144]{1,0:T(8,128)(2,1)S(1)}, u32[]{:S(2)}, u32[]{:S(2)}) collective-permute-start(bf16[48,6144]{1,0:T(8,128)(2,1)S(1)} %pad_maximum_fusion), channel_id=1, source_target_pairs={{2,4},{3,5},{4,2},{5,3},{10,12},{11,13},{12,10},{13,11},{18,20},{1... | collective-permute-start | bytes 1769480 | tf_op jit(solution)/shard_map/ppermute | solution.py:275
  50.0 38.4 %collective-permute-start.7 = (bf16[48,6144]{1,0:T(8,128)(2,1)S(1)}, bf16[48,6144]{1,0:T(8,128)(2,1)S(1)}, u32[]{:S(2)}, u32[]{:S(2)}) collective-permute-start(bf16[48,6144]{1,0:T(8,128)(2,1)S(1)} %collective-permute-done.4), channel_id=1, source_target_pairs={{2,0},{3,1},{4,6},{5,7},{10,8},{11,9},{12,14},{13,15},{18,16},{19,... | collective-permute-start | bytes 1769480 | tf_op jit(solution)/shard_map/ppermute | solution.py:275
  51.3 37.1 %collective-permute-start.6 = (bf16[48,3200]{1,0:T(8,128)(2,1)S(1)}, bf16[48,3200]{1,0:T(8,128)(2,1)S(1)}, u32[]{:S(2)}, u32[]{:S(2)}) collective-permute-start(bf16[48,3200]{1,0:T(8,128)(2,1)S(1)} %pad_maximum_fusion.3), channel_id=1, source_target_pairs={{0,1},{1,0},{2,3},{3,2},{4,5},{5,4},{6,7},{7,6},{8,24},{9,25},{10,... | collective-permute-start | bytes 921608 | tf_op jit(solution)/shard_map/ppermute | solution.py:275
  52.8 38.1 %collective-permute-start.12 = (bf16[48,3200]{1,0:T(8,128)(2,1)S(1)}, bf16[48,3200]{1,0:T(8,128)(2,1)}, u32[]{:S(2)}, u32[]{:S(2)}) collective-permute-start(bf16[48,3200]{1,0:T(8,128)(2,1)S(1)} %pad_maximum_fusion.3), channel_id=1, source_target_pairs={{0,16},{1,17},{2,18},{3,19},{4,20},{5,21},{6,22},{7,23},{8,9},{9,8... | collective-permute-start | bytes 921608 | tf_op jit(solution)/shard_map/ppermute | solution.py:275
  54.3 34.1 %collective-permute-start.5 = (bf16[48,3200]{1,0:T(8,128)(2,1)S(1)}, bf16[48,3200]{1,0:T(8,128)(2,1)}, u32[]{:S(2)}, u32[]{:S(2)}) collective-permute-start(bf16[48,3200]{1,0:T(8,128)(2,1)S(1)} %broadcast_select_fusion.1), channel_id=1, source_target_pairs={{0,16},{1,17},{2,18},{3,19},{4,20},{5,21},{6,22},{7,23},{8,9},{9,8... | collective-permute-start | bytes 921608 | tf_op jit(solution)/shard_map/ppermute | solution.py:275
  54.9 36.0 %collective-permute-start.13 = (bf16[48,3200]{1,0:T(8,128)(2,1)S(1)}, bf16[48,3200]{1,0:T(8,128)(2,1)}, u32[]{:S(2)}, u32[]{:S(2)}) collective-permute-start(bf16[48,3200]{1,0:T(8,128)(2,1)S(1)} %broadcast_select_fusion.1), channel_id=1, source_target_pairs={{0,1},{1,0},{2,3},{3,2},{4,5},{5,4},{6,7},{7,6},{8,24},{9,25},{10,... | collective-permute-start | bytes 921608 | tf_op jit(solution)/shard_map/ppermute | solution.py:275
  88.4 13.6 %collective-permute-start.10 = (bf16[48,3200]{1,0:T(8,128)(2,1)S(1)}, bf16[48,3200]{1,0:T(8,128)(2,1)S(1)}, u32[]{:S(2)}, u32[]{:S(2)}) collective-permute-start(bf16[48,3200]{1,0:T(8,128)(2,1)S(1)} %collective-permute-done.6), channel_id=1, source_target_pairs={{0,16},{1,17},{2,18},{3,19},{4,20},{5,21},{6,22},{7,23},{8,9},{9,8... | collective-permute-start | bytes 921608 | tf_op jit(solution)/shard_map/ppermute | solution.py:275
  89.2 17.0 %collective-permute-start.11 = (bf16[48,3200]{1,0:T(8,128)(2,1)}, bf16[48,3200]{1,0:T(8,128)(2,1)}, u32[]{:S(2)}, u32[]{:S(2)}) collective-permute-start(bf16[48,3200]{1,0:T(8,128)(2,1)} %collective-permute-done.5), channel_id=1, source_target_pairs={{0,1},{1,0},{2,3},{3,2},{4,5},{5,4},{6,7},{7,6},{8,24},{9,25},{10,... | collective-permute-start | bytes 921608 | tf_op jit(solution)/shard_map/ppermute | solution.py:275
  90.8 30.1 %collective-permute-start.24 = (bf16[48,6144]{1,0:T(8,128)(2,1)S(1)}, bf16[48,6144]{1,0:T(8,128)(2,1)S(1)}, u32[]{:S(2)}, u32[]{:S(2)}) collective-permute-start(bf16[48,6144]{1,0:T(8,128)(2,1)S(1)} %pad_maximum_fusion), channel_id=1, source_target_pairs={{0,16},{1,17},{2,18},{3,19},{4,20},{5,21},{6,22},{7,23},{8,9},{9,8... | collective-permute-start | bytes 1769480 | tf_op jit(solution)/shard_map/ppermute | solution.py:275
  106.2 15.6 %collective-permute-start.14 = (bf16[48,3200]{1,0:T(8,128)(2,1)S(1)}, bf16[48,3200]{1,0:T(8,128)(2,1)S(1)}, u32[]{:S(2)}, u32[]{:S(2)}) collective-permute-start(bf16[48,3200]{1,0:T(8,128)(2,1)S(1)} %collective-permute-done.10), channel_id=1, source_target_pairs={{0,8},{1,9},{2,10},{3,11},{4,12},{5,13},{6,14},{7,15},{8,0},{9,1},... | collective-permute-start | bytes 921608 | tf_op jit(solution)/shard_map/ppermute | solution.py:275
  106.9 16.1 %collective-permute-start.15 = (bf16[48,3200]{1,0:T(8,128)(2,1)}, bf16[48,3200]{1,0:T(8,128)(2,1)}, u32[]{:S(2)}, u32[]{:S(2)}) collective-permute-start(bf16[48,3200]{1,0:T(8,128)(2,1)} %collective-permute-done.11), channel_id=1, source_target_pairs={{0,8},{1,9},{2,10},{3,11},{4,12},{5,13},{6,14},{7,15},{8,0},{9,1},... | collective-permute-start | bytes 921608 | tf_op jit(solution)/shard_map/ppermute | solution.py:275
  107.4 16.2 %collective-permute-start.16 = (bf16[48,3200]{1,0:T(8,128)(2,1)}, bf16[48,3200]{1,0:T(8,128)(2,1)}, u32[]{:S(2)}, u32[]{:S(2)}) collective-permute-start(bf16[48,3200]{1,0:T(8,128)(2,1)} %collective-permute-done.12), channel_id=1, source_target_pairs={{0,8},{1,9},{2,10},{3,11},{4,12},{5,13},{6,14},{7,15},{8,0},{9,1},... | collective-permute-start | bytes 921608 | tf_op jit(solution)/shard_map/ppermute | solution.py:275
  107.5 17.8 %collective-permute-start.17 = (bf16[48,3200]{1,0:T(8,128)(2,1)}, bf16[48,3200]{1,0:T(8,128)(2,1)}, u32[]{:S(2)}, u32[]{:S(2)}) collective-permute-start(bf16[48,3200]{1,0:T(8,128)(2,1)} %collective-permute-done.5), channel_id=1, source_target_pairs={{0,8},{1,9},{2,10},{3,11},{4,12},{5,13},{6,14},{7,15},{8,0},{9,1},... | collective-permute-start | bytes 921608 | tf_op jit(solution)/shard_map/ppermute | solution.py:275
  123.0 17.2 %collective-permute-start.9 = (bf16[48,6144]{1,0:T(8,128)(2,1)S(1)}, bf16[48,6144]{1,0:T(8,128)(2,1)}, u32[]{:S(2)}, u32[]{:S(2)}) collective-permute-start(bf16[48,6144]{1,0:T(8,128)(2,1)S(1)} %pad_maximum_fusion), channel_id=1, source_target_pairs={{0,1},{1,0},{2,3},{3,2},{4,5},{5,4},{6,7},{7,6},{8,24},{9,25},{10,... | collective-permute-start | bytes 1769480 | tf_op jit(solution)/shard_map/ppermute | solution.py:275
  123.6 16.6 %collective-permute-start.8 = (bf16[48,6144]{1,0:T(8,128)(2,1)S(1)}, bf16[48,6144]{1,0:T(8,128)(2,1)}, u32[]{:S(2)}, u32[]{:S(2)}) collective-permute-start(bf16[48,6144]{1,0:T(8,128)(2,1)S(1)} %broadcast_select_fusion), channel_id=1, source_target_pairs={{0,16},{1,17},{2,18},{3,19},{4,20},{5,21},{6,22},{7,23},{8,9},{9,8... | collective-permute-start | bytes 1769480 | tf_op jit(solution)/shard_map/ppermute | solution.py:275
  125.3 22.6 %collective-permute-start.25 = (bf16[48,6144]{1,0:T(8,128)(2,1)S(1)}, bf16[48,6144]{1,0:T(8,128)(2,1)}, u32[]{:S(2)}, u32[]{:S(2)}) collective-permute-start(bf16[48,6144]{1,0:T(8,128)(2,1)S(1)} %broadcast_select_fusion), channel_id=1, source_target_pairs={{0,1},{1,0},{2,3},{3,2},{4,5},{5,4},{6,7},{7,6},{8,24},{9,25},{10,... | collective-permute-start | bytes 1769480 | tf_op jit(solution)/shard_map/ppermute | solution.py:275
  129.0 18.9 %collective-permute-start.32 = (bf16[48,6144]{1,0:T(8,128)(2,1)S(1)}, bf16[48,6144]{1,0:T(8,128)(2,1)}, u32[]{:S(2)}, u32[]{:S(2)}) collective-permute-start(bf16[48,6144]{1,0:T(8,128)(2,1)S(1)} %pad_maximum_fusion), channel_id=1, source_target_pairs={{0,8},{1,9},{2,10},{3,11},{4,12},{5,13},{6,14},{7,15},{8,0},{9,1},... | collective-permute-start | bytes 1769480 | tf_op jit(solution)/shard_map/ppermute | solution.py:275
  129.4 19.1 %collective-permute-start.28 = (bf16[48,6144]{1,0:T(8,128)(2,1)}, bf16[48,6144]{1,0:T(8,128)(2,1)}, u32[]{:S(2)}, u32[]{:S(2)}) collective-permute-start(bf16[48,6144]{1,0:T(8,128)(2,1)} %copy-done.9), channel_id=1, source_target_pairs={{0,8},{1,9},{2,10},{3,11},{4,12},{5,13},{6,14},{7,15},{8,0},{9,1},... | collective-permute-start | bytes 1769480 | tf_op jit(solution)/shard_map/ppermute | solution.py:275
  140.2 16.6 %collective-permute-start.22 = (bf16[48,6144]{1,0:T(8,128)(2,1)}, bf16[48,6144]{1,0:T(8,128)(2,1)}, u32[]{:S(2)}, u32[]{:S(2)}) collective-permute-start(bf16[48,6144]{1,0:T(8,128)(2,1)} %collective-permute-done.9), channel_id=1, source_target_pairs={{0,16},{1,17},{2,18},{3,19},{4,20},{5,21},{6,22},{7,23},{8,9},{9,8... | collective-permute-start | bytes 1769480 | tf_op jit(solution)/shard_map/ppermute | solution.py:275
  141.6 16.7 %collective-permute-start.23 = (bf16[48,6144]{1,0:T(8,128)(2,1)}, bf16[48,6144]{1,0:T(8,128)(2,1)}, u32[]{:S(2)}, u32[]{:S(2)}) collective-permute-start(bf16[48,6144]{1,0:T(8,128)(2,1)} %collective-permute-done.8), channel_id=1, source_target_pairs={{0,1},{1,0},{2,3},{3,2},{4,5},{5,4},{6,7},{7,6},{8,24},{9,25},{10,... | collective-permute-start | bytes 1769480 | tf_op jit(solution)/shard_map/ppermute | solution.py:275
  147.9 10.4 %collective-permute-start.31 = (bf16[48,6144]{1,0:T(8,128)(2,1)}, bf16[48,6144]{1,0:T(8,128)(2,1)}, u32[]{:S(2)}, u32[]{:S(2)}) collective-permute-start(bf16[48,6144]{1,0:T(8,128)(2,1)} %collective-permute-done.25), channel_id=1, source_target_pairs={{0,8},{1,9},{2,10},{3,11},{4,12},{5,13},{6,14},{7,15},{8,0},{9,1},... | collective-permute-start | bytes 1769480 | tf_op jit(solution)/shard_map/ppermute | solution.py:275
  147.9 10.9 %collective-permute-start.29 = (bf16[48,6144]{1,0:T(8,128)(2,1)}, bf16[48,6144]{1,0:T(8,128)(2,1)S(1)}, u32[]{:S(2)}, u32[]{:S(2)}) collective-permute-start(bf16[48,6144]{1,0:T(8,128)(2,1)} %collective-permute-done.8), channel_id=1, source_target_pairs={{0,8},{1,9},{2,10},{3,11},{4,12},{5,13},{6,14},{7,15},{8,0},{9,1},... | collective-permute-start | bytes 1769480 | tf_op jit(solution)/shard_map/ppermute | solution.py:275
  148.4 10.4 %collective-permute-start.30 = (bf16[48,6144]{1,0:T(8,128)(2,1)}, bf16[48,6144]{1,0:T(8,128)(2,1)S(1)}, u32[]{:S(2)}, u32[]{:S(2)}) collective-permute-start(bf16[48,6144]{1,0:T(8,128)(2,1)} %collective-permute-done.9), channel_id=1, source_target_pairs={{0,8},{1,9},{2,10},{3,11},{4,12},{5,13},{6,14},{7,15},{8,0},{9,1},... | collective-permute-start | bytes 1769480 | tf_op jit(solution)/shard_map/ppermute | solution.py:275
  185.2 10.4 %collective-permute-start.38 = (bf16[384,768]{1,0:T(8,128)(2,1)S(1)}, bf16[384,768]{1,0:T(8,128)(2,1)S(1)}, u32[]{:S(2)}, u32[]{:S(2)}) collective-permute-start(bf16[384,768]{1,0:T(8,128)(2,1)S(1)} %get-tuple-element.320), channel_id=1, source_target_pairs={{0,8},{1,9},{2,10},{3,11},{4,12},{5,13},{6,14},{7,15},{8,0},{9,1},... | collective-permute-start | bytes 1769480 | tf_op jit(solution)/shard_map/ppermute | solution.py:275
  193.5 15.8 %collective-permute-start.36 = (bf16[96,3072]{1,0:T(8,128)(2,1)S(1)}, bf16[96,3072]{1,0:T(8,128)(2,1)S(1)}, u32[]{:S(2)}, u32[]{:S(2)}) collective-permute-start(bf16[96,3072]{1,0:T(8,128)(2,1)S(1)} %get-tuple-element.303), channel_id=1, source_target_pairs={{0,16},{1,17},{2,18},{3,19},{4,20},{5,21},{6,22},{7,23},{8,9},{9,8... | collective-permute-start | bytes 1769480 | tf_op jit(solution)/shard_map/ppermute | solution.py:275
  194.2 15.2 %collective-permute-start.37 = (bf16[96,3072]{1,0:T(8,128)(2,1)S(1)}, bf16[96,3072]{1,0:T(8,128)(2,1)S(1)}, u32[]{:S(2)}, u32[]{:S(2)}) collective-permute-start(bf16[96,3072]{1,0:T(8,128)(2,1)S(1)} %get-tuple-element.304), channel_id=1, source_target_pairs={{0,1},{1,0},{2,3},{3,2},{4,5},{5,4},{6,7},{7,6},{8,24},{9,25},{10,... | collective-permute-start | bytes 1769480 | tf_op jit(solution)/shard_map/ppermute | solution.py:275
  195.6 7.8 %collective-permute-start.40 = (bf16[256,768]{1,0:T(8,128)(2,1)S(1)}, bf16[256,768]{1,0:T(8,128)(2,1)S(1)}, u32[]{:S(2)}, u32[]{:S(2)}) collective-permute-start(bf16[256,768]{1,0:T(8,128)(2,1)S(1)} %get-tuple-element.506), channel_id=1, source_target_pairs={{0,8},{1,9},{2,10},{3,11},{4,12},{5,13},{6,14},{7,15},{8,0},{9,1},... | collective-permute-start | bytes 1179656 | tf_op jit(solution)/shard_map/ppermute | solution.py:275
  195.6 7.8 %collective-permute-start.41 = (bf16[256,768]{1,0:T(8,128)(2,1)S(1)}, bf16[256,768]{1,0:T(8,128)(2,1)S(1)}, u32[]{:S(2)}, u32[]{:S(2)}) collective-permute-start(bf16[256,768]{1,0:T(8,128)(2,1)S(1)} %get-tuple-element.505), channel_id=1, source_target_pairs={{0,8},{1,9},{2,10},{3,11},{4,12},{5,13},{6,14},{7,15},{8,0},{9,1},... | collective-permute-start | bytes 1179656 | tf_op jit(solution)/shard_map/ppermute | solution.py:275
  211.4 22.1 %collective-permute-start.45 = (bf16[96,3072]{1,0:T(8,128)(2,1)S(1)}, bf16[96,3072]{1,0:T(8,128)(2,1)S(1)}, u32[]{:S(2)}, u32[]{:S(2)}) collective-permute-start(bf16[96,3072]{1,0:T(8,128)(2,1)S(1)} %get-tuple-element.334), channel_id=1, source_target_pairs={{0,16},{1,17},{2,18},{3,19},{4,20},{5,21},{6,22},{7,23},{8,9},{9,8... | collective-permute-start | bytes 1769480 | tf_op jit(solution)/shard_map/ppermute | solution.py:275
  211.9 21.7 %collective-permute-start.46 = (bf16[96,3072]{1,0:T(8,128)(2,1)S(1)}, bf16[96,3072]{1,0:T(8,128)(2,1)S(1)}, u32[]{:S(2)}, u32[]{:S(2)}) collective-permute-start(bf16[96,3072]{1,0:T(8,128)(2,1)S(1)} %get-tuple-element.335), channel_id=1, source_target_pairs={{0,1},{1,0},{2,3},{3,2},{4,5},{5,4},{6,7},{7,6},{8,24},{9,25},{10,... | collective-permute-start | bytes 1769480 | tf_op jit(solution)/shard_map/ppermute | solution.py:275
  213.7 19.8 %collective-permute-start.43 = (bf16[48,3072]{1,0:T(8,128)(2,1)S(1)}, bf16[48,3072]{1,0:T(8,128)(2,1)S(1)}, u32[]{:S(2)}, u32[]{:S(2)}) collective-permute-start(bf16[48,3072]{1,0:T(8,128)(2,1)S(1)} %get-tuple-element.331), channel_id=1, source_target_pairs={{0,16},{1,17},{2,18},{3,19},{4,20},{5,21},{6,22},{7,23},{8,9},{9,8... | collective-permute-start | bytes 884744 | tf_op jit(solution)/shard_map/ppermute | solution.py:275
  214.4 19.1 %collective-permute-start.44 = (bf16[48,3072]{1,0:T(8,128)(2,1)S(1)}, bf16[48,3072]{1,0:T(8,128)(2,1)S(1)}, u32[]{:S(2)}, u32[]{:S(2)}) collective-permute-start(bf16[48,3072]{1,0:T(8,128)(2,1)S(1)} %get-tuple-element.332), channel_id=1, source_target_pairs={{0,1},{1,0},{2,3},{3,2},{4,5},{5,4},{6,7},{7,6},{8,24},{9,25},{10,... | collective-permute-start | bytes 884744 | tf_op jit(solution)/shard_map/ppermute | solution.py:275
  215.7 23.0 %collective-permute-start.53 = (bf16[256,3072]{1,0:T(8,128)(2,1)S(1)}, bf16[256,3072]{1,0:T(8,128)(2,1)S(1)}, u32[]{:S(2)}, u32[]{:S(2)}) collective-permute-start(bf16[256,3072]{1,0:T(8,128)(2,1)S(1)} %get-tuple-element.381.refs_2_), channel_id=1, source_target_pairs={{0,8},{1,9},{2,10},{3,11},{4,12},{5,13},{6,14},{7,15},{8,0},{9,1},... | collective-permute-start | bytes 4718600 | tf_op jit(solution)/shard_map/ppermute | solution.py:275
  233.5 14.3 %collective-permute-start.55 = (bf16[256,3072]{1,0:T(8,128)(2,1)S(1)}, bf16[256,3072]{1,0:T(8,128)(2,1)S(1)}, u32[]{:S(2)}, u32[]{:S(2)}) collective-permute-start(bf16[256,3072]{1,0:T(8,128)(2,1)S(1)} %get-tuple-element.387.refs_6_), channel_id=1, source_target_pairs={{0,8},{1,9},{2,10},{3,11},{4,12},{5,13},{6,14},{7,15},{8,0},{9,1},... | collective-permute-start | bytes 4718600 | tf_op jit(solution)/shard_map/ppermute | solution.py:275
  235.4 23.0 %collective-permute-start.51 = (bf16[96,3200]{1,0:T(8,128)(2,1)S(1)}, bf16[96,3200]{1,0:T(8,128)(2,1)S(1)}, u32[]{:S(2)}, u32[]{:S(2)}) collective-permute-start(bf16[96,3200]{1,0:T(8,128)(2,1)S(1)} %get-tuple-element.369), channel_id=1, source_target_pairs={{0,16},{1,17},{2,18},{3,19},{4,20},{5,21},{6,22},{7,23},{8,9},{9,8... | collective-permute-start | bytes 1843208 | tf_op jit(solution)/shard_map/ppermute | solution.py:275
  235.8 22.5 %collective-permute-start.52 = (bf16[96,3200]{1,0:T(8,128)(2,1)S(1)}, bf16[96,3200]{1,0:T(8,128)(2,1)S(1)}, u32[]{:S(2)}, u32[]{:S(2)}) collective-permute-start(bf16[96,3200]{1,0:T(8,128)(2,1)S(1)} %get-tuple-element.370), channel_id=1, source_target_pairs={{0,1},{1,0},{2,3},{3,2},{4,5},{5,4},{6,7},{7,6},{8,24},{9,25},{10,... | collective-permute-start | bytes 1843208 | tf_op jit(solution)/shard_map/ppermute | solution.py:275
  237.9 20.5 %collective-permute-start.49 = (bf16[48,3072]{1,0:T(8,128)(2,1)S(1)}, bf16[48,3072]{1,0:T(8,128)(2,1)S(1)}, u32[]{:S(2)}, u32[]{:S(2)}) collective-permute-start(bf16[48,3072]{1,0:T(8,128)(2,1)S(1)} %get-tuple-element.366), channel_id=1, source_target_pairs={{0,16},{1,17},{2,18},{3,19},{4,20},{5,21},{6,22},{7,23},{8,9},{9,8... | collective-permute-start | bytes 884744 | tf_op jit(solution)/shard_map/ppermute | solution.py:275
  238.7 19.6 %collective-permute-start.50 = (bf16[48,3072]{1,0:T(8,128)(2,1)S(1)}, bf16[48,3072]{1,0:T(8,128)(2,1)S(1)}, u32[]{:S(2)}, u32[]{:S(2)}) collective-permute-start(bf16[48,3072]{1,0:T(8,128)(2,1)S(1)} %get-tuple-element.367), channel_id=1, source_target_pairs={{0,1},{1,0},{2,3},{3,2},{4,5},{5,4},{6,7},{7,6},{8,24},{9,25},{10,... | collective-permute-start | bytes 884744 | tf_op jit(solution)/shard_map/ppermute | solution.py:275
  258.4 26.0 %collective-permute-start.63 = (bf16[256,3072]{1,0:T(8,128)(2,1)S(1)}, bf16[256,3072]{1,0:T(8,128)(2,1)S(1)}, u32[]{:S(2)}, u32[]{:S(2)}) collective-permute-start(bf16[256,3072]{1,0:T(8,128)(2,1)S(1)} %get-tuple-element.420.ra), channel_id=1, source_target_pairs={{0,8},{1,9},{2,10},{3,11},{4,12},{5,13},{6,14},{7,15},{8,0},{9,1},... | collective-permute-start | bytes 4718600 | tf_op jit(solution)/shard_map/ppermute | solution.py:275
  258.4 35.4 %collective-permute-start.61 = (bf16[96,6144]{1,0:T(8,128)(2,1)S(1)}, bf16[96,6144]{1,0:T(8,128)(2,1)S(1)}, u32[]{:S(2)}, u32[]{:S(2)}) collective-permute-start(bf16[96,6144]{1,0:T(8,128)(2,1)S(1)} %get-tuple-element.415), channel_id=1, source_target_pairs={{0,16},{1,17},{2,18},{3,19},{4,20},{5,21},{6,22},{7,23},{8,9},{9,8... | collective-permute-start | bytes 3538952 | tf_op jit(solution)/shard_map/ppermute | solution.py:275
  258.7 35.1 %collective-permute-start.62 = (bf16[96,6144]{1,0:T(8,128)(2,1)S(1)}, bf16[96,6144]{1,0:T(8,128)(2,1)S(1)}, u32[]{:S(2)}, u32[]{:S(2)}) collective-permute-start(bf16[96,6144]{1,0:T(8,128)(2,1)S(1)} %get-tuple-element.416), channel_id=1, source_target_pairs={{0,1},{1,0},{2,3},{3,2},{4,5},{5,4},{6,7},{7,6},{8,24},{9,25},{10,... | collective-permute-start | bytes 3538952 | tf_op jit(solution)/shard_map/ppermute | solution.py:275
  261.8 18.6 %collective-permute-start.56 = (bf16[24,6144]{1,0:T(8,128)(2,1)S(1)}, bf16[24,6144]{1,0:T(8,128)(2,1)S(1)}, u32[]{:S(2)}, u32[]{:S(2)}) collective-permute-start(bf16[24,6144]{1,0:T(8,128)(2,1)S(1)} %get-tuple-element.404), channel_id=1, source_target_pairs={{0,2},{1,3},{2,0},{3,1},{4,6},{5,7},{6,4},{7,5},{8,10},{9,11},{10,... | collective-permute-start | bytes 884744 | tf_op jit(solution)/shard_map/ppermute | solution.py:275
  267.2 14.3 %collective-permute-start.57 = (bf16[24,6144]{1,0:T(8,128)(2,1)S(1)}, bf16[24,6144]{1,0:T(8,128)(2,1)S(1)}, u32[]{:S(2)}, u32[]{:S(2)}) collective-permute-start(bf16[24,6144]{1,0:T(8,128)(2,1)S(1)} %get-tuple-element.405), channel_id=1, source_target_pairs={{0,4},{1,5},{2,6},{3,7},{4,0},{5,1},{6,2},{7,3},{8,12},{9,13},{10,... | collective-permute-start | bytes 884744 | tf_op jit(solution)/shard_map/ppermute | solution.py:275
  280.4 13.4 %collective-permute-start.59 = (bf16[48,3200]{1,0:T(8,128)(2,1)S(1)}, bf16[48,3200]{1,0:T(8,128)(2,1)S(1)}, u32[]{:S(2)}, u32[]{:S(2)}) collective-permute-start(bf16[48,3200]{1,0:T(8,128)(2,1)S(1)} %get-tuple-element.412), channel_id=1, source_target_pairs={{0,16},{1,17},{2,18},{3,19},{4,20},{5,21},{6,22},{7,23},{8,9},{9,8... | collective-permute-start | bytes 921608 | tf_op jit(solution)/shard_map/ppermute | solution.py:275
  281.5 12.3 %collective-permute-start.60 = (bf16[48,3200]{1,0:T(8,128)(2,1)S(1)}, bf16[48,3200]{1,0:T(8,128)(2,1)S(1)}, u32[]{:S(2)}, u32[]{:S(2)}) collective-permute-start(bf16[48,3200]{1,0:T(8,128)(2,1)S(1)} %get-tuple-element.413), channel_id=1, source_target_pairs={{0,1},{1,0},{2,3},{3,2},{4,5},{5,4},{6,7},{7,6},{8,24},{9,25},{10,... | collective-permute-start | bytes 921608 | tf_op jit(solution)/shard_map/ppermute | solution.py:275
  284.4 8.6 %collective-permute-start.58 = (bf16[24,6144]{1,0:T(8,128)(2,1)S(1)}, bf16[24,6144]{1,0:T(8,128)(2,1)S(1)}, u32[]{:S(2)}, u32[]{:S(2)}) collective-permute-start(bf16[24,6144]{1,0:T(8,128)(2,1)S(1)} %get-tuple-element.406), channel_id=1, source_target_pairs={{0,6},{1,7},{2,4},{3,5},{4,2},{5,3},{6,0},{7,1},{8,14},{9,15},{10,... | collective-permute-start | bytes 884744 | tf_op jit(solution)/shard_map/ppermute | solution.py:275
  294.1 12.1 %collective-permute-start.65 = (bf16[24,3200]{1,0:T(8,128)(2,1)S(1)}, bf16[24,3200]{1,0:T(8,128)(2,1)S(1)}, u32[]{:S(2)}, u32[]{:S(2)}) collective-permute-start(bf16[24,3200]{1,0:T(8,128)(2,1)S(1)} %get-tuple-element.435), channel_id=1, source_target_pairs={{0,2},{1,3},{2,0},{3,1},{4,6},{5,7},{6,4},{7,5},{8,10},{9,11},{10,... | collective-permute-start | bytes 460808 | tf_op jit(solution)/shard_map/ppermute | solution.py:275
  301.4 13.1 %collective-permute-start.67 = (bf16[24,3200]{1,0:T(8,128)(2,1)S(1)}, bf16[24,3200]{1,0:T(8,128)(2,1)S(1)}, u32[]{:S(2)}, u32[]{:S(2)}) collective-permute-start(bf16[24,3200]{1,0:T(8,128)(2,1)S(1)} %get-tuple-element.437), channel_id=1, source_target_pairs={{0,6},{1,7},{2,4},{3,5},{4,2},{5,3},{6,0},{7,1},{8,14},{9,15},{10,... | collective-permute-start | bytes 460808 | tf_op jit(solution)/shard_map/ppermute | solution.py:275
  303.1 16.3 %collective-permute-start.68 = (bf16[48,6144]{1,0:T(8,128)(2,1)S(1)}, bf16[48,6144]{1,0:T(8,128)(2,1)S(1)}, u32[]{:S(2)}, u32[]{:S(2)}) collective-permute-start(bf16[48,6144]{1,0:T(8,128)(2,1)S(1)} %get-tuple-element.443), channel_id=1, source_target_pairs={{0,16},{1,17},{2,18},{3,19},{4,20},{5,21},{6,22},{7,23},{8,9},{9,8... | collective-permute-start | bytes 1769480 | tf_op jit(solution)/shard_map/ppermute | solution.py:275
  304.0 16.3 %collective-permute-start.69 = (bf16[48,6144]{1,0:T(8,128)(2,1)S(1)}, bf16[48,6144]{1,0:T(8,128)(2,1)S(1)}, u32[]{:S(2)}, u32[]{:S(2)}) collective-permute-start(bf16[48,6144]{1,0:T(8,128)(2,1)S(1)} %get-tuple-element.444), channel_id=1, source_target_pairs={{0,1},{1,0},{2,3},{3,2},{4,5},{5,4},{6,7},{7,6},{8,24},{9,25},{10,... | collective-permute-start | bytes 1769480 | tf_op jit(solution)/shard_map/ppermute | solution.py:275
  306.2 25.2 %collective-permute-start.73 = (bf16[96,3200]{1,0:T(8,128)(2,1)S(1)}, bf16[96,3200]{1,0:T(8,128)(2,1)S(1)}, u32[]{:S(2)}, u32[]{:S(2)}) collective-permute-start(bf16[96,3200]{1,0:T(8,128)(2,1)S(1)} %get-tuple-element.458), channel_id=1, source_target_pairs={{0,16},{1,17},{2,18},{3,19},{4,20},{5,21},{6,22},{7,23},{8,9},{9,8... | collective-permute-start | bytes 1843208 | tf_op jit(solution)/shard_map/ppermute | solution.py:275
  306.8 24.5 %collective-permute-start.74 = (bf16[96,3200]{1,0:T(8,128)(2,1)S(1)}, bf16[96,3200]{1,0:T(8,128)(2,1)S(1)}, u32[]{:S(2)}, u32[]{:S(2)}) collective-permute-start(bf16[96,3200]{1,0:T(8,128)(2,1)S(1)} %get-tuple-element.459), channel_id=1, source_target_pairs={{0,1},{1,0},{2,3},{3,2},{4,5},{5,4},{6,7},{7,6},{8,24},{9,25},{10,... | collective-permute-start | bytes 1843208 | tf_op jit(solution)/shard_map/ppermute | solution.py:275
  320.7 13.2 %collective-permute-start.70 = (bf16[24,6144]{1,0:T(8,128)(2,1)S(1)}, bf16[24,6144]{1,0:T(8,128)(2,1)S(1)}, u32[]{:S(2)}, u32[]{:S(2)}) collective-permute-start(bf16[24,6144]{1,0:T(8,128)(2,1)S(1)} %get-tuple-element.454), channel_id=1, source_target_pairs={{0,2},{1,3},{2,0},{3,1},{4,6},{5,7},{6,4},{7,5},{8,10},{9,11},{10,... | collective-permute-start | bytes 884744 | tf_op jit(solution)/shard_map/ppermute | solution.py:275
  321.8 22.0 %collective-permute-start.71 = (bf16[24,6144]{1,0:T(8,128)(2,1)S(1)}, bf16[24,6144]{1,0:T(8,128)(2,1)S(1)}, u32[]{:S(2)}, u32[]{:S(2)}) collective-permute-start(bf16[24,6144]{1,0:T(8,128)(2,1)S(1)} %get-tuple-element.455), channel_id=1, source_target_pairs={{0,4},{1,5},{2,6},{3,7},{4,0},{5,1},{6,2},{7,3},{8,12},{9,13},{10,... | collective-permute-start | bytes 884744 | tf_op jit(solution)/shard_map/ppermute | solution.py:275
  323.5 20.3 %collective-permute-start.72 = (bf16[24,6144]{1,0:T(8,128)(2,1)S(1)}, bf16[24,6144]{1,0:T(8,128)(2,1)S(1)}, u32[]{:S(2)}, u32[]{:S(2)}) collective-permute-start(bf16[24,6144]{1,0:T(8,128)(2,1)S(1)} %get-tuple-element.456), channel_id=1, source_target_pairs={{0,6},{1,7},{2,4},{3,5},{4,2},{5,3},{6,0},{7,1},{8,14},{9,15},{10,... | collective-permute-start | bytes 884744 | tf_op jit(solution)/shard_map/ppermute | solution.py:275
  331.5 12.2 %collective-permute-start.75 = (bf16[48,3200]{1,0:T(8,128)(2,1)S(1)}, bf16[48,3200]{1,0:T(8,128)(2,1)S(1)}, u32[]{:S(2)}, u32[]{:S(2)}) collective-permute-start(bf16[48,3200]{1,0:T(8,128)(2,1)S(1)} %get-tuple-element.462), channel_id=1, source_target_pairs={{0,16},{1,17},{2,18},{3,19},{4,20},{5,21},{6,22},{7,23},{8,9},{9,8... | collective-permute-start | bytes 921608 | tf_op jit(solution)/shard_map/ppermute | solution.py:275
  333.1 10.6 %collective-permute-start.76 = (bf16[48,3200]{1,0:T(8,128)(2,1)S(1)}, bf16[48,3200]{1,0:T(8,128)(2,1)S(1)}, u32[]{:S(2)}, u32[]{:S(2)}) collective-permute-start(bf16[48,3200]{1,0:T(8,128)(2,1)S(1)} %get-tuple-element.463), channel_id=1, source_target_pairs={{0,1},{1,0},{2,3},{3,2},{4,5},{5,4},{6,7},{7,6},{8,24},{9,25},{10,... | collective-permute-start | bytes 921608 | tf_op jit(solution)/shard_map/ppermute | solution.py:275
  344.0 8.2 %collective-permute-start.77 = (bf16[24,3200]{1,0:T(8,128)(2,1)S(1)}, bf16[24,3200]{1,0:T(8,128)(2,1)S(1)}, u32[]{:S(2)}, u32[]{:S(2)}) collective-permute-start(bf16[24,3200]{1,0:T(8,128)(2,1)S(1)} %get-tuple-element.470), channel_id=1, source_target_pairs={{0,2},{1,3},{2,0},{3,1},{4,6},{5,7},{6,4},{7,5},{8,10},{9,11},{10,... | collective-permute-start | bytes 460808 | tf_op jit(solution)/shard_map/ppermute | solution.py:275
  347.8 11.7 %collective-permute-start.78 = (bf16[24,3200]{1,0:T(8,128)(2,1)S(1)}, bf16[24,3200]{1,0:T(8,128)(2,1)S(1)}, u32[]{:S(2)}, u32[]{:S(2)}) collective-permute-start(bf16[24,3200]{1,0:T(8,128)(2,1)S(1)} %get-tuple-element.471), channel_id=1, source_target_pairs={{0,4},{1,5},{2,6},{3,7},{4,0},{5,1},{6,2},{7,3},{8,12},{9,13},{10,... | collective-permute-start | bytes 460808 | tf_op jit(solution)/shard_map/ppermute | solution.py:275
  348.6 10.8 %collective-permute-start.79 = (bf16[24,3200]{1,0:T(8,128)(2,1)S(1)}, bf16[24,3200]{1,0:T(8,128)(2,1)S(1)}, u32[]{:S(2)}, u32[]{:S(2)}) collective-permute-start(bf16[24,3200]{1,0:T(8,128)(2,1)S(1)} %get-tuple-element.472), channel_id=1, source_target_pairs={{0,6},{1,7},{2,4},{3,5},{4,2},{5,3},{6,0},{7,1},{8,14},{9,15},{10,... | collective-permute-start | bytes 460808 | tf_op jit(solution)/shard_map/ppermute | solution.py:275
  (57 other events, 754.1 us)
Sparse Core Ops, SparseCore 0:
  14.1 131.6 all-gather.1

commit v8 on v7

--- a/solution.py
+++ b/solution.py
@@ -1024,7 +1024,7 @@
     ffn.advance()
     hold(attention, ffn)
     attention.advance()
-    ffn.pieces = gate(ffn.pieces, attention.pieces[3])
+    ffn.pieces = gate(ffn.pieces, attention.pieces[2])
     ffn.advance()
     hold(attention)
     weights = attention.result()
@@ -1032,8 +1032,8 @@
     held, attended = lax.optimization_barrier((ffn.pieces[:2], attended))
     ffn.pieces = [*held, *ffn.pieces[2:]]
     ffn.advance()
-    held, second = lax.optimization_barrier((ffn.pieces[7:], second))
-    ffn.pieces = [*ffn.pieces[:7], *held]
+    held, second = lax.optimization_barrier((ffn.pieces[6:7], second))
+    ffn.pieces = [*ffn.pieces[:6], *held, ffn.pieces[7]]
     return weights, ffn.result(), second, order, attended
 
 

time: 373 us -> 373 us (level)
  no operation moved by 1% of the time
where the time goes in v8:
time: 373 us; the launch traced here: 368 us
  waiting for transfers between devices  174 us (47%)
  starting transfers between devices  85 us (23%)
  Pallas kernels  72.1 us (19%)
  local copies, waits for them, and re-layouts  16.5 us (4%)
  between operations  15.8 us (4%)
  other arithmetic  4.82 us (1%)
    ppermute x80, waiting for transfers between devices, swap(): return lax.ppermute(value, ('dp', 'fsdp'), route)  174 us
    ppermute x80, starting transfers between devices, swap(): return lax.ppermute(value, ('dp', 'fsdp'), route)  85 us
    unnamed x88, local copies, waits for them, and re-layouts  15.4 us
    pallas_call x2, Pallas kernels, attention_backward_kernel(): pl.pallas_call(body, in_specs=[SMEM_SPEC] + [VMEM_SPEC] * 4 + [ANY_SPEC],...  15.2 us
    pallas_call x2, Pallas kernels, ffn_forward(): pl.pallas_call(body, grid=(steps,), in_specs=[fixed((tokens, D)), fixed((...  12.9 us
    pallas_call x3, Pallas kernels, matrix_terms(): pl.pallas_call(body, grid=(wide // tile,), in_specs=in_specs, out_specs=[...  10.8 us
    pallas_call x2, Pallas kernels, up_backward_kernel(): pl.pallas_call(body, grid=(steps,), in_specs=[fixed((tokens, D)), fixed((...  9.29 us
    pallas_call x2, Pallas kernels, attention_forward(): pl.pallas_call(body, in_specs=[SMEM_SPEC, VMEM_SPEC, ANY_SPEC], out_specs...  7.84 us
  transfers between devices with their start and end apart: 81, of which 28 were waited for; matrix products, arithmetic and copies ran while one was open for 1% of the time, Pallas kernels for 14%

profile of v8, /device:TPU:0, one launch (start us, length us, event | category | flops | bytes accessed | tf_op | source)
XLA Modules:
  0.0 368.0 jit_solution(10023774027424831650)
XLA Ops:
  14.1 3.1 collective-permute-start
  17.3 3.9 %collective-permute-done = bf16[24,3200]{1,0:T(8,128)(2,1)S(1)} collective-permute-done((bf16[24,3200]{1,0:T(8,128)(2,1)S(1)}, bf16[24,3200]{1,0:T(8,128)(2,1)S(1)}, u32[]{:S(2)}, u32[]{:S(2)}) %collective-permute-start) | collective-permute-done | bytes 153632 | tf_op jit(solution)/shard_map/ppermute | solution.py:275
  21.2 1.8 collective-permute-start.2
  23.7 8.7 %collective-permute-done.2 = bf16[24,6144]{1,0:T(8,128)(2,1)S(1)} collective-permute-done((bf16[24,6144]{1,0:T(8,128)(2,1)S(1)}, bf16[24,6144]{1,0:T(8,128)(2,1)S(1)}, u32[]{:S(2)}, u32[]{:S(2)}) %collective-permute-start.2) | collective-permute-done | bytes 294944 | tf_op jit(solution)/shard_map/ppermute | solution.py:275
  32.5 1.3 collective-permute-start.3
  35.2 14.8 %collective-permute-done.3 = bf16[48,3200]{1,0:T(8,128)(2,1)S(1)} collective-permute-done((bf16[48,3200]{1,0:T(8,128)(2,1)S(1)}, bf16[48,3200]{1,0:T(8,128)(2,1)S(1)}, u32[]{:S(2)}, u32[]{:S(2)}) %collective-permute-start.3) | collective-permute-done | bytes 307232 | tf_op jit(solution)/shard_map/ppermute | solution.py:275
  50.0 1.3 collective-permute-start.7
  51.3 1.6 collective-permute-start.6
  52.8 1.5 collective-permute-start.8
  55.4 32.9 %collective-permute-done.7 = bf16[48,6144]{1,0:T(8,128)(2,1)S(1)} collective-permute-done((bf16[48,6144]{1,0:T(8,128)(2,1)S(1)}, bf16[48,6144]{1,0:T(8,128)(2,1)S(1)}, u32[]{:S(2)}, u32[]{:S(2)}) %collective-permute-start.7) | collective-permute-done | bytes 589856 | tf_op jit(solution)/shard_map/ppermute | solution.py:275
  89.2 1.6 collective-permute-start.12
  90.9 11.1 %collective-permute-done.11 = bf16[48,3200]{1,0:T(8,128)(2,1)S(1)} collective-permute-done((bf16[48,3200]{1,0:T(8,128)(2,1)S(1)}, bf16[48,3200]{1,0:T(8,128)(2,1)S(1)}, u32[]{:S(2)}, u32[]{:S(2)}) %collective-permute-start.11) | collective-permute-done | bytes 307232 | tf_op jit(solution)/shard_map/ppermute | solution.py:275
  102.0 4.2 %collective-permute-done.12 = bf16[48,3200]{1,0:T(8,128)(2,1)} collective-permute-done((bf16[48,3200]{1,0:T(8,128)(2,1)}, bf16[48,3200]{1,0:T(8,128)(2,1)}, u32[]{:S(2)}, u32[]{:S(2)}) %collective-permute-start.12) | collective-permute-done | bytes 307232 | tf_op jit(solution)/shard_map/ppermute | solution.py:275
  108.0 13.0 %collective-permute-done.24 = bf16[48,6144]{1,0:T(8,128)(2,1)S(1)} collective-permute-done((bf16[48,6144]{1,0:T(8,128)(2,1)S(1)}, bf16[48,6144]{1,0:T(8,128)(2,1)S(1)}, u32[]{:S(2)}, u32[]{:S(2)}) %collective-permute-start.24) | collective-permute-done | bytes 589856 | tf_op jit(solution)/shard_map/ppermute | solution.py:275
  123.6 1.6 collective-permute-start.9
  125.3 1.3 collective-permute-start.25
  131.5 2.1 shard_map.313
  133.6 4.0 %shard_map.314 = (bf16[256,768]{1,0:T(8,128)(2,1)S(1)}, bf16[256,2304]{1,0:T(8,128)(2,1)S(1)}, bf16[256,768]{1,0:T(8,128)(2,1)S(1)}, f32[256,768]{1,0:T(8,128)S(1)}, f32[8,768]{1,0:T(8,128)S(1)}) custom-call(s32[1]{0:T(128)S(6)} %copy.49.length_ref, f32[256,768]{1,0:T(8,128)S(1)} %bitcast_convert_fusion.hidden_ref, bf16[768,3200]{1,0:T(8,128)(2,1)S(1)} %bitcast.96), custom_call_target="tpu_custom_call" | custom-call | flops 1073741824 | bytes 4194304 | tf_op jit(solution)/shard_map/pallas_call | solution.py:451
  140.2 1.5 collective-permute-start.22
  141.6 1.3 collective-permute-start.23
  142.9 5.0 %collective-permute-done.25 = bf16[48,6144]{1,0:T(8,128)(2,1)} collective-permute-done((bf16[48,6144]{1,0:T(8,128)(2,1)S(1)}, bf16[48,6144]{1,0:T(8,128)(2,1)}, u32[]{:S(2)}, u32[]{:S(2)}) %collective-permute-start.25) | collective-permute-done | bytes 589856 | tf_op jit(solution)/shard_map/ppermute | solution.py:275
  148.5 8.3 %collective-permute-done.22 = bf16[48,6144]{1,0:T(8,128)(2,1)} collective-permute-done((bf16[48,6144]{1,0:T(8,128)(2,1)}, bf16[48,6144]{1,0:T(8,128)(2,1)}, u32[]{:S(2)}, u32[]{:S(2)}) %collective-permute-start.22) | collective-permute-done | bytes 589856 | tf_op jit(solution)/shard_map/ppermute | solution.py:275
  156.8 1.5 collective-permute-done.23
  159.0 2.3 collective-permute-done.27
  162.3 3.1 shard_map.315
  165.4 6.2 %shard_map.316 = (bf16[256,768]{1,0:T(8,128)(2,1)S(1)}, bf16[256,3072]{1,0:T(8,128)(2,1)S(1)}, bf16[256,3072]{1,0:T(8,128)(2,1)S(1)}, f32[256,768]{1,0:T(8,128)S(1)}, f32[256,768]{1,0:T(8,128)S(1)}) custom-call(f32[256,768]{1,0:T(8,128)S(1)} %get-tuple-element.281.sum_ref, f32[8,768]{1,0:T(8,128)S(1)} %get-tuple-element.282.gain_ref, ...), custom_call_target="tpu_custom_call" | custom-call | flops 1073741824 | bytes 4194304 | tf_op jit(solution)/shard_map/pallas_call | solution.py:506
  171.8 3.8 %shard_map.317 = (bf16[256,768]{1,0:T(8,128)(2,1)S(1)}, bf16[256,2304]{1,0:T(8,128)(2,1)S(1)}, bf16[256,768]{1,0:T(8,128)(2,1)S(1)}, f32[256,768]{1,0:T(8,128)S(1)}, f32[8,768]{1,0:T(8,128)S(1)}) custom-call(s32[1]{0:T(128)S(6)} %copy.49.length_ref, f32[256,768]{1,0:T(8,128)S(1)} %get-tuple-element.286.hidden_ref, bf16[768,9344]{1,0:T(8,128)(2,1)S(1)} %bitcast.91), custom_call_target="tpu_custom_call" | custom-call | flops 1073741824 | bytes 4194304 | tf_op jit(solution)/shard_map/pallas_call | solution.py:451
  175.6 6.6 %shard_map.318 = (bf16[256,768]{1,0:T(8,128)(2,1)S(1)}, bf16[256,3072]{1,0:T(8,128)(2,1)S(1)}, bf16[256,3072]{1,0:T(8,128)(2,1)S(1)}, f32[256,768]{1,0:T(8,128)S(1)}, f32[256,768]{1,0:T(8,128)S(1)}) custom-call(f32[256,768]{1,0:T(8,128)S(1)} %get-tuple-element.288.sum_ref, f32[8,768]{1,0:T(8,128)S(1)} %get-tuple-element.289.gain_ref, ...), custom_call_target="tpu_custom_call" | custom-call | flops 1073741824 | bytes 4194304 | tf_op jit(solution)/shard_map/pallas_call | solution.py:506
  186.0 2.4 shard_map.321
  188.5 4.7 %shard_map.322 = (bf16[256,3072]{1,0:T(8,128)(2,1)S(1)}, f32[256,768]{1,0:T(8,128)S(1)}) custom-call(f32[256,768]{1,0:T(8,128)S(1)} %get-tuple-element.308.grad_ref, bf16[256,768]{1,0:T(8,128)(2,1)S(1)} %get-tuple-element.309.refs_0_.low_ref, bf16[256,3072]{1,0:T(8,128)(2,1)S(1)} %get-tuple-element.310.slope_ref, bf16[768,9344]{1,0:T(8,128)(2,1)S(1)} %bitcast.91, ...), custom_call_target="tpu_custom_call" | custom-call | flops 1073741824 | bytes 4194304 | tf_op jit(solution)/shard_map/pallas_call | solution.py:571
  194.2 1.5 collective-permute-start.37
  196.2 7.2 %shard_map.323 = (bf16[256,3072]{1,0:T(8,128)(2,1)S(1)}, f32[256,768]{1,0:T(8,128)S(1)}, f32[1,768]{1,0:T(1,128)S(1)}) custom-call(s32[1]{0:T(128)S(6)} %copy.49.length_ref, f32[256,768]{1,0:T(8,128)S(1)} %get-tuple-element.311.grad_ref, f32[256,768]{1,0:T(8,128)S(1)} %get-tuple-element.288.sum_ref, f32[8,768]{1,0:T(8,128)S(1)} %get-tuple-element.289.gain_ref, ...), custom_call_target="tpu_custom_call" | custom-call | flops 1073741824 | bytes 4194304 | tf_op jit(solution)/shard_map/pallas_call | solution.py:626
  203.4 2.9 shard_map.325
  206.3 3.0 collective-permute-done.36.one.refs_1_
  211.9 1.7 collective-permute-start.46
  215.7 4.5 %shard_map.328 = (bf16[256,3072]{1,0:T(8,128)(2,1)S(1)}, f32[256,768]{1,0:T(8,128)S(1)}) custom-call(f32[256,768]{1,0:T(8,128)S(1)} %get-tuple-element.341.grad_ref, bf16[256,768]{1,0:T(8,128)(2,1)S(1)} %get-tuple-element.342.low_ref.refs_0_, bf16[256,3072]{1,0:T(8,128)(2,1)S(1)} %get-tuple-element.343.slope_ref, bf16[768,6144]{1,0:T(8,128)(2,1)S(1)} %bitcast.94, ...), custom_call_target="tpu_custom_call" | custom-call | flops 1073741824 | bytes 4194304 | tf_op jit(solution)/shard_map/pallas_call | solution.py:571
  220.3 1.4 shard_map.330
  221.7 11.8 %collective-permute-done.43.refs_3_ = bf16[48,3072]{1,0:T(8,128)(2,1)S(1)} collective-permute-done((bf16[48,3072]{1,0:T(8,128)(2,1)S(1)}, bf16[48,3072]{1,0:T(8,128)(2,1)S(1)}, u32[]{:S(2)}, u32[]{:S(2)}) %collective-permute-start.43) | collective-permute-done | bytes 294944 | tf_op jit(solution)/shard_map/ppermute | solution.py:275
  235.8 1.5 collective-permute-start.52
  239.8 8.1 %shard_map.332 = (bf16[256,3072]{1,0:T(8,128)(2,1)S(1)}, f32[256,768]{1,0:T(8,128)}, f32[1,768]{1,0:T(1,128)S(1)}) custom-call(s32[1]{0:T(128)S(6)} %copy.49.length_ref, f32[256,768]{1,0:T(8,128)S(1)} %get-tuple-element.374.grad_ref, f32[256,768]{1,0:T(8,128)S(1)} %get-tuple-element.281.sum_ref, f32[8,768]{1,0:T(8,128)S(1)} %get-tuple-element.282.gain_ref, ...), custom_call_target="tpu_custom_call" | custom-call | flops 1073741824 | bytes 4194304 | tf_op jit(solution)/shard_map/pallas_call | solution.py:626
  247.9 5.5 %shard_map.334 = (bf16[96,6144]{1,0:T(8,128)(2,1)S(1)}, bf16[96,6144]{1,0:T(8,128)(2,1)S(1)}, bf16[48,6144]{1,0:T(8,128)(2,1)S(1)}, bf16[48,6144]{1,0:T(8,128)(2,1)S(1)}, bf16[96,6144]{1,0:T(8,128)(2,1)S(1)}) custom-call(bf16[384,384]{1,0:T(8,128)(2,1)S(1)} %get-tuple-element.379.ga.refs_0_, bf16[384,384]{1,0:T(8,128)(2,1)S(1)} %collective-permute-done.47.gb.refs_1_, ...), custom_call_target="tpu_custom_call" | custom-call | flops 1073741824 | bytes 4194304 | tf_op jit(solution)/shard_map/pallas_call | solution.py:681
  253.4 4.9 %collective-permute-done.49.refs_8_ = bf16[48,3072]{1,0:T(8,128)(2,1)S(1)} collective-permute-done((bf16[48,3072]{1,0:T(8,128)(2,1)S(1)}, bf16[48,3072]{1,0:T(8,128)(2,1)S(1)}, u32[]{:S(2)}, u32[]{:S(2)}) %collective-permute-start.49) | collective-permute-done | bytes 294944 | tf_op jit(solution)/shard_map/ppermute | solution.py:275
  258.7 1.3 collective-permute-start.62
  261.8 5.4 %collective-permute-start.56 = (bf16[24,6144]{1,0:T(8,128)(2,1)S(1)}, bf16[24,6144]{1,0:T(8,128)(2,1)S(1)}, u32[]{:S(2)}, u32[]{:S(2)}) collective-permute-start(bf16[24,6144]{1,0:T(8,128)(2,1)S(1)} %get-tuple-element.404), channel_id=1, source_target_pairs={{0,2},{1,3},{2,0},{3,1},{4,6},{5,7},{6,4},{7,5},{8,10},{9,11},{10,... | collective-permute-start | bytes 884744 | tf_op jit(solution)/shard_map/ppermute | solution.py:275
  267.2 1.9 collective-permute-start.57
  269.2 11.2 %collective-permute-done.56 = bf16[24,6144]{1,0:T(8,128)(2,1)S(1)} collective-permute-done((bf16[24,6144]{1,0:T(8,128)(2,1)S(1)}, bf16[24,6144]{1,0:T(8,128)(2,1)S(1)}, u32[]{:S(2)}, u32[]{:S(2)}) %collective-permute-start.56) | collective-permute-done | bytes 294944 | tf_op jit(solution)/shard_map/ppermute | solution.py:275
  281.5 2.9 collective-permute-start.60
  284.4 2.5 collective-permute-start.58
  286.9 1.4 shard_map.338
  288.3 4.7 %collective-permute-done.58 = bf16[24,6144]{1,0:T(8,128)(2,1)S(1)} collective-permute-done((bf16[24,6144]{1,0:T(8,128)(2,1)S(1)}, bf16[24,6144]{1,0:T(8,128)(2,1)S(1)}, u32[]{:S(2)}, u32[]{:S(2)}) %collective-permute-start.58) | collective-permute-done | bytes 294944 | tf_op jit(solution)/shard_map/ppermute | solution.py:275
  294.1 5.0 %collective-permute-start.65 = (bf16[24,3200]{1,0:T(8,128)(2,1)S(1)}, bf16[24,3200]{1,0:T(8,128)(2,1)S(1)}, u32[]{:S(2)}, u32[]{:S(2)}) collective-permute-start(bf16[24,3200]{1,0:T(8,128)(2,1)S(1)} %get-tuple-element.435), channel_id=1, source_target_pairs={{0,2},{1,3},{2,0},{3,1},{4,6},{5,7},{6,4},{7,5},{8,10},{9,11},{10,... | collective-permute-start | bytes 460808 | tf_op jit(solution)/shard_map/ppermute | solution.py:275
  299.1 1.5 collective-permute-start.66
  301.4 1.4 collective-permute-start.67
  304.0 1.4 collective-permute-start.69
  306.8 7.5 %collective-permute-start.74 = (bf16[96,3200]{1,0:T(8,128)(2,1)S(1)}, bf16[96,3200]{1,0:T(8,128)(2,1)S(1)}, u32[]{:S(2)}, u32[]{:S(2)}) collective-permute-start(bf16[96,3200]{1,0:T(8,128)(2,1)S(1)} %get-tuple-element.459), channel_id=1, source_target_pairs={{0,1},{1,0},{2,3},{3,2},{4,5},{5,4},{6,7},{7,6},{8,24},{9,25},{10,... | collective-permute-start | bytes 1843208 | tf_op jit(solution)/shard_map/ppermute | solution.py:275
  314.5 4.9 %collective-permute-done.68.refs_3_ = bf16[48,6144]{1,0:T(8,128)(2,1)S(1)} collective-permute-done((bf16[48,6144]{1,0:T(8,128)(2,1)S(1)}, bf16[48,6144]{1,0:T(8,128)(2,1)S(1)}, u32[]{:S(2)}, u32[]{:S(2)}) %collective-permute-start.68) | collective-permute-done | bytes 589856 | tf_op jit(solution)/shard_map/ppermute | solution.py:275
  321.8 1.7 collective-permute-start.71
  323.5 1.6 collective-permute-start.72
  325.1 6.3 %collective-permute-done.73.one.refs_1_ = bf16[96,3200]{1,0:T(8,128)(2,1)S(1)} collective-permute-done((bf16[96,3200]{1,0:T(8,128)(2,1)S(1)}, bf16[96,3200]{1,0:T(8,128)(2,1)S(1)}, u32[]{:S(2)}, u32[]{:S(2)}) %collective-permute-start.73) | collective-permute-done | bytes 614432 | tf_op jit(solution)/shard_map/ppermute | solution.py:275
  331.5 1.6 collective-permute-start.75
  333.9 9.9 %collective-permute-done.71 = bf16[24,6144]{1,0:T(8,128)(2,1)S(1)} collective-permute-done((bf16[24,6144]{1,0:T(8,128)(2,1)S(1)}, bf16[24,6144]{1,0:T(8,128)(2,1)S(1)}, u32[]{:S(2)}, u32[]{:S(2)}) %collective-permute-start.71) | collective-permute-done | bytes 294944 | tf_op jit(solution)/shard_map/ppermute | solution.py:275
  344.0 3.8 %collective-permute-start.77 = (bf16[24,3200]{1,0:T(8,128)(2,1)S(1)}, bf16[24,3200]{1,0:T(8,128)(2,1)S(1)}, u32[]{:S(2)}, u32[]{:S(2)}) collective-permute-start(bf16[24,3200]{1,0:T(8,128)(2,1)S(1)} %get-tuple-element.470), channel_id=1, source_target_pairs={{0,2},{1,3},{2,0},{3,1},{4,6},{5,7},{6,4},{7,5},{8,10},{9,11},{10,... | collective-permute-start | bytes 460808 | tf_op jit(solution)/shard_map/ppermute | solution.py:275
  348.6 1.6 collective-permute-start.79
  352.2 7.3 %collective-permute-done.78.refs_2_ = bf16[24,3200]{1,0:T(8,128)(2,1)S(1)} collective-permute-done((bf16[24,3200]{1,0:T(8,128)(2,1)S(1)}, bf16[24,3200]{1,0:T(8,128)(2,1)S(1)}, u32[]{:S(2)}, u32[]{:S(2)}) %collective-permute-start.78) | collective-permute-done | bytes 153632 | tf_op jit(solution)/shard_map/ppermute | solution.py:275
  (251 shorter events, 55.0 us)
Async XLA Ops:
  7.2 140.7 %all-gather.2.cloned.1.call-start = ((), (), s32[]{:S(2)}) async-start(), calls=%async_computation | async-start | bytes 14800896 | tf_op jit(solution)/shard_map/all_gather | solution.py:57
  21.2 11.3 %collective-permute-start.2 = (bf16[24,6144]{1,0:T(8,128)(2,1)S(1)}, bf16[24,6144]{1,0:T(8,128)(2,1)S(1)}, u32[]{:S(2)}, u32[]{:S(2)}) collective-permute-start(bf16[24,6144]{1,0:T(8,128)(2,1)S(1)} %pad_maximum_fusion.4), channel_id=1, source_target_pairs={{0,2},{1,3},{2,0},{3,1},{4,6},{5,7},{6,4},{7,5},{8,10},{9,11},{10,... | collective-permute-start | bytes 884744 | tf_op jit(solution)/shard_map/ppermute | solution.py:275
  23.0 9.5 %collective-permute-start.1 = (bf16[48,3200]{1,0:T(8,128)(2,1)S(1)}, bf16[48,3200]{1,0:T(8,128)(2,1)S(1)}, u32[]{:S(2)}, u32[]{:S(2)}) collective-permute-start(bf16[48,3200]{1,0:T(8,128)(2,1)S(1)} %pad_maximum_fusion.3), channel_id=1, source_target_pairs={{2,4},{3,5},{4,2},{5,3},{10,12},{11,13},{12,10},{13,11},{18,20},{1... | collective-permute-start | bytes 921608 | tf_op jit(solution)/shard_map/ppermute | solution.py:275
  32.5 17.4 %collective-permute-start.3 = (bf16[48,3200]{1,0:T(8,128)(2,1)S(1)}, bf16[48,3200]{1,0:T(8,128)(2,1)S(1)}, u32[]{:S(2)}, u32[]{:S(2)}) collective-permute-start(bf16[48,3200]{1,0:T(8,128)(2,1)S(1)} %collective-permute-done.1), channel_id=1, source_target_pairs={{2,0},{3,1},{4,6},{5,7},{10,8},{11,9},{12,14},{13,15},{18,16},{19,... | collective-permute-start | bytes 921608 | tf_op jit(solution)/shard_map/ppermute | solution.py:275
  34.3 15.6 %collective-permute-start.4 = (bf16[48,6144]{1,0:T(8,128)(2,1)S(1)}, bf16[48,6144]{1,0:T(8,128)(2,1)S(1)}, u32[]{:S(2)}, u32[]{:S(2)}) collective-permute-start(bf16[48,6144]{1,0:T(8,128)(2,1)S(1)} %pad_maximum_fusion), channel_id=1, source_target_pairs={{2,4},{3,5},{4,2},{5,3},{10,12},{11,13},{12,10},{13,11},{18,20},{1... | collective-permute-start | bytes 1769480 | tf_op jit(solution)/shard_map/ppermute | solution.py:275
  50.0 38.4 %collective-permute-start.7 = (bf16[48,6144]{1,0:T(8,128)(2,1)S(1)}, bf16[48,6144]{1,0:T(8,128)(2,1)S(1)}, u32[]{:S(2)}, u32[]{:S(2)}) collective-permute-start(bf16[48,6144]{1,0:T(8,128)(2,1)S(1)} %collective-permute-done.4), channel_id=1, source_target_pairs={{2,0},{3,1},{4,6},{5,7},{10,8},{11,9},{12,14},{13,15},{18,16},{19,... | collective-permute-start | bytes 1769480 | tf_op jit(solution)/shard_map/ppermute | solution.py:275
  51.3 37.1 %collective-permute-start.6 = (bf16[48,3200]{1,0:T(8,128)(2,1)S(1)}, bf16[48,3200]{1,0:T(8,128)(2,1)S(1)}, u32[]{:S(2)}, u32[]{:S(2)}) collective-permute-start(bf16[48,3200]{1,0:T(8,128)(2,1)S(1)} %pad_maximum_fusion.3), channel_id=1, source_target_pairs={{0,1},{1,0},{2,3},{3,2},{4,5},{5,4},{6,7},{7,6},{8,24},{9,25},{10,... | collective-permute-start | bytes 921608 | tf_op jit(solution)/shard_map/ppermute | solution.py:275
  52.8 38.0 %collective-permute-start.8 = (bf16[48,3200]{1,0:T(8,128)(2,1)S(1)}, bf16[48,3200]{1,0:T(8,128)(2,1)}, u32[]{:S(2)}, u32[]{:S(2)}) collective-permute-start(bf16[48,3200]{1,0:T(8,128)(2,1)S(1)} %pad_maximum_fusion.3), channel_id=1, source_target_pairs={{0,16},{1,17},{2,18},{3,19},{4,20},{5,21},{6,22},{7,23},{8,9},{9,8... | collective-permute-start | bytes 921608 | tf_op jit(solution)/shard_map/ppermute | solution.py:275
  54.3 34.1 %collective-permute-start.5 = (bf16[48,3200]{1,0:T(8,128)(2,1)S(1)}, bf16[48,3200]{1,0:T(8,128)(2,1)}, u32[]{:S(2)}, u32[]{:S(2)}) collective-permute-start(bf16[48,3200]{1,0:T(8,128)(2,1)S(1)} %broadcast_select_fusion.1), channel_id=1, source_target_pairs={{0,16},{1,17},{2,18},{3,19},{4,20},{5,21},{6,22},{7,23},{8,9},{9,8... | collective-permute-start | bytes 921608 | tf_op jit(solution)/shard_map/ppermute | solution.py:275
  54.9 36.0 %collective-permute-start.13 = (bf16[48,3200]{1,0:T(8,128)(2,1)S(1)}, bf16[48,3200]{1,0:T(8,128)(2,1)}, u32[]{:S(2)}, u32[]{:S(2)}) collective-permute-start(bf16[48,3200]{1,0:T(8,128)(2,1)S(1)} %broadcast_select_fusion.1), channel_id=1, source_target_pairs={{0,1},{1,0},{2,3},{3,2},{4,5},{5,4},{6,7},{7,6},{8,24},{9,25},{10,... | collective-permute-start | bytes 921608 | tf_op jit(solution)/shard_map/ppermute | solution.py:275
  88.4 13.6 %collective-permute-start.11 = (bf16[48,3200]{1,0:T(8,128)(2,1)S(1)}, bf16[48,3200]{1,0:T(8,128)(2,1)S(1)}, u32[]{:S(2)}, u32[]{:S(2)}) collective-permute-start(bf16[48,3200]{1,0:T(8,128)(2,1)S(1)} %collective-permute-done.6), channel_id=1, source_target_pairs={{0,16},{1,17},{2,18},{3,19},{4,20},{5,21},{6,22},{7,23},{8,9},{9,8... | collective-permute-start | bytes 921608 | tf_op jit(solution)/shard_map/ppermute | solution.py:275
  89.2 17.0 %collective-permute-start.12 = (bf16[48,3200]{1,0:T(8,128)(2,1)}, bf16[48,3200]{1,0:T(8,128)(2,1)}, u32[]{:S(2)}, u32[]{:S(2)}) collective-permute-start(bf16[48,3200]{1,0:T(8,128)(2,1)} %collective-permute-done.5), channel_id=1, source_target_pairs={{0,1},{1,0},{2,3},{3,2},{4,5},{5,4},{6,7},{7,6},{8,24},{9,25},{10,... | collective-permute-start | bytes 921608 | tf_op jit(solution)/shard_map/ppermute | solution.py:275
  90.8 30.1 %collective-permute-start.24 = (bf16[48,6144]{1,0:T(8,128)(2,1)S(1)}, bf16[48,6144]{1,0:T(8,128)(2,1)S(1)}, u32[]{:S(2)}, u32[]{:S(2)}) collective-permute-start(bf16[48,6144]{1,0:T(8,128)(2,1)S(1)} %pad_maximum_fusion), channel_id=1, source_target_pairs={{0,16},{1,17},{2,18},{3,19},{4,20},{5,21},{6,22},{7,23},{8,9},{9,8... | collective-permute-start | bytes 1769480 | tf_op jit(solution)/shard_map/ppermute | solution.py:275
  106.2 15.6 %collective-permute-start.14 = (bf16[48,3200]{1,0:T(8,128)(2,1)S(1)}, bf16[48,3200]{1,0:T(8,128)(2,1)S(1)}, u32[]{:S(2)}, u32[]{:S(2)}) collective-permute-start(bf16[48,3200]{1,0:T(8,128)(2,1)S(1)} %collective-permute-done.11), channel_id=1, source_target_pairs={{0,8},{1,9},{2,10},{3,11},{4,12},{5,13},{6,14},{7,15},{8,0},{9,1},... | collective-permute-start | bytes 921608 | tf_op jit(solution)/shard_map/ppermute | solution.py:275
  106.9 16.1 %collective-permute-start.15 = (bf16[48,3200]{1,0:T(8,128)(2,1)}, bf16[48,3200]{1,0:T(8,128)(2,1)}, u32[]{:S(2)}, u32[]{:S(2)}) collective-permute-start(bf16[48,3200]{1,0:T(8,128)(2,1)} %collective-permute-done.12), channel_id=1, source_target_pairs={{0,8},{1,9},{2,10},{3,11},{4,12},{5,13},{6,14},{7,15},{8,0},{9,1},... | collective-permute-start | bytes 921608 | tf_op jit(solution)/shard_map/ppermute | solution.py:275
  107.4 16.2 %collective-permute-start.16 = (bf16[48,3200]{1,0:T(8,128)(2,1)}, bf16[48,3200]{1,0:T(8,128)(2,1)}, u32[]{:S(2)}, u32[]{:S(2)}) collective-permute-start(bf16[48,3200]{1,0:T(8,128)(2,1)} %collective-permute-done.8), channel_id=1, source_target_pairs={{0,8},{1,9},{2,10},{3,11},{4,12},{5,13},{6,14},{7,15},{8,0},{9,1},... | collective-permute-start | bytes 921608 | tf_op jit(solution)/shard_map/ppermute | solution.py:275
  107.5 17.8 %collective-permute-start.17 = (bf16[48,3200]{1,0:T(8,128)(2,1)}, bf16[48,3200]{1,0:T(8,128)(2,1)}, u32[]{:S(2)}, u32[]{:S(2)}) collective-permute-start(bf16[48,3200]{1,0:T(8,128)(2,1)} %collective-permute-done.5), channel_id=1, source_target_pairs={{0,8},{1,9},{2,10},{3,11},{4,12},{5,13},{6,14},{7,15},{8,0},{9,1},... | collective-permute-start | bytes 921608 | tf_op jit(solution)/shard_map/ppermute | solution.py:275
  123.0 17.2 %collective-permute-start.10 = (bf16[48,6144]{1,0:T(8,128)(2,1)S(1)}, bf16[48,6144]{1,0:T(8,128)(2,1)}, u32[]{:S(2)}, u32[]{:S(2)}) collective-permute-start(bf16[48,6144]{1,0:T(8,128)(2,1)S(1)} %pad_maximum_fusion), channel_id=1, source_target_pairs={{0,1},{1,0},{2,3},{3,2},{4,5},{5,4},{6,7},{7,6},{8,24},{9,25},{10,... | collective-permute-start | bytes 1769480 | tf_op jit(solution)/shard_map/ppermute | solution.py:275
  123.6 16.6 %collective-permute-start.9 = (bf16[48,6144]{1,0:T(8,128)(2,1)S(1)}, bf16[48,6144]{1,0:T(8,128)(2,1)}, u32[]{:S(2)}, u32[]{:S(2)}) collective-permute-start(bf16[48,6144]{1,0:T(8,128)(2,1)S(1)} %broadcast_select_fusion), channel_id=1, source_target_pairs={{0,16},{1,17},{2,18},{3,19},{4,20},{5,21},{6,22},{7,23},{8,9},{9,8... | collective-permute-start | bytes 1769480 | tf_op jit(solution)/shard_map/ppermute | solution.py:275
  125.3 22.6 %collective-permute-start.25 = (bf16[48,6144]{1,0:T(8,128)(2,1)S(1)}, bf16[48,6144]{1,0:T(8,128)(2,1)}, u32[]{:S(2)}, u32[]{:S(2)}) collective-permute-start(bf16[48,6144]{1,0:T(8,128)(2,1)S(1)} %broadcast_select_fusion), channel_id=1, source_target_pairs={{0,1},{1,0},{2,3},{3,2},{4,5},{5,4},{6,7},{7,6},{8,24},{9,25},{10,... | collective-permute-start | bytes 1769480 | tf_op jit(solution)/shard_map/ppermute | solution.py:275
  129.0 18.9 %collective-permute-start.33 = (bf16[48,6144]{1,0:T(8,128)(2,1)S(1)}, bf16[48,6144]{1,0:T(8,128)(2,1)}, u32[]{:S(2)}, u32[]{:S(2)}) collective-permute-start(bf16[48,6144]{1,0:T(8,128)(2,1)S(1)} %broadcast_select_fusion), channel_id=1, source_target_pairs={{0,8},{1,9},{2,10},{3,11},{4,12},{5,13},{6,14},{7,15},{8,0},{9,1},... | collective-permute-start | bytes 1769480 | tf_op jit(solution)/shard_map/ppermute | solution.py:275
  129.4 19.1 %collective-permute-start.28 = (bf16[48,6144]{1,0:T(8,128)(2,1)}, bf16[48,6144]{1,0:T(8,128)(2,1)}, u32[]{:S(2)}, u32[]{:S(2)}) collective-permute-start(bf16[48,6144]{1,0:T(8,128)(2,1)} %copy-done.9), channel_id=1, source_target_pairs={{0,8},{1,9},{2,10},{3,11},{4,12},{5,13},{6,14},{7,15},{8,0},{9,1},... | collective-permute-start | bytes 1769480 | tf_op jit(solution)/shard_map/ppermute | solution.py:275
  140.2 16.6 %collective-permute-start.22 = (bf16[48,6144]{1,0:T(8,128)(2,1)}, bf16[48,6144]{1,0:T(8,128)(2,1)}, u32[]{:S(2)}, u32[]{:S(2)}) collective-permute-start(bf16[48,6144]{1,0:T(8,128)(2,1)} %collective-permute-done.10), channel_id=1, source_target_pairs={{0,16},{1,17},{2,18},{3,19},{4,20},{5,21},{6,22},{7,23},{8,9},{9,8... | collective-permute-start | bytes 1769480 | tf_op jit(solution)/shard_map/ppermute | solution.py:275
  141.6 16.7 %collective-permute-start.23 = (bf16[48,6144]{1,0:T(8,128)(2,1)}, bf16[48,6144]{1,0:T(8,128)(2,1)}, u32[]{:S(2)}, u32[]{:S(2)}) collective-permute-start(bf16[48,6144]{1,0:T(8,128)(2,1)} %collective-permute-done.9), channel_id=1, source_target_pairs={{0,1},{1,0},{2,3},{3,2},{4,5},{5,4},{6,7},{7,6},{8,24},{9,25},{10,... | collective-permute-start | bytes 1769480 | tf_op jit(solution)/shard_map/ppermute | solution.py:275
  147.9 10.4 %collective-permute-start.31 = (bf16[48,6144]{1,0:T(8,128)(2,1)}, bf16[48,6144]{1,0:T(8,128)(2,1)}, u32[]{:S(2)}, u32[]{:S(2)}) collective-permute-start(bf16[48,6144]{1,0:T(8,128)(2,1)} %collective-permute-done.25), channel_id=1, source_target_pairs={{0,8},{1,9},{2,10},{3,11},{4,12},{5,13},{6,14},{7,15},{8,0},{9,1},... | collective-permute-start | bytes 1769480 | tf_op jit(solution)/shard_map/ppermute | solution.py:275
  147.9 10.9 %collective-permute-start.29 = (bf16[48,6144]{1,0:T(8,128)(2,1)}, bf16[48,6144]{1,0:T(8,128)(2,1)S(1)}, u32[]{:S(2)}, u32[]{:S(2)}) collective-permute-start(bf16[48,6144]{1,0:T(8,128)(2,1)} %collective-permute-done.9), channel_id=1, source_target_pairs={{0,8},{1,9},{2,10},{3,11},{4,12},{5,13},{6,14},{7,15},{8,0},{9,1},... | collective-permute-start | bytes 1769480 | tf_op jit(solution)/shard_map/ppermute | solution.py:275
  148.4 10.4 %collective-permute-start.30 = (bf16[48,6144]{1,0:T(8,128)(2,1)}, bf16[48,6144]{1,0:T(8,128)(2,1)S(1)}, u32[]{:S(2)}, u32[]{:S(2)}) collective-permute-start(bf16[48,6144]{1,0:T(8,128)(2,1)} %collective-permute-done.10), channel_id=1, source_target_pairs={{0,8},{1,9},{2,10},{3,11},{4,12},{5,13},{6,14},{7,15},{8,0},{9,1},... | collective-permute-start | bytes 1769480 | tf_op jit(solution)/shard_map/ppermute | solution.py:275
  185.2 10.4 %collective-permute-start.38 = (bf16[384,768]{1,0:T(8,128)(2,1)S(1)}, bf16[384,768]{1,0:T(8,128)(2,1)S(1)}, u32[]{:S(2)}, u32[]{:S(2)}) collective-permute-start(bf16[384,768]{1,0:T(8,128)(2,1)S(1)} %get-tuple-element.320), channel_id=1, source_target_pairs={{0,8},{1,9},{2,10},{3,11},{4,12},{5,13},{6,14},{7,15},{8,0},{9,1},... | collective-permute-start | bytes 1769480 | tf_op jit(solution)/shard_map/ppermute | solution.py:275
  193.5 15.8 %collective-permute-start.36 = (bf16[96,3072]{1,0:T(8,128)(2,1)S(1)}, bf16[96,3072]{1,0:T(8,128)(2,1)S(1)}, u32[]{:S(2)}, u32[]{:S(2)}) collective-permute-start(bf16[96,3072]{1,0:T(8,128)(2,1)S(1)} %get-tuple-element.303), channel_id=1, source_target_pairs={{0,16},{1,17},{2,18},{3,19},{4,20},{5,21},{6,22},{7,23},{8,9},{9,8... | collective-permute-start | bytes 1769480 | tf_op jit(solution)/shard_map/ppermute | solution.py:275
  194.2 15.2 %collective-permute-start.37 = (bf16[96,3072]{1,0:T(8,128)(2,1)S(1)}, bf16[96,3072]{1,0:T(8,128)(2,1)S(1)}, u32[]{:S(2)}, u32[]{:S(2)}) collective-permute-start(bf16[96,3072]{1,0:T(8,128)(2,1)S(1)} %get-tuple-element.304), channel_id=1, source_target_pairs={{0,1},{1,0},{2,3},{3,2},{4,5},{5,4},{6,7},{7,6},{8,24},{9,25},{10,... | collective-permute-start | bytes 1769480 | tf_op jit(solution)/shard_map/ppermute | solution.py:275
  195.6 7.8 %collective-permute-start.40 = (bf16[256,768]{1,0:T(8,128)(2,1)S(1)}, bf16[256,768]{1,0:T(8,128)(2,1)S(1)}, u32[]{:S(2)}, u32[]{:S(2)}) collective-permute-start(bf16[256,768]{1,0:T(8,128)(2,1)S(1)} %get-tuple-element.506), channel_id=1, source_target_pairs={{0,8},{1,9},{2,10},{3,11},{4,12},{5,13},{6,14},{7,15},{8,0},{9,1},... | collective-permute-start | bytes 1179656 | tf_op jit(solution)/shard_map/ppermute | solution.py:275
  195.6 7.8 %collective-permute-start.41 = (bf16[256,768]{1,0:T(8,128)(2,1)S(1)}, bf16[256,768]{1,0:T(8,128)(2,1)S(1)}, u32[]{:S(2)}, u32[]{:S(2)}) collective-permute-start(bf16[256,768]{1,0:T(8,128)(2,1)S(1)} %get-tuple-element.505), channel_id=1, source_target_pairs={{0,8},{1,9},{2,10},{3,11},{4,12},{5,13},{6,14},{7,15},{8,0},{9,1},... | collective-permute-start | bytes 1179656 | tf_op jit(solution)/shard_map/ppermute | solution.py:275
  211.4 22.1 %collective-permute-start.45 = (bf16[96,3072]{1,0:T(8,128)(2,1)S(1)}, bf16[96,3072]{1,0:T(8,128)(2,1)S(1)}, u32[]{:S(2)}, u32[]{:S(2)}) collective-permute-start(bf16[96,3072]{1,0:T(8,128)(2,1)S(1)} %get-tuple-element.334), channel_id=1, source_target_pairs={{0,16},{1,17},{2,18},{3,19},{4,20},{5,21},{6,22},{7,23},{8,9},{9,8... | collective-permute-start | bytes 1769480 | tf_op jit(solution)/shard_map/ppermute | solution.py:275
  211.9 21.7 %collective-permute-start.46 = (bf16[96,3072]{1,0:T(8,128)(2,1)S(1)}, bf16[96,3072]{1,0:T(8,128)(2,1)S(1)}, u32[]{:S(2)}, u32[]{:S(2)}) collective-permute-start(bf16[96,3072]{1,0:T(8,128)(2,1)S(1)} %get-tuple-element.335), channel_id=1, source_target_pairs={{0,1},{1,0},{2,3},{3,2},{4,5},{5,4},{6,7},{7,6},{8,24},{9,25},{10,... | collective-permute-start | bytes 1769480 | tf_op jit(solution)/shard_map/ppermute | solution.py:275
  213.7 19.8 %collective-permute-start.43 = (bf16[48,3072]{1,0:T(8,128)(2,1)S(1)}, bf16[48,3072]{1,0:T(8,128)(2,1)S(1)}, u32[]{:S(2)}, u32[]{:S(2)}) collective-permute-start(bf16[48,3072]{1,0:T(8,128)(2,1)S(1)} %get-tuple-element.331), channel_id=1, source_target_pairs={{0,16},{1,17},{2,18},{3,19},{4,20},{5,21},{6,22},{7,23},{8,9},{9,8... | collective-permute-start | bytes 884744 | tf_op jit(solution)/shard_map/ppermute | solution.py:275
  214.4 19.1 %collective-permute-start.44 = (bf16[48,3072]{1,0:T(8,128)(2,1)S(1)}, bf16[48,3072]{1,0:T(8,128)(2,1)S(1)}, u32[]{:S(2)}, u32[]{:S(2)}) collective-permute-start(bf16[48,3072]{1,0:T(8,128)(2,1)S(1)} %get-tuple-element.332), channel_id=1, source_target_pairs={{0,1},{1,0},{2,3},{3,2},{4,5},{5,4},{6,7},{7,6},{8,24},{9,25},{10,... | collective-permute-start | bytes 884744 | tf_op jit(solution)/shard_map/ppermute | solution.py:275
  215.7 23.0 %collective-permute-start.53 = (bf16[256,3072]{1,0:T(8,128)(2,1)S(1)}, bf16[256,3072]{1,0:T(8,128)(2,1)S(1)}, u32[]{:S(2)}, u32[]{:S(2)}) collective-permute-start(bf16[256,3072]{1,0:T(8,128)(2,1)S(1)} %get-tuple-element.381.refs_2_), channel_id=1, source_target_pairs={{0,8},{1,9},{2,10},{3,11},{4,12},{5,13},{6,14},{7,15},{8,0},{9,1},... | collective-permute-start | bytes 4718600 | tf_op jit(solution)/shard_map/ppermute | solution.py:275
  233.5 14.3 %collective-permute-start.55 = (bf16[256,3072]{1,0:T(8,128)(2,1)S(1)}, bf16[256,3072]{1,0:T(8,128)(2,1)S(1)}, u32[]{:S(2)}, u32[]{:S(2)}) collective-permute-start(bf16[256,3072]{1,0:T(8,128)(2,1)S(1)} %get-tuple-element.387.refs_6_), channel_id=1, source_target_pairs={{0,8},{1,9},{2,10},{3,11},{4,12},{5,13},{6,14},{7,15},{8,0},{9,1},... | collective-permute-start | bytes 4718600 | tf_op jit(solution)/shard_map/ppermute | solution.py:275
  235.4 23.0 %collective-permute-start.51 = (bf16[96,3200]{1,0:T(8,128)(2,1)S(1)}, bf16[96,3200]{1,0:T(8,128)(2,1)S(1)}, u32[]{:S(2)}, u32[]{:S(2)}) collective-permute-start(bf16[96,3200]{1,0:T(8,128)(2,1)S(1)} %get-tuple-element.369), channel_id=1, source_target_pairs={{0,16},{1,17},{2,18},{3,19},{4,20},{5,21},{6,22},{7,23},{8,9},{9,8... | collective-permute-start | bytes 1843208 | tf_op jit(solution)/shard_map/ppermute | solution.py:275
  235.8 22.5 %collective-permute-start.52 = (bf16[96,3200]{1,0:T(8,128)(2,1)S(1)}, bf16[96,3200]{1,0:T(8,128)(2,1)S(1)}, u32[]{:S(2)}, u32[]{:S(2)}) collective-permute-start(bf16[96,3200]{1,0:T(8,128)(2,1)S(1)} %get-tuple-element.370), channel_id=1, source_target_pairs={{0,1},{1,0},{2,3},{3,2},{4,5},{5,4},{6,7},{7,6},{8,24},{9,25},{10,... | collective-permute-start | bytes 1843208 | tf_op jit(solution)/shard_map/ppermute | solution.py:275
  237.9 20.5 %collective-permute-start.49 = (bf16[48,3072]{1,0:T(8,128)(2,1)S(1)}, bf16[48,3072]{1,0:T(8,128)(2,1)S(1)}, u32[]{:S(2)}, u32[]{:S(2)}) collective-permute-start(bf16[48,3072]{1,0:T(8,128)(2,1)S(1)} %get-tuple-element.366), channel_id=1, source_target_pairs={{0,16},{1,17},{2,18},{3,19},{4,20},{5,21},{6,22},{7,23},{8,9},{9,8... | collective-permute-start | bytes 884744 | tf_op jit(solution)/shard_map/ppermute | solution.py:275
  238.7 19.6 %collective-permute-start.50 = (bf16[48,3072]{1,0:T(8,128)(2,1)S(1)}, bf16[48,3072]{1,0:T(8,128)(2,1)S(1)}, u32[]{:S(2)}, u32[]{:S(2)}) collective-permute-start(bf16[48,3072]{1,0:T(8,128)(2,1)S(1)} %get-tuple-element.367), channel_id=1, source_target_pairs={{0,1},{1,0},{2,3},{3,2},{4,5},{5,4},{6,7},{7,6},{8,24},{9,25},{10,... | collective-permute-start | bytes 884744 | tf_op jit(solution)/shard_map/ppermute | solution.py:275
  258.4 26.0 %collective-permute-start.63 = (bf16[256,3072]{1,0:T(8,128)(2,1)S(1)}, bf16[256,3072]{1,0:T(8,128)(2,1)S(1)}, u32[]{:S(2)}, u32[]{:S(2)}) collective-permute-start(bf16[256,3072]{1,0:T(8,128)(2,1)S(1)} %get-tuple-element.420.ra), channel_id=1, source_target_pairs={{0,8},{1,9},{2,10},{3,11},{4,12},{5,13},{6,14},{7,15},{8,0},{9,1},... | collective-permute-start | bytes 4718600 | tf_op jit(solution)/shard_map/ppermute | solution.py:275
  258.4 35.4 %collective-permute-start.61 = (bf16[96,6144]{1,0:T(8,128)(2,1)S(1)}, bf16[96,6144]{1,0:T(8,128)(2,1)S(1)}, u32[]{:S(2)}, u32[]{:S(2)}) collective-permute-start(bf16[96,6144]{1,0:T(8,128)(2,1)S(1)} %get-tuple-element.415), channel_id=1, source_target_pairs={{0,16},{1,17},{2,18},{3,19},{4,20},{5,21},{6,22},{7,23},{8,9},{9,8... | collective-permute-start | bytes 3538952 | tf_op jit(solution)/shard_map/ppermute | solution.py:275
  258.7 35.1 %collective-permute-start.62 = (bf16[96,6144]{1,0:T(8,128)(2,1)S(1)}, bf16[96,6144]{1,0:T(8,128)(2,1)S(1)}, u32[]{:S(2)}, u32[]{:S(2)}) collective-permute-start(bf16[96,6144]{1,0:T(8,128)(2,1)S(1)} %get-tuple-element.416), channel_id=1, source_target_pairs={{0,1},{1,0},{2,3},{3,2},{4,5},{5,4},{6,7},{7,6},{8,24},{9,25},{10,... | collective-permute-start | bytes 3538952 | tf_op jit(solution)/shard_map/ppermute | solution.py:275
  261.8 18.6 %collective-permute-start.56 = (bf16[24,6144]{1,0:T(8,128)(2,1)S(1)}, bf16[24,6144]{1,0:T(8,128)(2,1)S(1)}, u32[]{:S(2)}, u32[]{:S(2)}) collective-permute-start(bf16[24,6144]{1,0:T(8,128)(2,1)S(1)} %get-tuple-element.404), channel_id=1, source_target_pairs={{0,2},{1,3},{2,0},{3,1},{4,6},{5,7},{6,4},{7,5},{8,10},{9,11},{10,... | collective-permute-start | bytes 884744 | tf_op jit(solution)/shard_map/ppermute | solution.py:275
  267.2 14.3 %collective-permute-start.57 = (bf16[24,6144]{1,0:T(8,128)(2,1)S(1)}, bf16[24,6144]{1,0:T(8,128)(2,1)S(1)}, u32[]{:S(2)}, u32[]{:S(2)}) collective-permute-start(bf16[24,6144]{1,0:T(8,128)(2,1)S(1)} %get-tuple-element.405), channel_id=1, source_target_pairs={{0,4},{1,5},{2,6},{3,7},{4,0},{5,1},{6,2},{7,3},{8,12},{9,13},{10,... | collective-permute-start | bytes 884744 | tf_op jit(solution)/shard_map/ppermute | solution.py:275
  280.4 13.4 %collective-permute-start.59 = (bf16[48,3200]{1,0:T(8,128)(2,1)S(1)}, bf16[48,3200]{1,0:T(8,128)(2,1)S(1)}, u32[]{:S(2)}, u32[]{:S(2)}) collective-permute-start(bf16[48,3200]{1,0:T(8,128)(2,1)S(1)} %get-tuple-element.412), channel_id=1, source_target_pairs={{0,16},{1,17},{2,18},{3,19},{4,20},{5,21},{6,22},{7,23},{8,9},{9,8... | collective-permute-start | bytes 921608 | tf_op jit(solution)/shard_map/ppermute | solution.py:275
  281.5 12.3 %collective-permute-start.60 = (bf16[48,3200]{1,0:T(8,128)(2,1)S(1)}, bf16[48,3200]{1,0:T(8,128)(2,1)S(1)}, u32[]{:S(2)}, u32[]{:S(2)}) collective-permute-start(bf16[48,3200]{1,0:T(8,128)(2,1)S(1)} %get-tuple-element.413), channel_id=1, source_target_pairs={{0,1},{1,0},{2,3},{3,2},{4,5},{5,4},{6,7},{7,6},{8,24},{9,25},{10,... | collective-permute-start | bytes 921608 | tf_op jit(solution)/shard_map/ppermute | solution.py:275
  284.4 8.6 %collective-permute-start.58 = (bf16[24,6144]{1,0:T(8,128)(2,1)S(1)}, bf16[24,6144]{1,0:T(8,128)(2,1)S(1)}, u32[]{:S(2)}, u32[]{:S(2)}) collective-permute-start(bf16[24,6144]{1,0:T(8,128)(2,1)S(1)} %get-tuple-element.406), channel_id=1, source_target_pairs={{0,6},{1,7},{2,4},{3,5},{4,2},{5,3},{6,0},{7,1},{8,14},{9,15},{10,... | collective-permute-start | bytes 884744 | tf_op jit(solution)/shard_map/ppermute | solution.py:275
  294.1 12.1 %collective-permute-start.65 = (bf16[24,3200]{1,0:T(8,128)(2,1)S(1)}, bf16[24,3200]{1,0:T(8,128)(2,1)S(1)}, u32[]{:S(2)}, u32[]{:S(2)}) collective-permute-start(bf16[24,3200]{1,0:T(8,128)(2,1)S(1)} %get-tuple-element.435), channel_id=1, source_target_pairs={{0,2},{1,3},{2,0},{3,1},{4,6},{5,7},{6,4},{7,5},{8,10},{9,11},{10,... | collective-permute-start | bytes 460808 | tf_op jit(solution)/shard_map/ppermute | solution.py:275
  301.4 13.1 %collective-permute-start.67 = (bf16[24,3200]{1,0:T(8,128)(2,1)S(1)}, bf16[24,3200]{1,0:T(8,128)(2,1)S(1)}, u32[]{:S(2)}, u32[]{:S(2)}) collective-permute-start(bf16[24,3200]{1,0:T(8,128)(2,1)S(1)} %get-tuple-element.437), channel_id=1, source_target_pairs={{0,6},{1,7},{2,4},{3,5},{4,2},{5,3},{6,0},{7,1},{8,14},{9,15},{10,... | collective-permute-start | bytes 460808 | tf_op jit(solution)/shard_map/ppermute | solution.py:275
  303.1 16.3 %collective-permute-start.68 = (bf16[48,6144]{1,0:T(8,128)(2,1)S(1)}, bf16[48,6144]{1,0:T(8,128)(2,1)S(1)}, u32[]{:S(2)}, u32[]{:S(2)}) collective-permute-start(bf16[48,6144]{1,0:T(8,128)(2,1)S(1)} %get-tuple-element.443), channel_id=1, source_target_pairs={{0,16},{1,17},{2,18},{3,19},{4,20},{5,21},{6,22},{7,23},{8,9},{9,8... | collective-permute-start | bytes 1769480 | tf_op jit(solution)/shard_map/ppermute | solution.py:275
  304.0 16.3 %collective-permute-start.69 = (bf16[48,6144]{1,0:T(8,128)(2,1)S(1)}, bf16[48,6144]{1,0:T(8,128)(2,1)S(1)}, u32[]{:S(2)}, u32[]{:S(2)}) collective-permute-start(bf16[48,6144]{1,0:T(8,128)(2,1)S(1)} %get-tuple-element.444), channel_id=1, source_target_pairs={{0,1},{1,0},{2,3},{3,2},{4,5},{5,4},{6,7},{7,6},{8,24},{9,25},{10,... | collective-permute-start | bytes 1769480 | tf_op jit(solution)/shard_map/ppermute | solution.py:275
  306.2 25.2 %collective-permute-start.73 = (bf16[96,3200]{1,0:T(8,128)(2,1)S(1)}, bf16[96,3200]{1,0:T(8,128)(2,1)S(1)}, u32[]{:S(2)}, u32[]{:S(2)}) collective-permute-start(bf16[96,3200]{1,0:T(8,128)(2,1)S(1)} %get-tuple-element.458), channel_id=1, source_target_pairs={{0,16},{1,17},{2,18},{3,19},{4,20},{5,21},{6,22},{7,23},{8,9},{9,8... | collective-permute-start | bytes 1843208 | tf_op jit(solution)/shard_map/ppermute | solution.py:275
  306.8 24.5 %collective-permute-start.74 = (bf16[96,3200]{1,0:T(8,128)(2,1)S(1)}, bf16[96,3200]{1,0:T(8,128)(2,1)S(1)}, u32[]{:S(2)}, u32[]{:S(2)}) collective-permute-start(bf16[96,3200]{1,0:T(8,128)(2,1)S(1)} %get-tuple-element.459), channel_id=1, source_target_pairs={{0,1},{1,0},{2,3},{3,2},{4,5},{5,4},{6,7},{7,6},{8,24},{9,25},{10,... | collective-permute-start | bytes 1843208 | tf_op jit(solution)/shard_map/ppermute | solution.py:275
  320.7 13.2 %collective-permute-start.70 = (bf16[24,6144]{1,0:T(8,128)(2,1)S(1)}, bf16[24,6144]{1,0:T(8,128)(2,1)S(1)}, u32[]{:S(2)}, u32[]{:S(2)}) collective-permute-start(bf16[24,6144]{1,0:T(8,128)(2,1)S(1)} %get-tuple-element.454), channel_id=1, source_target_pairs={{0,2},{1,3},{2,0},{3,1},{4,6},{5,7},{6,4},{7,5},{8,10},{9,11},{10,... | collective-permute-start | bytes 884744 | tf_op jit(solution)/shard_map/ppermute | solution.py:275
  321.8 22.0 %collective-permute-start.71 = (bf16[24,6144]{1,0:T(8,128)(2,1)S(1)}, bf16[24,6144]{1,0:T(8,128)(2,1)S(1)}, u32[]{:S(2)}, u32[]{:S(2)}) collective-permute-start(bf16[24,6144]{1,0:T(8,128)(2,1)S(1)} %get-tuple-element.455), channel_id=1, source_target_pairs={{0,4},{1,5},{2,6},{3,7},{4,0},{5,1},{6,2},{7,3},{8,12},{9,13},{10,... | collective-permute-start | bytes 884744 | tf_op jit(solution)/shard_map/ppermute | solution.py:275
  323.5 20.3 %collective-permute-start.72 = (bf16[24,6144]{1,0:T(8,128)(2,1)S(1)}, bf16[24,6144]{1,0:T(8,128)(2,1)S(1)}, u32[]{:S(2)}, u32[]{:S(2)}) collective-permute-start(bf16[24,6144]{1,0:T(8,128)(2,1)S(1)} %get-tuple-element.456), channel_id=1, source_target_pairs={{0,6},{1,7},{2,4},{3,5},{4,2},{5,3},{6,0},{7,1},{8,14},{9,15},{10,... | collective-permute-start | bytes 884744 | tf_op jit(solution)/shard_map/ppermute | solution.py:275
  331.5 12.2 %collective-permute-start.75 = (bf16[48,3200]{1,0:T(8,128)(2,1)S(1)}, bf16[48,3200]{1,0:T(8,128)(2,1)S(1)}, u32[]{:S(2)}, u32[]{:S(2)}) collective-permute-start(bf16[48,3200]{1,0:T(8,128)(2,1)S(1)} %get-tuple-element.462), channel_id=1, source_target_pairs={{0,16},{1,17},{2,18},{3,19},{4,20},{5,21},{6,22},{7,23},{8,9},{9,8... | collective-permute-start | bytes 921608 | tf_op jit(solution)/shard_map/ppermute | solution.py:275
  333.1 10.6 %collective-permute-start.76 = (bf16[48,3200]{1,0:T(8,128)(2,1)S(1)}, bf16[48,3200]{1,0:T(8,128)(2,1)S(1)}, u32[]{:S(2)}, u32[]{:S(2)}) collective-permute-start(bf16[48,3200]{1,0:T(8,128)(2,1)S(1)} %get-tuple-element.463), channel_id=1, source_target_pairs={{0,1},{1,0},{2,3},{3,2},{4,5},{5,4},{6,7},{7,6},{8,24},{9,25},{10,... | collective-permute-start | bytes 921608 | tf_op jit(solution)/shard_map/ppermute | solution.py:275
  344.0 8.2 %collective-permute-start.77 = (bf16[24,3200]{1,0:T(8,128)(2,1)S(1)}, bf16[24,3200]{1,0:T(8,128)(2,1)S(1)}, u32[]{:S(2)}, u32[]{:S(2)}) collective-permute-start(bf16[24,3200]{1,0:T(8,128)(2,1)S(1)} %get-tuple-element.470), channel_id=1, source_target_pairs={{0,2},{1,3},{2,0},{3,1},{4,6},{5,7},{6,4},{7,5},{8,10},{9,11},{10,... | collective-permute-start | bytes 460808 | tf_op jit(solution)/shard_map/ppermute | solution.py:275
  347.8 11.7 %collective-permute-start.78 = (bf16[24,3200]{1,0:T(8,128)(2,1)S(1)}, bf16[24,3200]{1,0:T(8,128)(2,1)S(1)}, u32[]{:S(2)}, u32[]{:S(2)}) collective-permute-start(bf16[24,3200]{1,0:T(8,128)(2,1)S(1)} %get-tuple-element.471), channel_id=1, source_target_pairs={{0,4},{1,5},{2,6},{3,7},{4,0},{5,1},{6,2},{7,3},{8,12},{9,13},{10,... | collective-permute-start | bytes 460808 | tf_op jit(solution)/shard_map/ppermute | solution.py:275
  348.6 10.8 %collective-permute-start.79 = (bf16[24,3200]{1,0:T(8,128)(2,1)S(1)}, bf16[24,3200]{1,0:T(8,128)(2,1)S(1)}, u32[]{:S(2)}, u32[]{:S(2)}) collective-permute-start(bf16[24,3200]{1,0:T(8,128)(2,1)S(1)} %get-tuple-element.472), channel_id=1, source_target_pairs={{0,6},{1,7},{2,4},{3,5},{4,2},{5,3},{6,0},{7,1},{8,14},{9,15},{10,... | collective-permute-start | bytes 460808 | tf_op jit(solution)/shard_map/ppermute | solution.py:275
  (57 other events, 754.1 us)
Sparse Core Ops, SparseCore 0:
  14.1 131.6 all-gather.1
